TPU v7x, 32 devices: a whole 2x2x4 slice. The times are simulated.
32 devices in a mesh: groups: 2 (over y), seq: 4 (over z), head: 2 (over x), rep: 2 (over core).
Axes of the slice: x: 2, y: 2, z: 4, core: 2. Of those that a mesh axis runs over, the one named last changes fastest.
Arguments:
- book_tokens: bfloat16 [16384, 1024], P(('groups', 'seq', 'rep')), parts along dimension 0, may hold values from -6 to 6
- norm_gain: float32 [1024], replicated, may hold values from 0.1 to 1.9
- query_weight: bfloat16 [1024, 1024], P(None, 'head'), may hold values from -0.1875 to 0.1875
- key_weight: bfloat16 [1024, 1024], P(None, 'head'), may hold values from -0.1875 to 0.1875
- value_weight: bfloat16 [1024, 1024], P(None, 'head'), may hold values from -0.1875 to 0.1875
- proj_weight: bfloat16 [1024, 4096], P(None, 'head'), may hold values from -0.75 to 0.75
- dual_gains: float32 [4, 1024], P(None, 'head'), may hold values from 0.1 to 1.9
- out_weight: bfloat16 [1024, 1024], P(None, 'head'), may hold values from -1.5 to 1.5
- span_bounds: int32 [128, 2], P('groups'), parts along dimension 0, may hold values from 0 to 8192, as said below
Outputs:
- attended: bfloat16 [16384, 1024], P(('groups', 'seq', 'rep'), 'head'), parts along dimension 0
- pooled: float32 [128, 1024], P(('groups', 'seq', 'rep'), 'head'), parts along dimension 0
There are 2 independent parts, one for each index of `groups`. A program takes and returns all parts, laid end to end along the dimension named above; an argument that names none is the same for every part. Nothing has to cross between parts.
Inputs may be any that keep to these rules, and one draw needn't show every extreme that they name: `span_bounds`: each span lies inside the book and holds 1 to 512 tokens; spans may intersect and come in any order; the longest holds exactly 512 tokens.
All inputs are finite; a program needn't handle non-finite values.
Results may differ from a plain program's by a relative error of at most 0.023.
Values may be sent and summed in bfloat16 or wider, within the bound.
No kernel may reach another device: no remote copies, remote signals or barrier semaphores. Data moves between devices by JAX's collectives and lax.ppermute only.
A program may use at most 64 MiB of HBM per device.

v0:
```python
import jax
import jax.numpy as jnp
from jax import lax
from jax.sharding import PartitionSpec as P

DH = 64
R = 256
SEG = 128


softcap = 5.0
epsilon = 1e-05


def with_halo(cells, sides, width):
    for axis, dim in sides:
        count = lax.axis_size(axis)
        ends = count - 1
        head = lax.slice_in_dim(cells, 0, width, axis=dim)
        tail = lax.slice_in_dim(cells, cells.shape[dim] - width, cells.shape[dim], axis=dim)
        cells = jnp.concatenate(
            [
                lax.ppermute(tail, axis, [(i, (i + 1) % count) for i in range(ends)]),
                cells,
                lax.ppermute(head, axis, [((i + 1) % count, i) for i in range(ends)]),
            ],
            axis=dim,
        )
    return cells


def normalize(values, gain_row):
    centre = jnp.mean(values, axis=-1, keepdims=True)
    spread = jnp.mean(jnp.square(values - centre), axis=-1, keepdims=True)
    return (values - centre) * lax.rsqrt(spread + epsilon) * gain_row


def capped(values):
    return softcap * jnp.tanh(values / softcap)


def finish(total_numer, gain_rows):
    land_keys = normalize(total_numer[:, :, :DH], gain_rows[2][:, None, :])
    land_values = normalize(total_numer[:, :, DH:], gain_rows[3][:, None, :])
    return jnp.concatenate([land_keys, land_values], axis=-1).astype(jnp.bfloat16)


def per_device(
    book_tokens,
    norm_gain,
    query_weight,
    key_weight,
    value_weight,
    proj_weight,
    dual_gains,
    out_weight,
    span_bounds,
):
    tok_rows = book_tokens.shape[0]
    seq_devices = lax.axis_size(("seq", "rep"))
    seq_index = lax.axis_index(("seq", "rep"))
    first_row = seq_index * tok_rows
    length = tok_rows * seq_devices
    head_local = query_weight.shape[1] // DH
    normed = normalize(book_tokens.astype(jnp.float32), norm_gain).astype(jnp.bfloat16)
    queries = jnp.dot(normed, query_weight, preferred_element_type=jnp.float32).astype(jnp.bfloat16)
    queries = queries.reshape(tok_rows, head_local, DH)
    key_raw = jnp.dot(normed, key_weight, preferred_element_type=jnp.float32).reshape(
        tok_rows, head_local, DH
    )
    value_raw = jnp.dot(normed, value_weight, preferred_element_type=jnp.float32).reshape(
        tok_rows, head_local, DH
    )
    gain_rows = dual_gains.reshape(4, head_local, DH)
    near_pairs = jnp.concatenate(
        [normalize(key_raw, gain_rows[0]), normalize(value_raw, gain_rows[1])], axis=-1
    )
    near_pairs = near_pairs.astype(jnp.bfloat16)
    raw_pairs = jnp.concatenate([key_raw, value_raw], axis=-1).astype(jnp.bfloat16)
    logits = jnp.dot(normed, proj_weight, preferred_element_type=jnp.float32)
    proj_weights = jnp.exp(capped(logits)).astype(jnp.bfloat16).reshape(tok_rows, head_local, R)
    numerator = jnp.einsum(
        "nhr,nhe->hre", proj_weights, raw_pairs, preferred_element_type=jnp.float32
    )
    flat_pairs = near_pairs.reshape(tok_rows, head_local * 2 * DH)
    padded = with_halo(flat_pairs, ((("seq", "rep"), 0),), SEG // 2)
    segments = tok_rows // SEG
    blocks = padded.reshape(segments + 1, SEG, head_local, 2 * DH)
    window = jnp.concatenate([blocks[:-1], blocks[1:]], axis=1)
    position = (
        first_row + jnp.arange(segments)[:, None] * SEG + jnp.arange(2 * SEG)[None, :] - SEG // 2
    )
    inside = (position >= 0) & (position < length)
    query_blocks = queries.reshape(segments, SEG, head_local, DH)
    near_scores = jnp.einsum(
        "sqhd,skhd->shqk", query_blocks, window[..., :DH], preferred_element_type=jnp.float32
    )
    near_exp = jnp.where(inside[:, None, None, :], jnp.exp(capped(near_scores * DH ** (-0.5))), 0.0)
    total_numer = lax.psum(numerator.astype(jnp.bfloat16), ("seq", "rep")).astype(jnp.float32)
    land_pairs = finish(total_numer, gain_rows)
    far_scores = jnp.einsum(
        "sqhd,hrd->shqr", query_blocks, land_pairs[..., :DH], preferred_element_type=jnp.float32
    )
    far_exp = jnp.exp(capped(far_scores * DH ** (-0.5)))
    summed = jnp.sum(near_exp, axis=-1, keepdims=True) + jnp.sum(far_exp, axis=-1, keepdims=True)
    near_probs = (near_exp / summed).astype(jnp.bfloat16)
    far_probs = (far_exp / summed).astype(jnp.bfloat16)
    output = jnp.einsum(
        "shqk,skhd->sqhd", near_probs, window[..., DH:], preferred_element_type=jnp.float32
    )
    output = output + jnp.einsum(
        "shqr,hrd->sqhd", far_probs, land_pairs[..., DH:], preferred_element_type=jnp.float32
    )
    heads_out = output.astype(jnp.bfloat16).reshape(tok_rows, head_local * DH)
    projected = jnp.dot(
        lax.all_gather(heads_out, "head", axis=1, tiled=True),
        out_weight,
        preferred_element_type=jnp.float32,
    )
    attended = projected.astype(jnp.bfloat16)
    span_start = span_bounds[:, 0]
    span_end = span_bounds[:, 1]
    position_rows = first_row + jnp.arange(tok_rows)
    member = (position_rows[None, :] >= span_start[:, None]) & (
        position_rows[None, :] < span_end[:, None]
    )
    partial_sums = jnp.dot(
        member.astype(jnp.bfloat16), attended, preferred_element_type=jnp.float32
    )
    own_sums = lax.psum_scatter(
        partial_sums.astype(jnp.bfloat16), ("seq", "rep"), scatter_dimension=0, tiled=True
    ).astype(jnp.float32)
    span_rows = own_sums.shape[0]
    own_bounds = lax.dynamic_slice_in_dim(span_bounds, seq_index * span_rows, span_rows, 0)
    own_counts = (own_bounds[:, 1] - own_bounds[:, 0]).astype(jnp.float32)
    pooled = own_sums / own_counts[:, None]
    return (attended, pooled)


def solution(mesh):
    placed = (
        P(("groups", "seq", "rep"), None),
        P(),
        P(None, "head"),
        P(None, "head"),
        P(None, "head"),
        P(None, "head"),
        P(None, "head"),
        P(None, "head"),
        P("groups", None),
    )
    return jax.shard_map(
        per_device,
        mesh=mesh,
        in_specs=placed,
        out_specs=(P(("groups", "seq", "rep"), "head"), P(("groups", "seq", "rep"), "head")),
        check_vma=False,
    )
```

profile of v0, /device:TPU:0, one launch (start us, length us, event | category | flops | bytes accessed | tf_op | source)
XLA Modules:
  0.0 200.5 jit_solution(12161471431930354215)
XLA Ops:
  7.2 2.1 %convert_reduce_fusion = f32[1024]{0:T(1024)S(1)} fusion(bf16[1024,1024]{1,0:T(8,128)(2,1)} %param.9), kind=kLoop, calls=%fused_computation.9 | loop fusion | flops 2096128 | bytes 2101248 | tf_op jit(solution)/shard_map/reduce_sum | solution.py:33
  9.3 0.2 copy-done.2
  9.5 0.7 fusion.4
  10.2 0.7 fusion.6
  10.9 2.3 %bitcast_convert_fusion = (bf16[1024,8,64]{0,2,1:T(8,128)(2,1)}, f32[1024,512]{0,1:T(8,128)S(1)}) fusion(bf16[1024,1024]{1,0:T(8,128)(2,1)S(1)} %fusion.6, bf16[1024,512]{1,0:T(8,128)(2,1)S(1)} %copy-done), kind=kOutput, calls=%fused_computation.34 | convolution fusion | flops 1074266112 | bytes 6291456 | tf_op jit(solution)/shard_map/dot_general | solution.py:71
  13.2 0.2 bitcast_reduce_fusion.1
  13.4 0.3 multiply_reduce_fusion
  13.8 0.6 copy-done.15
  14.4 2.3 %bitcast_convert_fusion.1 = (bf16[1024,8,64]{0,2,1:T(8,128)(2,1)}, f32[1024,512]{0,1:T(8,128)S(1)}) fusion(bf16[1024,1024]{1,0:T(8,128)(2,1)S(1)} %fusion.6, bf16[1024,512]{1,0:T(8,128)(2,1)S(1)} %copy-done.15), kind=kOutput, calls=%fused_computation.37 | convolution fusion | flops 1074266112 | bytes 6291456 | tf_op jit(solution)/shard_map/dot_general | solution.py:68
  16.7 0.2 bitcast_reduce_fusion.2
  17.0 0.3 multiply_reduce_fusion.1
  17.3 0.8 copy-done.3
  18.1 0.1 mul.123
  18.3 2.2 %multiply_multiply_fusion = (bf16[1024,8,64]{0,2,1:T(8,128)(2,1)S(1)}, bf16[1024,8,64]{0,2,1:T(8,128)(2,1)S(1)}) fusion(f32[1024,512]{0,1:T(8,128)S(1)} %get-tuple-element.17, f32[8,64]{1,0:T(8,128)S(1)} %mul.128, f32[1024,8]{0,1:T(8,128)S(1)} %add_rsqrt_fusion, f32[1024,8]{0,1:T(8,128)S(1)} %broadcast_multiply_fusion, f32[8,64]{1,0:T(8,128)S(1)} %mul.123, ...), kind=kLoop, calls=%fused_computation.40 | loop fusion | flops 4194304 | bytes 6426624 | tf_op jit(solution)/shard_map/mul | solution.py:35
  20.5 0.3 maximum_convert_fusion
  20.7 0.2 fusion.54
  20.9 0.1 copy.38
  21.0 2.4 %collective-permute-start = (bf16[64,1024]{1,0:T(8,128)(2,1)S(1)}, bf16[64,1024]{1,0:T(8,128)(2,1)S(1)}, u32[]{:S(2)}, u32[]{:S(2)}) collective-permute-start(bf16[64,1024]{1,0:T(8,128)(2,1)S(1)} %copy.38), channel_id=1, source_target_pairs={{0,1},{1,4},{4,5},{5,8},{8,9},{9,12},{12,13},{2,3},{3,6},{6,7},{7,... | collective-permute-start | bytes 393224 | tf_op jit(solution)/shard_map/ppermute | solution.py:23
  23.4 0.8 copy.40
  24.2 1.5 collective-permute-start.1
  25.6 9.9 %exponential_convert_fusion = bf16[1024,2048]{1,0:T(8,128)(2,1)} fusion(bf16[1024,1024]{1,0:T(8,128)(2,1)} %copy-done.6, bf16[1024,2048]{1,0:T(8,128)(2,1)} %param.14), kind=kOutput, calls=%fused_computation.5 | convolution fusion | flops 4301258752 | bytes 10485760 | tf_op jit(solution)/shard_map/dot_general | solution.py:80
  35.6 6.5 %copy.58 = bf16[1024,2048]{0,1:T(8,128)(2,1)} copy(bf16[1024,2048]{1,0:T(8,128)(2,1)} %exponential_convert_fusion) | data formatting | bytes 8388608 | tf_op jit(solution)/shard_map/reshape | solution.py:81
  42.1 4.5 %fusion.23 = bf16[8,256,128]{2,1,0:T(8,128)(2,1)} fusion(bf16[1024,8,256]{0,2,1:T(8,128)(2,1)} %bitcast.78, bf16[1024,8,64]{0,2,1:T(8,128)(2,1)S(1)} %copy-done.17, bf16[1024,8,64]{0,2,1:T(8,128)(2,1)} %get-tuple-element.18), kind=kOutput, calls=%fused_computation.46 | convolution fusion | flops 541327360 | bytes 6815744 | tf_op jit(solution)/shard_map/nhr,nhe->hre/dot_general | solution.py:82
  46.6 0.3 all-gather.2.cloned.1.call-start
  46.9 2.6 %copy.39 = bf16[1024,1024]{1,0:T(8,128)(2,1)} copy(bf16[1024,1024]{0,1:T(8,128)(2,1)S(1)} %bitcast.75) | data formatting | bytes 4194304 | tf_op jit(solution)/shard_map/convert_element_type | solution.py:78
  49.5 3.1 %convolution_convert_fusion.1 = bf16[1024,512]{1,0:T(8,128)(2,1)S(1)} fusion(bf16[1024,1024]{1,0:T(8,128)(2,1)} %copy-done.6, bf16[1024,512]{1,0:T(8,128)(2,1)} %param.11), kind=kOutput, calls=%fused_computation.45 | convolution fusion | flops 1074266112 | bytes 4194304 | tf_op jit(solution)/shard_map/dot_general | solution.py:66
  52.6 2.1 %reshape.140 = bf16[8,128,8,64]{3,2,1,0:T(8,128)(2,1)} reshape(bf16[1024,512]{1,0:T(8,128)(2,1)S(1)} %convolution_convert_fusion.1) | data formatting | bytes 2097152 | tf_op jit(solution)/shard_map/reshape;reshape | solution.py:94
  54.7 2.4 %copy.45 = bf16[8,128,8,64]{1,3,2,0:T(8,128)(2,1)S(1)} copy(bf16[8,128,8,64]{3,2,1,0:T(8,128)(2,1)} %reshape.140) | data formatting | bytes 2097152 | tf_op jit(solution)/shard_map/reshape;reshape | solution.py:94
  57.4 1.9 fusion.15
  59.3 2.0 copy.64
  61.2 4.3 %copy.42 = bf16[8,128,8,128]{1,3,2,0:T(8,128)(2,1)} copy(bf16[8,128,8,128]{3,2,1,0:T(8,128)(2,1)} %bitcast.76) | data formatting | bytes 4194304 | tf_op jit(solution)/shard_map/slice | solution.py:89
  65.5 1.9 copy.65
  67.5 4.3 %copy.43 = bf16[8,128,8,128]{1,3,2,0:T(8,128)(2,1)} copy(bf16[8,128,8,128]{3,2,1,0:T(8,128)(2,1)} %bitcast.77) | data formatting | bytes 4194304 | tf_op jit(solution)/shard_map/slice | solution.py:89
  71.7 7.5 %fusion.1 = (f32[8,8,128]{2,1,0:T(8,128)S(1)}, f32[8,8,128,256]{3,2,1,0:T(8,128)}) fusion(pred[8,256]{1,0:T(8,128)(4,1)S(1)} %fusion.45, bf16[8,128,8,64]{1,3,2,0:T(8,128)(2,1)S(1)} %copy.45, bf16[8,128,8,128]{1,3,2,0:T(8,128)(2,1)} %copy.43, bf16[8,128,8,128]{1,3,2,0:T(8,128)(2,1)S(1)} %copy-done.7), kind=kOutput, calls=%fused_computation.7 | convolution fusion | flops 281010176 | bytes 13666304 | tf_op jit(solution)/shard_map/sqhd,skhd->shqk/dot_general | solution.py:95
  79.2 28.3 %all-reduce.2.cloned.1.call-done = bf16[8,256,128]{2,1,0:T(8,128)(2,1)} async-done(((bf16[8,256,128]{2,1,0:T(8,128)(2,1)}), bf16[8,256,128]{2,1,0:T(8,128)(2,1)}) %all-reduce.2.cloned.1.call-update) | async-done | bytes 524304 | tf_op jit(solution)/shard_map/psum | solution.py:99
  107.5 1.1 convert_element_type.57
  108.7 0.9 slice_reduce_fusion
  109.6 1.6 multiply_reduce_fusion.2
  111.2 3.9 %bitcast_reduce_fusion = (f32[8,8,128]{2,1,0:T(8,128)S(1)}, f32[8,256,8,128]{1,3,0,2:T(8,128)S(1)}) fusion(bf16[8,128,8,64]{1,3,2,0:T(8,128)(2,1)S(1)} %copy-done.10, f32[8,256,128]{2,1,0:T(8,128)S(1)} %convert_element_type.57, f32[8,64]{1,0:T(8,128)S(1)} %mul.138, f32[8,256]{1,0:T(8,128)S(1)} %add_rsqrt_fusion.3, f32[8,256]{1,0:T(8,128)S(1)} %get-tuple-element.25), kind=kOutput, calls=%fused_computation.1 | convolution fusion | flops 275243008 | bytes 10536960 | tf_op jit(solution)/shard_map/sqhd,hrd->shqr/dot_general | solution.py:101
  115.2 5.2 %fusion.8 = f32[8,64,8,128]{3,1,0,2:T(8,128)S(1)} fusion(f32[8,256,8,128]{1,3,0,2:T(8,128)S(1)} %get-tuple-element.23, f32[8,8,128]{2,1,0:T(8,128)S(1)} %add.118, f32[8,256,128]{2,1,0:T(8,128)S(1)} %convert_element_type.57, f32[8,64]{1,0:T(8,128)S(1)} %mul.144, f32[8,256]{1,0:T(8,128)S(1)} %add_rsqrt_fusion.2, f32[8,256]{1,0:T(8,128)S(1)} %get-tuple-element.24), kind=kOutput, calls=%fused_computation.19 | convolution fusion | flops 277348352 | bytes 11585536 | tf_op jit(solution)/shard_map/shqr,hrd->sqhd/dot_general | solution.py:111
  120.4 3.8 %fusion.20 = bf16[8,128,8,64]{1,3,2,0:T(8,128)(2,1)S(1)} fusion(f32[8,64,8,128]{3,1,0,2:T(8,128)S(1)} %fusion.8, f32[8,8,128,256]{3,2,1,0:T(8,128)S(1)} %bitcast.84, f32[8,8,128]{2,1,0:T(8,128)S(1)} %add.118, pred[8,256]{1,0:T(8,128)(4,1)S(1)} %fusion.45, bf16[8,128,8,128]{1,3,2,0:T(8,128)(2,1)S(1)} %copy-done.7, bf16[8,128,8,128]{1,3,2,0:T(8,128)(2,1)S(1)} %copy-done.8), kind=kOutput, calls=%fused_computation.33 | convolution fusion | flops 284164096 | bytes 15763456 | tf_op jit(solution)/shard_map/shqk,skhd->sqhd/dot_general | solution.py:108
  124.1 0.7 copy.52
  124.9 1.3 copy.68
  126.3 32.1 %all-gather.2.cloned.1.call-done = bf16[1024,1024]{0,1:T(8,128)(2,1)} async-done(((bf16[1024,512]{0,1:T(8,128)(2,1)}), bf16[1024,1024]{0,1:T(8,128)(2,1)}) %all-gather.2.cloned.1.call-update) | async-done | bytes 2097168 | tf_op jit(solution)/shard_map/all_gather | solution.py:116
  158.4 3.0 %convolution_convert_fusion = bf16[1024,512]{1,0:T(8,128)(2,1)S(1)} fusion(bf16[1024,1024]{0,1:T(8,128)(2,1)} %all-gather.2.cloned.1.call-done, bf16[1024,512]{1,0:T(8,128)(2,1)S(1)} %copy-done.16), kind=kOutput, calls=%fused_computation.44 | convolution fusion | flops 1074266112 | bytes 4194304 | tf_op jit(solution)/shard_map/dot_general | solution.py:115
  161.4 1.0 convolution_convert_fusion.2
  162.4 30.2 %reduce-scatter.2.cloned.1.call-done = bf16[8,512]{1,0:T(8,128)(2,1)} async-done(((bf16[64,512]{1,0:T(8,128)(2,1)}), bf16[8,512]{1,0:T(8,128)(2,1)}) %reduce-scatter.2.cloned.1.call-update) | async-done | bytes 8208 | tf_op jit(solution)/shard_map/reduce_scatter | solution.py:130
  192.6 1.4 convert_divide_fusion
  (65 shorter events, 0.7 us)
Async XLA Ops:
  7.2 3.7 %copy-start = (bf16[1024,512]{1,0:T(8,128)(2,1)S(1)}, bf16[1024,512]{1,0:T(8,128)(2,1)}, u32[]{:S(2)}) copy-start(bf16[1024,512]{1,0:T(8,128)(2,1)} %param.13) | copy-start | bytes 3145732
  7.2 2.3 %copy-start.2 = (bf16[1024,1024]{1,0:T(8,128)(2,1)S(1)}, bf16[1024,1024]{1,0:T(8,128)(2,1)}, u32[]{:S(2)}) copy-start(bf16[1024,1024]{1,0:T(8,128)(2,1)} %param.9) | copy-start | bytes 6291460
  7.2 3.0 %copy-start.13 = (f32[1024]{0:T(1024)S(1)}, f32[1024]{0:T(1024)}, u32[]{:S(2)}) copy-start(f32[1024]{0:T(1024)} %param.10) | copy-start | bytes 12292
  7.2 100.3 %all-reduce.2.cloned.1.call-start = ((), (), s32[]{:S(2)}) async-start(), calls=%async_computation.1 | async-start | bytes 1048576 | tf_op jit(solution)/shard_map/psum | solution.py:99
  10.9 2.9 %copy-start.6 = (bf16[1024,1024]{1,0:T(8,128)(2,1)}, bf16[1024,1024]{1,0:T(8,128)(2,1)S(1)}, u32[]{:S(2)}) copy-start(bf16[1024,1024]{1,0:T(8,128)(2,1)S(1)} %fusion.6) | copy-start | bytes 6291460
  13.2 1.2 copy-start.15
  16.7 1.4 copy-start.3
  16.7 1.4 copy-start.12
  21.0 36.3 %collective-permute-start = (bf16[64,1024]{1,0:T(8,128)(2,1)S(1)}, bf16[64,1024]{1,0:T(8,128)(2,1)S(1)}, u32[]{:S(2)}, u32[]{:S(2)}) collective-permute-start(bf16[64,1024]{1,0:T(8,128)(2,1)S(1)} %copy.38), channel_id=1, source_target_pairs={{0,1},{1,4},{4,5},{5,8},{8,9},{9,12},{12,13},{2,3},{3,6},{6,7},{7,... | collective-permute-start | bytes 393224 | tf_op jit(solution)/shard_map/ppermute | solution.py:23
  24.2 33.2 %collective-permute-start.1 = (bf16[64,1024]{1,0:T(8,128)(2,1)}, bf16[64,1024]{1,0:T(8,128)(2,1)S(1)}, u32[]{:S(2)}, u32[]{:S(2)}) collective-permute-start(bf16[64,1024]{1,0:T(8,128)(2,1)} %copy.40), channel_id=1, source_target_pairs={{1,0},{4,1},{5,4},{8,5},{9,8},{12,9},{13,12},{3,2},{6,3},{7,6},{10... | collective-permute-start | bytes 393224 | tf_op jit(solution)/shard_map/ppermute | solution.py:25
  35.6 6.5 %copy-start.17 = (bf16[1024,8,64]{0,2,1:T(8,128)(2,1)S(1)}, bf16[1024,8,64]{0,2,1:T(8,128)(2,1)}, u32[]{:S(2)}) copy-start(bf16[1024,8,64]{0,2,1:T(8,128)(2,1)} %get-tuple-element.16) | copy-start | bytes 3145732
  46.6 111.8 %all-gather.2.cloned.1.call-start = ((), (), s32[]{:S(2)}) async-start(), calls=%async_computation.2 | async-start | bytes 3145728 | tf_op jit(solution)/shard_map/all_gather | solution.py:116
  54.7 2.7 %copy-start.4 = (bf16[1024,1024]{1,0:T(8,128)(2,1)S(1)}, bf16[1024,1024]{1,0:T(8,128)(2,1)}, u32[]{:S(2)}) copy-start(bf16[1024,1024]{1,0:T(8,128)(2,1)} %copy.39) | copy-start | bytes 6291460
  57.1 14.6 %copy-start.9 = (bf16[8,128,8,64]{1,3,2,0:T(8,128)(2,1)}, bf16[8,128,8,64]{1,3,2,0:T(8,128)(2,1)S(1)}, u32[]{:S(2)}) copy-start(bf16[8,128,8,64]{1,3,2,0:T(8,128)(2,1)S(1)} %copy.45) | copy-start | bytes 3145732
  61.2 4.3 %copy-start.5 = (bf16[128,8,8,128]{3,1,2,0:T(8,128)(2,1)S(1)}, bf16[128,8,8,128]{3,1,2,0:T(8,128)(2,1)}, u32[]{:S(2)}) copy-start(bf16[128,8,8,128]{3,1,2,0:T(8,128)(2,1)} %get-tuple-element.11) | copy-start | bytes 6291460
  67.5 4.3 %copy-start.7 = (bf16[8,128,8,128]{1,3,2,0:T(8,128)(2,1)S(1)}, bf16[8,128,8,128]{1,3,2,0:T(8,128)(2,1)}, u32[]{:S(2)}) copy-start(bf16[8,128,8,128]{1,3,2,0:T(8,128)(2,1)} %copy.42) | copy-start | bytes 6291460
  108.6 2.5 %copy-start.10 = (bf16[8,128,8,64]{1,3,2,0:T(8,128)(2,1)S(1)}, bf16[8,128,8,64]{1,3,2,0:T(8,128)(2,1)}, u32[]{:S(2)}) copy-start(bf16[8,128,8,64]{1,3,2,0:T(8,128)(2,1)} %copy-done.9) | copy-start | bytes 3145732
  111.2 9.2 %slice-start = ((s8[8388608]{0:T(1024)(128)(4,1)}), s8[4194304]{0:T(1024)(128)(4,1)S(1)}, s32[]{:S(2)}) async-start(s8[8388608]{0:T(1024)(128)(4,1)} %bitcast.83), calls=%async_computation.4 | async-start | bytes 8388608
  115.2 5.2 %copy-start.8 = (bf16[8,128,8,128]{1,3,2,0:T(8,128)(2,1)S(1)}, bf16[8,128,8,128]{1,3,2,0:T(8,128)(2,1)}, u32[]{:S(2)}) copy-start(bf16[8,128,8,128]{1,3,2,0:T(8,128)(2,1)} %copy.43) | copy-start | bytes 6291460
  115.2 5.2 %slice-start.1 = ((s8[8388608]{0:T(1024)(128)(4,1)}), s8[4194304]{0:T(1024)(128)(4,1)S(1)}, s32[]{:S(2)}) async-start(s8[8388608]{0:T(1024)(128)(4,1)} %bitcast.83), calls=%async_computation.5 | async-start | bytes 8388608
  124.8 1.4 copy-start.14
  124.9 33.5 %copy-start.16 = (bf16[1024,512]{1,0:T(8,128)(2,1)S(1)}, bf16[1024,512]{1,0:T(8,128)(2,1)}, u32[]{:S(2)}) copy-start(bf16[1024,512]{1,0:T(8,128)(2,1)} %param.16) | copy-start | bytes 3145732
  126.1 66.4 %reduce-scatter.2.cloned.1.call-start = ((), (), s32[]{:S(2)}) async-start(), calls=%async_computation.3 | async-start | bytes 73728 | tf_op jit(solution)/shard_map/reduce_scatter | solution.py:130
  158.4 35.6 %copy-start.1 = (bf16[1024,512]{1,0:T(8,128)(2,1)S(1)}, bf16[1024,512]{1,0:T(8,128)(2,1)}, u32[]{:S(2)}) copy-start(bf16[1024,512]{1,0:T(8,128)(2,1)} %param.13) | copy-start | bytes 3145732
  161.4 32.6 %copy-start.11 = (bf16[1024,512]{1,0:T(8,128)(2,1)}, bf16[1024,512]{1,0:T(8,128)(2,1)S(1)}, u32[]{:S(2)}) copy-start(bf16[1024,512]{1,0:T(8,128)(2,1)S(1)} %convolution_convert_fusion) | copy-start | bytes 3145732
Sparse Core Ops, SparseCore 0:
  46.8 60.7 all-reduce.1
  126.3 32.0 all-gather.1
  162.5 30.0 reduce-scatter.1
where the time goes:
time: 201 us; the launch traced here: 200 us
  waiting for transfers between devices  90.6 us (45%)
  matrix products  46.4 us (23%)
  local copies, waits for them, and re-layouts  31.1 us (15%)
  between operations  14.2 us (7%)
  other arithmetic  14 us (7%)
  starting transfers between devices  4.17 us (2%)
    all_gather x1, waiting for transfers between devices, per_device(): lax.all_gather(heads_out, 'head', axis=1, tiled=True)  32.1 us
    reduce_scatter x1, waiting for transfers between devices, per_device(): lax.psum_scatter(partial_sums.astype(jnp.bfloat16), ('seq', 'rep'), scatt...  30.2 us
    psum x1, waiting for transfers between devices, per_device(): lax.psum(numerator.astype(jnp.bfloat16), ('seq', 'rep')).astype(jnp.float32)  28.3 us
    dot_general x1, matrix products, per_device(): logits = jnp.dot(normed, proj_weight, preferred_element_type=jnp.float32)  9.95 us
    slice x2, local copies, waits for them, and re-layouts, per_device(): window = jnp.concatenate([blocks[:-1], blocks[1:]], axis=1)  8.56 us
    dot_general x1, matrix products, per_device(): jnp.einsum('sqhd,skhd->shqk', query_blocks, window[..., :DH], preferred_e...  7.46 us
    unnamed x43, local copies, waits for them, and re-layouts  6.76 us
    reshape x1, local copies, waits for them, and re-layouts, per_device(): jnp.exp(capped(logits)).astype(jnp.bfloat16)  6.49 us
  transfers between devices with their start and end apart: 5, of which 3 were waited for; matrix products, arithmetic and copies ran while one was open for 27% of the time, Pallas kernels for 0%

commit v1 on v0

v1 whole, which is shorter than its diff:
```python
import functools

import jax
import jax.numpy as jnp
from jax import lax
from jax.experimental import pallas as pl
from jax.experimental.pallas import tpu as pltpu
from jax.sharding import PartitionSpec as P

DH = 64
R = 256
SEG = 128
HALF = SEG // 2
LANES = 2 * DH
SCORE_SCALE = DH ** (-0.5)
LOG2E = 1.4426950408889634

softcap = 5.0
epsilon = 1e-05

BF = jnp.bfloat16
F32 = jnp.float32
VMEM_LIMIT = 48 << 20


def dot(a, b, dims=((1,), (0,))):
    return lax.dot_general(a, b, (dims, ((), ())), preferred_element_type=F32)


def exp_capped(values, scale):
    return jnp.exp2((softcap * LOG2E) * jnp.tanh(values * (scale / softcap)))


def vmem():
    return pl.BlockSpec(memory_space=pltpu.VMEM)


def smem():
    return pl.BlockSpec(memory_space=pltpu.SMEM)


def head_mean_matrix(width):
    row = lax.broadcasted_iota(jnp.int32, (width, width), 0) // DH
    col = lax.broadcasted_iota(jnp.int32, (width, width), 1) // DH
    return jnp.where(row == col, 1.0 / DH, 0.0).astype(BF)


def head_norm(values, means, gain):
    high = values.astype(BF)
    low = (values - high.astype(F32)).astype(BF)
    centred = values - (dot(high, means) + dot(low, means))
    spread = dot((centred * centred).astype(BF), means)
    return (centred * lax.rsqrt(spread + epsilon) * gain).astype(BF)


def front_kernel(first, pairs, tile, *refs):
    if first:
        (ids_ref, x_ref, gain_ref, wq_ref, wk_ref, wv_ref, wp_ref, dual_ref,
         normed_ref, q_ref, near_ref, keep_ref, send_ref, raw_ref, p_ref) = refs
    else:
        (ids_ref, normed_ref, wq_ref, wk_ref, wv_ref, wp_ref, dual_ref,
         q_ref, near_ref, keep_ref, send_ref, raw_ref, p_ref) = refs
    rows = normed_ref.shape[0]
    width = pairs * LANES
    means = head_mean_matrix(width)
    for start in range(0, rows, tile):
        at = pl.ds(start, tile)
        if first:
            x = x_ref[at, :].astype(F32)
            centred = x - jnp.mean(x, axis=-1, keepdims=True)
            spread = jnp.mean(centred * centred, axis=-1, keepdims=True)
            normed_ref[at, :] = (centred * lax.rsqrt(spread + epsilon) * gain_ref[...]).astype(BF)
        normed = normed_ref[at, :]
        q_ref[at, :] = dot(normed, wq_ref[...]).astype(BF)
        key = dot(normed, wk_ref[...])
        value = dot(normed, wv_ref[...])
        near_ref[at, :width] = head_norm(key, means, dual_ref[0:1, :])
        near_ref[at, width:] = head_norm(value, means, dual_ref[1:2, :])
        for p in range(pairs):
            raw_ref[at, 2 * p * LANES : (2 * p + 1) * LANES] = key[:, p * LANES : (p + 1) * LANES].astype(BF)
            raw_ref[at, (2 * p + 1) * LANES : (2 * p + 2) * LANES] = value[:, p * LANES : (p + 1) * LANES].astype(BF)
        for p in range(pairs):
            cols = slice(2 * p * R, 2 * (p + 1) * R)
            p_ref[at, cols] = exp_capped(dot(normed, wp_ref[:, cols]), 1.0).astype(BF)
    total = []
    for p in range(pairs):
        full = dot(raw_ref[:, 2 * p * LANES : 2 * (p + 1) * LANES], p_ref[:, 2 * p * R : 2 * (p + 1) * R], ((0,), (0,)))
        for part in range(4):
            head = part % 2
            total.append(full[part * DH : (part + 1) * DH, head * R : (head + 1) * R])
    total = jnp.concatenate(total, axis=0).astype(BF)
    half = total.shape[0] // 2
    mine = ids_ref[0] == 0
    keep_ref[...] = jnp.where(mine, total[:half], total[half:])
    send_ref[...] = jnp.where(mine, total[half:], total[:half])


def front(first, group, pairs, ids, tokens, gain, wq, wk, wv, wp, dual):
    rows, depth = tokens.shape
    width = pairs * LANES
    half = pairs * R // 2
    outs = [
        jax.ShapeDtypeStruct((rows, width), BF),
        jax.ShapeDtypeStruct((rows, 2 * width), BF),
        jax.ShapeDtypeStruct((half, R), BF),
        jax.ShapeDtypeStruct((half, R), BF),
    ]
    ins = [smem(), vmem()]
    args = [ids, tokens]
    if first:
        outs = [jax.ShapeDtypeStruct((rows, depth), BF)] + outs
        ins.append(vmem())
        args.append(gain)
    at = lambda i: (0, group)
    ins += [pl.BlockSpec((depth, width), at)] * 3
    ins += [pl.BlockSpec((depth, 2 * pairs * R), at), pl.BlockSpec((4, width), at)]
    args += [wq, wk, wv, wp, dual]
    whole = lambda s: pl.BlockSpec(s.shape, lambda i: (0, 0))
    ins = [
        s if s.block_shape is not None or s.memory_space == pltpu.SMEM else pl.BlockSpec(a.shape, lambda i: (0, 0))
        for s, a in zip(ins, args)
    ]
    return pl.pallas_call(
        functools.partial(front_kernel, first, pairs, min(256, rows)),
        grid=(1,),
        in_specs=ins,
        out_specs=[whole(s) for s in outs],
        out_shape=outs,
        scratch_shapes=[pltpu.VMEM((rows, 2 * width), BF), pltpu.VMEM((rows, 2 * pairs * R), BF)],
        compiler_params=pltpu.CompilerParams(vmem_limit_bytes=VMEM_LIMIT),
        cost_estimate=pl.CostEstimate(
            flops=2 * rows * depth * (3 * width + 2 * pairs * R) * 2, bytes_accessed=8 << 20, transcendentals=0
        ),
        name="front",
    )(*args)


def lane_is_first(shape):
    return lax.broadcasted_iota(jnp.int32, shape, 1) < DH


def stacked(q):
    first = lane_is_first(q.shape)
    zero = jnp.zeros_like(q)
    return jnp.concatenate([jnp.where(first, q, zero), jnp.where(first, zero, q)], axis=0)


def unstack(both):
    rows = both.shape[0] // 2
    first = lane_is_first((rows, LANES))
    return (
        jnp.where(first, both[:rows, :LANES], both[rows:, :LANES]),
        jnp.where(first, both[:rows, LANES:], both[rows:, LANES:]),
    )


def near_kernel(pairs, ids_ref, q_ref, near_ref, prev_ref, next_ref, out_ref, pad_ref):
    rows = q_ref.shape[0]
    width = pairs * LANES
    pad_ref[0:HALF, :] = prev_ref[...]
    pad_ref[HALF : HALF + rows, :] = near_ref[...]
    pad_ref[HALF + rows :, :] = next_ref[...]
    row = lax.broadcasted_iota(jnp.int32, (2 * SEG, LANES), 0)
    ones = jnp.ones((2 * SEG, LANES), F32)
    has_prev = jnp.where(ids_ref[1] != 0, 1.0, 0.0)
    has_next = jnp.where(ids_ref[2] != 0, 1.0, 0.0)
    segments = rows // SEG
    for s in range(segments):
        count = ones
        if s == 0:
            count = jnp.where(row < HALF, has_prev, count)
        if s == segments - 1:
            count = jnp.where(row >= 3 * HALF, has_next, count)
        count = count.astype(BF)
        window = pl.ds(s * SEG, 2 * SEG)
        for p in range(pairs):
            cols = slice(p * LANES, (p + 1) * LANES)
            q = stacked(q_ref[s * SEG : (s + 1) * SEG, cols])
            scores = dot(q, pad_ref[window, cols], ((1,), (1,)))
            weights = exp_capped(scores, SCORE_SCALE).astype(BF)
            values = jnp.concatenate([pad_ref[window, width + p * LANES : width + (p + 1) * LANES], count], axis=1)
            top, bottom = unstack(dot(weights, values))
            out_ref[s * SEG : (s + 1) * SEG, 2 * p * LANES : (2 * p + 1) * LANES] = top
            out_ref[s * SEG : (s + 1) * SEG, (2 * p + 1) * LANES : (2 * p + 2) * LANES] = bottom


def near(pairs, ids, q, pairs_own, prev, following, group):
    rows = q.shape[0]
    width = pairs * LANES
    at = lambda i: (0, 0)
    return pl.pallas_call(
        functools.partial(near_kernel, pairs),
        grid=(1,),
        in_specs=[smem(), pl.BlockSpec(q.shape, at), pl.BlockSpec(pairs_own.shape, at)]
        + [pl.BlockSpec((HALF, 2 * width), lambda i: (0, group))] * 2,
        out_specs=pl.BlockSpec((rows, 2 * width), at),
        out_shape=jax.ShapeDtypeStruct((rows, 2 * width), F32),
        scratch_shapes=[pltpu.VMEM((rows + SEG, 2 * width), BF)],
        compiler_params=pltpu.CompilerParams(vmem_limit_bytes=VMEM_LIMIT),
        cost_estimate=pl.CostEstimate(flops=rows * pairs * (1 << 19), bytes_accessed=4 << 20, transcendentals=0),
        name="near",
    )(ids, q, pairs_own, prev, following)


def far_kernel(pairs, block, ids_ref, q_ref, near_ref, mine_ref, other_ref, gains_ref, bounds_ref, out_ref, sums_ref):
    rows = q_ref.shape[0]
    is_first = ids_ref[0] == 0
    top = jnp.where(is_first, mine_ref[...], other_ref[...])
    bottom = jnp.where(is_first, other_ref[...], mine_ref[...])
    total = jnp.concatenate([top, bottom], axis=0)
    ones = jnp.ones((LANES, R), BF)
    for p in range(pairs):
        cols = slice(p * LANES, (p + 1) * LANES)

        def land(kind):
            parts = []
            for h in range(2):
                at = p * R + kind * LANES + h * DH
                values = total[at : at + DH].astype(F32)
                centred = values - jnp.mean(values, axis=0, keepdims=True)
                spread = jnp.mean(centred * centred, axis=0, keepdims=True)
                gain = gains_ref[p * LANES + h * DH : p * LANES + (h + 1) * DH, 2 + kind : 3 + kind]
                parts.append((centred * lax.rsqrt(spread + epsilon) * gain).astype(BF))
            return jnp.concatenate(parts, axis=0)

        keys = land(0)
        values = jnp.concatenate([land(1), ones], axis=0)
        for start in range(0, rows, block):
            q = stacked(q_ref[start : start + block, cols])
            weights = exp_capped(dot(q, keys), SCORE_SCALE).astype(BF)
            top, bottom = unstack(dot(weights, values, ((1,), (1,))))
            top = top + near_ref[start : start + block, 2 * p * LANES : (2 * p + 1) * LANES]
            bottom = bottom + near_ref[start : start + block, (2 * p + 1) * LANES : (2 * p + 2) * LANES]
            out_ref[start : start + block, cols] = (top / bottom).astype(BF)
    spans = bounds_ref.shape[0]
    position = ids_ref[3] + lax.broadcasted_iota(jnp.int32, (spans, rows), 1)
    member = (position >= bounds_ref[:, 0:1]) & (position < bounds_ref[:, 1:2])
    member = jnp.where(member, 1.0, 0.0).astype(BF)
    sums_ref[...] = dot(member, out_ref[...]).astype(BF)


def far(pairs, ids, q, near_sums, mine, other, gains, bounds, group):
    rows = q.shape[0]
    width = pairs * LANES
    at = lambda i: (0, 0)
    return pl.pallas_call(
        functools.partial(far_kernel, pairs, 256),
        grid=(1,),
        in_specs=[
            smem(),
            pl.BlockSpec(q.shape, at),
            pl.BlockSpec(near_sums.shape, at),
            pl.BlockSpec(mine.shape, at),
            pl.BlockSpec(other.shape, at),
            pl.BlockSpec((width, 4), lambda i: (group, 0)),
            pl.BlockSpec(bounds.shape, at),
        ],
        out_specs=[pl.BlockSpec((rows, width), at), pl.BlockSpec((bounds.shape[0], width), at)],
        out_shape=[jax.ShapeDtypeStruct((rows, width), BF), jax.ShapeDtypeStruct((bounds.shape[0], width), BF)],
        compiler_params=pltpu.CompilerParams(vmem_limit_bytes=VMEM_LIMIT),
        cost_estimate=pl.CostEstimate(flops=rows * pairs * (1 << 19), bytes_accessed=4 << 20, transcendentals=0),
        name="far",
    )(ids, q, near_sums, mine, other, gains, bounds)


def out_kernel(count, final, *refs):
    refs = refs[1:]
    tokens, weights = refs[:count], refs[count : 2 * count]
    out_ref = refs[-1]
    acc = refs[2 * count][...] if len(refs) == 2 * count + 2 else None
    for a, w in zip(tokens, weights):
        term = dot(a[...], w[...])
        acc = term if acc is None else acc + term
    out_ref[...] = acc.astype(out_ref.dtype)


def out_part(parts, index, weight, acc, dtype):
    count = len(parts)
    rows, width = parts[0].shape
    columns = weight.shape[1]
    tile = min(256, rows)
    row_spec = pl.BlockSpec((tile, width), lambda i, ids: (i, 0))
    weight_specs = [pl.BlockSpec((width, columns), lambda i, ids, j=j: (ids[j], 0)) for j in range(count)]
    out_spec = pl.BlockSpec((tile, columns), lambda i, ids: (i, 0))
    extra = [] if acc is None else [acc]
    return pl.pallas_call(
        functools.partial(out_kernel, count, acc is not None),
        grid_spec=pltpu.PrefetchScalarGridSpec(
            num_scalar_prefetch=1,
            grid=(rows // tile,),
            in_specs=[row_spec] * count + weight_specs + [out_spec] * len(extra),
            out_specs=out_spec,
        ),
        out_shape=jax.ShapeDtypeStruct((rows, columns), dtype),
        compiler_params=pltpu.CompilerParams(vmem_limit_bytes=VMEM_LIMIT),
        cost_estimate=pl.CostEstimate(
            flops=2 * rows * width * columns * count, bytes_accessed=4 << 20, transcendentals=0
        ),
        name="out",
    )(index, *parts, *([weight] * count), *extra)


def swap(values, axis, step):
    count = lax.axis_size(axis)
    return lax.ppermute(values, axis, [(i, i ^ step) for i in range(count)])


def add(a, b):
    return (a.astype(F32) + b.astype(F32)).astype(BF)


def steps_of(axis):
    step = 1
    while step < lax.axis_size(axis):
        yield step
        step *= 2


def per_device(
    book_tokens,
    norm_gain,
    query_weight,
    key_weight,
    value_weight,
    proj_weight,
    dual_gains,
    out_weight,
    span_bounds,
):
    rows = book_tokens.shape[0]
    seq_devices = lax.axis_size(("seq", "rep"))
    seq_index = lax.axis_index(("seq", "rep"))
    head_devices = lax.axis_size("head")
    head_index = lax.axis_index("head")
    first_row = seq_index * rows
    all_pairs = query_weight.shape[1] // LANES
    groups = 2 if all_pairs % 2 == 0 else 1
    pairs = all_pairs // groups
    ids = jnp.stack(
        [lax.axis_index("rep"), (seq_index > 0).astype(jnp.int32), (seq_index < seq_devices - 1).astype(jnp.int32), first_row]
    ).astype(jnp.int32)
    gain = norm_gain[None, :]
    gain_columns = dual_gains.T

    fronts = []
    tokens = book_tokens
    for g in range(groups):
        outs = front(g == 0, g, pairs, ids, tokens, gain, query_weight, key_weight, value_weight, proj_weight, dual_gains)
        if g == 0:
            tokens, outs = outs[0], outs[1:]
        fronts.append(outs)

    totals = []
    for q, near_pairs, keep, send in fronts:
        mine = add(keep, swap(send, "rep", 1))
        for step in steps_of("seq"):
            mine = add(mine, swap(mine, "seq", step))
        totals.append((mine, swap(mine, "rep", 1)))

    tails = jnp.concatenate([f[1][rows - HALF :] for f in fronts], axis=1)
    heads = jnp.concatenate([f[1][:HALF] for f in fronts], axis=1)
    both = ("seq", "rep")
    prev = lax.ppermute(tails, both, [(i, i + 1) for i in range(seq_devices - 1)])
    following = lax.ppermute(heads, both, [(i + 1, i) for i in range(seq_devices - 1)])

    nears = [near(pairs, ids, f[0], f[1], prev, following, g) for g, f in enumerate(fronts)]
    outs = [
        far(pairs, ids, fronts[g][0], nears[g], *totals[g], gain_columns, span_bounds, g) for g in range(groups)
    ]

    own_index = [head_index * groups + g for g in range(groups)]
    others, other_index = [], []
    for g in range(groups):
        for k in range(1, head_devices):
            others.append(lax.ppermute(outs[g][0], "head", [(i, (i + k) % head_devices) for i in range(head_devices)]))
            other_index.append(lax.rem(head_index - k + head_devices, head_devices) * groups + g)
    early = len(others) - (head_devices - 1)
    parts = [o[0] for o in outs] + others[:early]
    index = jnp.stack(own_index + other_index[:early]).astype(jnp.int32)
    acc = out_part(parts, index, out_weight, None, F32)
    index = jnp.stack(other_index[early:]).astype(jnp.int32)
    attended = out_part(others[early:], index, out_weight, acc, BF)

    sums = jnp.concatenate([o[1] for o in outs], axis=1)
    sums = add(sums, swap(sums, "rep", 1))
    for step in steps_of("seq"):
        sums = add(sums, swap(sums, "seq", step))
    span_rows = sums.shape[0] // seq_devices
    own_bounds = lax.dynamic_slice_in_dim(span_bounds, seq_index * span_rows, span_rows, 0)
    counts = (own_bounds[:, 1] - own_bounds[:, 0]).astype(F32)
    own = lax.dynamic_slice_in_dim(sums, seq_index * span_rows, span_rows, 0)
    width = own.shape[1]
    spread = [own] + [
        lax.ppermute(own, "head", [(i, (i + k) % head_devices) for i in range(head_devices)])
        for k in range(1, head_devices)
    ]
    pooled = None
    for k, values in enumerate(spread):
        source = lax.rem(head_index - k + head_devices, head_devices)
        weight = lax.dynamic_slice_in_dim(out_weight, source * width, width, 0)
        term = jnp.dot(values, weight, preferred_element_type=F32)
        pooled = term if pooled is None else pooled + term
    pooled = pooled / counts[:, None]
    return (attended, pooled)


def solution(mesh):
    placed = (
        P(("groups", "seq", "rep"), None),
        P(),
        P(None, "head"),
        P(None, "head"),
        P(None, "head"),
        P(None, "head"),
        P(None, "head"),
        P(None, "head"),
        P("groups", None),
    )
    return jax.shard_map(
        per_device,
        mesh=mesh,
        in_specs=placed,
        out_specs=(P(("groups", "seq", "rep"), "head"), P(("groups", "seq", "rep"), "head")),
        check_vma=False,
    )
```

time: 201 us -> 97.5 us (0.49)
  waiting for transfers between devices: 90.6 us -> 33.8 us
  matrix products: 46.4 us -> 0.97 us
  Pallas kernels: 0 us -> 32.5 us
  local copies, waits for them, and re-layouts: 31.1 us -> 6.25 us
  starting transfers between devices: 4.17 us -> 19.2 us
  between operations: 14.2 us -> 0.88 us
  other arithmetic: 14 us -> 3.58 us
    dot_general x11 -> x2, matrix products: 46.4 us -> 0.97 us  [per_device(): term = jnp.dot(values, weight, preferred_element_type=F32)]
    ppermute x2 -> x16, waiting for transfers between devices: 0.01 us -> 33.8 us  [the longest x11 18.7 us: swap(): return lax.ppermute(values, axis, [(i, i ^ step) for i in range(count)])]
    pallas_call x0 -> x8, Pallas kernels: none -> 32.5 us  [the longest x2 19.5 us: front(): pl.pallas_call(functools.partial(front_kernel, first, pairs, min(256, row...]
    all_gather x1 -> x0, waiting for transfers between devices: 32.1 us -> none  [per_device(): lax.all_gather(heads_out, 'head', axis=1, tiled=True)]
    reduce_scatter x1 -> x0, waiting for transfers between devices: 30.2 us -> none  [per_device(): lax.psum_scatter(partial_sums.astype(jnp.bfloat16), ('seq', 'rep'), scatt...]
    psum x1 -> x0, waiting for transfers between devices: 28.3 us -> none  [per_device(): lax.psum(numerator.astype(jnp.bfloat16), ('seq', 'rep')).astype(jnp.float32)]
    ppermute x2 -> x16, starting transfers between devices: 3.83 us -> 19.2 us  [the longest x11 11.3 us: swap(): return lax.ppermute(values, axis, [(i, i ^ step) for i in range(count)])]
    slice x6 -> x2, local copies, waits for them, and re-layouts: 9.66 us -> 0.02 us  [per_device(): heads = jnp.concatenate([f[1][:HALF] for f in fronts], axis=1)]
  transfers between devices with their start and end apart: 5 -> 16, of which waited for: 3 -> 7; matrix products, arithmetic and copies ran while one was open for 27% -> 5% of each run, Pallas kernels for 0% -> 18%
where the time goes in v1:
time: 97.5 us; the launch traced here: 97.1 us
  waiting for transfers between devices  33.8 us (35%)
  Pallas kernels  32.5 us (33%)
  starting transfers between devices  19.2 us (20%)
  local copies, waits for them, and re-layouts  6.25 us (6%)
  other arithmetic  3.58 us (4%)
    pallas_call x2, Pallas kernels, front(): pl.pallas_call(functools.partial(front_kernel, first, pairs, min(256, row...  19.5 us
    ppermute x11, waiting for transfers between devices, swap(): return lax.ppermute(values, axis, [(i, i ^ step) for i in range(count)])  18.7 us
    ppermute x11, starting transfers between devices, swap(): return lax.ppermute(values, axis, [(i, i ^ step) for i in range(count)])  11.3 us
    ppermute x1, waiting for transfers between devices, per_device(): lax.ppermute(own, 'head', [(i, (i + k) % head_devices) for i in range(hea...  8.41 us
    ppermute x2, waiting for transfers between devices, per_device(): lax.ppermute(outs[g][0], 'head', [(i, (i + k) % head_devices) for i in ra...  6.66 us
    unnamed x31, local copies, waits for them, and re-layouts  6.14 us
    pallas_call x2, Pallas kernels, far(): pl.pallas_call(functools.partial(far_kernel, pairs, 256), grid=(1,), in_s...  4.9 us
    pallas_call x2, Pallas kernels, out_part(): pl.pallas_call(functools.partial(out_kernel, count, acc is not None), gri...  4.17 us
  transfers between devices with their start and end apart: 16, of which 7 were waited for; matrix products, arithmetic and copies ran while one was open for 5% of the time, Pallas kernels for 18%

profile of v1, /device:TPU:0, one launch (start us, length us, event | category | flops | bytes accessed | tf_op | source)
XLA Modules:
  0.0 97.1 jit_solution(2735587400780345751)
XLA Ops:
  0.6 0.1 pad_add_fusion.refs_0_.ids_ref
  0.7 0.7 copy-done.1
  1.4 1.2 %copy-done.3 = bf16[1024,512]{1,0:T(8,128)(2,1)S(1)} copy-done((bf16[1024,512]{1,0:T(8,128)(2,1)S(1)}, bf16[1024,512]{1,0:T(8,128)(2,1)}, u32[]{:S(2)}) %copy-start.3) | copy-done | bytes 1048600
  2.6 1.2 %copy-done.5 = bf16[1024,512]{1,0:T(8,128)(2,1)S(1)} copy-done((bf16[1024,512]{1,0:T(8,128)(2,1)S(1)}, bf16[1024,512]{1,0:T(8,128)(2,1)}, u32[]{:S(2)}) %copy-start.5) | copy-done | bytes 1048600
  3.9 1.2 %copy-done.7 = bf16[1024,512]{1,0:T(8,128)(2,1)S(1)} copy-done((bf16[1024,512]{1,0:T(8,128)(2,1)S(1)}, bf16[1024,512]{1,0:T(8,128)(2,1)}, u32[]{:S(2)}) %copy-start.7) | copy-done | bytes 1048600
  5.1 0.7 copy-done.8
  5.8 10.0 %front.2 = (bf16[1024,1024]{1,0:T(8,128)(2,1)}, bf16[1024,256]{1,0:T(8,128)(2,1)S(1)}, bf16[1024,512]{1,0:T(8,128)(2,1)S(1)}, bf16[256,256]{1,0:T(8,128)(2,1)S(1)}, bf16[256,256]{1,0:T(8,128)(2,1)}) custom-call(s32[4]{0:T(128)S(1)} %pad_add_fusion.refs_0_.ids_ref, bf16[1024,1024]{1,0:T(8,128)(2,1)} %refs_1_.1, f32[1,1024]{1,0:T(1,128)S(1)} %bitcast.16, ...), custom_call_target="tpu_custom_call" | custom-call | flops 7516192768 | bytes 8388608 | tf_op jit(solution)/shard_map/front/pallas_call | solution.py:123
  15.8 0.8 copy-done.11
  16.6 0.5 collective-permute-start.7
  17.1 9.5 %front.3 = (bf16[1024,256]{1,0:T(8,128)(2,1)S(1)}, bf16[1024,512]{1,0:T(8,128)(2,1)S(1)}, bf16[256,256]{1,0:T(8,128)(2,1)S(1)}, bf16[256,256]{1,0:T(8,128)(2,1)}) custom-call(s32[4]{0:T(128)S(1)} %pad_add_fusion.refs_0_.ids_ref, bf16[1024,1024]{1,0:T(8,128)(2,1)} %get-tuple-element.15.refs_1_, bf16[1024,512]{1,0:T(8,128)(2,1)S(1)} %copy-done.4, ...), custom_call_target="tpu_custom_call" | custom-call | flops 7516192768 | bytes 8388608 | tf_op jit(solution)/shard_map/front/pallas_call | solution.py:123
  26.6 0.7 pad_maximum_fusion.1
  27.3 1.3 %collective-permute-start.1 = (bf16[64,1024]{1,0:T(8,128)(2,1)}, bf16[64,1024]{1,0:T(8,128)(2,1)S(1)}, u32[]{:S(2)}, u32[]{:S(2)}) collective-permute-start(bf16[64,1024]{1,0:T(8,128)(2,1)} %pad_maximum_fusion.1), channel_id=1, source_target_pairs={{1,0},{4,1},{5,4},{8,5},{9,8},{12,9},{13,12},{3,2},{6,3},{7,6},{10... | collective-permute-start | bytes 393224 | tf_op jit(solution)/shard_map/ppermute | solution.py:364
  28.6 0.6 pad_maximum_fusion
  29.2 3.0 %collective-permute-start = (bf16[64,1024]{1,0:T(8,128)(2,1)}, bf16[64,1024]{1,0:T(8,128)(2,1)S(1)}, u32[]{:S(2)}, u32[]{:S(2)}) collective-permute-start(bf16[64,1024]{1,0:T(8,128)(2,1)} %pad_maximum_fusion), channel_id=1, source_target_pairs={{0,1},{1,4},{4,5},{5,8},{8,9},{9,12},{12,13},{2,3},{3,6},{6,7},{7,... | collective-permute-start | bytes 393224 | tf_op jit(solution)/shard_map/ppermute | solution.py:363
  32.3 2.3 %collective-permute-start.2 = (bf16[256,256]{1,0:T(8,128)(2,1)}, bf16[256,256]{1,0:T(8,128)(2,1)}, u32[]{:S(2)}, u32[]{:S(2)}) collective-permute-start(bf16[256,256]{1,0:T(8,128)(2,1)} %get-tuple-element.20), channel_id=1, source_target_pairs={{0,1},{1,0},{2,3},{3,2},{4,5},{5,4},{6,7},{7,6},{8,9},{9,8},{10,11... | collective-permute-start | bytes 393224 | tf_op jit(solution)/shard_map/ppermute | solution.py:305
  34.5 0.1 copy.11
  34.7 0.1 copy.12.bounds_ref
  34.8 0.9 add_convert_fusion.2
  35.7 2.2 %collective-permute-start.8 = (bf16[256,256]{1,0:T(8,128)(2,1)S(1)}, bf16[256,256]{1,0:T(8,128)(2,1)S(1)}, u32[]{:S(2)}, u32[]{:S(2)}) collective-permute-start(bf16[256,256]{1,0:T(8,128)(2,1)S(1)} %add_convert_fusion.2), channel_id=1, source_target_pairs={{0,4},{4,0},{8,12},{12,8},{1,5},{5,1},{9,13},{13,9},{2,6},{6,2},{1... | collective-permute-start | bytes 393224 | tf_op jit(solution)/shard_map/ppermute | solution.py:305
  37.9 1.0 %add_convert_fusion.5 = bf16[256,256]{1,0:T(8,128)(2,1)S(1)} fusion(bf16[256,256]{1,0:T(8,128)(2,1)} %collective-permute-done.2, bf16[256,256]{1,0:T(8,128)(2,1)S(1)} %get-tuple-element.19), kind=kLoop, calls=%fused_computation.10 | loop fusion | flops 262144 | bytes 393216 | tf_op jit(solution)/shard_map/convert_element_type | solution.py:309
  38.9 0.1 collective-permute-start.3
  39.1 1.9 %near.3.near_ref = f32[1024,512]{1,0:T(8,128)S(1)} custom-call(s32[4]{0:T(128)S(1)} %pad_add_fusion.refs_0_.ids_ref, bf16[1024,256]{1,0:T(8,128)(2,1)S(1)} %copy-done.12, bf16[1024,512]{1,0:T(8,128)(2,1)S(1)} %get-tuple-element.18.near_ref, bf16[64,1024]{1,0:T(8,128)(2,1)S(1)} %collective-permute-done.prev_ref, ...), custom_call_target="tpu_custom_call" | custom-call | flops 1073741824 | bytes 4194304 | tf_op jit(solution)/shard_map/near/pallas_call | solution.py:191
  41.0 2.0 %near.2.near_ref = f32[1024,512]{1,0:T(8,128)S(1)} custom-call(s32[4]{0:T(128)S(1)} %pad_add_fusion.refs_0_.ids_ref, bf16[1024,256]{1,0:T(8,128)(2,1)S(1)} %copy-done.10, bf16[1024,512]{1,0:T(8,128)(2,1)S(1)} %get-tuple-element.17.near_ref, bf16[64,1024]{1,0:T(8,128)(2,1)S(1)} %collective-permute-done.prev_ref, ...), custom_call_target="tpu_custom_call" | custom-call | flops 1073741824 | bytes 4194304 | tf_op jit(solution)/shard_map/near/pallas_call | solution.py:191
  43.0 3.0 %collective-permute-start.9 = (bf16[256,256]{1,0:T(8,128)(2,1)S(1)}, bf16[256,256]{1,0:T(8,128)(2,1)S(1)}, u32[]{:S(2)}, u32[]{:S(2)}) collective-permute-start(bf16[256,256]{1,0:T(8,128)(2,1)S(1)} %add_convert_fusion.1), channel_id=1, source_target_pairs={{0,8},{4,12},{8,0},{12,4},{1,9},{5,13},{9,1},{13,5},{2,10},{6,14},... | collective-permute-start | bytes 393224 | tf_op jit(solution)/shard_map/ppermute | solution.py:305
  46.1 1.1 %collective-permute-start.4 = (bf16[256,256]{1,0:T(8,128)(2,1)S(1)}, bf16[256,256]{1,0:T(8,128)(2,1)S(1)}, u32[]{:S(2)}, u32[]{:S(2)}) collective-permute-start(bf16[256,256]{1,0:T(8,128)(2,1)S(1)} %add_convert_fusion.4), channel_id=1, source_target_pairs={{0,8},{4,12},{8,0},{12,4},{1,9},{5,13},{9,1},{13,5},{2,10},{6,14},... | collective-permute-start | bytes 393224 | tf_op jit(solution)/shard_map/ppermute | solution.py:305
  47.3 8.7 %collective-permute-done.9 = bf16[256,256]{1,0:T(8,128)(2,1)S(1)} collective-permute-done((bf16[256,256]{1,0:T(8,128)(2,1)S(1)}, bf16[256,256]{1,0:T(8,128)(2,1)S(1)}, u32[]{:S(2)}, u32[]{:S(2)}) %collective-permute-start.9) | collective-permute-done | bytes 131104 | tf_op jit(solution)/shard_map/ppermute | solution.py:305
  56.0 0.1 collective-permute-start.10
  56.1 1.8 %collective-permute-done.4 = bf16[256,256]{1,0:T(8,128)(2,1)S(1)} collective-permute-done((bf16[256,256]{1,0:T(8,128)(2,1)S(1)}, bf16[256,256]{1,0:T(8,128)(2,1)S(1)}, u32[]{:S(2)}, u32[]{:S(2)}) %collective-permute-start.4) | collective-permute-done | bytes 131104 | tf_op jit(solution)/shard_map/ppermute | solution.py:305
  57.9 0.1 collective-permute-start.5
  58.0 2.4 %far.3 = (bf16[1024,256]{1,0:T(8,128)(2,1)S(1)}, bf16[64,256]{1,0:T(8,128)(2,1)S(1)}) custom-call(s32[4]{0:T(128)S(1)} %pad_add_fusion.refs_0_.ids_ref, bf16[1024,256]{1,0:T(8,128)(2,1)S(1)} %copy-done.12, f32[1024,512]{1,0:T(8,128)S(1)} %near.3.near_ref, bf16[256,256]{1,0:T(8,128)(2,1)S(1)} %add_convert_fusion.mine_ref, ...), custom_call_target="tpu_custom_call" | custom-call | flops 1073741824 | bytes 4194304 | tf_op jit(solution)/shard_map/far/pallas_call | solution.py:246
  60.5 2.5 %far.2 = (bf16[1024,256]{1,0:T(8,128)(2,1)S(1)}, bf16[64,256]{1,0:T(8,128)(2,1)S(1)}) custom-call(s32[4]{0:T(128)S(1)} %pad_add_fusion.refs_0_.ids_ref, bf16[1024,256]{1,0:T(8,128)(2,1)S(1)} %copy-done.10, f32[1024,512]{1,0:T(8,128)S(1)} %near.2.near_ref, bf16[256,256]{1,0:T(8,128)(2,1)S(1)} %add_convert_fusion.3.mine_ref, ...), custom_call_target="tpu_custom_call" | custom-call | flops 1073741824 | bytes 4194304 | tf_op jit(solution)/shard_map/far/pallas_call | solution.py:246
  63.0 0.6 collective-permute-start.12
  63.5 0.9 collective-permute-done.12
  64.5 0.1 collective-permute-start.13
  64.6 0.1 constant_dynamic-slice_fusion
  64.6 4.3 %collective-permute-done.13 = bf16[64,512]{1,0:T(8,128)(2,1)S(1)} collective-permute-done((bf16[64,512]{1,0:T(8,128)(2,1)S(1)}, bf16[64,512]{1,0:T(8,128)(2,1)S(1)}, u32[]{:S(2)}, u32[]{:S(2)}) %collective-permute-start.13) | collective-permute-done | bytes 65568 | tf_op jit(solution)/shard_map/ppermute | solution.py:305
  68.9 1.4 %collective-permute-start.14 = (bf16[64,512]{1,0:T(8,128)(2,1)S(1)}, bf16[64,512]{1,0:T(8,128)(2,1)S(1)}, u32[]{:S(2)}, u32[]{:S(2)}) collective-permute-start(bf16[64,512]{1,0:T(8,128)(2,1)S(1)} %add_convert_fusion.6), channel_id=1, source_target_pairs={{0,8},{4,12},{8,0},{12,4},{1,9},{5,13},{9,1},{13,5},{2,10},{6,14},... | collective-permute-start | bytes 196616 | tf_op jit(solution)/shard_map/ppermute | solution.py:305
  70.3 1.5 %collective-permute-start.11 = (bf16[1024,256]{1,0:T(8,128)(2,1)S(1)}, bf16[1024,256]{1,0:T(8,128)(2,1)S(1)}, u32[]{:S(2)}, u32[]{:S(2)}) collective-permute-start(bf16[1024,256]{1,0:T(8,128)(2,1)S(1)} %get-tuple-element.25.refs_1_), channel_id=1, source_target_pairs={{0,2},{2,0},{1,3},{3,1},{4,6},{6,4},{5,7},{7,5},{8,10},{10,8},{9,1... | collective-permute-start | bytes 1572872 | tf_op jit(solution)/shard_map/ppermute | solution.py:375
  71.8 3.0 %collective-permute-done.14 = bf16[64,512]{1,0:T(8,128)(2,1)S(1)} collective-permute-done((bf16[64,512]{1,0:T(8,128)(2,1)S(1)}, bf16[64,512]{1,0:T(8,128)(2,1)S(1)}, u32[]{:S(2)}, u32[]{:S(2)}) %collective-permute-start.14) | collective-permute-done | bytes 65568 | tf_op jit(solution)/shard_map/ppermute | solution.py:305
  74.8 1.5 %collective-permute-start.15 = (bf16[8,512]{1,0:T(8,128)(2,1)S(1)}, bf16[8,512]{1,0:T(8,128)(2,1)S(1)}, u32[]{:S(2)}, u32[]{:S(2)}) collective-permute-start(bf16[8,512]{1,0:T(8,128)(2,1)S(1)} %add_convert_fusion.8), channel_id=1, source_target_pairs={{0,2},{2,0},{1,3},{3,1},{4,6},{6,4},{5,7},{7,5},{8,10},{10,8},{9,1... | collective-permute-start | bytes 24584 | tf_op jit(solution)/shard_map/ppermute | solution.py:394
  76.3 0.1 pad_add_fusion.1.refs_0_
  76.4 0.5 collective-permute-start.6
  76.9 8.4 %collective-permute-done.15 = bf16[8,512]{1,0:T(8,128)(2,1)S(1)} collective-permute-done((bf16[8,512]{1,0:T(8,128)(2,1)S(1)}, bf16[8,512]{1,0:T(8,128)(2,1)S(1)}, u32[]{:S(2)}, u32[]{:S(2)}) %collective-permute-start.15) | collective-permute-done | bytes 8224 | tf_op jit(solution)/shard_map/ppermute | solution.py:394
  85.3 0.2 fusion.1
  85.5 0.8 fusion
  86.3 2.1 %out.2.refs_3_ = f32[1024,512]{1,0:T(8,128)S(1)} custom-call(s32[3]{0:T(128)S(1)} %pad_add_fusion.1.refs_0_, bf16[1024,256]{1,0:T(8,128)(2,1)S(1)} %get-tuple-element.25.refs_1_, bf16[1024,256]{1,0:T(8,128)(2,1)S(1)} %get-tuple-element.21.refs_2_, bf16[1024,256]{1,0:T(8,128)(2,1)S(1)} %collective-permute-done.11.refs_3_, bf16[1024,512]{1,0:T(8,128)(2,1)S(1)} %copy-done, ...), custom_call_target="tpu_custom_call" | custom-call | flops 805306368 | bytes 4194304 | tf_op jit(solution)/shard_map/out/pallas_call | solution.py:286
  88.4 6.7 %collective-permute-done.6.refs_1_ = bf16[1024,256]{1,0:T(8,128)(2,1)S(1)} collective-permute-done((bf16[1024,256]{1,0:T(8,128)(2,1)S(1)}, bf16[1024,256]{1,0:T(8,128)(2,1)S(1)}, u32[]{:S(2)}, u32[]{:S(2)}) %collective-permute-start.6) | collective-permute-done | bytes 524320 | tf_op jit(solution)/shard_map/ppermute | solution.py:375
  95.0 2.1 %out.3 = bf16[1024,512]{1,0:T(8,128)(2,1)} custom-call(s32[1]{0:T(128)} %bitcast.refs_0_, bf16[1024,256]{1,0:T(8,128)(2,1)S(1)} %collective-permute-done.6.refs_1_, bf16[1024,512]{1,0:T(8,128)(2,1)S(1)} %copy-done, f32[1024,512]{1,0:T(8,128)S(1)} %out.2.refs_3_), custom_call_target="tpu_custom_call" | custom-call | flops 268435456 | bytes 4194304 | tf_op jit(solution)/shard_map/out/pallas_call | solution.py:286
  (43 shorter events, 0.3 us)
Async XLA Ops:
  0.7 0.7 copy-start.1
  1.4 1.2 %copy-start.3 = (bf16[1024,512]{1,0:T(8,128)(2,1)S(1)}, bf16[1024,512]{1,0:T(8,128)(2,1)}, u32[]{:S(2)}) copy-start(bf16[1024,512]{1,0:T(8,128)(2,1)} %refs_2_.2) | copy-start | bytes 3145732
  2.6 1.2 %copy-start.5 = (bf16[1024,512]{1,0:T(8,128)(2,1)S(1)}, bf16[1024,512]{1,0:T(8,128)(2,1)}, u32[]{:S(2)}) copy-start(bf16[1024,512]{1,0:T(8,128)(2,1)} %refs_3_.3) | copy-start | bytes 3145732
  3.9 1.2 %copy-start.7 = (bf16[1024,512]{1,0:T(8,128)(2,1)S(1)}, bf16[1024,512]{1,0:T(8,128)(2,1)}, u32[]{:S(2)}) copy-start(bf16[1024,512]{1,0:T(8,128)(2,1)} %refs_4_.4) | copy-start | bytes 3145732
  5.1 0.7 copy-start.8
  5.8 11.3 %copy-start.2 = (f32[4,512]{1,0:T(4,128)S(1)}, f32[4,512]{1,0:T(4,128)}, u32[]{:S(2)}) copy-start(f32[4,512]{1,0:T(4,128)} %refs_6_.4) | copy-start | bytes 24580
  5.8 11.3 %copy-start.4 = (bf16[1024,512]{1,0:T(8,128)(2,1)S(1)}, bf16[1024,512]{1,0:T(8,128)(2,1)}, u32[]{:S(2)}) copy-start(bf16[1024,512]{1,0:T(8,128)(2,1)} %refs_2_.2) | copy-start | bytes 3145732
  5.8 11.3 %copy-start.6 = (bf16[1024,512]{1,0:T(8,128)(2,1)S(1)}, bf16[1024,512]{1,0:T(8,128)(2,1)}, u32[]{:S(2)}) copy-start(bf16[1024,512]{1,0:T(8,128)(2,1)} %refs_3_.3) | copy-start | bytes 3145732
  15.8 0.8 copy-start.11
  16.6 18.2 %collective-permute-start.7 = (bf16[256,256]{1,0:T(8,128)(2,1)}, bf16[256,256]{1,0:T(8,128)(2,1)}, u32[]{:S(2)}, u32[]{:S(2)}) collective-permute-start(bf16[256,256]{1,0:T(8,128)(2,1)} %get-tuple-element.24), channel_id=1, source_target_pairs={{0,1},{1,0},{2,3},{3,2},{4,5},{5,4},{6,7},{7,6},{8,9},{9,8},{10,11... | collective-permute-start | bytes 393224 | tf_op jit(solution)/shard_map/ppermute | solution.py:305
  17.1 17.6 %copy-start.13 = (s32[64,2]{0,1:T(2,128)S(1)}, s32[64,2]{0,1:T(2,128)}, u32[]{:S(2)}) copy-start(s32[64,2]{0,1:T(2,128)} %param.17) | copy-start | bytes 1540
  26.6 5.7 %copy-start.9 = (bf16[1024,256]{1,0:T(8,128)(2,1)}, bf16[1024,256]{1,0:T(8,128)(2,1)S(1)}, u32[]{:S(2)}) copy-start(bf16[1024,256]{1,0:T(8,128)(2,1)S(1)} %get-tuple-element.16.q_ref) | copy-start | bytes 1572868
  26.6 12.5 %copy-start.12 = (bf16[1024,256]{1,0:T(8,128)(2,1)S(1)}, bf16[1024,256]{1,0:T(8,128)(2,1)}, u32[]{:S(2)}) copy-start(bf16[1024,256]{1,0:T(8,128)(2,1)} %copy-done.11) | copy-start | bytes 1572868
  27.3 11.8 %collective-permute-start.1 = (bf16[64,1024]{1,0:T(8,128)(2,1)}, bf16[64,1024]{1,0:T(8,128)(2,1)S(1)}, u32[]{:S(2)}, u32[]{:S(2)}) collective-permute-start(bf16[64,1024]{1,0:T(8,128)(2,1)} %pad_maximum_fusion.1), channel_id=1, source_target_pairs={{1,0},{4,1},{5,4},{8,5},{9,8},{12,9},{13,12},{3,2},{6,3},{7,6},{10... | collective-permute-start | bytes 393224 | tf_op jit(solution)/shard_map/ppermute | solution.py:364
  29.2 9.8 %collective-permute-start = (bf16[64,1024]{1,0:T(8,128)(2,1)}, bf16[64,1024]{1,0:T(8,128)(2,1)S(1)}, u32[]{:S(2)}, u32[]{:S(2)}) collective-permute-start(bf16[64,1024]{1,0:T(8,128)(2,1)} %pad_maximum_fusion), channel_id=1, source_target_pairs={{0,1},{1,4},{4,5},{5,8},{8,9},{9,12},{12,13},{2,3},{3,6},{6,7},{7,... | collective-permute-start | bytes 393224 | tf_op jit(solution)/shard_map/ppermute | solution.py:363
  32.3 5.6 %collective-permute-start.2 = (bf16[256,256]{1,0:T(8,128)(2,1)}, bf16[256,256]{1,0:T(8,128)(2,1)}, u32[]{:S(2)}, u32[]{:S(2)}) collective-permute-start(bf16[256,256]{1,0:T(8,128)(2,1)} %get-tuple-element.20), channel_id=1, source_target_pairs={{0,1},{1,0},{2,3},{3,2},{4,5},{5,4},{6,7},{7,6},{8,9},{9,8},{10,11... | collective-permute-start | bytes 393224 | tf_op jit(solution)/shard_map/ppermute | solution.py:305
  35.7 7.2 %collective-permute-start.8 = (bf16[256,256]{1,0:T(8,128)(2,1)S(1)}, bf16[256,256]{1,0:T(8,128)(2,1)S(1)}, u32[]{:S(2)}, u32[]{:S(2)}) collective-permute-start(bf16[256,256]{1,0:T(8,128)(2,1)S(1)} %add_convert_fusion.2), channel_id=1, source_target_pairs={{0,4},{4,0},{8,12},{12,8},{1,5},{5,1},{9,13},{13,9},{2,6},{6,2},{1... | collective-permute-start | bytes 393224 | tf_op jit(solution)/shard_map/ppermute | solution.py:305
  37.9 3.1 %copy-start.10 = (bf16[1024,256]{1,0:T(8,128)(2,1)S(1)}, bf16[1024,256]{1,0:T(8,128)(2,1)}, u32[]{:S(2)}) copy-start(bf16[1024,256]{1,0:T(8,128)(2,1)} %copy-done.9) | copy-start | bytes 1572868
  38.9 7.2 %collective-permute-start.3 = (bf16[256,256]{1,0:T(8,128)(2,1)S(1)}, bf16[256,256]{1,0:T(8,128)(2,1)S(1)}, u32[]{:S(2)}, u32[]{:S(2)}) collective-permute-start(bf16[256,256]{1,0:T(8,128)(2,1)S(1)} %add_convert_fusion.5), channel_id=1, source_target_pairs={{0,4},{4,0},{8,12},{12,8},{1,5},{5,1},{9,13},{13,9},{2,6},{6,2},{1... | collective-permute-start | bytes 393224 | tf_op jit(solution)/shard_map/ppermute | solution.py:305
  43.0 12.9 %collective-permute-start.9 = (bf16[256,256]{1,0:T(8,128)(2,1)S(1)}, bf16[256,256]{1,0:T(8,128)(2,1)S(1)}, u32[]{:S(2)}, u32[]{:S(2)}) collective-permute-start(bf16[256,256]{1,0:T(8,128)(2,1)S(1)} %add_convert_fusion.1), channel_id=1, source_target_pairs={{0,8},{4,12},{8,0},{12,4},{1,9},{5,13},{9,1},{13,5},{2,10},{6,14},... | collective-permute-start | bytes 393224 | tf_op jit(solution)/shard_map/ppermute | solution.py:305
  46.1 11.8 %collective-permute-start.4 = (bf16[256,256]{1,0:T(8,128)(2,1)S(1)}, bf16[256,256]{1,0:T(8,128)(2,1)S(1)}, u32[]{:S(2)}, u32[]{:S(2)}) collective-permute-start(bf16[256,256]{1,0:T(8,128)(2,1)S(1)} %add_convert_fusion.4), channel_id=1, source_target_pairs={{0,8},{4,12},{8,0},{12,4},{1,9},{5,13},{9,1},{13,5},{2,10},{6,14},... | collective-permute-start | bytes 393224 | tf_op jit(solution)/shard_map/ppermute | solution.py:305
  56.0 2.0 %collective-permute-start.10 = (bf16[256,256]{1,0:T(8,128)(2,1)S(1)}, bf16[256,256]{1,0:T(8,128)(2,1)S(1)}, u32[]{:S(2)}, u32[]{:S(2)}) collective-permute-start(bf16[256,256]{1,0:T(8,128)(2,1)S(1)} %add_convert_fusion.mine_ref), channel_id=1, source_target_pairs={{0,1},{1,0},{2,3},{3,2},{4,5},{5,4},{6,7},{7,6},{8,9},{9,8},{10,11... | collective-permute-start | bytes 393224 | tf_op jit(solution)/shard_map/ppermute | solution.py:305
  57.9 2.6 %collective-permute-start.5 = (bf16[256,256]{1,0:T(8,128)(2,1)S(1)}, bf16[256,256]{1,0:T(8,128)(2,1)S(1)}, u32[]{:S(2)}, u32[]{:S(2)}) collective-permute-start(bf16[256,256]{1,0:T(8,128)(2,1)S(1)} %add_convert_fusion.3.mine_ref), channel_id=1, source_target_pairs={{0,1},{1,0},{2,3},{3,2},{4,5},{5,4},{6,7},{7,6},{8,9},{9,8},{10,11... | collective-permute-start | bytes 393224 | tf_op jit(solution)/shard_map/ppermute | solution.py:305
  60.5 24.8 %copy-start = (bf16[1024,512]{1,0:T(8,128)(2,1)S(1)}, bf16[1024,512]{1,0:T(8,128)(2,1)}, u32[]{:S(2)}) copy-start(bf16[1024,512]{1,0:T(8,128)(2,1)} %refs_2_.3) | copy-start | bytes 3145732
  63.0 1.5 %collective-permute-start.12 = (bf16[64,512]{1,0:T(8,128)(2,1)S(1)}, bf16[64,512]{1,0:T(8,128)(2,1)S(1)}, u32[]{:S(2)}, u32[]{:S(2)}) collective-permute-start(bf16[64,512]{1,0:T(8,128)(2,1)S(1)} %constant_dynamic-update-slice_fusion), channel_id=1, source_target_pairs={{0,1},{1,0},{2,3},{3,2},{4,5},{5,4},{6,7},{7,6},{8,9},{9,8},{10,11... | collective-permute-start | bytes 196616 | tf_op jit(solution)/shard_map/ppermute | solution.py:305
  64.5 4.4 %collective-permute-start.13 = (bf16[64,512]{1,0:T(8,128)(2,1)S(1)}, bf16[64,512]{1,0:T(8,128)(2,1)S(1)}, u32[]{:S(2)}, u32[]{:S(2)}) collective-permute-start(bf16[64,512]{1,0:T(8,128)(2,1)S(1)} %add_convert_fusion.7), channel_id=1, source_target_pairs={{0,4},{4,0},{8,12},{12,8},{1,5},{5,1},{9,13},{13,9},{2,6},{6,2},{1... | collective-permute-start | bytes 196616 | tf_op jit(solution)/shard_map/ppermute | solution.py:305
  68.9 5.9 %collective-permute-start.14 = (bf16[64,512]{1,0:T(8,128)(2,1)S(1)}, bf16[64,512]{1,0:T(8,128)(2,1)S(1)}, u32[]{:S(2)}, u32[]{:S(2)}) collective-permute-start(bf16[64,512]{1,0:T(8,128)(2,1)S(1)} %add_convert_fusion.6), channel_id=1, source_target_pairs={{0,8},{4,12},{8,0},{12,4},{1,9},{5,13},{9,1},{13,5},{2,10},{6,14},... | collective-permute-start | bytes 196616 | tf_op jit(solution)/shard_map/ppermute | solution.py:305
  70.3 16.0 %collective-permute-start.11 = (bf16[1024,256]{1,0:T(8,128)(2,1)S(1)}, bf16[1024,256]{1,0:T(8,128)(2,1)S(1)}, u32[]{:S(2)}, u32[]{:S(2)}) collective-permute-start(bf16[1024,256]{1,0:T(8,128)(2,1)S(1)} %get-tuple-element.25.refs_1_), channel_id=1, source_target_pairs={{0,2},{2,0},{1,3},{3,1},{4,6},{6,4},{5,7},{7,5},{8,10},{10,8},{9,1... | collective-permute-start | bytes 1572872 | tf_op jit(solution)/shard_map/ppermute | solution.py:375
  74.8 10.5 %collective-permute-start.15 = (bf16[8,512]{1,0:T(8,128)(2,1)S(1)}, bf16[8,512]{1,0:T(8,128)(2,1)S(1)}, u32[]{:S(2)}, u32[]{:S(2)}) collective-permute-start(bf16[8,512]{1,0:T(8,128)(2,1)S(1)} %add_convert_fusion.8), channel_id=1, source_target_pairs={{0,2},{2,0},{1,3},{3,1},{4,6},{6,4},{5,7},{7,5},{8,10},{10,8},{9,1... | collective-permute-start | bytes 24584 | tf_op jit(solution)/shard_map/ppermute | solution.py:394
  76.4 18.7 %collective-permute-start.6 = (bf16[1024,256]{1,0:T(8,128)(2,1)S(1)}, bf16[1024,256]{1,0:T(8,128)(2,1)S(1)}, u32[]{:S(2)}, u32[]{:S(2)}) collective-permute-start(bf16[1024,256]{1,0:T(8,128)(2,1)S(1)} %get-tuple-element.21.refs_2_), channel_id=1, source_target_pairs={{0,2},{2,0},{1,3},{3,1},{4,6},{6,4},{5,7},{7,5},{8,10},{10,8},{9,1... | collective-permute-start | bytes 1572872 | tf_op jit(solution)/shard_map/ppermute | solution.py:375

commit v2 on v1

v2 whole, which is shorter than its diff:
```python
import functools

import jax
import jax.numpy as jnp
from jax import lax
from jax.experimental import pallas as pl
from jax.experimental.pallas import tpu as pltpu
from jax.sharding import PartitionSpec as P

DH = 64
R = 256
SEG = 128
HALF = SEG // 2
LANES = 2 * DH
SCORE_SCALE = DH ** (-0.5)
LOG2E = 1.4426950408889634

softcap = 5.0
epsilon = 1e-05

BF = jnp.bfloat16
F32 = jnp.float32


def dot(a, b, dims=((1,), (0,))):
    return lax.dot_general(a, b, (dims, ((), ())), preferred_element_type=F32)


def exp_capped(values, scale):
    return jnp.exp2((softcap * LOG2E) * jnp.tanh(values * (scale / softcap)))


def vmem():
    return pl.BlockSpec(memory_space=pltpu.VMEM)


def smem():
    return pl.BlockSpec(memory_space=pltpu.SMEM)


def head_norm(values, gain):
    out = []
    for at in range(0, values.shape[1], LANES):
        x = values[:, at : at + LANES]
        first = lane_is_first(x.shape)

        def mean(y):
            low = jnp.sum(jnp.where(first, y, 0.0), axis=-1, keepdims=True)
            high = jnp.sum(jnp.where(first, 0.0, y), axis=-1, keepdims=True)
            return jnp.where(first, low, high) * (1.0 / DH)

        centred = x - mean(x)
        spread = mean(centred * centred)
        out.append((centred * lax.rsqrt(spread + epsilon) * gain[:, at : at + LANES]).astype(BF))
    return jnp.concatenate(out, axis=1)


def token_norm(x, gain):
    x = x.astype(F32)
    centred = x - jnp.mean(x, axis=-1, keepdims=True)
    spread = jnp.mean(centred * centred, axis=-1, keepdims=True)
    return (centred * lax.rsqrt(spread + epsilon) * gain).astype(BF)


def front_kernel(first, group, pairs, tile, *refs):
    if first:
        (ids_ref, x_hbm, gain_ref, wk_hbm, wv_hbm, wp_hbm, dual_ref,
         normed_ref, near_ref, keep_ref, send_ref, raw_ref, p_ref, wk_ref, wv_ref, wp_ref, sem, x_ref) = refs
    else:
        (ids_ref, normed_ref, wk_hbm, wv_hbm, wp_hbm, dual_ref,
         near_ref, keep_ref, send_ref, raw_ref, p_ref, wk_ref, wv_ref, wp_ref, sem) = refs
    rows = normed_ref.shape[0]
    width = pairs * LANES
    chunks = rows // tile
    own = pl.ds(group * width, width)

    def copy(source, target, slot):
        made = pltpu.make_async_copy(source, target, sem.at[slot])
        made.start()
        return made

    def token_copy(i):
        at = pl.ds(i * tile, tile)
        return copy(x_hbm.at[at, :], x_ref.at[at, :], i)

    token_copies = [token_copy(0)] if first else []
    key_copy = copy(wk_hbm.at[:, own], wk_ref, chunks)
    value_copy = copy(wv_hbm.at[:, own], wv_ref, chunks + 1)
    proj_copies = []
    for p in range(pairs):
        cols = pl.ds((group * pairs + p) * 2 * R, 2 * R)
        proj_copies.append(copy(wp_hbm.at[:, cols], wp_ref.at[:, pl.ds(p * 2 * R, 2 * R)], chunks + 2 + p))
        if first and p == 0:
            token_copies += [token_copy(i) for i in range(1, chunks)]
    for i in range(chunks):
        at = pl.ds(i * tile, tile)
        if first:
            token_copies[i].wait()
            normed_ref[at, :] = token_norm(x_ref[at, :], gain_ref[...])
        normed = normed_ref[at, :]
        if i == 0:
            key_copy.wait()
            value_copy.wait()
        key = dot(normed, wk_ref[...])
        value = dot(normed, wv_ref[...])
        for p in range(pairs):
            cols = slice(p * LANES, (p + 1) * LANES)
            raw = jnp.concatenate([key[:, cols], value[:, cols]], axis=1).astype(BF)
            raw_ref[2 * p * LANES : 2 * (p + 1) * LANES, at] = raw.T
        for p in range(pairs):
            cols = slice(2 * p * R, 2 * (p + 1) * R)
            if i == 0:
                proj_copies[p].wait()
            p_ref[at, cols] = exp_capped(dot(normed, wp_ref[:, cols]), 1.0).astype(BF)
        near_ref[at, :width] = head_norm(key, dual_ref[0:1, group * width : (group + 1) * width])
        near_ref[at, width:] = head_norm(value, dual_ref[1:2, group * width : (group + 1) * width])
    total = []
    for p in range(pairs):
        full = dot(raw_ref[2 * p * LANES : 2 * (p + 1) * LANES, :], p_ref[:, 2 * p * R : 2 * (p + 1) * R])
        for part in range(4):
            head = part % 2
            total.append(full[part * DH : (part + 1) * DH, head * R : (head + 1) * R])
    total = jnp.concatenate(total, axis=0).astype(BF)
    half = total.shape[0] // 2
    mine = ids_ref[0] == 0
    keep_ref[...] = jnp.where(mine, total[:half], total[half:])
    send_ref[...] = jnp.where(mine, total[half:], total[:half])


def in_hbm(values):
    return pltpu.with_memory_space_constraint(values, pltpu.HBM)


def front(first, group, pairs, ids, tokens, gain, wk, wv, wp, dual):
    rows, depth = tokens.shape
    width = pairs * LANES
    half = pairs * R // 2
    tile = min(256, rows)
    outs = [
        jax.ShapeDtypeStruct((rows, 2 * width), BF),
        jax.ShapeDtypeStruct((half, R), BF),
        jax.ShapeDtypeStruct((half, R), BF),
    ]
    hbm = pl.BlockSpec(memory_space=pltpu.HBM)
    ins = [smem(), hbm if first else vmem()] + ([vmem()] if first else []) + [hbm] * 3 + [vmem()]
    args = [ids, in_hbm(tokens) if first else tokens] + ([gain] if first else [])
    args += [in_hbm(wk), in_hbm(wv), in_hbm(wp), dual]
    scratch = [
        pltpu.VMEM((2 * width, rows), BF),
        pltpu.VMEM((rows, 2 * pairs * R), BF),
        pltpu.VMEM((depth, width), BF),
        pltpu.VMEM((depth, width), BF),
        pltpu.VMEM((depth, 2 * pairs * R), BF),
        pltpu.SemaphoreType.DMA((rows // tile + 2 + pairs,)),
    ]
    if first:
        outs = [jax.ShapeDtypeStruct((rows, depth), BF)] + outs
        scratch.append(pltpu.VMEM((rows, depth), BF))
    return pl.pallas_call(
        functools.partial(front_kernel, first, group, pairs, tile),
        in_specs=ins,
        out_specs=[vmem()] * len(outs),
        out_shape=outs,
        scratch_shapes=scratch,
        compiler_params=pltpu.CompilerParams(vmem_limit_bytes=24 << 20),
        cost_estimate=pl.CostEstimate(
            flops=2 * rows * depth * (2 * width + 2 * pairs * R) * 2, bytes_accessed=4 << 20, transcendentals=0
        ),
        name="front",
    )(*args)


def lane_is_first(shape):
    return lax.broadcasted_iota(jnp.int32, shape, 1) < DH


def stacked(q):
    first = lane_is_first(q.shape)
    zero = jnp.zeros_like(q)
    return jnp.concatenate([jnp.where(first, q, zero), jnp.where(first, zero, q)], axis=0)


def unstack(both):
    rows = both.shape[0] // 2
    first = lane_is_first((rows, LANES))
    return (
        jnp.where(first, both[:rows, :LANES], both[rows:, :LANES]),
        jnp.where(first, both[:rows, LANES:], both[rows:, LANES:]),
    )


def near_kernel(pairs, group, ids_ref, normed_ref, near_ref, prev_ref, next_ref, gain_ref, wq_ref, wk_ref, wv_ref, dual_ref,
                q_ref, out_ref, pad_ref):
    rows = normed_ref.shape[0]
    width = pairs * LANES
    mine = slice(group * width, (group + 1) * width)
    halo = token_norm(jnp.concatenate([prev_ref[...], next_ref[...]], axis=0), gain_ref[...])
    key = head_norm(dot(halo, wk_ref[:, mine]), dual_ref[0:1, mine])
    value = head_norm(dot(halo, wv_ref[:, mine]), dual_ref[1:2, mine])
    q_ref[...] = dot(normed_ref[...], wq_ref[:, mine]).astype(BF)
    pad_ref[0:HALF, :width] = key[:HALF]
    pad_ref[0:HALF, width:] = value[:HALF]
    pad_ref[HALF : HALF + rows, :] = near_ref[...]
    pad_ref[HALF + rows :, :width] = key[HALF:]
    pad_ref[HALF + rows :, width:] = value[HALF:]
    row = lax.broadcasted_iota(jnp.int32, (2 * SEG, LANES), 0)
    ones = jnp.ones((2 * SEG, LANES), F32)
    has_prev = jnp.where(ids_ref[1] != 0, 1.0, 0.0)
    has_next = jnp.where(ids_ref[2] != 0, 1.0, 0.0)
    segments = rows // SEG
    for s in range(segments):
        count = ones
        if s == 0:
            count = jnp.where(row < HALF, has_prev, count)
        if s == segments - 1:
            count = jnp.where(row >= 3 * HALF, has_next, count)
        count = count.astype(BF)
        window = pl.ds(s * SEG, 2 * SEG)
        for p in range(pairs):
            cols = slice(p * LANES, (p + 1) * LANES)
            q = stacked(q_ref[s * SEG : (s + 1) * SEG, cols])
            scores = dot(q, pad_ref[window, cols], ((1,), (1,)))
            weights = exp_capped(scores, SCORE_SCALE).astype(BF)
            values = jnp.concatenate([pad_ref[window, width + p * LANES : width + (p + 1) * LANES], count], axis=1)
            top, bottom = unstack(dot(weights, values))
            out_ref[s * SEG : (s + 1) * SEG, 2 * p * LANES : (2 * p + 1) * LANES] = top
            out_ref[s * SEG : (s + 1) * SEG, (2 * p + 1) * LANES : (2 * p + 2) * LANES] = bottom


def near(pairs, group, ids, normed, near_pairs, prev, following, gain, wq, wk, wv, dual):
    rows = normed.shape[0]
    width = pairs * LANES
    return pl.pallas_call(
        functools.partial(near_kernel, pairs, group),
        in_specs=[smem()] + [vmem()] * 9,
        out_specs=[vmem()] * 2,
        out_shape=[jax.ShapeDtypeStruct((rows, width), BF), jax.ShapeDtypeStruct((rows, 2 * width), F32)],
        scratch_shapes=[pltpu.VMEM((rows + SEG, 2 * width), BF)],
        compiler_params=pltpu.CompilerParams(vmem_limit_bytes=16 << 20),
        cost_estimate=pl.CostEstimate(flops=rows * pairs * (1 << 20), bytes_accessed=4 << 20, transcendentals=0),
        name="near",
    )(ids, normed, near_pairs, prev, following, gain, wq, wk, wv, dual)


def far_kernel(pairs, group, block, spread, *refs):
    (ids_ref, q_ref, near_ref, mine_ref, other_ref, gains_ref, bounds_ref), refs = refs[:7], refs[7:]
    before, (out_ref, keep_ref, send_ref) = refs[:-3], refs[-3:]
    rows = q_ref.shape[0]
    width = pairs * LANES
    is_first = ids_ref[0] == 0
    top = jnp.where(is_first, mine_ref[...], other_ref[...])
    bottom = jnp.where(is_first, other_ref[...], mine_ref[...])
    total = jnp.concatenate([top, bottom], axis=0)
    ones = jnp.ones((LANES, R), BF)
    for p in range(pairs):
        cols = slice(p * LANES, (p + 1) * LANES)

        def land(kind):
            parts = []
            for h in range(2):
                at = p * R + kind * LANES + h * DH
                values = total[at : at + DH].astype(F32)
                centred = values - jnp.mean(values, axis=0, keepdims=True)
                spread = jnp.mean(centred * centred, axis=0, keepdims=True)
                base = group * width + p * LANES + h * DH
                gain = gains_ref[base : base + DH, 2 + kind : 3 + kind]
                parts.append((centred * lax.rsqrt(spread + epsilon) * gain).astype(BF))
            return jnp.concatenate(parts, axis=0)

        keys = land(0)
        values = jnp.concatenate([land(1), ones], axis=0)
        for start in range(0, rows, block):
            q = stacked(q_ref[start : start + block, cols])
            weights = exp_capped(dot(q, keys), SCORE_SCALE).astype(BF)
            top, bottom = unstack(dot(weights, values, ((1,), (1,))))
            top = top + near_ref[start : start + block, 2 * p * LANES : (2 * p + 1) * LANES]
            bottom = bottom + near_ref[start : start + block, (2 * p + 1) * LANES : (2 * p + 2) * LANES]
            out_ref[start : start + block, cols] = (top / bottom).astype(BF)
    spans = bounds_ref.shape[0]
    position = ids_ref[3] + lax.broadcasted_iota(jnp.int32, (spans, rows), 1)
    member = (position >= bounds_ref[:, 0:1]) & (position < bounds_ref[:, 1:2])
    member = jnp.where(member, 1.0, 0.0).astype(BF)
    sums = dot(member, out_ref[...])
    count = spans // (2 * spread)
    even = jnp.concatenate([sums[2 * i * count : (2 * i + 1) * count] for i in range(spread)], axis=0)
    odd = jnp.concatenate([sums[(2 * i + 1) * count : (2 * i + 2) * count] for i in range(spread)], axis=0)
    lanes = slice(group * width, (group + 1) * width)
    if before:
        keep_ref[:, : group * width] = before[0][...]
        send_ref[:, : group * width] = before[1][...]
    keep_ref[:, lanes] = jnp.where(is_first, even, odd)
    send_ref[:, lanes] = jnp.where(is_first, odd, even).astype(BF)


def far(pairs, group, spread, ids, q, near_sums, mine, other, gains, bounds, before):
    rows = q.shape[0]
    width = pairs * LANES
    spans = bounds.shape[0]
    shape = (spans // 2, (group + 1) * width)
    return pl.pallas_call(
        functools.partial(far_kernel, pairs, group, 256, spread),
        in_specs=[smem()] + [vmem()] * (6 + len(before)),
        out_specs=[vmem()] * 3,
        out_shape=[
            jax.ShapeDtypeStruct((rows, width), BF),
            jax.ShapeDtypeStruct(shape, F32),
            jax.ShapeDtypeStruct(shape, BF),
        ],
        compiler_params=pltpu.CompilerParams(vmem_limit_bytes=16 << 20),
        cost_estimate=pl.CostEstimate(flops=rows * pairs * (1 << 20), bytes_accessed=4 << 20, transcendentals=0),
        name="far",
    )(ids, q, near_sums, mine, other, gains, bounds, *before)


def out_kernel(count, *refs):
    ids_ref, refs = refs[0], refs[1:]
    tokens, (weight_ref, *acc), out_ref = refs[:count], refs[count:-1], refs[-1]
    rows, width = tokens[0].shape
    for start in range(0, rows, 256):
        at = slice(start, start + 256)
        total = acc[0][at, :] if acc else None
        for j in range(count):
            weight = weight_ref[pl.ds(pl.multiple_of(ids_ref[j] * width, width), width), :]
            term = dot(tokens[j][at, :], weight)
            total = term if total is None else total + term
        out_ref[at, :] = total.astype(out_ref.dtype)


def out_part(parts, index, weight, acc, dtype):
    count = len(parts)
    rows, width = parts[0].shape
    columns = weight.shape[1]
    extra = [] if acc is None else [acc]
    return pl.pallas_call(
        functools.partial(out_kernel, count),
        in_specs=[smem()] + [vmem()] * (count + 1 + len(extra)),
        out_specs=vmem(),
        out_shape=jax.ShapeDtypeStruct((rows, columns), dtype),
        compiler_params=pltpu.CompilerParams(vmem_limit_bytes=16 << 20),
        cost_estimate=pl.CostEstimate(
            flops=2 * rows * width * columns * count, bytes_accessed=4 << 20, transcendentals=0
        ),
        name="out",
    )(index, *parts, weight, *extra)


def swap(values, axis, step):
    count = lax.axis_size(axis)
    return lax.ppermute(values, axis, [(i, i ^ step) for i in range(count)])


def add(a, b):
    return (a.astype(F32) + b.astype(F32)).astype(BF)


def steps_of(axis):
    step = 1
    while step < lax.axis_size(axis):
        yield step
        step *= 2


def per_device(
    book_tokens,
    norm_gain,
    query_weight,
    key_weight,
    value_weight,
    proj_weight,
    dual_gains,
    out_weight,
    span_bounds,
):
    rows = book_tokens.shape[0]
    seq_devices = lax.axis_size(("seq", "rep"))
    seq_index = lax.axis_index(("seq", "rep"))
    head_devices = lax.axis_size("head")
    head_index = lax.axis_index("head")
    first_row = seq_index * rows
    all_pairs = query_weight.shape[1] // LANES
    groups = 2 if all_pairs % 2 == 0 else 1
    pairs = all_pairs // groups
    ids = jnp.stack(
        [lax.axis_index("rep"), (seq_index > 0).astype(jnp.int32), (seq_index < seq_devices - 1).astype(jnp.int32), first_row]
    ).astype(jnp.int32)
    gain = norm_gain[None, :]
    gain_columns = dual_gains.T

    both = ("seq", "rep")
    totals, nears, tokens, normed = [], [], book_tokens, None
    for g in range(groups):
        outs = front(g == 0, g, pairs, ids, tokens, gain, key_weight, value_weight, proj_weight, dual_gains)
        if g == 0:
            tokens, outs = outs[0], outs[1:]
            normed = tokens
        near_pairs, keep, send = outs
        if g == 0:
            prev = lax.ppermute(book_tokens[rows - HALF :], both, [(i, i + 1) for i in range(seq_devices - 1)])
            following = lax.ppermute(book_tokens[:HALF], both, [(i + 1, i) for i in range(seq_devices - 1)])
        mine = add(keep, swap(send, "rep", 1))
        tokens, mine = lax.optimization_barrier((tokens, mine))
        for step in steps_of("seq"):
            mine = add(mine, swap(mine, "seq", step))
        totals.append((mine, swap(mine, "rep", 1)))
        nears.append(near(pairs, g, ids, normed, near_pairs, prev, following, gain, query_weight, key_weight, value_weight, dual_gains))

    spread = lax.axis_size("seq")
    outs, before = [], ()
    for g in range(groups):
        q, near_sums = nears[g]
        out, *before = far(pairs, g, spread, ids, q, near_sums, *totals[g], gain_columns, span_bounds, before)
        outs.append(out)

    own_index = [head_index * groups + g for g in range(groups)]
    others, other_index = [], []
    for g in range(groups):
        for k in range(1, head_devices):
            others.append(lax.ppermute(outs[g], "head", [(i, (i + k) % head_devices) for i in range(head_devices)]))
            other_index.append(lax.rem(head_index - k + head_devices, head_devices) * groups + g)
    early = len(others) - (head_devices - 1)
    parts = outs + others[:early]
    index = jnp.stack(own_index + other_index[:early]).astype(jnp.int32)
    acc = out_part(parts, index, out_weight, None, F32)
    index = jnp.stack(other_index[early:]).astype(jnp.int32)
    attended = out_part(others[early:], index, out_weight, acc, BF)

    keep, send = before
    sums = keep + swap(send, "rep", 1).astype(F32)
    span_rows = sums.shape[0] // spread
    place = lax.axis_index("seq")
    own = lax.dynamic_slice_in_dim(sums, place * span_rows, span_rows, 0)
    for k in range(1, spread):
        target = lax.rem(place + k, spread)
        piece = lax.dynamic_slice_in_dim(sums, target * span_rows, span_rows, 0).astype(BF)
        own = own + lax.ppermute(piece, "seq", [(i, (i + k) % spread) for i in range(spread)]).astype(F32)
    own_bounds = lax.dynamic_slice_in_dim(span_bounds, seq_index * span_rows, span_rows, 0)
    counts = (own_bounds[:, 1] - own_bounds[:, 0]).astype(F32)
    own = (own / counts[:, None]).astype(BF)
    width = own.shape[1]
    spread = [own] + [
        lax.ppermute(own, "head", [(i, (i + k) % head_devices) for i in range(head_devices)])
        for k in range(1, head_devices)
    ]
    pooled = None
    for k, values in enumerate(spread):
        source = lax.rem(head_index - k + head_devices, head_devices)
        weight = lax.dynamic_slice_in_dim(out_weight, source * width, width, 0)
        term = jnp.dot(values, weight, preferred_element_type=F32)
        pooled = term if pooled is None else pooled + term
    return (attended, pooled)


def solution(mesh):
    placed = (
        P(("groups", "seq", "rep"), None),
        P(),
        P(None, "head"),
        P(None, "head"),
        P(None, "head"),
        P(None, "head"),
        P(None, "head"),
        P(None, "head"),
        P("groups", None),
    )
    return jax.shard_map(
        per_device,
        mesh=mesh,
        in_specs=placed,
        out_specs=(P(("groups", "seq", "rep"), "head"), P(("groups", "seq", "rep"), "head")),
        check_vma=False,
    )
```

time: 97.5 us -> 93.7 us (0.961)
  other arithmetic: 3.58 us -> 0.44 us
  starting transfers between devices: 19.2 us -> 20.7 us
  waiting for transfers between devices: 33.8 us -> 32.4 us
    ppermute x11 -> x9, waiting for transfers between devices: 18.7 us -> 13.5 us  [swap(): return lax.ppermute(values, axis, [(i, i ^ step) for i in range(count)])]
    ppermute x4 -> x7, starting transfers between devices: 6.35 us -> 9.35 us  [the longest x3 3.87 us: per_device(): lax.ppermute(piece, 'seq', [(i, (i + k) % spread) for i in range(spread)])]
    ppermute x4 -> x7, waiting for transfers between devices: 6.66 us -> 8.94 us  [the longest x2 7.54 us: per_device(): lax.ppermute(outs[g], 'head', [(i, (i + k) % head_devices) for i in range...]
    convert_element_type x9 -> x6, other arithmetic: 2.12 us -> 0.21 us  [add(): return (a.astype(F32) + b.astype(F32)).astype(BF)]
    unnamed x31 -> x26, local copies, waits for them, and re-layouts: 6.14 us -> 4.59 us
    ppermute x1, waiting for transfers between devices: 8.41 us -> 9.9 us  [per_device(): lax.ppermute(own, 'head', [(i, (i + k) % head_devices) for i in range(hea...]
    ppermute x11 -> x9, starting transfers between devices: 11.3 us -> 9.85 us  [swap(): return lax.ppermute(values, axis, [(i, i ^ step) for i in range(count)])]
    concatenate x2 -> x0, other arithmetic: 1.3 us -> none  [the longest x1 0.65 us: per_device(): heads = jnp.concatenate([f[1][:HALF] for f in fronts], axis=1)]
  transfers between devices with their start and end apart: 16 -> 17, of which waited for: 7 -> 7; matrix products, arithmetic and copies ran while one was open for 5% -> 3% of each run, Pallas kernels for 18% -> 21%
where the time goes in v2:
time: 93.7 us; the launch traced here: 93.4 us
  waiting for transfers between devices  32.4 us (35%)
  Pallas kernels  32.3 us (34%)
  starting transfers between devices  20.7 us (22%)
  local copies, waits for them, and re-layouts  5.66 us (6%)
  matrix products  0.97 us (1%)
  between operations  0.94 us (1%)
    pallas_call x2, Pallas kernels, front(): pl.pallas_call(functools.partial(front_kernel, first, group, pairs, tile)...  15.3 us
    ppermute x9, waiting for transfers between devices, swap(): return lax.ppermute(values, axis, [(i, i ^ step) for i in range(count)])  13.5 us
    ppermute x1, waiting for transfers between devices, per_device(): lax.ppermute(own, 'head', [(i, (i + k) % head_devices) for i in range(hea...  9.9 us
    ppermute x9, starting transfers between devices, swap(): return lax.ppermute(values, axis, [(i, i ^ step) for i in range(count)])  9.85 us
    pallas_call x2, Pallas kernels, near(): pl.pallas_call(functools.partial(near_kernel, pairs, group), in_specs=[sm...  8.94 us
    ppermute x2, waiting for transfers between devices, per_device(): lax.ppermute(outs[g], 'head', [(i, (i + k) % head_devices) for i in range...  7.54 us
    pallas_call x2, Pallas kernels, far(): pl.pallas_call(functools.partial(far_kernel, pairs, group, 256, spread),...  5.09 us
    unnamed x26, local copies, waits for them, and re-layouts  4.59 us
  transfers between devices with their start and end apart: 17, of which 7 were waited for; matrix products, arithmetic and copies ran while one was open for 3% of the time, Pallas kernels for 21%

profile of v2, /device:TPU:0, one launch (start us, length us, event | category | flops | bytes accessed | tf_op | source)
XLA Modules:
  0.0 93.4 jit_solution(6948410293298996220)
XLA Ops:
  0.6 0.1 pad_add_fusion.refs_0_.ids_ref
  0.7 0.7 copy-done.1
  1.4 0.7 copy-done.6
  2.1 8.7 %front.2 = (bf16[1024,1024]{1,0:T(8,128)(2,1)S(1)}, bf16[1024,512]{1,0:T(8,128)(2,1)S(1)}, bf16[256,256]{1,0:T(8,128)(2,1)S(1)}, bf16[256,256]{1,0:T(8,128)(2,1)S(1)}) custom-call(s32[4]{0:T(128)S(1)} %pad_add_fusion.refs_0_.ids_ref, bf16[1024,1024]{1,0:T(8,128)(2,1)} %refs_1_.1, f32[1,1024]{1,0:T(1,128)S(1)} %bitcast.16, bf16[1024,512]{1,0:T(8,128)(2,1)} %wk_ref.3, ...), custom_call_target="tpu_custom_call" | custom-call | flops 6442450944 | bytes 4194304 | tf_op jit(solution)/shard_map/front/pallas_call | solution.py:159
  10.9 1.3 %copy-done.8 = bf16[1024,1024]{1,0:T(8,128)(2,1)} copy-done((bf16[1024,1024]{1,0:T(8,128)(2,1)}, bf16[1024,1024]{1,0:T(8,128)(2,1)S(1)}, u32[]{:S(2)}) %copy-start.8) | copy-done | bytes 2097176
  12.2 0.5 collective-permute-start
  12.6 1.0 %fusion.5 = (bf16[64,1024]{1,0:T(8,128)(2,1)S(1)}, bf16[64,1024]{1,0:T(8,128)(2,1)S(1)}) fusion(bf16[1024,1024]{1,0:T(8,128)(2,1)} %refs_1_.1), kind=kLoop, calls=%fused_computation.21 | loop fusion | bytes 524288 | tf_op jit(solution)/shard_map/slice | solution.py:399
  13.6 2.0 %collective-permute-start.1 = (bf16[64,1024]{1,0:T(8,128)(2,1)S(1)}, bf16[64,1024]{1,0:T(8,128)(2,1)S(1)}, u32[]{:S(2)}, u32[]{:S(2)}) collective-permute-start(bf16[64,1024]{1,0:T(8,128)(2,1)S(1)} %get-tuple-element.43), channel_id=1, source_target_pairs={{0,1},{1,4},{4,5},{5,8},{8,9},{9,12},{12,13},{2,3},{3,6},{6,7},{7,... | collective-permute-start | bytes 393224 | tf_op jit(solution)/shard_map/ppermute | solution.py:398
  15.6 1.5 %collective-permute-start.2 = (bf16[64,1024]{1,0:T(8,128)(2,1)S(1)}, bf16[64,1024]{1,0:T(8,128)(2,1)S(1)}, u32[]{:S(2)}, u32[]{:S(2)}) collective-permute-start(bf16[64,1024]{1,0:T(8,128)(2,1)S(1)} %get-tuple-element.42), channel_id=1, source_target_pairs={{1,0},{4,1},{5,4},{8,5},{9,8},{12,9},{13,12},{3,2},{6,3},{7,6},{10... | collective-permute-start | bytes 393224 | tf_op jit(solution)/shard_map/ppermute | solution.py:399
  17.1 0.1 copy.11
  17.3 0.1 copy.13.refs_6_
  17.4 0.0 copy-start.3
  17.4 0.0 copy-start.4
  17.4 0.0 copy-start.5
  17.4 4.9 %collective-permute-start.7 = (bf16[256,256]{1,0:T(8,128)(2,1)S(1)}, bf16[256,256]{1,0:T(8,128)(2,1)S(1)}, u32[]{:S(2)}, u32[]{:S(2)}) collective-permute-start(bf16[256,256]{1,0:T(8,128)(2,1)S(1)} %add_convert_fusion.5), channel_id=1, source_target_pairs={{0,4},{4,0},{8,12},{12,8},{1,5},{5,1},{9,13},{13,9},{2,6},{6,2},{1... | collective-permute-start | bytes 393224 | tf_op jit(solution)/shard_map/ppermute | solution.py:349
  22.4 1.6 %copy-done.9 = bf16[1024,1024]{1,0:T(8,128)(2,1)S(1)} copy-done((bf16[1024,1024]{1,0:T(8,128)(2,1)S(1)}, bf16[1024,1024]{1,0:T(8,128)(2,1)}, u32[]{:S(2)}) %copy-start.9) | copy-done | bytes 2097176
  24.0 6.6 %front.3 = (bf16[1024,512]{1,0:T(8,128)(2,1)S(1)}, bf16[256,256]{1,0:T(8,128)(2,1)S(1)}, bf16[256,256]{1,0:T(8,128)(2,1)S(1)}) custom-call(s32[4]{0:T(128)S(1)} %pad_add_fusion.refs_0_.ids_ref, bf16[1024,1024]{1,0:T(8,128)(2,1)S(1)} %copy-done.9, bf16[1024,512]{1,0:T(8,128)(2,1)} %wk_ref.3, bf16[1024,512]{1,0:T(8,128)(2,1)} %wv_ref.3, ...), custom_call_target="tpu_custom_call" | custom-call | flops 6442450944 | bytes 4194304 | tf_op jit(solution)/shard_map/front/pallas_call | solution.py:159
  30.6 0.1 collective-permute-start.3
  30.7 4.5 %near.3 = (bf16[1024,256]{1,0:T(8,128)(2,1)S(1)}, f32[1024,512]{1,0:T(8,128)S(1)}) custom-call(s32[4]{0:T(128)S(1)} %pad_add_fusion.refs_0_.ids_ref, bf16[1024,1024]{1,0:T(8,128)(2,1)S(1)} %copy-done.10, bf16[1024,512]{1,0:T(8,128)(2,1)S(1)} %get-tuple-element.32.near_ref, bf16[64,1024]{1,0:T(8,128)(2,1)S(1)} %collective-permute-done.1.prev_ref, ...), custom_call_target="tpu_custom_call" | custom-call | flops 2147483648 | bytes 4194304 | tf_op jit(solution)/shard_map/near/pallas_call | solution.py:233
  35.2 4.5 %near.2 = (bf16[1024,256]{1,0:T(8,128)(2,1)S(1)}, f32[1024,512]{1,0:T(8,128)S(1)}) custom-call(s32[4]{0:T(128)S(1)} %pad_add_fusion.refs_0_.ids_ref, bf16[1024,1024]{1,0:T(8,128)(2,1)S(1)} %copy-done.10, bf16[1024,512]{1,0:T(8,128)(2,1)S(1)} %get-tuple-element.26.near_ref, bf16[64,1024]{1,0:T(8,128)(2,1)S(1)} %collective-permute-done.1.prev_ref, ...), custom_call_target="tpu_custom_call" | custom-call | flops 2147483648 | bytes 4194304 | tf_op jit(solution)/shard_map/near/pallas_call | solution.py:233
  39.7 0.3 collective-permute-start.4
  40.1 3.1 %collective-permute-start.8 = (bf16[256,256]{1,0:T(8,128)(2,1)S(1)}, bf16[256,256]{1,0:T(8,128)(2,1)S(1)}, u32[]{:S(2)}, u32[]{:S(2)}) collective-permute-start(bf16[256,256]{1,0:T(8,128)(2,1)S(1)} %add_convert_fusion.1), channel_id=1, source_target_pairs={{0,8},{4,12},{8,0},{12,4},{1,9},{5,13},{9,1},{13,5},{2,10},{6,14},... | collective-permute-start | bytes 393224 | tf_op jit(solution)/shard_map/ppermute | solution.py:349
  43.2 5.3 %collective-permute-done.4 = bf16[256,256]{1,0:T(8,128)(2,1)S(1)} collective-permute-done((bf16[256,256]{1,0:T(8,128)(2,1)S(1)}, bf16[256,256]{1,0:T(8,128)(2,1)S(1)}, u32[]{:S(2)}, u32[]{:S(2)}) %collective-permute-start.4) | collective-permute-done | bytes 131104 | tf_op jit(solution)/shard_map/ppermute | solution.py:349
  48.5 0.3 collective-permute-start.5
  48.8 0.1 collective-permute-start.9
  48.9 7.5 %collective-permute-done.5 = bf16[256,256]{1,0:T(8,128)(2,1)S(1)} collective-permute-done((bf16[256,256]{1,0:T(8,128)(2,1)S(1)}, bf16[256,256]{1,0:T(8,128)(2,1)S(1)}, u32[]{:S(2)}, u32[]{:S(2)}) %collective-permute-start.5) | collective-permute-done | bytes 131104 | tf_op jit(solution)/shard_map/ppermute | solution.py:349
  56.4 0.1 collective-permute-start.6
  56.5 2.7 %far.2 = (bf16[1024,256]{1,0:T(8,128)(2,1)S(1)}, f32[32,256]{1,0:T(8,128)S(1)}, bf16[32,256]{1,0:T(8,128)(2,1)S(1)}) custom-call(s32[4]{0:T(128)S(1)} %pad_add_fusion.refs_0_.ids_ref, bf16[1024,256]{1,0:T(8,128)(2,1)S(1)} %get-tuple-element.33.refs_1_, f32[1024,512]{1,0:T(8,128)S(1)} %get-tuple-element.34.refs_2_, ...), custom_call_target="tpu_custom_call" | custom-call | flops 2147483648 | bytes 4194304 | tf_op jit(solution)/shard_map/far/pallas_call | solution.py:300
  59.2 2.4 %far.3 = (bf16[1024,256]{1,0:T(8,128)(2,1)S(1)}, f32[32,512]{1,0:T(8,128)S(1)}, bf16[32,512]{1,0:T(8,128)(2,1)S(1)}) custom-call(s32[4]{0:T(128)S(1)} %pad_add_fusion.refs_0_.ids_ref, bf16[1024,256]{1,0:T(8,128)(2,1)S(1)} %get-tuple-element.27.refs_1_, f32[1024,512]{1,0:T(8,128)S(1)} %get-tuple-element.28.refs_2_, ...), custom_call_target="tpu_custom_call" | custom-call | flops 2147483648 | bytes 4194304 | tf_op jit(solution)/shard_map/far/pallas_call | solution.py:300
  61.6 0.6 collective-permute-start.12
  62.2 0.1 constant_dynamic-slice_fusion
  62.2 0.8 collective-permute-done.12
  63.1 0.1 collective-permute-start.13
  63.1 3.1 %collective-permute-start.14 = (bf16[8,512]{1,0:T(8,128)(2,1)S(1)}, bf16[8,512]{1,0:T(8,128)(2,1)S(1)}, u32[]{:S(2)}, u32[]{:S(2)}) collective-permute-start(bf16[8,512]{1,0:T(8,128)(2,1)S(1)} %get-tuple-element.46), channel_id=1, source_target_pairs={{0,8},{4,12},{8,0},{12,4},{1,9},{5,13},{9,1},{13,5},{2,10},{6,14},... | collective-permute-start | bytes 24584 | tf_op jit(solution)/shard_map/ppermute | solution.py:435
  66.2 0.8 collective-permute-start.15
  66.9 1.5 %collective-permute-start.11 = (bf16[1024,256]{1,0:T(8,128)(2,1)S(1)}, bf16[1024,256]{1,0:T(8,128)(2,1)S(1)}, u32[]{:S(2)}, u32[]{:S(2)}) collective-permute-start(bf16[1024,256]{1,0:T(8,128)(2,1)S(1)} %get-tuple-element.39.refs_1_), channel_id=1, source_target_pairs={{0,2},{2,0},{1,3},{3,1},{4,6},{6,4},{5,7},{7,5},{8,10},{10,8},{9,1... | collective-permute-start | bytes 1572872 | tf_op jit(solution)/shard_map/ppermute | solution.py:418
  68.4 0.1 collective-permute-done.13
  68.6 1.3 %collective-permute-done.15 = bf16[8,512]{1,0:T(8,128)(2,1)S(1)} collective-permute-done((bf16[8,512]{1,0:T(8,128)(2,1)S(1)}, bf16[8,512]{1,0:T(8,128)(2,1)S(1)}, u32[]{:S(2)}, u32[]{:S(2)}) %collective-permute-start.15) | collective-permute-done | bytes 8224 | tf_op jit(solution)/shard_map/ppermute | solution.py:435
  69.8 0.1 divide_convert_fusion
  69.9 1.5 %collective-permute-start.16 = (bf16[8,512]{1,0:T(8,128)(2,1)S(1)}, bf16[8,512]{1,0:T(8,128)(2,1)S(1)}, u32[]{:S(2)}, u32[]{:S(2)}) collective-permute-start(bf16[8,512]{1,0:T(8,128)(2,1)S(1)} %divide_convert_fusion), channel_id=1, source_target_pairs={{0,2},{2,0},{1,3},{3,1},{4,6},{6,4},{5,7},{7,5},{8,10},{10,8},{9,1... | collective-permute-start | bytes 24584 | tf_op jit(solution)/shard_map/ppermute | solution.py:441
  71.4 0.1 pad_add_fusion.1.refs_0_
  71.5 0.5 collective-permute-start.10
  72.0 9.9 %collective-permute-done.16 = bf16[8,512]{1,0:T(8,128)(2,1)S(1)} collective-permute-done((bf16[8,512]{1,0:T(8,128)(2,1)S(1)}, bf16[8,512]{1,0:T(8,128)(2,1)S(1)}, u32[]{:S(2)}, u32[]{:S(2)}) %collective-permute-start.16) | collective-permute-done | bytes 8224 | tf_op jit(solution)/shard_map/ppermute | solution.py:441
  81.9 0.2 fusion
  82.1 0.8 convolution_add_fusion
  82.9 1.5 %out.2.refs_3_ = f32[1024,512]{1,0:T(8,128)S(1)} custom-call(s32[3]{0:T(128)S(1)} %pad_add_fusion.1.refs_0_, bf16[1024,256]{1,0:T(8,128)(2,1)S(1)} %get-tuple-element.39.refs_1_, bf16[1024,256]{1,0:T(8,128)(2,1)S(1)} %get-tuple-element.38.refs_2_, bf16[1024,256]{1,0:T(8,128)(2,1)S(1)} %collective-permute-done.11.refs_3_, bf16[1024,512]{1,0:T(8,128)(2,1)S(1)} %copy-done), custom_call_target="tpu_custom_call" | custom-call | flops 805306368 | bytes 4194304 | tf_op jit(solution)/shard_map/out/pallas_call | solution.py:334
  84.4 7.5 %collective-permute-done.10.refs_1_ = bf16[1024,256]{1,0:T(8,128)(2,1)S(1)} collective-permute-done((bf16[1024,256]{1,0:T(8,128)(2,1)S(1)}, bf16[1024,256]{1,0:T(8,128)(2,1)S(1)}, u32[]{:S(2)}, u32[]{:S(2)}) %collective-permute-start.10) | collective-permute-done | bytes 524320 | tf_op jit(solution)/shard_map/ppermute | solution.py:418
  92.0 1.4 %out.3 = bf16[1024,512]{1,0:T(8,128)(2,1)} custom-call(s32[1]{0:T(128)} %bitcast.refs_0_, bf16[1024,256]{1,0:T(8,128)(2,1)S(1)} %collective-permute-done.10.refs_1_, bf16[1024,512]{1,0:T(8,128)(2,1)S(1)} %copy-done, f32[1024,512]{1,0:T(8,128)S(1)} %out.2.refs_3_), custom_call_target="tpu_custom_call" | custom-call | flops 268435456 | bytes 4194304 | tf_op jit(solution)/shard_map/out/pallas_call | solution.py:334
  (36 shorter events, 0.3 us)
Async XLA Ops:
  0.7 0.7 copy-start.1
  1.4 0.7 copy-start.6
  2.1 15.0 %copy-start.2 = (f32[4,512]{1,0:T(4,128)S(1)}, f32[4,512]{1,0:T(4,128)}, u32[]{:S(2)}) copy-start(f32[4,512]{1,0:T(4,128)} %dual_ref.3) | copy-start | bytes 24580
  2.1 15.1 %copy-start.11 = (s32[64,2]{0,1:T(2,128)S(1)}, s32[64,2]{0,1:T(2,128)}, u32[]{:S(2)}) copy-start(s32[64,2]{0,1:T(2,128)} %param.17) | copy-start | bytes 1540
  10.8 1.3 %copy-start.8 = (bf16[1024,1024]{1,0:T(8,128)(2,1)}, bf16[1024,1024]{1,0:T(8,128)(2,1)S(1)}, u32[]{:S(2)}) copy-start(bf16[1024,1024]{1,0:T(8,128)(2,1)S(1)} %get-tuple-element.25.refs_1_.normed_ref) | copy-start | bytes 6291460
  12.2 5.2 %collective-permute-start = (bf16[256,256]{1,0:T(8,128)(2,1)S(1)}, bf16[256,256]{1,0:T(8,128)(2,1)S(1)}, u32[]{:S(2)}, u32[]{:S(2)}) collective-permute-start(bf16[256,256]{1,0:T(8,128)(2,1)S(1)} %get-tuple-element.24), channel_id=1, source_target_pairs={{0,1},{1,0},{2,3},{3,2},{4,5},{5,4},{6,7},{7,6},{8,9},{9,8},{10,11... | collective-permute-start | bytes 393224 | tf_op jit(solution)/shard_map/ppermute | solution.py:349
  13.6 17.0 %collective-permute-start.1 = (bf16[64,1024]{1,0:T(8,128)(2,1)S(1)}, bf16[64,1024]{1,0:T(8,128)(2,1)S(1)}, u32[]{:S(2)}, u32[]{:S(2)}) collective-permute-start(bf16[64,1024]{1,0:T(8,128)(2,1)S(1)} %get-tuple-element.43), channel_id=1, source_target_pairs={{0,1},{1,4},{4,5},{5,8},{8,9},{9,12},{12,13},{2,3},{3,6},{6,7},{7,... | collective-permute-start | bytes 393224 | tf_op jit(solution)/shard_map/ppermute | solution.py:398
  15.6 15.1 %collective-permute-start.2 = (bf16[64,1024]{1,0:T(8,128)(2,1)S(1)}, bf16[64,1024]{1,0:T(8,128)(2,1)S(1)}, u32[]{:S(2)}, u32[]{:S(2)}) collective-permute-start(bf16[64,1024]{1,0:T(8,128)(2,1)S(1)} %get-tuple-element.42), channel_id=1, source_target_pairs={{1,0},{4,1},{5,4},{8,5},{9,8},{12,9},{13,12},{3,2},{6,3},{7,6},{10... | collective-permute-start | bytes 393224 | tf_op jit(solution)/shard_map/ppermute | solution.py:399
  17.4 13.3 %copy-start.3 = (bf16[1024,512]{1,0:T(8,128)(2,1)S(1)}, bf16[1024,512]{1,0:T(8,128)(2,1)}, u32[]{:S(2)}) copy-start(bf16[1024,512]{1,0:T(8,128)(2,1)} %wk_ref.3) | copy-start | bytes 3145732
  17.4 13.3 %copy-start.4 = (bf16[1024,512]{1,0:T(8,128)(2,1)S(1)}, bf16[1024,512]{1,0:T(8,128)(2,1)}, u32[]{:S(2)}) copy-start(bf16[1024,512]{1,0:T(8,128)(2,1)} %wv_ref.3) | copy-start | bytes 3145732
  17.4 13.3 %copy-start.5 = (bf16[1024,512]{1,0:T(8,128)(2,1)S(1)}, bf16[1024,512]{1,0:T(8,128)(2,1)}, u32[]{:S(2)}) copy-start(bf16[1024,512]{1,0:T(8,128)(2,1)} %wq_ref.3) | copy-start | bytes 3145732
  17.4 13.3 %copy-start.7 = (f32[1024]{0:T(1024)S(1)}, f32[1024]{0:T(1024)}, u32[]{:S(2)}) copy-start(f32[1024]{0:T(1024)} %param.10) | copy-start | bytes 12292
  17.4 22.6 %collective-permute-start.7 = (bf16[256,256]{1,0:T(8,128)(2,1)S(1)}, bf16[256,256]{1,0:T(8,128)(2,1)S(1)}, u32[]{:S(2)}, u32[]{:S(2)}) collective-permute-start(bf16[256,256]{1,0:T(8,128)(2,1)S(1)} %add_convert_fusion.5), channel_id=1, source_target_pairs={{0,4},{4,0},{8,12},{12,8},{1,5},{5,1},{9,13},{13,9},{2,6},{6,2},{1... | collective-permute-start | bytes 393224 | tf_op jit(solution)/shard_map/ppermute | solution.py:349
  22.4 1.6 %copy-start.9 = (bf16[1024,1024]{1,0:T(8,128)(2,1)S(1)}, bf16[1024,1024]{1,0:T(8,128)(2,1)}, u32[]{:S(2)}) copy-start(bf16[1024,1024]{1,0:T(8,128)(2,1)} %copy-done.8) | copy-start | bytes 6291460
  24.0 6.7 %copy-start.10 = (bf16[1024,1024]{1,0:T(8,128)(2,1)S(1)}, bf16[1024,1024]{1,0:T(8,128)(2,1)}, u32[]{:S(2)}) copy-start(bf16[1024,1024]{1,0:T(8,128)(2,1)} %copy-done.8) | copy-start | bytes 6291460
  30.6 9.1 %collective-permute-start.3 = (bf16[256,256]{1,0:T(8,128)(2,1)S(1)}, bf16[256,256]{1,0:T(8,128)(2,1)S(1)}, u32[]{:S(2)}, u32[]{:S(2)}) collective-permute-start(bf16[256,256]{1,0:T(8,128)(2,1)S(1)} %get-tuple-element.30), channel_id=1, source_target_pairs={{0,1},{1,0},{2,3},{3,2},{4,5},{5,4},{6,7},{7,6},{8,9},{9,8},{10,11... | collective-permute-start | bytes 393224 | tf_op jit(solution)/shard_map/ppermute | solution.py:349
  39.7 8.8 %collective-permute-start.4 = (bf16[256,256]{1,0:T(8,128)(2,1)S(1)}, bf16[256,256]{1,0:T(8,128)(2,1)S(1)}, u32[]{:S(2)}, u32[]{:S(2)}) collective-permute-start(bf16[256,256]{1,0:T(8,128)(2,1)S(1)} %add_convert_fusion.4), channel_id=1, source_target_pairs={{0,4},{4,0},{8,12},{12,8},{1,5},{5,1},{9,13},{13,9},{2,6},{6,2},{1... | collective-permute-start | bytes 393224 | tf_op jit(solution)/shard_map/ppermute | solution.py:349
  40.1 8.7 %collective-permute-start.8 = (bf16[256,256]{1,0:T(8,128)(2,1)S(1)}, bf16[256,256]{1,0:T(8,128)(2,1)S(1)}, u32[]{:S(2)}, u32[]{:S(2)}) collective-permute-start(bf16[256,256]{1,0:T(8,128)(2,1)S(1)} %add_convert_fusion.1), channel_id=1, source_target_pairs={{0,8},{4,12},{8,0},{12,4},{1,9},{5,13},{9,1},{13,5},{2,10},{6,14},... | collective-permute-start | bytes 393224 | tf_op jit(solution)/shard_map/ppermute | solution.py:349
  48.5 7.8 %collective-permute-start.5 = (bf16[256,256]{1,0:T(8,128)(2,1)S(1)}, bf16[256,256]{1,0:T(8,128)(2,1)S(1)}, u32[]{:S(2)}, u32[]{:S(2)}) collective-permute-start(bf16[256,256]{1,0:T(8,128)(2,1)S(1)} %add_convert_fusion.3), channel_id=1, source_target_pairs={{0,8},{4,12},{8,0},{12,4},{1,9},{5,13},{9,1},{13,5},{2,10},{6,14},... | collective-permute-start | bytes 393224 | tf_op jit(solution)/shard_map/ppermute | solution.py:349
  48.8 7.7 %collective-permute-start.9 = (bf16[256,256]{1,0:T(8,128)(2,1)S(1)}, bf16[256,256]{1,0:T(8,128)(2,1)S(1)}, u32[]{:S(2)}, u32[]{:S(2)}) collective-permute-start(bf16[256,256]{1,0:T(8,128)(2,1)S(1)} %add_convert_fusion.refs_3_), channel_id=1, source_target_pairs={{0,1},{1,0},{2,3},{3,2},{4,5},{5,4},{6,7},{7,6},{8,9},{9,8},{10,11... | collective-permute-start | bytes 393224 | tf_op jit(solution)/shard_map/ppermute | solution.py:349
  56.4 2.8 %collective-permute-start.6 = (bf16[256,256]{1,0:T(8,128)(2,1)S(1)}, bf16[256,256]{1,0:T(8,128)(2,1)S(1)}, u32[]{:S(2)}, u32[]{:S(2)}) collective-permute-start(bf16[256,256]{1,0:T(8,128)(2,1)S(1)} %add_convert_fusion.2.refs_3_), channel_id=1, source_target_pairs={{0,1},{1,0},{2,3},{3,2},{4,5},{5,4},{6,7},{7,6},{8,9},{9,8},{10,11... | collective-permute-start | bytes 393224 | tf_op jit(solution)/shard_map/ppermute | solution.py:349
  59.2 22.8 %copy-start = (bf16[1024,512]{1,0:T(8,128)(2,1)S(1)}, bf16[1024,512]{1,0:T(8,128)(2,1)}, u32[]{:S(2)}) copy-start(bf16[1024,512]{1,0:T(8,128)(2,1)} %refs_2_.3) | copy-start | bytes 3145732
  61.6 1.4 %collective-permute-start.12 = (bf16[32,512]{1,0:T(8,128)(2,1)S(1)}, bf16[32,512]{1,0:T(8,128)(2,1)S(1)}, u32[]{:S(2)}, u32[]{:S(2)}) collective-permute-start(bf16[32,512]{1,0:T(8,128)(2,1)S(1)} %get-tuple-element.41), channel_id=1, source_target_pairs={{0,1},{1,0},{2,3},{3,2},{4,5},{5,4},{6,7},{7,6},{8,9},{9,8},{10,11... | collective-permute-start | bytes 98312 | tf_op jit(solution)/shard_map/ppermute | solution.py:349
  63.1 5.5 %collective-permute-start.13 = (bf16[8,512]{1,0:T(8,128)(2,1)S(1)}, bf16[8,512]{1,0:T(8,128)(2,1)S(1)}, u32[]{:S(2)}, u32[]{:S(2)}) collective-permute-start(bf16[8,512]{1,0:T(8,128)(2,1)S(1)} %get-tuple-element.44), channel_id=1, source_target_pairs={{0,4},{4,8},{8,12},{12,0},{1,5},{5,9},{9,13},{13,1},{2,6},{6,10},{... | collective-permute-start | bytes 24584 | tf_op jit(solution)/shard_map/ppermute | solution.py:435
  63.1 5.4 %collective-permute-start.14 = (bf16[8,512]{1,0:T(8,128)(2,1)S(1)}, bf16[8,512]{1,0:T(8,128)(2,1)S(1)}, u32[]{:S(2)}, u32[]{:S(2)}) collective-permute-start(bf16[8,512]{1,0:T(8,128)(2,1)S(1)} %get-tuple-element.46), channel_id=1, source_target_pairs={{0,8},{4,12},{8,0},{12,4},{1,9},{5,13},{9,1},{13,5},{2,10},{6,14},... | collective-permute-start | bytes 24584 | tf_op jit(solution)/shard_map/ppermute | solution.py:435
  66.2 3.7 %collective-permute-start.15 = (bf16[8,512]{1,0:T(8,128)(2,1)S(1)}, bf16[8,512]{1,0:T(8,128)(2,1)S(1)}, u32[]{:S(2)}, u32[]{:S(2)}) collective-permute-start(bf16[8,512]{1,0:T(8,128)(2,1)S(1)} %get-tuple-element.45), channel_id=1, source_target_pairs={{0,12},{4,0},{8,4},{12,8},{1,13},{5,1},{9,5},{13,9},{2,14},{6,2},{... | collective-permute-start | bytes 24584 | tf_op jit(solution)/shard_map/ppermute | solution.py:435
  66.9 16.0 %collective-permute-start.11 = (bf16[1024,256]{1,0:T(8,128)(2,1)S(1)}, bf16[1024,256]{1,0:T(8,128)(2,1)S(1)}, u32[]{:S(2)}, u32[]{:S(2)}) collective-permute-start(bf16[1024,256]{1,0:T(8,128)(2,1)S(1)} %get-tuple-element.39.refs_1_), channel_id=1, source_target_pairs={{0,2},{2,0},{1,3},{3,1},{4,6},{6,4},{5,7},{7,5},{8,10},{10,8},{9,1... | collective-permute-start | bytes 1572872 | tf_op jit(solution)/shard_map/ppermute | solution.py:418
  69.9 12.0 %collective-permute-start.16 = (bf16[8,512]{1,0:T(8,128)(2,1)S(1)}, bf16[8,512]{1,0:T(8,128)(2,1)S(1)}, u32[]{:S(2)}, u32[]{:S(2)}) collective-permute-start(bf16[8,512]{1,0:T(8,128)(2,1)S(1)} %divide_convert_fusion), channel_id=1, source_target_pairs={{0,2},{2,0},{1,3},{3,1},{4,6},{6,4},{5,7},{7,5},{8,10},{10,8},{9,1... | collective-permute-start | bytes 24584 | tf_op jit(solution)/shard_map/ppermute | solution.py:441
  71.5 20.5 %collective-permute-start.10 = (bf16[1024,256]{1,0:T(8,128)(2,1)S(1)}, bf16[1024,256]{1,0:T(8,128)(2,1)S(1)}, u32[]{:S(2)}, u32[]{:S(2)}) collective-permute-start(bf16[1024,256]{1,0:T(8,128)(2,1)S(1)} %get-tuple-element.38.refs_2_), channel_id=1, source_target_pairs={{0,2},{2,0},{1,3},{3,1},{4,6},{6,4},{5,7},{7,5},{8,10},{10,8},{9,1... | collective-permute-start | bytes 1572872 | tf_op jit(solution)/shard_map/ppermute | solution.py:418

commit v3 on v2

--- a/solution.py
+++ b/solution.py
@@ -15,6 +15,11 @@
 SCORE_SCALE = DH ** (-0.5)
 LOG2E = 1.4426950408889634
 
+VMEM_LIMIT = 40 << 20
+COST = pl.CostEstimate(flops=1 << 20, bytes_accessed=1 << 10, transcendentals=0)
+
+TURN = jax.ShapeDtypeStruct((4,), jnp.int32)
+
 softcap = 5.0
 epsilon = 1e-05
 
@@ -28,6 +33,11 @@
 
 def exp_capped(values, scale):
     return jnp.exp2((softcap * LOG2E) * jnp.tanh(values * (scale / softcap)))
+
+
+def pass_turn(ids_ref, turn_ref):
+    for i in range(4):
+        turn_ref[i] = ids_ref[i]
 
 
 def vmem():
@@ -62,13 +72,31 @@
     return (centred * lax.rsqrt(spread + epsilon) * gain).astype(BF)
 
 
-def front_kernel(first, group, pairs, tile, *refs):
+def edge_rows(near_ref):
+    rows = near_ref.shape[0]
+    columns = [slice(at, at + 2 * LANES) for at in range(0, near_ref.shape[1], 2 * LANES)]
+    return [jnp.concatenate([near_ref[at, c] for c in columns], axis=0) for at in (slice(0, HALF), slice(rows - HALF, rows))]
+
+
+def front_kernel(first, last, group, pairs, tile, *refs):
+    ids_ref, refs = refs[0], list(refs[1:])
     if first:
-        (ids_ref, x_hbm, gain_ref, wk_hbm, wv_hbm, wp_hbm, dual_ref,
-         normed_ref, near_ref, keep_ref, send_ref, raw_ref, p_ref, wk_ref, wv_ref, wp_ref, sem, x_ref) = refs
+        x_hbm, gain_ref = refs.pop(0), refs.pop(0)
     else:
-        (ids_ref, normed_ref, wk_hbm, wv_hbm, wp_hbm, dual_ref,
-         near_ref, keep_ref, send_ref, raw_ref, p_ref, wk_ref, wv_ref, wp_ref, sem) = refs
+        normed_ref = refs.pop(0)
+    wk_hbm, wv_hbm, wp_hbm, dual_ref = refs[:4]
+    refs = refs[4:]
+    earlier = [refs.pop(0) for _ in range(group)] if last else []
+    out = refs.pop(0)
+    if first:
+        normed_ref = out
+    near_ref, keep_ref, send_ref, edge_ref, turn_ref = refs[:5]
+    refs = refs[5:]
+    pass_turn(ids_ref, turn_ref)
+    raw_ref, p_ref, wk_ref, wv_ref, wp_ref, sem = refs[:6]
+    if first:
+        x_ref, gain_hbm, dual_hbm = refs[6], gain_ref, dual_ref
+        gain_ref, dual_ref = refs[7:]
     rows = normed_ref.shape[0]
     width = pairs * LANES
     chunks = rows // tile
@@ -84,6 +112,9 @@
         return copy(x_hbm.at[at, :], x_ref.at[at, :], i)
 
     token_copies = [token_copy(0)] if first else []
+    if first:
+        gain_copy = copy(gain_hbm, gain_ref, chunks + 2 + pairs)
+        dual_copy = copy(dual_hbm, dual_ref, chunks + 3 + pairs)
     key_copy = copy(wk_hbm.at[:, own], wk_ref, chunks)
     value_copy = copy(wv_hbm.at[:, own], wv_ref, chunks + 1)
     proj_copies = []
@@ -96,6 +127,9 @@
         at = pl.ds(i * tile, tile)
         if first:
             token_copies[i].wait()
+            if i == 0:
+                gain_copy.wait()
+                dual_copy.wait()
             normed_ref[at, :] = token_norm(x_ref[at, :], gain_ref[...])
         normed = normed_ref[at, :]
         if i == 0:
@@ -124,48 +158,64 @@
     half = total.shape[0] // 2
     mine = ids_ref[0] == 0
     keep_ref[...] = jnp.where(mine, total[:half], total[half:])
-    send_ref[...] = jnp.where(mine, total[half:], total[:half])
+    send_ref[:half, :] = jnp.where(mine, total[half:], total[:half])
+    head, tail = edge_rows(near_ref)
+    edge = head.shape[0]
+    if last:
+        for i, ref in enumerate(earlier):
+            before = jnp.where(mine, ref[edge:, :], ref[:edge, :])
+            send_ref[half + i * edge : half + (i + 1) * edge, :] = before
+            edge_ref[i * edge : (i + 1) * edge, :] = jnp.where(mine, ref[:edge, :], ref[edge:, :])
+        send_ref[half + group * edge :, :] = jnp.where(mine, tail, head)
+        edge_ref[group * edge :, :] = jnp.where(mine, head, tail)
+    else:
+        edge_ref[:edge, :] = head
+        edge_ref[edge:, :] = tail
 
 
 def in_hbm(values):
     return pltpu.with_memory_space_constraint(values, pltpu.HBM)
 
 
-def front(first, group, pairs, ids, tokens, gain, wk, wv, wp, dual):
+def front(first, last, group, pairs, ids, tokens, gain, wk, wv, wp, dual, earlier):
     rows, depth = tokens.shape
     width = pairs * LANES
     half = pairs * R // 2
     tile = min(256, rows)
+    edge = (group + 1) * pairs * HALF if last else 0
     outs = [
+        jax.ShapeDtypeStruct((rows, depth), BF),
         jax.ShapeDtypeStruct((rows, 2 * width), BF),
         jax.ShapeDtypeStruct((half, R), BF),
-        jax.ShapeDtypeStruct((half, R), BF),
+        jax.ShapeDtypeStruct((half + edge, R), BF),
+        jax.ShapeDtypeStruct((edge if last else 2 * pairs * HALF, R), BF),
+        TURN,
     ]
     hbm = pl.BlockSpec(memory_space=pltpu.HBM)
-    ins = [smem(), hbm if first else vmem()] + ([vmem()] if first else []) + [hbm] * 3 + [vmem()]
-    args = [ids, in_hbm(tokens) if first else tokens] + ([gain] if first else [])
-    args += [in_hbm(wk), in_hbm(wv), in_hbm(wp), dual]
+    earlier = earlier if last else []
+    ins = [smem()] + [hbm if first else vmem()] * (2 if first else 1) + [hbm] * 3 + [hbm if first else vmem()]
+    ins += [vmem()] * len(earlier)
+    args = [ids] + ([in_hbm(tokens), in_hbm(gain)] if first else [tokens])
+    args += [in_hbm(wk), in_hbm(wv), in_hbm(wp), in_hbm(dual) if first else dual] + earlier
     scratch = [
         pltpu.VMEM((2 * width, rows), BF),
         pltpu.VMEM((rows, 2 * pairs * R), BF),
         pltpu.VMEM((depth, width), BF),
         pltpu.VMEM((depth, width), BF),
         pltpu.VMEM((depth, 2 * pairs * R), BF),
-        pltpu.SemaphoreType.DMA((rows // tile + 2 + pairs,)),
+        pltpu.SemaphoreType.DMA((rows // tile + 4 + pairs,)),
     ]
     if first:
-        outs = [jax.ShapeDtypeStruct((rows, depth), BF)] + outs
-        scratch.append(pltpu.VMEM((rows, depth), BF))
+        scratch += [pltpu.VMEM((rows, depth), BF), pltpu.VMEM((1, depth), F32), pltpu.VMEM(dual.shape, F32)]
     return pl.pallas_call(
-        functools.partial(front_kernel, first, group, pairs, tile),
+        functools.partial(front_kernel, first, last, group, pairs, tile),
+        input_output_aliases={} if first else {1: 0},
         in_specs=ins,
-        out_specs=[vmem()] * len(outs),
+        out_specs=[vmem()] * (len(outs) - 1) + [smem()],
         out_shape=outs,
         scratch_shapes=scratch,
-        compiler_params=pltpu.CompilerParams(vmem_limit_bytes=24 << 20),
-        cost_estimate=pl.CostEstimate(
-            flops=2 * rows * depth * (2 * width + 2 * pairs * R) * 2, bytes_accessed=4 << 20, transcendentals=0
-        ),
+        compiler_params=pltpu.CompilerParams(vmem_limit_bytes=VMEM_LIMIT),
+        cost_estimate=COST,
         name="front",
     )(*args)
 
@@ -189,62 +239,73 @@
     )
 
 
-def near_kernel(pairs, group, ids_ref, normed_ref, near_ref, prev_ref, next_ref, gain_ref, wq_ref, wk_ref, wv_ref, dual_ref,
-                q_ref, out_ref, pad_ref):
+def near_kernel(groups, pairs, *refs):
+    ids_ref, normed_ref, core_ref, chip_ref, wq_ref = refs[:5]
+    near_refs, refs = refs[5 : 5 + groups], refs[5 + groups :]
+    q_refs, out_refs, (turn_ref, pad_ref) = refs[:groups], refs[groups : 2 * groups], refs[2 * groups :]
     rows = normed_ref.shape[0]
     width = pairs * LANES
-    mine = slice(group * width, (group + 1) * width)
-    halo = token_norm(jnp.concatenate([prev_ref[...], next_ref[...]], axis=0), gain_ref[...])
-    key = head_norm(dot(halo, wk_ref[:, mine]), dual_ref[0:1, mine])
-    value = head_norm(dot(halo, wv_ref[:, mine]), dual_ref[1:2, mine])
-    q_ref[...] = dot(normed_ref[...], wq_ref[:, mine]).astype(BF)
-    pad_ref[0:HALF, :width] = key[:HALF]
-    pad_ref[0:HALF, width:] = value[:HALF]
-    pad_ref[HALF : HALF + rows, :] = near_ref[...]
-    pad_ref[HALF + rows :, :width] = key[HALF:]
-    pad_ref[HALF + rows :, width:] = value[HALF:]
+    is_first = ids_ref[0] == 0
     row = lax.broadcasted_iota(jnp.int32, (2 * SEG, LANES), 0)
     ones = jnp.ones((2 * SEG, LANES), F32)
     has_prev = jnp.where(ids_ref[1] != 0, 1.0, 0.0)
     has_next = jnp.where(ids_ref[2] != 0, 1.0, 0.0)
     segments = rows // SEG
-    for s in range(segments):
-        count = ones
-        if s == 0:
-            count = jnp.where(row < HALF, has_prev, count)
-        if s == segments - 1:
-            count = jnp.where(row >= 3 * HALF, has_next, count)
-        count = count.astype(BF)
-        window = pl.ds(s * SEG, 2 * SEG)
-        for p in range(pairs):
-            cols = slice(p * LANES, (p + 1) * LANES)
-            q = stacked(q_ref[s * SEG : (s + 1) * SEG, cols])
-            scores = dot(q, pad_ref[window, cols], ((1,), (1,)))
-            weights = exp_capped(scores, SCORE_SCALE).astype(BF)
-            values = jnp.concatenate([pad_ref[window, width + p * LANES : width + (p + 1) * LANES], count], axis=1)
-            top, bottom = unstack(dot(weights, values))
-            out_ref[s * SEG : (s + 1) * SEG, 2 * p * LANES : (2 * p + 1) * LANES] = top
-            out_ref[s * SEG : (s + 1) * SEG, (2 * p + 1) * LANES : (2 * p + 2) * LANES] = bottom
-
-
-def near(pairs, group, ids, normed, near_pairs, prev, following, gain, wq, wk, wv, dual):
+    offset = core_ref.shape[0] - chip_ref.shape[0]
+    for g in range(groups):
+        q_ref, near_ref, out_ref = q_refs[g], near_refs[g], out_refs[g]
+        q_ref[...] = dot(normed_ref[...], wq_ref[:, g * width : (g + 1) * width]).astype(BF)
+        pad_ref[HALF : HALF + rows, :] = near_ref[...]
+        for c in range(pairs):
+            at = (g * pairs + c) * HALF
+            core = core_ref[offset + at : offset + at + HALF, :]
+            chip = chip_ref[at : at + HALF, :]
+            lanes = slice(2 * c * LANES, 2 * (c + 1) * LANES)
+            pad_ref[0:HALF, lanes] = jnp.where(is_first, chip, core)
+            pad_ref[HALF + rows :, lanes] = jnp.where(is_first, core, chip)
+        for s in range(segments):
+            count = ones
+            if s == 0:
+                count = jnp.where(row < HALF, has_prev, count)
+            if s == segments - 1:
+                count = jnp.where(row >= 3 * HALF, has_next, count)
+            count = count.astype(BF)
+            window = pl.ds(s * SEG, 2 * SEG)
+            here = slice(s * SEG, (s + 1) * SEG)
+            for p in range(pairs):
+                cols = slice(p * LANES, (p + 1) * LANES)
+                scores = dot(stacked(q_ref[here, cols]), pad_ref[window, cols], ((1,), (1,)))
+                weights = exp_capped(scores, SCORE_SCALE).astype(BF)
+                values = jnp.concatenate([pad_ref[window, width + p * LANES : width + (p + 1) * LANES], count], axis=1)
+                top, bottom = unstack(dot(weights, values))
+                out_ref[here, 2 * p * LANES : (2 * p + 1) * LANES] = top
+                out_ref[here, (2 * p + 1) * LANES : (2 * p + 2) * LANES] = bottom
+    pass_turn(ids_ref, turn_ref)
+
+
+def near(pairs, ids, normed, core, chip, wq, near_pairs):
     rows = normed.shape[0]
     width = pairs * LANES
-    return pl.pallas_call(
-        functools.partial(near_kernel, pairs, group),
-        in_specs=[smem()] + [vmem()] * 9,
-        out_specs=[vmem()] * 2,
-        out_shape=[jax.ShapeDtypeStruct((rows, width), BF), jax.ShapeDtypeStruct((rows, 2 * width), F32)],
+    groups = len(near_pairs)
+    outs = pl.pallas_call(
+        functools.partial(near_kernel, groups, pairs),
+        in_specs=[smem()] + [vmem()] * (4 + groups),
+        out_specs=[vmem()] * (2 * groups) + [smem()],
+        out_shape=[jax.ShapeDtypeStruct((rows, width), BF)] * groups
+        + [jax.ShapeDtypeStruct((rows, 2 * width), F32)] * groups
+        + [TURN],
         scratch_shapes=[pltpu.VMEM((rows + SEG, 2 * width), BF)],
-        compiler_params=pltpu.CompilerParams(vmem_limit_bytes=16 << 20),
-        cost_estimate=pl.CostEstimate(flops=rows * pairs * (1 << 20), bytes_accessed=4 << 20, transcendentals=0),
+        compiler_params=pltpu.CompilerParams(vmem_limit_bytes=VMEM_LIMIT),
+        cost_estimate=COST,
         name="near",
-    )(ids, normed, near_pairs, prev, following, gain, wq, wk, wv, dual)
+    )(ids, normed, core, chip, wq, *near_pairs)
+    return list(zip(outs[:groups], outs[groups : 2 * groups])), outs[-1]
 
 
 def far_kernel(pairs, group, block, spread, *refs):
     (ids_ref, q_ref, near_ref, mine_ref, other_ref, gains_ref, bounds_ref), refs = refs[:7], refs[7:]
-    before, (out_ref, keep_ref, send_ref) = refs[:-3], refs[-3:]
+    before, (out_ref, keep_ref, send_ref, turn_ref) = refs[:-4], refs[-4:]
+    pass_turn(ids_ref, turn_ref)
     rows = q_ref.shape[0]
     width = pairs * LANES
     is_first = ids_ref[0] == 0
@@ -255,6 +316,9 @@
     for p in range(pairs):
         cols = slice(p * LANES, (p + 1) * LANES)
 
+        base = group * width + p * LANES
+        gains = jnp.concatenate([gains_ref[:, base : base + LANES]] * 2, axis=0).T
+
         def land(kind):
             parts = []
             for h in range(2):
@@ -262,8 +326,7 @@
                 values = total[at : at + DH].astype(F32)
                 centred = values - jnp.mean(values, axis=0, keepdims=True)
                 spread = jnp.mean(centred * centred, axis=0, keepdims=True)
-                base = group * width + p * LANES + h * DH
-                gain = gains_ref[base : base + DH, 2 + kind : 3 + kind]
+                gain = gains[h * DH : (h + 1) * DH, 2 + kind : 3 + kind]
                 parts.append((centred * lax.rsqrt(spread + epsilon) * gain).astype(BF))
             return jnp.concatenate(parts, axis=0)
 
@@ -276,11 +339,10 @@
             top = top + near_ref[start : start + block, 2 * p * LANES : (2 * p + 1) * LANES]
             bottom = bottom + near_ref[start : start + block, (2 * p + 1) * LANES : (2 * p + 2) * LANES]
             out_ref[start : start + block, cols] = (top / bottom).astype(BF)
-    spans = bounds_ref.shape[0]
-    position = ids_ref[3] + lax.broadcasted_iota(jnp.int32, (spans, rows), 1)
-    member = (position >= bounds_ref[:, 0:1]) & (position < bounds_ref[:, 1:2])
-    member = jnp.where(member, 1.0, 0.0).astype(BF)
-    sums = dot(member, out_ref[...])
+    spans = bounds_ref.shape[1]
+    position = ids_ref[3] + lax.broadcasted_iota(jnp.int32, (rows, spans), 0)
+    member = (position >= bounds_ref[0:1, :]) & (position < bounds_ref[1:2, :])
+    sums = dot(jnp.where(member, 1.0, 0.0).astype(BF), out_ref[...], ((0,), (0,)))
     count = spans // (2 * spread)
     even = jnp.concatenate([sums[2 * i * count : (2 * i + 1) * count] for i in range(spread)], axis=0)
     odd = jnp.concatenate([sums[(2 * i + 1) * count : (2 * i + 2) * count] for i in range(spread)], axis=0)
@@ -295,19 +357,20 @@
 def far(pairs, group, spread, ids, q, near_sums, mine, other, gains, bounds, before):
     rows = q.shape[0]
     width = pairs * LANES
-    spans = bounds.shape[0]
+    spans = bounds.shape[1]
     shape = (spans // 2, (group + 1) * width)
     return pl.pallas_call(
         functools.partial(far_kernel, pairs, group, 256, spread),
         in_specs=[smem()] + [vmem()] * (6 + len(before)),
-        out_specs=[vmem()] * 3,
+        out_specs=[vmem()] * 3 + [smem()],
         out_shape=[
             jax.ShapeDtypeStruct((rows, width), BF),
             jax.ShapeDtypeStruct(shape, F32),
             jax.ShapeDtypeStruct(shape, BF),
+            TURN,
         ],
-        compiler_params=pltpu.CompilerParams(vmem_limit_bytes=16 << 20),
-        cost_estimate=pl.CostEstimate(flops=rows * pairs * (1 << 20), bytes_accessed=4 << 20, transcendentals=0),
+        compiler_params=pltpu.CompilerParams(vmem_limit_bytes=VMEM_LIMIT),
+        cost_estimate=COST,
         name="far",
     )(ids, q, near_sums, mine, other, gains, bounds, *before)
 
@@ -336,10 +399,8 @@
         in_specs=[smem()] + [vmem()] * (count + 1 + len(extra)),
         out_specs=vmem(),
         out_shape=jax.ShapeDtypeStruct((rows, columns), dtype),
-        compiler_params=pltpu.CompilerParams(vmem_limit_bytes=16 << 20),
-        cost_estimate=pl.CostEstimate(
-            flops=2 * rows * width * columns * count, bytes_accessed=4 << 20, transcendentals=0
-        ),
+        compiler_params=pltpu.CompilerParams(vmem_limit_bytes=VMEM_LIMIT),
+        cost_estimate=COST,
         name="out",
     )(index, *parts, weight, *extra)
 
@@ -384,31 +445,48 @@
         [lax.axis_index("rep"), (seq_index > 0).astype(jnp.int32), (seq_index < seq_devices - 1).astype(jnp.int32), first_row]
     ).astype(jnp.int32)
     gain = norm_gain[None, :]
-    gain_columns = dual_gains.T
+    bounds = span_bounds.T
 
     both = ("seq", "rep")
-    totals, nears, tokens, normed = [], [], book_tokens, None
+    chips = [(i, i + 1) for i in range(1, seq_devices - 1, 2)]
+    chips = chips + [(b, a) for a, b in chips]
+    steps = list(steps_of("seq"))
+    tie = lax.optimization_barrier
+
+    fronts, mine, normed = [], [], book_tokens
+    turn = ids
     for g in range(groups):
-        outs = front(g == 0, g, pairs, ids, tokens, gain, key_weight, value_weight, proj_weight, dual_gains)
-        if g == 0:
-            tokens, outs = outs[0], outs[1:]
-            normed = tokens
-        near_pairs, keep, send = outs
-        if g == 0:
-            prev = lax.ppermute(book_tokens[rows - HALF :], both, [(i, i + 1) for i in range(seq_devices - 1)])
-            following = lax.ppermute(book_tokens[:HALF], both, [(i + 1, i) for i in range(seq_devices - 1)])
-        mine = add(keep, swap(send, "rep", 1))
-        tokens, mine = lax.optimization_barrier((tokens, mine))
-        for step in steps_of("seq"):
-            mine = add(mine, swap(mine, "seq", step))
-        totals.append((mine, swap(mine, "rep", 1)))
-        nears.append(near(pairs, g, ids, normed, near_pairs, prev, following, gain, query_weight, key_weight, value_weight, dual_gains))
+        last = g == groups - 1
+        normed, *outs, turn = front(g == 0, last, g, pairs, turn, normed, gain, key_weight, value_weight, proj_weight,
+                                    dual_gains, [f[3] for f in fronts])
+        fronts.append(outs)
+        core = swap(outs[2], "rep", 1)
+        if last:
+            chip = lax.ppermute(outs[3], both, chips)
+            for f in range(g):
+                for step in steps[:-1]:
+                    got, turn = tie((swap(mine[f], "seq", step), turn))
+                    mine[f] = add(mine[f], got)
+                mine[f], turn = tie((mine[f], turn))
+        got, turn = tie((core[: outs[1].shape[0]], turn))
+        mine.append(add(outs[1], got))
+        mine[g], turn = tie((mine[g], turn))
+
+    nears, turn = near(pairs, turn, normed, core, chip, query_weight, [f[0] for f in fronts])
+    got, turn = tie((swap(mine[-1], "seq", steps[0]), turn))
+    mine[-1] = add(mine[-1], got)
+    for step in steps[1:-1]:
+        mine[-1] = add(mine[-1], swap(mine[-1], "seq", step))
+    mine[-1], turn = tie((mine[-1], turn))
 
     spread = lax.axis_size("seq")
     outs, before = [], ()
     for g in range(groups):
+        got, turn = tie((swap(mine[g], "seq", steps[-1]), turn))
+        total = add(mine[g], got)
         q, near_sums = nears[g]
-        out, *before = far(pairs, g, spread, ids, q, near_sums, *totals[g], gain_columns, span_bounds, before)
+        out, *before, turn = far(pairs, g, spread, turn, q, near_sums, total, swap(total, "rep", 1), dual_gains,
+                                 bounds, before)
         outs.append(out)
 
     own_index = [head_index * groups + g for g in range(groups)]

time: 93.7 us -> 87.7 us (0.936)
  waiting for transfers between devices: 32.4 us -> 28.2 us
  Pallas kernels: 32.3 us -> 30.8 us
    ppermute x1, waiting for transfers between devices: 9.9 us -> 20.8 us  [per_device(): lax.ppermute(own, 'head', [(i, (i + k) % head_devices) for i in range(hea...]
    ppermute x2, waiting for transfers between devices: 7.54 us -> 0.01 us  [per_device(): lax.ppermute(outs[g], 'head', [(i, (i + k) % head_devices) for i in range...]
    ppermute x9, waiting for transfers between devices: 13.5 us -> 6.82 us  [swap(): return lax.ppermute(values, axis, [(i, i ^ step) for i in range(count)])]
    ppermute x9, starting transfers between devices: 9.85 us -> 13.1 us  [swap(): return lax.ppermute(values, axis, [(i, i ^ step) for i in range(count)])]
    pallas_call x4 -> x3, Pallas kernels: 24.3 us -> 21.6 us  [the longest x2 15.3 us: front(): pl.pallas_call(functools.partial(front_kernel, first, last, group, pairs,...]
    ppermute x2 -> x1, starting transfers between devices: 3.44 us -> 0.85 us  [per_device(): chip = lax.ppermute(outs[3], both, chips)]
    pallas_call x2, Pallas kernels: 5.09 us -> 6.23 us  [far(): pl.pallas_call(functools.partial(far_kernel, pairs, group, 256, spread),...]
    slice x1, local copies, waits for them, and re-layouts: 0.98 us -> 0.01 us  [per_device(): got, turn = tie((core[:outs[1].shape[0]], turn))]
  transfers between devices with their start and end apart: 17 -> 16, of which waited for: 7 -> 7; matrix products, arithmetic and copies ran while one was open for 3% -> 2% of each run, Pallas kernels for 21% -> 20%
where the time goes in v3:
time: 87.7 us; the launch traced here: 87.4 us
  Pallas kernels  30.8 us (35%)
  waiting for transfers between devices  28.2 us (32%)
  starting transfers between devices  21.3 us (24%)
  local copies, waits for them, and re-layouts  4.83 us (6%)
  matrix products  0.97 us (1%)
    ppermute x1, waiting for transfers between devices, per_device(): lax.ppermute(own, 'head', [(i, (i + k) % head_devices) for i in range(hea...  20.8 us
    pallas_call x2, Pallas kernels, front(): pl.pallas_call(functools.partial(front_kernel, first, last, group, pairs,...  15.3 us
    ppermute x9, starting transfers between devices, swap(): return lax.ppermute(values, axis, [(i, i ^ step) for i in range(count)])  13.1 us
    ppermute x9, waiting for transfers between devices, swap(): return lax.ppermute(values, axis, [(i, i ^ step) for i in range(count)])  6.82 us
    pallas_call x1, Pallas kernels, near(): pl.pallas_call(functools.partial(near_kernel, groups, pairs), in_specs=[s...  6.29 us
    pallas_call x2, Pallas kernels, far(): pl.pallas_call(functools.partial(far_kernel, pairs, group, 256, spread),...  6.23 us
    unnamed x20, local copies, waits for them, and re-layouts  4.74 us
    ppermute x3, starting transfers between devices, per_device(): lax.ppermute(piece, 'seq', [(i, (i + k) % spread) for i in range(spread)])  3.87 us
  transfers between devices with their start and end apart: 16, of which 7 were waited for; matrix products, arithmetic and copies ran while one was open for 2% of the time, Pallas kernels for 20%

profile of v3, /device:TPU:0, one launch (start us, length us, event | category | flops | bytes accessed | tf_op | source)
XLA Modules:
  0.0 87.4 jit_solution(8182063159841953811)
XLA Ops:
  0.6 0.1 pad_add_fusion.refs_0_
  0.7 8.8 %front.2 = (bf16[1024,1024]{1,0:T(8,128)(2,1)S(1)}, bf16[1024,512]{1,0:T(8,128)(2,1)S(1)}, bf16[256,256]{1,0:T(8,128)(2,1)S(1)}, bf16[256,256]{1,0:T(8,128)(2,1)...) custom-call(s32[4]{0:T(128)S(1)} %pad_add_fusion.refs_0_, bf16[1024,1024]{1,0:T(8,128)(2,1)} %refs_1_.1, ...), custom_call_target="tpu_custom_call" | custom-call | flops 1048576 | bytes 1024 | tf_op jit(solution)/shard_map/front/pallas_call | solution.py:210
  9.5 0.5 collective-permute-start
  10.0 1.0 %collective-permute-done = bf16[256,256]{1,0:T(8,128)(2,1)S(1)} collective-permute-done((bf16[256,256]{1,0:T(8,128)(2,1)S(1)}, bf16[256,256]{1,0:T(8,128)(2,1)S(1)}, u32[]{:S(2)}, u32[]{:S(2)}) %collective-permute-start) | collective-permute-done | bytes 131104 | tf_op jit(solution)/shard_map/ppermute | solution.py:410
  11.1 3.0 %collective-permute-start.2 = (bf16[256,256]{1,0:T(8,128)(2,1)S(1)}, bf16[256,256]{1,0:T(8,128)(2,1)S(1)}, u32[]{:S(2)}, u32[]{:S(2)}) collective-permute-start(bf16[256,256]{1,0:T(8,128)(2,1)S(1)} %add_convert_fusion.5), channel_id=1, source_target_pairs={{0,4},{4,0},{8,12},{12,8},{1,5},{5,1},{9,13},{13,9},{2,6},{6,2},{1... | collective-permute-start | bytes 393224 | tf_op jit(solution)/shard_map/ppermute | solution.py:410
  14.1 6.5 %front.3 = (bf16[1024,1024]{1,0:T(8,128)(2,1)S(1)}, bf16[1024,512]{1,0:T(8,128)(2,1)S(1)}, bf16[256,256]{1,0:T(8,128)(2,1)S(1)}, bf16[512,256]{1,0:T(8,128)(2,1)...) custom-call(s32[4]{0:T(128)S(1)} %get-tuple-element.51.refs_0_, ...), custom_call_target="tpu_custom_call", output_to_operand_aliasing={{0}: (1, {})} | custom-call | flops 1048576 | bytes 1024 | tf_op jit(solution)/shard_map/front/pallas_call | solution.py:210
  20.6 0.1 collective-permute-start.1
  20.7 0.8 collective-permute-start.4
  21.6 0.6 collective-permute-done.1.refs_2_
  22.3 2.8 %collective-permute-start.3 = (bf16[256,256]{1,0:T(8,128)(2,1)S(1)}, bf16[256,256]{1,0:T(8,128)(2,1)S(1)}, u32[]{:S(2)}, u32[]{:S(2)}) collective-permute-start(bf16[256,256]{1,0:T(8,128)(2,1)S(1)} %add_convert_fusion.3), channel_id=1, source_target_pairs={{0,4},{4,0},{8,12},{12,8},{1,5},{5,1},{9,13},{13,9},{2,6},{6,2},{1... | collective-permute-start | bytes 393224 | tf_op jit(solution)/shard_map/ppermute | solution.py:410
  25.1 2.6 %collective-permute-start.6 = (bf16[256,256]{1,0:T(8,128)(2,1)S(1)}, bf16[256,256]{1,0:T(8,128)(2,1)S(1)}, u32[]{:S(2)}, u32[]{:S(2)}) collective-permute-start(bf16[256,256]{1,0:T(8,128)(2,1)S(1)} %add_convert_fusion.4), channel_id=1, source_target_pairs={{0,8},{4,12},{8,0},{12,4},{1,9},{5,13},{9,1},{13,5},{2,10},{6,14},... | collective-permute-start | bytes 393224 | tf_op jit(solution)/shard_map/ppermute | solution.py:410
  27.7 0.0 collective-permute-done.4.refs_3_
  27.7 6.3 %near.1 = (bf16[1024,256]{1,0:T(8,128)(2,1)S(1)}, bf16[1024,256]{1,0:T(8,128)(2,1)S(1)}, f32[1024,512]{1,0:T(8,128)S(1)}, f32[1024,512]{1,0:T(8,128)S(1)}, s32[4]{0:T(128)S(1)}) custom-call(s32[4]{0:T(128)S(1)} %get-tuple-element.64.refs_0_, bf16[1024,1024]{1,0:T(8,128)(2,1)S(1)} %get-tuple-element.65.refs_1_, ...), custom_call_target="tpu_custom_call" | custom-call | flops 1048576 | bytes 1024 | tf_op jit(solution)/shard_map/near/pallas_call | solution.py:290
  34.0 0.0 copy-start.6
  34.1 0.0 collective-permute-done.6
  34.1 0.4 collective-permute-start.7
  34.5 3.4 %collective-permute-start.5 = (bf16[256,256]{1,0:T(8,128)(2,1)S(1)}, bf16[256,256]{1,0:T(8,128)(2,1)S(1)}, u32[]{:S(2)}, u32[]{:S(2)}) collective-permute-start(bf16[256,256]{1,0:T(8,128)(2,1)S(1)} %add_convert_fusion.2), channel_id=1, source_target_pairs={{0,8},{4,12},{8,0},{12,4},{1,9},{5,13},{9,1},{13,5},{2,10},{6,14},... | collective-permute-start | bytes 393224 | tf_op jit(solution)/shard_map/ppermute | solution.py:410
  37.9 0.0 collective-permute-done.7.refs_4_
  37.9 3.0 %far.2 = (bf16[1024,256]{1,0:T(8,128)(2,1)S(1)}, f32[32,256]{1,0:T(8,128)S(1)}, bf16[32,256]{1,0:T(8,128)(2,1)S(1)}, s32[4]{0:T(128)S(1)}) custom-call(s32[4]{0:T(128)S(1)} %get-tuple-element.75.refs_0_, bf16[1024,256]{1,0:T(8,128)(2,1)S(1)} %get-tuple-element.76.refs_1_, f32[1024,512]{1,0:T(8,128)S(1)} %get-tuple-element.77.refs_2_, ...), custom_call_target="tpu_custom_call" | custom-call | flops 1048576 | bytes 1024 | tf_op jit(solution)/shard_map/far/pallas_call | solution.py:362
  41.0 0.8 copy-done.2
  41.8 2.7 %collective-permute-done.5 = bf16[256,256]{1,0:T(8,128)(2,1)S(1)} collective-permute-done((bf16[256,256]{1,0:T(8,128)(2,1)S(1)}, bf16[256,256]{1,0:T(8,128)(2,1)S(1)}, u32[]{:S(2)}, u32[]{:S(2)}) %collective-permute-start.5) | collective-permute-done | bytes 131104 | tf_op jit(solution)/shard_map/ppermute | solution.py:410
  44.5 0.1 collective-permute-start.8
  44.6 1.3 %collective-permute-done.8.refs_4_ = bf16[256,256]{1,0:T(8,128)(2,1)S(1)} collective-permute-done((bf16[256,256]{1,0:T(8,128)(2,1)S(1)}, bf16[256,256]{1,0:T(8,128)(2,1)S(1)}, u32[]{:S(2)}, u32[]{:S(2)}) %collective-permute-start.8) | collective-permute-done | bytes 131104 | tf_op jit(solution)/shard_map/ppermute | solution.py:410
  45.9 1.0 %copy-done.7 = bf16[1024,256]{1,0:T(8,128)(2,1)S(1)} copy-done((bf16[1024,256]{1,0:T(8,128)(2,1)S(1)}, bf16[1024,256]{1,0:T(8,128)(2,1)}, u32[]{:S(2)}) %copy-start.7) | copy-done | bytes 524312
  47.0 3.2 %far.3 = (bf16[1024,256]{1,0:T(8,128)(2,1)S(1)}, f32[32,512]{1,0:T(8,128)S(1)}, bf16[32,512]{1,0:T(8,128)(2,1)}, s32[4]{0:T(128)}) custom-call(s32[4]{0:T(128)S(1)} %get-tuple-element.80.refs_0_, bf16[1024,256]{1,0:T(8,128)(2,1)S(1)} %copy-done.7, f32[1024,512]{1,0:T(8,128)S(1)} %get-tuple-element.82.refs_2_, bf16[256,256]{1,0:T(8,128)(2,1)S(1)} %add_convert_fusion.refs_3_, ...), custom_call_target="tpu_custom_call" | custom-call | flops 1048576 | bytes 1024 | tf_op jit(solution)/shard_map/far/pallas_call | solution.py:362
  50.2 0.0 copy-start.4
  50.2 0.8 copy-done.4
  51.0 0.1 collective-permute-start.11
  51.1 0.1 constant_dynamic-slice_fusion
  51.2 1.2 %collective-permute-done.11 = bf16[32,512]{1,0:T(8,128)(2,1)S(1)} collective-permute-done((bf16[32,512]{1,0:T(8,128)(2,1)}, bf16[32,512]{1,0:T(8,128)(2,1)S(1)}, u32[]{:S(2)}, u32[]{:S(2)}) %collective-permute-start.11) | collective-permute-done | bytes 32800 | tf_op jit(solution)/shard_map/ppermute | solution.py:410
  52.4 0.1 collective-permute-start.12
  52.5 2.8 %collective-permute-start.13 = (bf16[8,512]{1,0:T(8,128)(2,1)S(1)}, bf16[8,512]{1,0:T(8,128)(2,1)S(1)}, u32[]{:S(2)}, u32[]{:S(2)}) collective-permute-start(bf16[8,512]{1,0:T(8,128)(2,1)S(1)} %get-tuple-element.92), channel_id=1, source_target_pairs={{0,8},{4,12},{8,0},{12,4},{1,9},{5,13},{9,1},{13,5},{2,10},{6,14},... | collective-permute-start | bytes 24584 | tf_op jit(solution)/shard_map/ppermute | solution.py:513
  55.3 1.0 %collective-permute-start.14 = (bf16[8,512]{1,0:T(8,128)(2,1)S(1)}, bf16[8,512]{1,0:T(8,128)(2,1)S(1)}, u32[]{:S(2)}, u32[]{:S(2)}) collective-permute-start(bf16[8,512]{1,0:T(8,128)(2,1)S(1)} %get-tuple-element.91), channel_id=1, source_target_pairs={{0,12},{4,0},{8,4},{12,8},{1,13},{5,1},{9,5},{13,9},{2,14},{6,2},{... | collective-permute-start | bytes 24584 | tf_op jit(solution)/shard_map/ppermute | solution.py:513
  56.3 1.5 %collective-permute-start.10 = (bf16[1024,256]{1,0:T(8,128)(2,1)}, bf16[1024,256]{1,0:T(8,128)(2,1)S(1)}, u32[]{:S(2)}, u32[]{:S(2)}) collective-permute-start(bf16[1024,256]{1,0:T(8,128)(2,1)} %copy-done.2), channel_id=1, source_target_pairs={{0,2},{2,0},{1,3},{3,1},{4,6},{6,4},{5,7},{7,5},{8,10},{10,8},{9,1... | collective-permute-start | bytes 1572872 | tf_op jit(solution)/shard_map/ppermute | solution.py:496
  57.8 0.5 collective-permute-start.9
  58.4 0.0 collective-permute-done.12
  58.4 0.0 collective-permute-done.13
  58.4 0.6 collective-permute-done.14
  58.9 0.1 divide_convert_fusion
  59.0 1.5 %collective-permute-start.15 = (bf16[8,512]{1,0:T(8,128)(2,1)S(1)}, bf16[8,512]{1,0:T(8,128)(2,1)S(1)}, u32[]{:S(2)}, u32[]{:S(2)}) collective-permute-start(bf16[8,512]{1,0:T(8,128)(2,1)S(1)} %divide_convert_fusion), channel_id=1, source_target_pairs={{0,2},{2,0},{1,3},{3,1},{4,6},{6,4},{5,7},{7,5},{8,10},{10,8},{9,1... | collective-permute-start | bytes 24584 | tf_op jit(solution)/shard_map/ppermute | solution.py:519
  60.5 0.1 pad_add_fusion.1.refs_0_
  60.6 20.8 %collective-permute-done.15 = bf16[8,512]{1,0:T(8,128)(2,1)S(1)} collective-permute-done((bf16[8,512]{1,0:T(8,128)(2,1)S(1)}, bf16[8,512]{1,0:T(8,128)(2,1)S(1)}, u32[]{:S(2)}, u32[]{:S(2)}) %collective-permute-start.15) | collective-permute-done | bytes 8224 | tf_op jit(solution)/shard_map/ppermute | solution.py:519
  81.4 0.2 fusion
  81.5 0.8 convolution_add_fusion
  82.4 1.0 %copy-done.3 = bf16[1024,256]{1,0:T(8,128)(2,1)S(1)} copy-done((bf16[1024,256]{1,0:T(8,128)(2,1)S(1)}, bf16[1024,256]{1,0:T(8,128)(2,1)}, u32[]{:S(2)}) %copy-start.3) | copy-done | bytes 524312
  83.4 1.0 %copy-done.5 = bf16[1024,256]{1,0:T(8,128)(2,1)S(1)} copy-done((bf16[1024,256]{1,0:T(8,128)(2,1)S(1)}, bf16[1024,256]{1,0:T(8,128)(2,1)}, u32[]{:S(2)}) %copy-start.5) | copy-done | bytes 524312
  84.4 1.5 %out.2.refs_3_ = f32[1024,512]{1,0:T(8,128)S(1)} custom-call(s32[3]{0:T(128)S(1)} %pad_add_fusion.1.refs_0_, bf16[1024,256]{1,0:T(8,128)(2,1)S(1)} %copy-done.3, bf16[1024,256]{1,0:T(8,128)(2,1)S(1)} %copy-done.5, bf16[1024,256]{1,0:T(8,128)(2,1)S(1)} %collective-permute-done.10.refs_3_, bf16[1024,512]{1,0:T(8,128)(2,1)S(1)} %copy-done), custom_call_target="tpu_custom_call" | custom-call | flops 1048576 | bytes 1024 | tf_op jit(solution)/shard_map/out/pallas_call | solution.py:397
  86.0 1.4 %out.3 = bf16[1024,512]{1,0:T(8,128)(2,1)} custom-call(s32[1]{0:T(128)} %bitcast.refs_0_, bf16[1024,256]{1,0:T(8,128)(2,1)S(1)} %collective-permute-done.9.refs_1_, bf16[1024,512]{1,0:T(8,128)(2,1)S(1)} %copy-done, f32[1024,512]{1,0:T(8,128)S(1)} %out.2.refs_3_), custom_call_target="tpu_custom_call" | custom-call | flops 1048576 | bytes 1024 | tf_op jit(solution)/shard_map/out/pallas_call | solution.py:397
  (27 shorter events, 0.3 us)
Async XLA Ops:
  0.7 13.3 %copy-start.8 = (f32[4,512]{1,0:T(4,128)S(1)}, f32[4,512]{1,0:T(4,128)}, u32[]{:S(2)}) copy-start(f32[4,512]{1,0:T(4,128)} %refs_5_.7) | copy-start | bytes 24580
  9.5 1.5 %collective-permute-start = (bf16[256,256]{1,0:T(8,128)(2,1)S(1)}, bf16[256,256]{1,0:T(8,128)(2,1)S(1)}, u32[]{:S(2)}, u32[]{:S(2)}) collective-permute-start(bf16[256,256]{1,0:T(8,128)(2,1)S(1)} %get-tuple-element.47), channel_id=1, source_target_pairs={{0,1},{1,0},{2,3},{3,2},{4,5},{5,4},{6,7},{7,6},{8,9},{9,8},{10,11... | collective-permute-start | bytes 393224 | tf_op jit(solution)/shard_map/ppermute | solution.py:410
  11.1 10.5 %collective-permute-start.2 = (bf16[256,256]{1,0:T(8,128)(2,1)S(1)}, bf16[256,256]{1,0:T(8,128)(2,1)S(1)}, u32[]{:S(2)}, u32[]{:S(2)}) collective-permute-start(bf16[256,256]{1,0:T(8,128)(2,1)S(1)} %add_convert_fusion.5), channel_id=1, source_target_pairs={{0,4},{4,0},{8,12},{12,8},{1,5},{5,1},{9,13},{13,9},{2,6},{6,2},{1... | collective-permute-start | bytes 393224 | tf_op jit(solution)/shard_map/ppermute | solution.py:410
  14.1 13.6 %copy-start.1 = (bf16[1024,512]{1,0:T(8,128)(2,1)S(1)}, bf16[1024,512]{1,0:T(8,128)(2,1)}, u32[]{:S(2)}) copy-start(bf16[1024,512]{1,0:T(8,128)(2,1)} %refs_4_.6) | copy-start | bytes 3145732
  20.6 1.6 %collective-permute-start.1 = (bf16[512,256]{1,0:T(8,128)(2,1)S(1)}, bf16[512,256]{1,0:T(8,128)(2,1)S(1)}, u32[]{:S(2)}, u32[]{:S(2)}) collective-permute-start(bf16[512,256]{1,0:T(8,128)(2,1)S(1)} %get-tuple-element.55), channel_id=1, source_target_pairs={{0,1},{1,0},{2,3},{3,2},{4,5},{5,4},{6,7},{7,6},{8,9},{9,8},{10,11... | collective-permute-start | bytes 786440 | tf_op jit(solution)/shard_map/ppermute | solution.py:410
  20.7 7.0 %collective-permute-start.4 = (bf16[256,256]{1,0:T(8,128)(2,1)S(1)}, bf16[256,256]{1,0:T(8,128)(2,1)S(1)}, u32[]{:S(2)}, u32[]{:S(2)}) collective-permute-start(bf16[256,256]{1,0:T(8,128)(2,1)S(1)} %get-tuple-element.66), channel_id=1, source_target_pairs={{1,4},{5,8},{9,12},{4,1},{8,5},{12,9},{3,6},{7,10},{11,14},{6,3},{... | collective-permute-start | bytes 393224 | tf_op jit(solution)/shard_map/ppermute | solution.py:465
  22.3 11.7 %collective-permute-start.3 = (bf16[256,256]{1,0:T(8,128)(2,1)S(1)}, bf16[256,256]{1,0:T(8,128)(2,1)S(1)}, u32[]{:S(2)}, u32[]{:S(2)}) collective-permute-start(bf16[256,256]{1,0:T(8,128)(2,1)S(1)} %add_convert_fusion.3), channel_id=1, source_target_pairs={{0,4},{4,0},{8,12},{12,8},{1,5},{5,1},{9,13},{13,9},{2,6},{6,2},{1... | collective-permute-start | bytes 393224 | tf_op jit(solution)/shard_map/ppermute | solution.py:410
  25.1 9.0 %collective-permute-start.6 = (bf16[256,256]{1,0:T(8,128)(2,1)S(1)}, bf16[256,256]{1,0:T(8,128)(2,1)S(1)}, u32[]{:S(2)}, u32[]{:S(2)}) collective-permute-start(bf16[256,256]{1,0:T(8,128)(2,1)S(1)} %add_convert_fusion.4), channel_id=1, source_target_pairs={{0,8},{4,12},{8,0},{12,4},{1,9},{5,13},{9,1},{13,5},{2,10},{6,14},... | collective-permute-start | bytes 393224 | tf_op jit(solution)/shard_map/ppermute | solution.py:410
  27.7 10.3 %copy-start.9 = (s32[64,2]{0,1:T(2,128)S(1)}, s32[64,2]{0,1:T(2,128)}, u32[]{:S(2)}) copy-start(s32[64,2]{0,1:T(2,128)} %param.17) | copy-start | bytes 1540
  34.0 10.5 %copy-start.6 = (bf16[1024,256]{1,0:T(8,128)(2,1)}, bf16[1024,256]{1,0:T(8,128)(2,1)S(1)}, u32[]{:S(2)}) copy-start(bf16[1024,256]{1,0:T(8,128)(2,1)S(1)} %get-tuple-element.81.refs_1_) | copy-start | bytes 1572868
  34.1 3.8 %collective-permute-start.7 = (bf16[256,256]{1,0:T(8,128)(2,1)S(1)}, bf16[256,256]{1,0:T(8,128)(2,1)S(1)}, u32[]{:S(2)}, u32[]{:S(2)}) collective-permute-start(bf16[256,256]{1,0:T(8,128)(2,1)S(1)} %add_convert_fusion.1.refs_3_), channel_id=1, source_target_pairs={{0,1},{1,0},{2,3},{3,2},{4,5},{5,4},{6,7},{7,6},{8,9},{9,8},{10,11... | collective-permute-start | bytes 393224 | tf_op jit(solution)/shard_map/ppermute | solution.py:410
  34.5 10.0 %collective-permute-start.5 = (bf16[256,256]{1,0:T(8,128)(2,1)S(1)}, bf16[256,256]{1,0:T(8,128)(2,1)S(1)}, u32[]{:S(2)}, u32[]{:S(2)}) collective-permute-start(bf16[256,256]{1,0:T(8,128)(2,1)S(1)} %add_convert_fusion.2), channel_id=1, source_target_pairs={{0,8},{4,12},{8,0},{12,4},{1,9},{5,13},{9,1},{13,5},{2,10},{6,14},... | collective-permute-start | bytes 393224 | tf_op jit(solution)/shard_map/ppermute | solution.py:410
  41.0 0.8 copy-start.2
  41.8 39.6 %copy-start = (bf16[1024,512]{1,0:T(8,128)(2,1)S(1)}, bf16[1024,512]{1,0:T(8,128)(2,1)}, u32[]{:S(2)}) copy-start(bf16[1024,512]{1,0:T(8,128)(2,1)} %refs_2_.3) | copy-start | bytes 3145732
  44.5 1.4 %collective-permute-start.8 = (bf16[256,256]{1,0:T(8,128)(2,1)S(1)}, bf16[256,256]{1,0:T(8,128)(2,1)S(1)}, u32[]{:S(2)}, u32[]{:S(2)}) collective-permute-start(bf16[256,256]{1,0:T(8,128)(2,1)S(1)} %add_convert_fusion.refs_3_), channel_id=1, source_target_pairs={{0,1},{1,0},{2,3},{3,2},{4,5},{5,4},{6,7},{7,6},{8,9},{9,8},{10,11... | collective-permute-start | bytes 393224 | tf_op jit(solution)/shard_map/ppermute | solution.py:410
  45.9 1.0 %copy-start.7 = (bf16[1024,256]{1,0:T(8,128)(2,1)S(1)}, bf16[1024,256]{1,0:T(8,128)(2,1)}, u32[]{:S(2)}) copy-start(bf16[1024,256]{1,0:T(8,128)(2,1)} %copy-done.6) | copy-start | bytes 1572868
  50.2 0.8 copy-start.4
  51.0 1.4 %collective-permute-start.11 = (bf16[32,512]{1,0:T(8,128)(2,1)}, bf16[32,512]{1,0:T(8,128)(2,1)S(1)}, u32[]{:S(2)}, u32[]{:S(2)}) collective-permute-start(bf16[32,512]{1,0:T(8,128)(2,1)} %get-tuple-element.89), channel_id=1, source_target_pairs={{0,1},{1,0},{2,3},{3,2},{4,5},{5,4},{6,7},{7,6},{8,9},{9,8},{10,11... | collective-permute-start | bytes 98312 | tf_op jit(solution)/shard_map/ppermute | solution.py:410
  52.4 5.9 %collective-permute-start.12 = (bf16[8,512]{1,0:T(8,128)(2,1)S(1)}, bf16[8,512]{1,0:T(8,128)(2,1)S(1)}, u32[]{:S(2)}, u32[]{:S(2)}) collective-permute-start(bf16[8,512]{1,0:T(8,128)(2,1)S(1)} %get-tuple-element.90), channel_id=1, source_target_pairs={{0,4},{4,8},{8,12},{12,0},{1,5},{5,9},{9,13},{13,1},{2,6},{6,10},{... | collective-permute-start | bytes 24584 | tf_op jit(solution)/shard_map/ppermute | solution.py:513
  52.5 5.9 %collective-permute-start.13 = (bf16[8,512]{1,0:T(8,128)(2,1)S(1)}, bf16[8,512]{1,0:T(8,128)(2,1)S(1)}, u32[]{:S(2)}, u32[]{:S(2)}) collective-permute-start(bf16[8,512]{1,0:T(8,128)(2,1)S(1)} %get-tuple-element.92), channel_id=1, source_target_pairs={{0,8},{4,12},{8,0},{12,4},{1,9},{5,13},{9,1},{13,5},{2,10},{6,14},... | collective-permute-start | bytes 24584 | tf_op jit(solution)/shard_map/ppermute | solution.py:513
  55.3 3.7 %collective-permute-start.14 = (bf16[8,512]{1,0:T(8,128)(2,1)S(1)}, bf16[8,512]{1,0:T(8,128)(2,1)S(1)}, u32[]{:S(2)}, u32[]{:S(2)}) collective-permute-start(bf16[8,512]{1,0:T(8,128)(2,1)S(1)} %get-tuple-element.91), channel_id=1, source_target_pairs={{0,12},{4,0},{8,4},{12,8},{1,13},{5,1},{9,5},{13,9},{2,14},{6,2},{... | collective-permute-start | bytes 24584 | tf_op jit(solution)/shard_map/ppermute | solution.py:513
  56.3 26.0 %collective-permute-start.10 = (bf16[1024,256]{1,0:T(8,128)(2,1)}, bf16[1024,256]{1,0:T(8,128)(2,1)S(1)}, u32[]{:S(2)}, u32[]{:S(2)}) collective-permute-start(bf16[1024,256]{1,0:T(8,128)(2,1)} %copy-done.2), channel_id=1, source_target_pairs={{0,2},{2,0},{1,3},{3,1},{4,6},{6,4},{5,7},{7,5},{8,10},{10,8},{9,1... | collective-permute-start | bytes 1572872 | tf_op jit(solution)/shard_map/ppermute | solution.py:496
  57.8 28.1 %collective-permute-start.9 = (bf16[1024,256]{1,0:T(8,128)(2,1)}, bf16[1024,256]{1,0:T(8,128)(2,1)S(1)}, u32[]{:S(2)}, u32[]{:S(2)}) collective-permute-start(bf16[1024,256]{1,0:T(8,128)(2,1)} %copy-done.4), channel_id=1, source_target_pairs={{0,2},{2,0},{1,3},{3,1},{4,6},{6,4},{5,7},{7,5},{8,10},{10,8},{9,1... | collective-permute-start | bytes 1572872 | tf_op jit(solution)/shard_map/ppermute | solution.py:496
  59.0 22.4 %collective-permute-start.15 = (bf16[8,512]{1,0:T(8,128)(2,1)S(1)}, bf16[8,512]{1,0:T(8,128)(2,1)S(1)}, u32[]{:S(2)}, u32[]{:S(2)}) collective-permute-start(bf16[8,512]{1,0:T(8,128)(2,1)S(1)} %divide_convert_fusion), channel_id=1, source_target_pairs={{0,2},{2,0},{1,3},{3,1},{4,6},{6,4},{5,7},{7,5},{8,10},{10,8},{9,1... | collective-permute-start | bytes 24584 | tf_op jit(solution)/shard_map/ppermute | solution.py:519
  82.4 1.0 %copy-start.3 = (bf16[1024,256]{1,0:T(8,128)(2,1)S(1)}, bf16[1024,256]{1,0:T(8,128)(2,1)}, u32[]{:S(2)}) copy-start(bf16[1024,256]{1,0:T(8,128)(2,1)} %copy-done.2) | copy-start | bytes 1572868
  83.4 1.0 %copy-start.5 = (bf16[1024,256]{1,0:T(8,128)(2,1)S(1)}, bf16[1024,256]{1,0:T(8,128)(2,1)}, u32[]{:S(2)}) copy-start(bf16[1024,256]{1,0:T(8,128)(2,1)} %copy-done.4) | copy-start | bytes 1572868

commit v4 on v3

--- a/solution.py
+++ b/solution.py
@@ -375,34 +375,90 @@
     )(ids, q, near_sums, mine, other, gains, bounds, *before)
 
 
-def out_kernel(count, *refs):
+def out_kernel(count, spans, *refs):
     ids_ref, refs = refs[0], refs[1:]
-    tokens, (weight_ref, *acc), out_ref = refs[:count], refs[count:-1], refs[-1]
+    tokens, refs = refs[:count], refs[count:]
+    pooled, refs = refs[:spans], refs[spans:]
+    outs = refs[-2:] if spans else refs[-1:]
+    weight_ref, *acc = refs[: -len(outs)]
     rows, width = tokens[0].shape
+
+    def weight(j, size):
+        return weight_ref[pl.ds(pl.multiple_of(ids_ref[j] * size, size), size), :]
+
     for start in range(0, rows, 256):
         at = slice(start, start + 256)
         total = acc[0][at, :] if acc else None
         for j in range(count):
-            weight = weight_ref[pl.ds(pl.multiple_of(ids_ref[j] * width, width), width), :]
-            term = dot(tokens[j][at, :], weight)
+            term = dot(tokens[j][at, :], weight(j, width))
             total = term if total is None else total + term
-        out_ref[at, :] = total.astype(out_ref.dtype)
-
-
-def out_part(parts, index, weight, acc, dtype):
+        outs[0][at, :] = total.astype(outs[0].dtype)
+    if spans:
+        outs[1][...] = sum(dot(ref[...], weight(count + k, ref.shape[1])) for k, ref in enumerate(pooled))
+
+
+def out_part(parts, index, weight, acc, dtype, pooled=()):
     count = len(parts)
-    rows, width = parts[0].shape
+    rows = parts[0].shape[0]
     columns = weight.shape[1]
     extra = [] if acc is None else [acc]
+    shapes = [jax.ShapeDtypeStruct((rows, columns), dtype)]
+    shapes += [jax.ShapeDtypeStruct((pooled[0].shape[0], columns), F32)] if pooled else []
     return pl.pallas_call(
-        functools.partial(out_kernel, count),
-        in_specs=[smem()] + [vmem()] * (count + 1 + len(extra)),
-        out_specs=vmem(),
-        out_shape=jax.ShapeDtypeStruct((rows, columns), dtype),
+        functools.partial(out_kernel, count, len(pooled)),
+        in_specs=[smem()] + [vmem()] * (count + len(pooled) + 1 + len(extra)),
+        out_specs=[vmem()] * len(shapes),
+        out_shape=shapes,
         compiler_params=pltpu.CompilerParams(vmem_limit_bytes=VMEM_LIMIT),
         cost_estimate=COST,
         name="out",
-    )(index, *parts, weight, *extra)
+    )(index, *parts, *pooled, weight, *extra)
+
+
+def pieces_kernel(ids_ref, keep_ref, got_ref, *out_refs):
+    spread = len(out_refs)
+    count = keep_ref.shape[0] // spread
+    for k, ref in enumerate(out_refs):
+        at = pl.ds(pl.multiple_of(lax.rem(ids_ref[0] + k, spread) * count, count), count)
+        ref[...] = (keep_ref[at, :] + got_ref[at, :].astype(F32)).astype(ref.dtype)
+
+
+def pool_pieces(place, keep, got, spread):
+    count = keep.shape[0] // spread
+    shape = (count, keep.shape[1])
+    return pl.pallas_call(
+        pieces_kernel,
+        in_specs=[smem(), vmem(), vmem()],
+        out_specs=[vmem()] * spread,
+        out_shape=[jax.ShapeDtypeStruct(shape, F32)] + [jax.ShapeDtypeStruct(shape, BF)] * (spread - 1),
+        compiler_params=pltpu.CompilerParams(vmem_limit_bytes=VMEM_LIMIT),
+        cost_estimate=COST,
+        name="pool_pieces",
+    )(place, keep, got)
+
+
+def own_kernel(ids_ref, bounds_ref, own_ref, *refs):
+    total = own_ref[...]
+    for ref in refs[:-1]:
+        total = total + ref[...].astype(F32)
+    count = total.shape[0]
+    rows = [
+        total[i : i + 1] / (bounds_ref[1, ids_ref[0] + i] - bounds_ref[0, ids_ref[0] + i]).astype(F32)
+        for i in range(count)
+    ]
+    refs[-1][...] = jnp.concatenate(rows, axis=0).astype(BF)
+
+
+def pool_own(place, bounds, own, others):
+    return pl.pallas_call(
+        own_kernel,
+        in_specs=[smem(), smem()] + [vmem()] * (1 + len(others)),
+        out_specs=vmem(),
+        out_shape=jax.ShapeDtypeStruct(own.shape, BF),
+        compiler_params=pltpu.CompilerParams(vmem_limit_bytes=VMEM_LIMIT),
+        cost_estimate=COST,
+        name="pool_own",
+    )(place, bounds, own, *others)
 
 
 def swap(values, axis, step):
@@ -410,8 +466,29 @@
     return lax.ppermute(values, axis, [(i, i ^ step) for i in range(count)])
 
 
+def across_heads(values, step):
+    count = lax.axis_size("head")
+    return lax.ppermute(values, "head", [(i, (i + step) % count) for i in range(count)])
+
+
 def add(a, b):
     return (a.astype(F32) + b.astype(F32)).astype(BF)
+
+
+def add_kernel(a_ref, b_ref, out_ref):
+    out_ref[...] = (a_ref[...].astype(F32) + b_ref[...].astype(F32)).astype(BF)
+
+
+def add_call(a, b):
+    return pl.pallas_call(
+        add_kernel,
+        in_specs=[vmem()] * 2,
+        out_specs=vmem(),
+        out_shape=jax.ShapeDtypeStruct(a.shape, BF),
+        compiler_params=pltpu.CompilerParams(vmem_limit_bytes=VMEM_LIMIT),
+        cost_estimate=COST,
+        name="add",
+    )(a, b)
 
 
 def steps_of(axis):
@@ -483,7 +560,7 @@
     outs, before = [], ()
     for g in range(groups):
         got, turn = tie((swap(mine[g], "seq", steps[-1]), turn))
-        total = add(mine[g], got)
+        total = add_call(mine[g], got)
         q, near_sums = nears[g]
         out, *before, turn = far(pairs, g, spread, turn, q, near_sums, total, swap(total, "rep", 1), dual_gains,
                                  bounds, before)
@@ -493,39 +570,25 @@
     others, other_index = [], []
     for g in range(groups):
         for k in range(1, head_devices):
-            others.append(lax.ppermute(outs[g], "head", [(i, (i + k) % head_devices) for i in range(head_devices)]))
+            others.append(across_heads(outs[g], k))
             other_index.append(lax.rem(head_index - k + head_devices, head_devices) * groups + g)
     early = len(others) - (head_devices - 1)
+
+    keep, send = before
+    place = lax.axis_index("seq").astype(jnp.int32)[None]
+    own, *pieces = pool_pieces(place, keep, swap(send, "rep", 1), spread)
+    pieces = [
+        lax.ppermute(piece, "seq", [(i, (i + k + 1) % spread) for i in range(spread)]) for k, piece in enumerate(pieces)
+    ]
+    own = pool_own((seq_index * own.shape[0]).astype(jnp.int32)[None], bounds, own, pieces)
+    pooled = [own] + [across_heads(own, k) for k in range(1, head_devices)]
+    pooled_index = [lax.rem(head_index - k + head_devices, head_devices) for k in range(head_devices)]
+
     parts = outs + others[:early]
     index = jnp.stack(own_index + other_index[:early]).astype(jnp.int32)
-    acc = out_part(parts, index, out_weight, None, F32)
-    index = jnp.stack(other_index[early:]).astype(jnp.int32)
-    attended = out_part(others[early:], index, out_weight, acc, BF)
-
-    keep, send = before
-    sums = keep + swap(send, "rep", 1).astype(F32)
-    span_rows = sums.shape[0] // spread
-    place = lax.axis_index("seq")
-    own = lax.dynamic_slice_in_dim(sums, place * span_rows, span_rows, 0)
-    for k in range(1, spread):
-        target = lax.rem(place + k, spread)
-        piece = lax.dynamic_slice_in_dim(sums, target * span_rows, span_rows, 0).astype(BF)
-        own = own + lax.ppermute(piece, "seq", [(i, (i + k) % spread) for i in range(spread)]).astype(F32)
-    own_bounds = lax.dynamic_slice_in_dim(span_bounds, seq_index * span_rows, span_rows, 0)
-    counts = (own_bounds[:, 1] - own_bounds[:, 0]).astype(F32)
-    own = (own / counts[:, None]).astype(BF)
-    width = own.shape[1]
-    spread = [own] + [
-        lax.ppermute(own, "head", [(i, (i + k) % head_devices) for i in range(head_devices)])
-        for k in range(1, head_devices)
-    ]
-    pooled = None
-    for k, values in enumerate(spread):
-        source = lax.rem(head_index - k + head_devices, head_devices)
-        weight = lax.dynamic_slice_in_dim(out_weight, source * width, width, 0)
-        term = jnp.dot(values, weight, preferred_element_type=F32)
-        pooled = term if pooled is None else pooled + term
-    return (attended, pooled)
+    (acc,) = out_part(parts, index, out_weight, None, F32)
+    index = jnp.stack(other_index[early:] + pooled_index).astype(jnp.int32)
+    return tuple(out_part(others[early:], index, out_weight, acc, BF, pooled))
 
 
 def solution(mesh):

time: 87.7 us -> 72.7 us (0.83)
  waiting for transfers between devices: 28.2 us -> 18.3 us
  local copies, waits for them, and re-layouts: 4.83 us -> 0.03 us
  matrix products: 0.97 us -> 0 us
  Pallas kernels: 30.8 us -> 31.7 us
    ppermute x6, waiting for transfers between devices: 21.4 us -> 12 us  [the longest x3 9.47 us: across_heads(): lax.ppermute(values, 'head', [(i, (i + step) % count) for i in range(coun...]
    unnamed x20 -> x8, local copies, waits for them, and re-layouts: 4.74 us -> 0.02 us
    pallas_call x2 -> x6, Pallas kernels: 2.94 us -> 4.2 us  [the longest x2 3.53 us: out_part(): pl.pallas_call(functools.partial(out_kernel, count, len(pooled)), in_spec...]
    dot_general x2 -> x0, matrix products: 0.97 us -> none  [per_device(): term = jnp.dot(values, weight, preferred_element_type=F32)]
  transfers between devices with their start and end apart: 16 -> 16, of which waited for: 7 -> 7; matrix products, arithmetic and copies ran while one was open for 2% -> 0% of each run, Pallas kernels for 20% -> 29%
where the time goes in v4:
time: 72.7 us; the launch traced here: 72.5 us
  Pallas kernels  31.7 us (44%)
  starting transfers between devices  21.3 us (29%)
  waiting for transfers between devices  18.3 us (25%)
  between operations  0.81 us (1%)
    pallas_call x2, Pallas kernels, front(): pl.pallas_call(functools.partial(front_kernel, first, last, group, pairs,...  15.4 us
    ppermute x9, starting transfers between devices, swap(): return lax.ppermute(values, axis, [(i, i ^ step) for i in range(count)])  12.9 us
    ppermute x3, waiting for transfers between devices, across_heads(): lax.ppermute(values, 'head', [(i, (i + step) % count) for i in range(coun...  9.47 us
    pallas_call x1, Pallas kernels, near(): pl.pallas_call(functools.partial(near_kernel, groups, pairs), in_specs=[s...  6.4 us
    ppermute x9, waiting for transfers between devices, swap(): return lax.ppermute(values, axis, [(i, i ^ step) for i in range(count)])  6.26 us
    pallas_call x2, Pallas kernels, far(): pl.pallas_call(functools.partial(far_kernel, pairs, group, 256, spread),...  5.7 us
    ppermute x3, starting transfers between devices, per_device(): lax.ppermute(piece, 'seq', [(i, (i + k + 1) % spread) for i in range(spre...  3.87 us
    ppermute x3, starting transfers between devices, across_heads(): lax.ppermute(values, 'head', [(i, (i + step) % count) for i in range(coun...  3.71 us
  transfers between devices with their start and end apart: 16, of which 7 were waited for; matrix products, arithmetic and copies ran while one was open for 0% of the time, Pallas kernels for 29%

profile of v4, /device:TPU:0, one launch (start us, length us, event | category | flops | bytes accessed | tf_op | source)
XLA Modules:
  0.0 72.5 jit_solution(10143488062867227821)
XLA Ops:
  0.6 0.1 pad_add_fusion.1.refs_0_
  0.7 8.8 %front.2 = (bf16[1024,1024]{1,0:T(8,128)(2,1)S(1)}, bf16[1024,512]{1,0:T(8,128)(2,1)S(1)}, bf16[256,256]{1,0:T(8,128)(2,1)S(1)}, bf16[256,256]{1,0:T(8,128)(2,1)...) custom-call(s32[4]{0:T(128)S(1)} %pad_add_fusion.1.refs_0_, bf16[1024,1024]{1,0:T(8,128)(2,1)} %refs_1_.1, ...), custom_call_target="tpu_custom_call" | custom-call | flops 1048576 | bytes 1024 | tf_op jit(solution)/shard_map/front/pallas_call | solution.py:210
  9.5 0.5 collective-permute-start
  10.0 1.0 %collective-permute-done = bf16[256,256]{1,0:T(8,128)(2,1)S(1)} collective-permute-done((bf16[256,256]{1,0:T(8,128)(2,1)S(1)}, bf16[256,256]{1,0:T(8,128)(2,1)S(1)}, u32[]{:S(2)}, u32[]{:S(2)}) %collective-permute-start) | collective-permute-done | bytes 131104 | tf_op jit(solution)/shard_map/ppermute | solution.py:466
  11.1 3.0 %collective-permute-start.2 = (bf16[256,256]{1,0:T(8,128)(2,1)S(1)}, bf16[256,256]{1,0:T(8,128)(2,1)S(1)}, u32[]{:S(2)}, u32[]{:S(2)}) collective-permute-start(bf16[256,256]{1,0:T(8,128)(2,1)S(1)} %add_convert_fusion.3), channel_id=1, source_target_pairs={{0,4},{4,0},{8,12},{12,8},{1,5},{5,1},{9,13},{13,9},{2,6},{6,2},{1... | collective-permute-start | bytes 393224 | tf_op jit(solution)/shard_map/ppermute | solution.py:466
  14.1 0.0 copy-done.2
  14.1 6.6 %front.3 = (bf16[1024,1024]{1,0:T(8,128)(2,1)S(1)}, bf16[1024,512]{1,0:T(8,128)(2,1)S(1)}, bf16[256,256]{1,0:T(8,128)(2,1)S(1)}, bf16[512,256]{1,0:T(8,128)(2,1)...) custom-call(s32[4]{0:T(128)S(1)} %get-tuple-element.55.refs_0_, ...), custom_call_target="tpu_custom_call", output_to_operand_aliasing={{0}: (1, {})} | custom-call | flops 1048576 | bytes 1024 | tf_op jit(solution)/shard_map/front/pallas_call | solution.py:210
  20.7 0.1 collective-permute-start.1
  20.8 0.8 %collective-permute-start.4 = (bf16[256,256]{1,0:T(8,128)(2,1)S(1)}, bf16[256,256]{1,0:T(8,128)(2,1)S(1)}, u32[]{:S(2)}, u32[]{:S(2)}) collective-permute-start(bf16[256,256]{1,0:T(8,128)(2,1)S(1)} %get-tuple-element.70), channel_id=1, source_target_pairs={{1,4},{5,8},{9,12},{4,1},{8,5},{12,9},{3,6},{7,10},{11,14},{6,3},{... | collective-permute-start | bytes 393224 | tf_op jit(solution)/shard_map/ppermute | solution.py:542
  21.6 0.0 collective-permute-done.2
  21.7 0.6 collective-permute-done.1.refs_2_
  22.3 2.8 %collective-permute-start.3 = (bf16[256,256]{1,0:T(8,128)(2,1)S(1)}, bf16[256,256]{1,0:T(8,128)(2,1)S(1)}, u32[]{:S(2)}, u32[]{:S(2)}) collective-permute-start(bf16[256,256]{1,0:T(8,128)(2,1)S(1)} %add_convert_fusion.1), channel_id=1, source_target_pairs={{0,4},{4,0},{8,12},{12,8},{1,5},{5,1},{9,13},{13,9},{2,6},{6,2},{1... | collective-permute-start | bytes 393224 | tf_op jit(solution)/shard_map/ppermute | solution.py:466
  25.2 2.6 %collective-permute-start.6 = (bf16[256,256]{1,0:T(8,128)(2,1)S(1)}, bf16[256,256]{1,0:T(8,128)(2,1)S(1)}, u32[]{:S(2)}, u32[]{:S(2)}) collective-permute-start(bf16[256,256]{1,0:T(8,128)(2,1)S(1)} %add_convert_fusion.2.a_ref), channel_id=1, source_target_pairs={{0,8},{4,12},{8,0},{12,4},{1,9},{5,13},{9,1},{13,5},{2,10},{6,14},... | collective-permute-start | bytes 393224 | tf_op jit(solution)/shard_map/ppermute | solution.py:466
  27.8 0.0 collective-permute-done.4.refs_3_
  27.8 0.0 copy-done.1
  27.8 6.4 %near.1 = (bf16[1024,256]{1,0:T(8,128)(2,1)S(1)}, bf16[1024,256]{1,0:T(8,128)(2,1)S(1)}, f32[1024,512]{1,0:T(8,128)S(1)}, f32[1024,512]{1,0:T(8,128)S(1)}, s32[4]{0:T(128)S(1)}) custom-call(s32[4]{0:T(128)S(1)} %get-tuple-element.68.refs_0_, bf16[1024,1024]{1,0:T(8,128)(2,1)S(1)} %get-tuple-element.69.refs_1_, ...), custom_call_target="tpu_custom_call" | custom-call | flops 1048576 | bytes 1024 | tf_op jit(solution)/shard_map/near/pallas_call | solution.py:290
  34.2 0.0 collective-permute-done.3
  34.2 0.0 collective-permute-done.6.b_ref
  34.3 0.4 collective-permute-start.7
  34.7 3.4 %collective-permute-start.5 = (bf16[256,256]{1,0:T(8,128)(2,1)S(1)}, bf16[256,256]{1,0:T(8,128)(2,1)S(1)}, u32[]{:S(2)}, u32[]{:S(2)}) collective-permute-start(bf16[256,256]{1,0:T(8,128)(2,1)S(1)} %add_convert_fusion.a_ref), channel_id=1, source_target_pairs={{0,8},{4,12},{8,0},{12,4},{1,9},{5,13},{9,1},{13,5},{2,10},{6,14},... | collective-permute-start | bytes 393224 | tf_op jit(solution)/shard_map/ppermute | solution.py:466
  38.1 0.0 collective-permute-done.7.refs_4_
  38.1 0.0 copy-done.3
  38.1 3.1 %far.2 = (bf16[1024,256]{1,0:T(8,128)(2,1)S(1)}, f32[32,256]{1,0:T(8,128)S(1)}, bf16[32,256]{1,0:T(8,128)(2,1)S(1)}, s32[4]{0:T(128)S(1)}) custom-call(s32[4]{0:T(128)S(1)} %get-tuple-element.79.refs_0_, bf16[1024,256]{1,0:T(8,128)(2,1)S(1)} %get-tuple-element.80.refs_1_, f32[1024,512]{1,0:T(8,128)S(1)} %get-tuple-element.81.refs_2_, ...), custom_call_target="tpu_custom_call" | custom-call | flops 1048576 | bytes 1024 | tf_op jit(solution)/shard_map/far/pallas_call | solution.py:362
  41.2 0.0 copy-start
  41.2 3.4 %collective-permute-done.5.b_ref = bf16[256,256]{1,0:T(8,128)(2,1)S(1)} collective-permute-done((bf16[256,256]{1,0:T(8,128)(2,1)S(1)}, bf16[256,256]{1,0:T(8,128)(2,1)S(1)}, u32[]{:S(2)}, u32[]{:S(2)}) %collective-permute-start.5) | collective-permute-done | bytes 131104 | tf_op jit(solution)/shard_map/ppermute | solution.py:466
  44.7 0.1 collective-permute-start.8
  44.8 1.6 %collective-permute-start.15 = (bf16[1024,256]{1,0:T(8,128)(2,1)S(1)}, bf16[1024,256]{1,0:T(8,128)(2,1)S(1)}, u32[]{:S(2)}, u32[]{:S(2)}) collective-permute-start(bf16[1024,256]{1,0:T(8,128)(2,1)S(1)} %get-tuple-element.97.refs_1_), channel_id=1, source_target_pairs={{0,2},{2,0},{1,3},{3,1},{4,6},{6,4},{5,7},{7,5},{8,10},{10,8},{9,1... | collective-permute-start | bytes 1572872 | tf_op jit(solution)/shard_map/ppermute | solution.py:471
  46.3 0.0 collective-permute-done.8.refs_4_
  46.3 2.6 %far.3 = (bf16[1024,256]{1,0:T(8,128)(2,1)S(1)}, f32[32,512]{1,0:T(8,128)S(1)}, bf16[32,512]{1,0:T(8,128)(2,1)S(1)}, s32[4]{0:T(128)}) custom-call(s32[4]{0:T(128)S(1)} %get-tuple-element.84.refs_0_, bf16[1024,256]{1,0:T(8,128)(2,1)S(1)} %get-tuple-element.85.refs_1_, f32[1024,512]{1,0:T(8,128)S(1)} %get-tuple-element.86.refs_2_, ...), custom_call_target="tpu_custom_call" | custom-call | flops 1048576 | bytes 1024 | tf_op jit(solution)/shard_map/far/pallas_call | solution.py:362
  49.0 1.3 %collective-permute-start.9 = (bf16[1024,256]{1,0:T(8,128)(2,1)S(1)}, bf16[1024,256]{1,0:T(8,128)(2,1)S(1)}, u32[]{:S(2)}, u32[]{:S(2)}) collective-permute-start(bf16[1024,256]{1,0:T(8,128)(2,1)S(1)} %get-tuple-element.90.refs_2_), channel_id=1, source_target_pairs={{0,2},{2,0},{1,3},{3,1},{4,6},{6,4},{5,7},{7,5},{8,10},{10,8},{9,1... | collective-permute-start | bytes 1572872 | tf_op jit(solution)/shard_map/ppermute | solution.py:471
  50.3 0.0 collective-permute-start.10
  50.3 1.2 %collective-permute-done.10.got_ref = bf16[32,512]{1,0:T(8,128)(2,1)S(1)} collective-permute-done((bf16[32,512]{1,0:T(8,128)(2,1)S(1)}, bf16[32,512]{1,0:T(8,128)(2,1)S(1)}, u32[]{:S(2)}, u32[]{:S(2)}) %collective-permute-start.10) | collective-permute-done | bytes 32800 | tf_op jit(solution)/shard_map/ppermute | solution.py:466
  51.5 0.1 collective-permute-start.11
  51.6 2.8 %collective-permute-start.12 = (bf16[8,512]{1,0:T(8,128)(2,1)S(1)}, bf16[8,512]{1,0:T(8,128)(2,1)S(1)}, u32[]{:S(2)}, u32[]{:S(2)}) collective-permute-start(bf16[8,512]{1,0:T(8,128)(2,1)S(1)} %get-tuple-element.95), channel_id=1, source_target_pairs={{0,8},{4,12},{8,0},{12,4},{1,9},{5,13},{9,1},{13,5},{2,10},{6,14},... | collective-permute-start | bytes 24584 | tf_op jit(solution)/shard_map/ppermute | solution.py:581
  54.4 1.0 %collective-permute-start.13 = (bf16[8,512]{1,0:T(8,128)(2,1)S(1)}, bf16[8,512]{1,0:T(8,128)(2,1)S(1)}, u32[]{:S(2)}, u32[]{:S(2)}) collective-permute-start(bf16[8,512]{1,0:T(8,128)(2,1)S(1)} %get-tuple-element.96), channel_id=1, source_target_pairs={{0,12},{4,0},{8,4},{12,8},{1,13},{5,1},{9,5},{13,9},{2,14},{6,2},{... | collective-permute-start | bytes 24584 | tf_op jit(solution)/shard_map/ppermute | solution.py:581
  55.4 0.1 pad_add_fusion.2.refs_0_
  55.5 1.5 %collective-permute-done.11.refs_0_ = bf16[8,512]{1,0:T(8,128)(2,1)S(1)} collective-permute-done((bf16[8,512]{1,0:T(8,128)(2,1)S(1)}, bf16[8,512]{1,0:T(8,128)(2,1)S(1)}, u32[]{:S(2)}, u32[]{:S(2)}) %collective-permute-start.11) | collective-permute-done | bytes 8224 | tf_op jit(solution)/shard_map/ppermute | solution.py:581
  57.0 0.0 collective-permute-done.12.refs_1_
  57.0 1.0 %collective-permute-done.13.refs_2_ = bf16[8,512]{1,0:T(8,128)(2,1)S(1)} collective-permute-done((bf16[8,512]{1,0:T(8,128)(2,1)S(1)}, bf16[8,512]{1,0:T(8,128)(2,1)S(1)}, u32[]{:S(2)}, u32[]{:S(2)}) %collective-permute-start.13) | collective-permute-done | bytes 8224 | tf_op jit(solution)/shard_map/ppermute | solution.py:581
  58.0 0.6 pool_own.1.refs_2_
  58.6 0.8 %collective-permute-start.14 = (bf16[8,512]{1,0:T(8,128)(2,1)S(1)}, bf16[8,512]{1,0:T(8,128)(2,1)S(1)}, u32[]{:S(2)}, u32[]{:S(2)}) collective-permute-start(bf16[8,512]{1,0:T(8,128)(2,1)S(1)} %pool_own.1.refs_2_), channel_id=1, source_target_pairs={{0,2},{2,0},{1,3},{3,1},{4,6},{6,4},{5,7},{7,5},{8,10},{10,8},{9,1... | collective-permute-start | bytes 24584 | tf_op jit(solution)/shard_map/ppermute | solution.py:471
  59.4 0.1 pad_add_fusion.refs_0_
  59.5 0.0 collective-permute-done.15.refs_3_
  59.6 0.0 copy-done
  59.6 1.5 %out.2.refs_5_ = f32[1024,512]{1,0:T(8,128)S(1)} custom-call(s32[3]{0:T(128)S(1)} %pad_add_fusion.2.refs_0_, bf16[1024,256]{1,0:T(8,128)(2,1)S(1)} %get-tuple-element.97.refs_1_, bf16[1024,256]{1,0:T(8,128)(2,1)S(1)} %get-tuple-element.90.refs_2_, bf16[1024,256]{1,0:T(8,128)(2,1)S(1)} %collective-permute-done.15.refs_3_, bf16[1024,512]{1,0:T(8,128)(2,1)S(1)} %copy-done), custom_call_target="tpu_custom_call" | custom-call | flops 1048576 | bytes 1024 | tf_op jit(solution)/shard_map/out/pallas_call | solution.py:407
  61.1 9.4 %collective-permute-done.14.refs_3_ = bf16[8,512]{1,0:T(8,128)(2,1)S(1)} collective-permute-done((bf16[8,512]{1,0:T(8,128)(2,1)S(1)}, bf16[8,512]{1,0:T(8,128)(2,1)S(1)}, u32[]{:S(2)}, u32[]{:S(2)}) %collective-permute-start.14) | collective-permute-done | bytes 8224 | tf_op jit(solution)/shard_map/ppermute | solution.py:471
  70.5 0.0 collective-permute-done.9.refs_1_
  70.5 2.0 %out.3 = (bf16[1024,512]{1,0:T(8,128)(2,1)}, f32[8,512]{1,0:T(8,128)}) custom-call(s32[3]{0:T(128)S(1)} %pad_add_fusion.refs_0_, bf16[1024,256]{1,0:T(8,128)(2,1)S(1)} %collective-permute-done.9.refs_1_, bf16[8,512]{1,0:T(8,128)(2,1)S(1)} %pool_own.1.refs_2_, bf16[8,512]{1,0:T(8,128)(2,1)S(1)} %collective-permute-done.14.refs_3_, ...), custom_call_target="tpu_custom_call" | custom-call | flops 1048576 | bytes 1024 | tf_op jit(solution)/shard_map/out/pallas_call | solution.py:407
  (11 shorter events, 0.2 us)
Async XLA Ops:
  0.7 13.3 %copy-start.2 = (f32[4,512]{1,0:T(4,128)S(1)}, f32[4,512]{1,0:T(4,128)}, u32[]{:S(2)}) copy-start(f32[4,512]{1,0:T(4,128)} %refs_5_.7) | copy-start | bytes 24580
  9.5 1.5 %collective-permute-start = (bf16[256,256]{1,0:T(8,128)(2,1)S(1)}, bf16[256,256]{1,0:T(8,128)(2,1)S(1)}, u32[]{:S(2)}, u32[]{:S(2)}) collective-permute-start(bf16[256,256]{1,0:T(8,128)(2,1)S(1)} %get-tuple-element.51), channel_id=1, source_target_pairs={{0,1},{1,0},{2,3},{3,2},{4,5},{5,4},{6,7},{7,6},{8,9},{9,8},{10,11... | collective-permute-start | bytes 393224 | tf_op jit(solution)/shard_map/ppermute | solution.py:466
  11.1 10.6 %collective-permute-start.2 = (bf16[256,256]{1,0:T(8,128)(2,1)S(1)}, bf16[256,256]{1,0:T(8,128)(2,1)S(1)}, u32[]{:S(2)}, u32[]{:S(2)}) collective-permute-start(bf16[256,256]{1,0:T(8,128)(2,1)S(1)} %add_convert_fusion.3), channel_id=1, source_target_pairs={{0,4},{4,0},{8,12},{12,8},{1,5},{5,1},{9,13},{13,9},{2,6},{6,2},{1... | collective-permute-start | bytes 393224 | tf_op jit(solution)/shard_map/ppermute | solution.py:466
  14.1 13.7 %copy-start.1 = (bf16[1024,512]{1,0:T(8,128)(2,1)S(1)}, bf16[1024,512]{1,0:T(8,128)(2,1)}, u32[]{:S(2)}) copy-start(bf16[1024,512]{1,0:T(8,128)(2,1)} %refs_4_.7) | copy-start | bytes 3145732
  20.7 1.6 %collective-permute-start.1 = (bf16[512,256]{1,0:T(8,128)(2,1)S(1)}, bf16[512,256]{1,0:T(8,128)(2,1)S(1)}, u32[]{:S(2)}, u32[]{:S(2)}) collective-permute-start(bf16[512,256]{1,0:T(8,128)(2,1)S(1)} %get-tuple-element.59), channel_id=1, source_target_pairs={{0,1},{1,0},{2,3},{3,2},{4,5},{5,4},{6,7},{7,6},{8,9},{9,8},{10,11... | collective-permute-start | bytes 786440 | tf_op jit(solution)/shard_map/ppermute | solution.py:466
  20.8 7.0 %collective-permute-start.4 = (bf16[256,256]{1,0:T(8,128)(2,1)S(1)}, bf16[256,256]{1,0:T(8,128)(2,1)S(1)}, u32[]{:S(2)}, u32[]{:S(2)}) collective-permute-start(bf16[256,256]{1,0:T(8,128)(2,1)S(1)} %get-tuple-element.70), channel_id=1, source_target_pairs={{1,4},{5,8},{9,12},{4,1},{8,5},{12,9},{3,6},{7,10},{11,14},{6,3},{... | collective-permute-start | bytes 393224 | tf_op jit(solution)/shard_map/ppermute | solution.py:542
  22.3 11.8 %collective-permute-start.3 = (bf16[256,256]{1,0:T(8,128)(2,1)S(1)}, bf16[256,256]{1,0:T(8,128)(2,1)S(1)}, u32[]{:S(2)}, u32[]{:S(2)}) collective-permute-start(bf16[256,256]{1,0:T(8,128)(2,1)S(1)} %add_convert_fusion.1), channel_id=1, source_target_pairs={{0,4},{4,0},{8,12},{12,8},{1,5},{5,1},{9,13},{13,9},{2,6},{6,2},{1... | collective-permute-start | bytes 393224 | tf_op jit(solution)/shard_map/ppermute | solution.py:466
  25.2 9.1 %collective-permute-start.6 = (bf16[256,256]{1,0:T(8,128)(2,1)S(1)}, bf16[256,256]{1,0:T(8,128)(2,1)S(1)}, u32[]{:S(2)}, u32[]{:S(2)}) collective-permute-start(bf16[256,256]{1,0:T(8,128)(2,1)S(1)} %add_convert_fusion.2.a_ref), channel_id=1, source_target_pairs={{0,8},{4,12},{8,0},{12,4},{1,9},{5,13},{9,1},{13,5},{2,10},{6,14},... | collective-permute-start | bytes 393224 | tf_op jit(solution)/shard_map/ppermute | solution.py:466
  27.8 10.3 %copy-start.3 = (s32[64,2]{0,1:T(2,128)S(1)}, s32[64,2]{0,1:T(2,128)}, u32[]{:S(2)}) copy-start(s32[64,2]{0,1:T(2,128)} %param.17) | copy-start | bytes 1540
  34.3 3.8 %collective-permute-start.7 = (bf16[256,256]{1,0:T(8,128)(2,1)S(1)}, bf16[256,256]{1,0:T(8,128)(2,1)S(1)}, u32[]{:S(2)}, u32[]{:S(2)}) collective-permute-start(bf16[256,256]{1,0:T(8,128)(2,1)S(1)} %add.61.refs_3_), channel_id=1, source_target_pairs={{0,1},{1,0},{2,3},{3,2},{4,5},{5,4},{6,7},{7,6},{8,9},{9,8},{10,11... | collective-permute-start | bytes 393224 | tf_op jit(solution)/shard_map/ppermute | solution.py:466
  34.7 10.0 %collective-permute-start.5 = (bf16[256,256]{1,0:T(8,128)(2,1)S(1)}, bf16[256,256]{1,0:T(8,128)(2,1)S(1)}, u32[]{:S(2)}, u32[]{:S(2)}) collective-permute-start(bf16[256,256]{1,0:T(8,128)(2,1)S(1)} %add_convert_fusion.a_ref), channel_id=1, source_target_pairs={{0,8},{4,12},{8,0},{12,4},{1,9},{5,13},{9,1},{13,5},{2,10},{6,14},... | collective-permute-start | bytes 393224 | tf_op jit(solution)/shard_map/ppermute | solution.py:466
  41.2 18.4 %copy-start = (bf16[1024,512]{1,0:T(8,128)(2,1)S(1)}, bf16[1024,512]{1,0:T(8,128)(2,1)}, u32[]{:S(2)}) copy-start(bf16[1024,512]{1,0:T(8,128)(2,1)} %refs_4_.9) | copy-start | bytes 3145732
  44.7 1.6 %collective-permute-start.8 = (bf16[256,256]{1,0:T(8,128)(2,1)S(1)}, bf16[256,256]{1,0:T(8,128)(2,1)S(1)}, u32[]{:S(2)}, u32[]{:S(2)}) collective-permute-start(bf16[256,256]{1,0:T(8,128)(2,1)S(1)} %add.62.refs_3_), channel_id=1, source_target_pairs={{0,1},{1,0},{2,3},{3,2},{4,5},{5,4},{6,7},{7,6},{8,9},{9,8},{10,11... | collective-permute-start | bytes 393224 | tf_op jit(solution)/shard_map/ppermute | solution.py:466
  44.8 14.8 %collective-permute-start.15 = (bf16[1024,256]{1,0:T(8,128)(2,1)S(1)}, bf16[1024,256]{1,0:T(8,128)(2,1)S(1)}, u32[]{:S(2)}, u32[]{:S(2)}) collective-permute-start(bf16[1024,256]{1,0:T(8,128)(2,1)S(1)} %get-tuple-element.97.refs_1_), channel_id=1, source_target_pairs={{0,2},{2,0},{1,3},{3,1},{4,6},{6,4},{5,7},{7,5},{8,10},{10,8},{9,1... | collective-permute-start | bytes 1572872 | tf_op jit(solution)/shard_map/ppermute | solution.py:471
  49.0 21.6 %collective-permute-start.9 = (bf16[1024,256]{1,0:T(8,128)(2,1)S(1)}, bf16[1024,256]{1,0:T(8,128)(2,1)S(1)}, u32[]{:S(2)}, u32[]{:S(2)}) collective-permute-start(bf16[1024,256]{1,0:T(8,128)(2,1)S(1)} %get-tuple-element.90.refs_2_), channel_id=1, source_target_pairs={{0,2},{2,0},{1,3},{3,1},{4,6},{6,4},{5,7},{7,5},{8,10},{10,8},{9,1... | collective-permute-start | bytes 1572872 | tf_op jit(solution)/shard_map/ppermute | solution.py:471
  50.3 1.2 %collective-permute-start.10 = (bf16[32,512]{1,0:T(8,128)(2,1)S(1)}, bf16[32,512]{1,0:T(8,128)(2,1)S(1)}, u32[]{:S(2)}, u32[]{:S(2)}) collective-permute-start(bf16[32,512]{1,0:T(8,128)(2,1)S(1)} %get-tuple-element.92), channel_id=1, source_target_pairs={{0,1},{1,0},{2,3},{3,2},{4,5},{5,4},{6,7},{7,6},{8,9},{9,8},{10,11... | collective-permute-start | bytes 98312 | tf_op jit(solution)/shard_map/ppermute | solution.py:466
  51.5 5.5 %collective-permute-start.11 = (bf16[8,512]{1,0:T(8,128)(2,1)S(1)}, bf16[8,512]{1,0:T(8,128)(2,1)S(1)}, u32[]{:S(2)}, u32[]{:S(2)}) collective-permute-start(bf16[8,512]{1,0:T(8,128)(2,1)S(1)} %get-tuple-element.94), channel_id=1, source_target_pairs={{0,4},{4,8},{8,12},{12,0},{1,5},{5,9},{9,13},{13,1},{2,6},{6,10},{... | collective-permute-start | bytes 24584 | tf_op jit(solution)/shard_map/ppermute | solution.py:581
  51.6 5.4 %collective-permute-start.12 = (bf16[8,512]{1,0:T(8,128)(2,1)S(1)}, bf16[8,512]{1,0:T(8,128)(2,1)S(1)}, u32[]{:S(2)}, u32[]{:S(2)}) collective-permute-start(bf16[8,512]{1,0:T(8,128)(2,1)S(1)} %get-tuple-element.95), channel_id=1, source_target_pairs={{0,8},{4,12},{8,0},{12,4},{1,9},{5,13},{9,1},{13,5},{2,10},{6,14},... | collective-permute-start | bytes 24584 | tf_op jit(solution)/shard_map/ppermute | solution.py:581
  54.4 3.7 %collective-permute-start.13 = (bf16[8,512]{1,0:T(8,128)(2,1)S(1)}, bf16[8,512]{1,0:T(8,128)(2,1)S(1)}, u32[]{:S(2)}, u32[]{:S(2)}) collective-permute-start(bf16[8,512]{1,0:T(8,128)(2,1)S(1)} %get-tuple-element.96), channel_id=1, source_target_pairs={{0,12},{4,0},{8,4},{12,8},{1,13},{5,1},{9,5},{13,9},{2,14},{6,2},{... | collective-permute-start | bytes 24584 | tf_op jit(solution)/shard_map/ppermute | solution.py:581
  58.6 11.9 %collective-permute-start.14 = (bf16[8,512]{1,0:T(8,128)(2,1)S(1)}, bf16[8,512]{1,0:T(8,128)(2,1)S(1)}, u32[]{:S(2)}, u32[]{:S(2)}) collective-permute-start(bf16[8,512]{1,0:T(8,128)(2,1)S(1)} %pool_own.1.refs_2_), channel_id=1, source_target_pairs={{0,2},{2,0},{1,3},{3,1},{4,6},{6,4},{5,7},{7,5},{8,10},{10,8},{9,1... | collective-permute-start | bytes 24584 | tf_op jit(solution)/shard_map/ppermute | solution.py:471

commit v5 on v4

--- a/solution.py
+++ b/solution.py
@@ -181,7 +181,7 @@
     rows, depth = tokens.shape
     width = pairs * LANES
     half = pairs * R // 2
-    tile = min(256, rows)
+    tile = min(512 if first else 256, rows)
     edge = (group + 1) * pairs * HALF if last else 0
     outs = [
         jax.ShapeDtypeStruct((rows, depth), BF),
@@ -239,10 +239,8 @@
     )
 
 
-def near_kernel(groups, pairs, *refs):
-    ids_ref, normed_ref, core_ref, chip_ref, wq_ref = refs[:5]
-    near_refs, refs = refs[5 : 5 + groups], refs[5 + groups :]
-    q_refs, out_refs, (turn_ref, pad_ref) = refs[:groups], refs[groups : 2 * groups], refs[2 * groups :]
+def near_kernel(pairs, group, ids_ref, tokens_ref, core_ref, chip_ref, wq_ref, near_ref,
+                normed_ref, q_ref, out_ref, turn_ref, pad_ref):
     rows = normed_ref.shape[0]
     width = pairs * LANES
     is_first = ids_ref[0] == 0
@@ -252,59 +250,61 @@
     has_next = jnp.where(ids_ref[2] != 0, 1.0, 0.0)
     segments = rows // SEG
     offset = core_ref.shape[0] - chip_ref.shape[0]
-    for g in range(groups):
-        q_ref, near_ref, out_ref = q_refs[g], near_refs[g], out_refs[g]
-        q_ref[...] = dot(normed_ref[...], wq_ref[:, g * width : (g + 1) * width]).astype(BF)
-        pad_ref[HALF : HALF + rows, :] = near_ref[...]
-        for c in range(pairs):
-            at = (g * pairs + c) * HALF
-            core = core_ref[offset + at : offset + at + HALF, :]
-            chip = chip_ref[at : at + HALF, :]
-            lanes = slice(2 * c * LANES, 2 * (c + 1) * LANES)
-            pad_ref[0:HALF, lanes] = jnp.where(is_first, chip, core)
-            pad_ref[HALF + rows :, lanes] = jnp.where(is_first, core, chip)
-        for s in range(segments):
-            count = ones
-            if s == 0:
-                count = jnp.where(row < HALF, has_prev, count)
-            if s == segments - 1:
-                count = jnp.where(row >= 3 * HALF, has_next, count)
-            count = count.astype(BF)
-            window = pl.ds(s * SEG, 2 * SEG)
-            here = slice(s * SEG, (s + 1) * SEG)
-            for p in range(pairs):
-                cols = slice(p * LANES, (p + 1) * LANES)
-                scores = dot(stacked(q_ref[here, cols]), pad_ref[window, cols], ((1,), (1,)))
-                weights = exp_capped(scores, SCORE_SCALE).astype(BF)
-                values = jnp.concatenate([pad_ref[window, width + p * LANES : width + (p + 1) * LANES], count], axis=1)
-                top, bottom = unstack(dot(weights, values))
-                out_ref[here, 2 * p * LANES : (2 * p + 1) * LANES] = top
-                out_ref[here, (2 * p + 1) * LANES : (2 * p + 2) * LANES] = bottom
+    q_ref[...] = dot(normed_ref[...], wq_ref[:, group * width : (group + 1) * width]).astype(BF)
+    pad_ref[HALF : HALF + rows, :] = near_ref[...]
+    for c in range(pairs):
+        at = (group * pairs + c) * HALF
+        core = core_ref[offset + at : offset + at + HALF, :]
+        chip = chip_ref[at : at + HALF, :]
+        lanes = slice(2 * c * LANES, 2 * (c + 1) * LANES)
+        pad_ref[0:HALF, lanes] = jnp.where(is_first, chip, core)
+        pad_ref[HALF + rows :, lanes] = jnp.where(is_first, core, chip)
+    for s in range(segments):
+        count = ones
+        if s == 0:
+            count = jnp.where(row < HALF, has_prev, count)
+        if s == segments - 1:
+            count = jnp.where(row >= 3 * HALF, has_next, count)
+        count = count.astype(BF)
+        window = pl.ds(s * SEG, 2 * SEG)
+        here = slice(s * SEG, (s + 1) * SEG)
+        for p in range(pairs):
+            cols = slice(p * LANES, (p + 1) * LANES)
+            scores = dot(stacked(q_ref[here, cols]), pad_ref[window, cols], ((1,), (1,)))
+            weights = exp_capped(scores, SCORE_SCALE).astype(BF)
+            values = jnp.concatenate([pad_ref[window, width + p * LANES : width + (p + 1) * LANES], count], axis=1)
+            top, bottom = unstack(dot(weights, values))
+            out_ref[here, 2 * p * LANES : (2 * p + 1) * LANES] = top
+            out_ref[here, (2 * p + 1) * LANES : (2 * p + 2) * LANES] = bottom
     pass_turn(ids_ref, turn_ref)
 
 
-def near(pairs, ids, normed, core, chip, wq, near_pairs):
+def near(pairs, group, ids, normed, core, chip, wq, near_pairs):
     rows = normed.shape[0]
     width = pairs * LANES
-    groups = len(near_pairs)
-    outs = pl.pallas_call(
-        functools.partial(near_kernel, groups, pairs),
-        in_specs=[smem()] + [vmem()] * (4 + groups),
-        out_specs=[vmem()] * (2 * groups) + [smem()],
-        out_shape=[jax.ShapeDtypeStruct((rows, width), BF)] * groups
-        + [jax.ShapeDtypeStruct((rows, 2 * width), F32)] * groups
-        + [TURN],
+    return pl.pallas_call(
+        functools.partial(near_kernel, pairs, group),
+        in_specs=[smem()] + [vmem()] * 5,
+        out_specs=[vmem()] * 3 + [smem()],
+        out_shape=[
+            jax.ShapeDtypeStruct(normed.shape, BF),
+            jax.ShapeDtypeStruct((rows, width), BF),
+            jax.ShapeDtypeStruct((rows, 2 * width), F32),
+            TURN,
+        ],
+        input_output_aliases={1: 0},
         scratch_shapes=[pltpu.VMEM((rows + SEG, 2 * width), BF)],
         compiler_params=pltpu.CompilerParams(vmem_limit_bytes=VMEM_LIMIT),
         cost_estimate=COST,
         name="near",
-    )(ids, normed, core, chip, wq, *near_pairs)
-    return list(zip(outs[:groups], outs[groups : 2 * groups])), outs[-1]
+    )(ids, normed, core, chip, wq, near_pairs)
 
 
 def far_kernel(pairs, group, block, spread, *refs):
     (ids_ref, q_ref, near_ref, mine_ref, other_ref, gains_ref, bounds_ref), refs = refs[:7], refs[7:]
-    before, (out_ref, keep_ref, send_ref, turn_ref) = refs[:-4], refs[-4:]
+    keep_ref, send_ref, turn_ref = refs[-3:]
+    out_refs = refs[-3 - pairs : -3]
+    before = refs[:2] if group else ()
     pass_turn(ids_ref, turn_ref)
     rows = q_ref.shape[0]
     width = pairs * LANES
@@ -338,11 +338,12 @@
             top, bottom = unstack(dot(weights, values, ((1,), (1,))))
             top = top + near_ref[start : start + block, 2 * p * LANES : (2 * p + 1) * LANES]
             bottom = bottom + near_ref[start : start + block, (2 * p + 1) * LANES : (2 * p + 2) * LANES]
-            out_ref[start : start + block, cols] = (top / bottom).astype(BF)
+            out_refs[p][start : start + block, :] = (top / bottom).astype(BF)
     spans = bounds_ref.shape[1]
     position = ids_ref[3] + lax.broadcasted_iota(jnp.int32, (rows, spans), 0)
     member = (position >= bounds_ref[0:1, :]) & (position < bounds_ref[1:2, :])
-    sums = dot(jnp.where(member, 1.0, 0.0).astype(BF), out_ref[...], ((0,), (0,)))
+    outs = jnp.concatenate([ref[...] for ref in out_refs], axis=1)
+    sums = dot(jnp.where(member, 1.0, 0.0).astype(BF), outs, ((0,), (0,)))
     count = spans // (2 * spread)
     even = jnp.concatenate([sums[2 * i * count : (2 * i + 1) * count] for i in range(spread)], axis=0)
     odd = jnp.concatenate([sums[(2 * i + 1) * count : (2 * i + 2) * count] for i in range(spread)], axis=0)
@@ -354,17 +355,17 @@
     send_ref[:, lanes] = jnp.where(is_first, odd, even).astype(BF)
 
 
-def far(pairs, group, spread, ids, q, near_sums, mine, other, gains, bounds, before):
+def far(pairs, group, spread, ids, q, near_sums, mine, other, gains, bounds, before, arrived):
     rows = q.shape[0]
     width = pairs * LANES
     spans = bounds.shape[1]
     shape = (spans // 2, (group + 1) * width)
     return pl.pallas_call(
         functools.partial(far_kernel, pairs, group, 256, spread),
-        in_specs=[smem()] + [vmem()] * (6 + len(before)),
-        out_specs=[vmem()] * 3 + [smem()],
+        in_specs=[smem()] + [vmem()] * (6 + len(before)) + [pl.BlockSpec(memory_space=pl.ANY)] * len(arrived),
+        out_specs=[vmem()] * (2 + pairs) + [smem()],
         out_shape=[
-            jax.ShapeDtypeStruct((rows, width), BF),
+            *[jax.ShapeDtypeStruct((rows, LANES), BF)] * pairs,
             jax.ShapeDtypeStruct(shape, F32),
             jax.ShapeDtypeStruct(shape, BF),
             TURN,
@@ -372,16 +373,18 @@
         compiler_params=pltpu.CompilerParams(vmem_limit_bytes=VMEM_LIMIT),
         cost_estimate=COST,
         name="far",
-    )(ids, q, near_sums, mine, other, gains, bounds, *before)
-
-
-def out_kernel(count, spans, *refs):
+    )(ids, q, near_sums, mine, other, gains, bounds, *before, *arrived)
+
+
+def out_kernel(count, pairs, spans, *refs):
     ids_ref, refs = refs[0], refs[1:]
-    tokens, refs = refs[:count], refs[count:]
+    tokens, refs = [refs[j * pairs : (j + 1) * pairs] for j in range(count)], refs[count * pairs :]
     pooled, refs = refs[:spans], refs[spans:]
+    *refs, turn_ref = refs
+    turn_ref[0] = ids_ref[0]
     outs = refs[-2:] if spans else refs[-1:]
     weight_ref, *acc = refs[: -len(outs)]
-    rows, width = tokens[0].shape
+    rows, width = tokens[0][0].shape[0], pairs * LANES
 
     def weight(j, size):
         return weight_ref[pl.ds(pl.multiple_of(ids_ref[j] * size, size), size), :]
@@ -390,7 +393,7 @@
         at = slice(start, start + 256)
         total = acc[0][at, :] if acc else None
         for j in range(count):
-            term = dot(tokens[j][at, :], weight(j, width))
+            term = dot(jnp.concatenate([ref[at, :] for ref in tokens[j]], axis=1), weight(j, width))
             total = term if total is None else total + term
         outs[0][at, :] = total.astype(outs[0].dtype)
     if spans:
@@ -399,20 +402,21 @@
 
 def out_part(parts, index, weight, acc, dtype, pooled=()):
     count = len(parts)
-    rows = parts[0].shape[0]
+    pairs = len(parts[0])
+    rows = parts[0][0].shape[0]
     columns = weight.shape[1]
     extra = [] if acc is None else [acc]
     shapes = [jax.ShapeDtypeStruct((rows, columns), dtype)]
     shapes += [jax.ShapeDtypeStruct((pooled[0].shape[0], columns), F32)] if pooled else []
     return pl.pallas_call(
-        functools.partial(out_kernel, count, len(pooled)),
-        in_specs=[smem()] + [vmem()] * (count + len(pooled) + 1 + len(extra)),
-        out_specs=[vmem()] * len(shapes),
-        out_shape=shapes,
+        functools.partial(out_kernel, count, pairs, len(pooled)),
+        in_specs=[smem()] + [vmem()] * (count * pairs + len(pooled) + 1 + len(extra)),
+        out_specs=[vmem()] * len(shapes) + [smem()],
+        out_shape=shapes + [jax.ShapeDtypeStruct((1,), jnp.int32)],
         compiler_params=pltpu.CompilerParams(vmem_limit_bytes=VMEM_LIMIT),
         cost_estimate=COST,
         name="out",
-    )(index, *parts, *pooled, weight, *extra)
+    )(index, *[piece for part in parts for piece in part], *pooled, weight, *extra)
 
 
 def pieces_kernel(ids_ref, keep_ref, got_ref, *out_refs):
@@ -537,41 +541,45 @@
         normed, *outs, turn = front(g == 0, last, g, pairs, turn, normed, gain, key_weight, value_weight, proj_weight,
                                     dual_gains, [f[3] for f in fronts])
         fronts.append(outs)
-        core = swap(outs[2], "rep", 1)
+        send, edge = outs[2], outs[3]
         if last:
-            chip = lax.ppermute(outs[3], both, chips)
             for f in range(g):
                 for step in steps[:-1]:
                     got, turn = tie((swap(mine[f], "seq", step), turn))
                     mine[f] = add(mine[f], got)
                 mine[f], turn = tie((mine[f], turn))
+        core = swap(send, "rep", 1)
+        if last:
+            chip = lax.ppermute(edge, both, chips)
         got, turn = tie((core[: outs[1].shape[0]], turn))
         mine.append(add(outs[1], got))
         mine[g], turn = tie((mine[g], turn))
 
-    nears, turn = near(pairs, turn, normed, core, chip, query_weight, [f[0] for f in fronts])
-    got, turn = tie((swap(mine[-1], "seq", steps[0]), turn))
-    mine[-1] = add(mine[-1], got)
-    for step in steps[1:-1]:
-        mine[-1] = add(mine[-1], swap(mine[-1], "seq", step))
-    mine[-1], turn = tie((mine[-1], turn))
+    if groups == 1:
+        for step in steps[:-1]:
+            mine[0] = add_call(mine[0], swap(mine[0], "seq", step))
 
     spread = lax.axis_size("seq")
-    outs, before = [], ()
+    outs, before, arrived, others, other_index = [], (), [], [], []
     for g in range(groups):
+        normed, q, near_sums, turn = near(pairs, g, turn, normed, core, chip, query_weight, fronts[g][0])
         got, turn = tie((swap(mine[g], "seq", steps[-1]), turn))
         total = add_call(mine[g], got)
-        q, near_sums = nears[g]
-        out, *before, turn = far(pairs, g, spread, turn, q, near_sums, total, swap(total, "rep", 1), dual_gains,
-                                 bounds, before)
+        other = swap(total, "rep", 1)
+        if g == groups - 2:
+            for step in steps[:-1]:
+                got, turn = tie((swap(mine[-1], "seq", step), turn))
+                mine[-1] = add_call(mine[-1], got)
+            mine[-1], turn = tie((mine[-1], turn))
+        *out, keep, send, turn = far(pairs, g, spread, turn, q, near_sums, total, other, dual_gains, bounds, before, arrived)
+        before = [keep, send]
         outs.append(out)
+        moved = [[across_heads(piece, k) for piece in out] for k in range(1, head_devices)]
+        arrived = [moved[0][0]] if g < groups - 1 and moved else []
+        others += moved
+        other_index += [lax.rem(head_index - k + head_devices, head_devices) * groups + g for k in range(1, head_devices)]
 
     own_index = [head_index * groups + g for g in range(groups)]
-    others, other_index = [], []
-    for g in range(groups):
-        for k in range(1, head_devices):
-            others.append(across_heads(outs[g], k))
-            other_index.append(lax.rem(head_index - k + head_devices, head_devices) * groups + g)
     early = len(others) - (head_devices - 1)
 
     keep, send = before
@@ -580,15 +588,16 @@
     pieces = [
         lax.ppermute(piece, "seq", [(i, (i + k + 1) % spread) for i in range(spread)]) for k, piece in enumerate(pieces)
     ]
-    own = pool_own((seq_index * own.shape[0]).astype(jnp.int32)[None], bounds, own, pieces)
+    parts = outs + others[:early]
+    index = jnp.stack(own_index + other_index[:early]).astype(jnp.int32)
+    acc, turn = out_part(parts, index, out_weight, None, F32)
+    place = (seq_index * own.shape[0]).astype(jnp.int32)[None]
+    place = place + (turn - index[:1])
+    own = pool_own(place, bounds, own, pieces)
     pooled = [own] + [across_heads(own, k) for k in range(1, head_devices)]
     pooled_index = [lax.rem(head_index - k + head_devices, head_devices) for k in range(head_devices)]
-
-    parts = outs + others[:early]
-    index = jnp.stack(own_index + other_index[:early]).astype(jnp.int32)
-    (acc,) = out_part(parts, index, out_weight, None, F32)
     index = jnp.stack(other_index[early:] + pooled_index).astype(jnp.int32)
-    return tuple(out_part(others[early:], index, out_weight, acc, BF, pooled))
+    return tuple(out_part(others[early:], index, out_weight, acc, BF, pooled)[:2])
 
 
 def solution(mesh):

time: 72.7 us -> 67.3 us (0.926)
  waiting for transfers between devices: 18.3 us -> 9.1 us
  Pallas kernels: 31.7 us -> 33.8 us
  starting transfers between devices: 21.3 us -> 22.3 us
  between operations: 0.81 us -> 1.64 us
    ppermute x3 -> x5, waiting for transfers between devices: 9.47 us -> 5.02 us  [across_heads(): lax.ppermute(values, 'head', [(i, (i + step) % count) for i in range(coun...]
    ppermute x3, waiting for transfers between devices: 2.56 us -> 0.01 us  [per_device(): lax.ppermute(piece, 'seq', [(i, (i + k + 1) % spread) for i in range(spre...]
    ppermute x9, waiting for transfers between devices: 6.26 us -> 4.07 us  [swap(): return lax.ppermute(values, axis, [(i, i ^ step) for i in range(count)])]
    ppermute x3 -> x5, starting transfers between devices: 3.71 us -> 5.74 us  [across_heads(): lax.ppermute(values, 'head', [(i, (i + step) % count) for i in range(coun...]
    pallas_call x3 -> x4, Pallas kernels: 9.93 us -> 11.8 us  [the longest x2 8.27 us: near(): pl.pallas_call(functools.partial(near_kernel, pairs, group), in_specs=[sm...]
    ppermute x9, starting transfers between devices: 12.9 us -> 11.8 us  [swap(): return lax.ppermute(values, axis, [(i, i ^ step) for i in range(count)])]
  transfers between devices with their start and end apart: 16 -> 18, of which waited for: 7 -> 5; matrix products, arithmetic and copies ran while one was open for 0% -> 0% of each run, Pallas kernels for 29% -> 34%
where the time goes in v5:
time: 67.3 us; the launch traced here: 67.2 us
  Pallas kernels  33.8 us (50%)
  starting transfers between devices  22.3 us (33%)
  waiting for transfers between devices  9.1 us (14%)
  between operations  1.64 us (2%)
    pallas_call x2, Pallas kernels, front(): pl.pallas_call(functools.partial(front_kernel, first, last, group, pairs,...  15.2 us
    ppermute x9, starting transfers between devices, swap(): return lax.ppermute(values, axis, [(i, i ^ step) for i in range(count)])  11.8 us
    pallas_call x2, Pallas kernels, near(): pl.pallas_call(functools.partial(near_kernel, pairs, group), in_specs=[sm...  8.27 us
    pallas_call x2, Pallas kernels, far(): pl.pallas_call(functools.partial(far_kernel, pairs, group, 256, spread),...  6.06 us
    ppermute x5, starting transfers between devices, across_heads(): lax.ppermute(values, 'head', [(i, (i + step) % count) for i in range(coun...  5.74 us
    ppermute x5, waiting for transfers between devices, across_heads(): lax.ppermute(values, 'head', [(i, (i + step) % count) for i in range(coun...  5.02 us
    ppermute x9, waiting for transfers between devices, swap(): return lax.ppermute(values, axis, [(i, i ^ step) for i in range(count)])  4.07 us
    ppermute x3, starting transfers between devices, per_device(): lax.ppermute(piece, 'seq', [(i, (i + k + 1) % spread) for i in range(spre...  3.88 us
  transfers between devices with their start and end apart: 18, of which 5 were waited for; matrix products, arithmetic and copies ran while one was open for 0% of the time, Pallas kernels for 34%

profile of v5, /device:TPU:0, one launch (start us, length us, event | category | flops | bytes accessed | tf_op | source)
XLA Modules:
  0.0 67.2 jit_solution(5927228512620599311)
XLA Ops:
  0.6 0.1 pad_add_fusion.1.refs_0_
  0.7 8.6 %front.2 = (bf16[1024,1024]{1,0:T(8,128)(2,1)S(1)}, bf16[1024,512]{1,0:T(8,128)(2,1)S(1)}, bf16[256,256]{1,0:T(8,128)(2,1)S(1)}, bf16[256,256]{1,0:T(8,128)(2,1)...) custom-call(s32[4]{0:T(128)S(1)} %pad_add_fusion.1.refs_0_, bf16[1024,1024]{1,0:T(8,128)(2,1)} %refs_1_.1, ...), custom_call_target="tpu_custom_call" | custom-call | flops 1048576 | bytes 1024 | tf_op jit(solution)/shard_map/front/pallas_call | solution.py:210
  9.3 0.5 collective-permute-start
  9.9 1.0 %collective-permute-done = bf16[256,256]{1,0:T(8,128)(2,1)S(1)} collective-permute-done((bf16[256,256]{1,0:T(8,128)(2,1)S(1)}, bf16[256,256]{1,0:T(8,128)(2,1)S(1)}, u32[]{:S(2)}, u32[]{:S(2)}) %collective-permute-start) | collective-permute-done | bytes 131104 | tf_op jit(solution)/shard_map/ppermute | solution.py:470
  10.9 3.0 %collective-permute-start.2 = (bf16[256,256]{1,0:T(8,128)(2,1)S(1)}, bf16[256,256]{1,0:T(8,128)(2,1)S(1)}, u32[]{:S(2)}, u32[]{:S(2)}) collective-permute-start(bf16[256,256]{1,0:T(8,128)(2,1)S(1)} %add_convert_fusion.2), channel_id=1, source_target_pairs={{0,4},{4,0},{8,12},{12,8},{1,5},{5,1},{9,13},{13,9},{2,6},{6,2},{1... | collective-permute-start | bytes 393224 | tf_op jit(solution)/shard_map/ppermute | solution.py:470
  13.9 6.6 %front.3 = (bf16[1024,1024]{1,0:T(8,128)(2,1)S(1)}, bf16[1024,512]{1,0:T(8,128)(2,1)S(1)}, bf16[256,256]{1,0:T(8,128)(2,1)S(1)}, bf16[512,256]{1,0:T(8,128)(2,1)...) custom-call(s32[4]{0:T(128)S(1)} %get-tuple-element.63.refs_0_, ...), custom_call_target="tpu_custom_call", output_to_operand_aliasing={{0}: (1, {})} | custom-call | flops 1048576 | bytes 1024 | tf_op jit(solution)/shard_map/front/pallas_call | solution.py:210
  20.5 0.1 collective-permute-start.1
  20.6 0.8 %collective-permute-start.5 = (bf16[256,256]{1,0:T(8,128)(2,1)S(1)}, bf16[256,256]{1,0:T(8,128)(2,1)S(1)}, u32[]{:S(2)}, u32[]{:S(2)}) collective-permute-start(bf16[256,256]{1,0:T(8,128)(2,1)S(1)} %get-tuple-element.79), channel_id=1, source_target_pairs={{1,4},{5,8},{9,12},{4,1},{8,5},{12,9},{3,6},{7,10},{11,14},{6,3},{... | collective-permute-start | bytes 393224 | tf_op jit(solution)/shard_map/ppermute | solution.py:553
  21.4 0.0 collective-permute-done.2
  21.5 3.9 %collective-permute-start.4 = (bf16[256,256]{1,0:T(8,128)(2,1)S(1)}, bf16[256,256]{1,0:T(8,128)(2,1)S(1)}, u32[]{:S(2)}, u32[]{:S(2)}) collective-permute-start(bf16[256,256]{1,0:T(8,128)(2,1)S(1)} %add_convert_fusion.1.a_ref), channel_id=1, source_target_pairs={{0,8},{4,12},{8,0},{12,4},{1,9},{5,13},{9,1},{13,5},{2,10},{6,14},... | collective-permute-start | bytes 393224 | tf_op jit(solution)/shard_map/ppermute | solution.py:470
  25.4 0.0 collective-permute-done.1.core_ref
  25.5 2.2 %collective-permute-start.3 = (bf16[256,256]{1,0:T(8,128)(2,1)S(1)}, bf16[256,256]{1,0:T(8,128)(2,1)S(1)}, u32[]{:S(2)}, u32[]{:S(2)}) collective-permute-start(bf16[256,256]{1,0:T(8,128)(2,1)S(1)} %add_convert_fusion.a_ref), channel_id=1, source_target_pairs={{0,4},{4,0},{8,12},{12,8},{1,5},{5,1},{9,13},{13,9},{2,6},{6,2},{1... | collective-permute-start | bytes 393224 | tf_op jit(solution)/shard_map/ppermute | solution.py:470
  27.6 0.0 collective-permute-done.5.chip_ref
  27.6 4.1 %near.2 = (bf16[1024,1024]{1,0:T(8,128)(2,1)S(1)}, bf16[1024,256]{1,0:T(8,128)(2,1)S(1)}, f32[1024,512]{1,0:T(8,128)S(1)}, s32[4]{0:T(128)S(1)}) custom-call(s32[4]{0:T(128)S(1)} %get-tuple-element.77.ids_ref, bf16[1024,1024]{1,0:T(8,128)(2,1)S(1)} %get-tuple-element.78.tokens_ref, ...), custom_call_target="tpu_custom_call", output_to_operand_aliasing={{0}: (1, {})} | custom-call | flops 1048576 | bytes 1024 | tf_op jit(solution)/shard_map/near/pallas_call | solution.py:285
  31.8 1.9 %collective-permute-done.4.b_ref = bf16[256,256]{1,0:T(8,128)(2,1)S(1)} collective-permute-done((bf16[256,256]{1,0:T(8,128)(2,1)S(1)}, bf16[256,256]{1,0:T(8,128)(2,1)S(1)}, u32[]{:S(2)}, u32[]{:S(2)}) %collective-permute-start.4) | collective-permute-done | bytes 131104 | tf_op jit(solution)/shard_map/ppermute | solution.py:470
  33.7 0.1 collective-permute-start.7
  33.8 0.0 collective-permute-done.3.b_ref
  33.8 2.0 %collective-permute-start.6 = (bf16[256,256]{1,0:T(8,128)(2,1)S(1)}, bf16[256,256]{1,0:T(8,128)(2,1)S(1)}, u32[]{:S(2)}, u32[]{:S(2)}) collective-permute-start(bf16[256,256]{1,0:T(8,128)(2,1)S(1)} %add.61.a_ref), channel_id=1, source_target_pairs={{0,8},{4,12},{8,0},{12,4},{1,9},{5,13},{9,1},{13,5},{2,10},{6,14},... | collective-permute-start | bytes 393224 | tf_op jit(solution)/shard_map/ppermute | solution.py:470
  35.8 0.0 collective-permute-done.7.refs_4_
  35.8 3.1 %far.2 = (bf16[1024,128]{1,0:T(8,128)(2,1)S(1)}, bf16[1024,128]{1,0:T(8,128)(2,1)S(1)}, f32[32,256]{1,0:T(8,128)S(1)}, bf16[32,256]{1,0:T(8,128)(2,1)S(1)}, s32[4]{0:T(128)S(1)}) custom-call(s32[4]{0:T(128)S(1)} %get-tuple-element.86.refs_0_, bf16[1024,256]{1,0:T(8,128)(2,1)S(1)} %get-tuple-element.87.refs_1_, f32[1024,512]{1,0:T(8,128)S(1)} %get-tuple-element.88.refs_2_, ...), custom_call_target="tpu_custom_call" | custom-call | flops 1048576 | bytes 1024 | tf_op jit(solution)/shard_map/far/pallas_call | solution.py:363
  38.9 1.6 %collective-permute-start.9 = (bf16[1024,128]{1,0:T(8,128)(2,1)S(1)}, bf16[1024,128]{1,0:T(8,128)(2,1)S(1)}, u32[]{:S(2)}, u32[]{:S(2)}) collective-permute-start(bf16[1024,128]{1,0:T(8,128)(2,1)S(1)} %get-tuple-element.100.refs_1_), channel_id=1, source_target_pairs={{0,2},{2,0},{1,3},{3,1},{4,6},{6,4},{5,7},{7,5},{8,10},{10,8},{9,1... | collective-permute-start | bytes 786440 | tf_op jit(solution)/shard_map/ppermute | solution.py:475
  40.5 0.5 collective-permute-start.12
  41.0 4.1 %near.3 = (bf16[1024,1024]{1,0:T(8,128)(2,1)S(1)}, bf16[1024,256]{1,0:T(8,128)(2,1)S(1)}, f32[1024,512]{1,0:T(8,128)S(1)}, s32[4]{0:T(128)S(1)}) custom-call(s32[4]{0:T(128)S(1)} %get-tuple-element.90.ids_ref, bf16[1024,1024]{1,0:T(8,128)(2,1)S(1)} %get-tuple-element.91.tokens_ref, ...), custom_call_target="tpu_custom_call", output_to_operand_aliasing={{0}: (1, {})} | custom-call | flops 1048576 | bytes 1024 | tf_op jit(solution)/shard_map/near/pallas_call | solution.py:285
  45.2 0.0 copy-start.1
  45.2 0.0 collective-permute-done.6.b_ref
  45.2 0.1 collective-permute-start.8
  45.3 2.9 %collective-permute-done.9.refs_9_.refs_5_ = bf16[1024,128]{1,0:T(8,128)(2,1)S(1)} collective-permute-done((bf16[1024,128]{1,0:T(8,128)(2,1)S(1)}, bf16[1024,128]{1,0:T(8,128)(2,1)S(1)}, u32[]{:S(2)}, u32[]{:S(2)}) %collective-permute-start.9) | collective-permute-done | bytes 262176 | tf_op jit(solution)/shard_map/ppermute | solution.py:475
  48.2 0.0 collective-permute-done.8.refs_4_
  48.3 3.0 %far.3 = (bf16[1024,128]{1,0:T(8,128)(2,1)S(1)}, bf16[1024,128]{1,0:T(8,128)(2,1)S(1)}, f32[32,512]{1,0:T(8,128)S(1)}, bf16[32,512]{1,0:T(8,128)(2,1)S(1)}, s32[4]{0:T(128)}) custom-call(s32[4]{0:T(128)S(1)} %get-tuple-element.94.refs_0_, bf16[1024,256]{1,0:T(8,128)(2,1)S(1)} %get-tuple-element.95.refs_1_, f32[1024,512]{1,0:T(8,128)S(1)} %get-tuple-element.96.refs_2_, ...), custom_call_target="tpu_custom_call" | custom-call | flops 1048576 | bytes 1024 | tf_op jit(solution)/shard_map/far/pallas_call | solution.py:363
  51.2 1.6 %collective-permute-start.10 = (bf16[1024,128]{1,0:T(8,128)(2,1)S(1)}, bf16[1024,128]{1,0:T(8,128)(2,1)S(1)}, u32[]{:S(2)}, u32[]{:S(2)}) collective-permute-start(bf16[1024,128]{1,0:T(8,128)(2,1)S(1)} %get-tuple-element.101.refs_3_), channel_id=1, source_target_pairs={{0,2},{2,0},{1,3},{3,1},{4,6},{6,4},{5,7},{7,5},{8,10},{10,8},{9,1... | collective-permute-start | bytes 786440 | tf_op jit(solution)/shard_map/ppermute | solution.py:475
  52.8 0.5 collective-permute-start.11
  53.3 0.0 collective-permute-start.13
  53.3 1.2 %collective-permute-done.13.got_ref = bf16[32,512]{1,0:T(8,128)(2,1)S(1)} collective-permute-done((bf16[32,512]{1,0:T(8,128)(2,1)S(1)}, bf16[32,512]{1,0:T(8,128)(2,1)S(1)}, u32[]{:S(2)}, u32[]{:S(2)}) %collective-permute-start.13) | collective-permute-done | bytes 32800 | tf_op jit(solution)/shard_map/ppermute | solution.py:470
  54.6 1.2 %collective-permute-start.14 = (bf16[8,512]{1,0:T(8,128)(2,1)S(1)}, bf16[8,512]{1,0:T(8,128)(2,1)S(1)}, u32[]{:S(2)}, u32[]{:S(2)}) collective-permute-start(bf16[8,512]{1,0:T(8,128)(2,1)S(1)} %get-tuple-element.108), channel_id=1, source_target_pairs={{0,4},{4,8},{8,12},{12,0},{1,5},{5,9},{9,13},{13,1},{2,6},{6,10},{... | collective-permute-start | bytes 24584 | tf_op jit(solution)/shard_map/ppermute | solution.py:589
  55.8 1.0 %collective-permute-start.15 = (bf16[8,512]{1,0:T(8,128)(2,1)S(1)}, bf16[8,512]{1,0:T(8,128)(2,1)S(1)}, u32[]{:S(2)}, u32[]{:S(2)}) collective-permute-start(bf16[8,512]{1,0:T(8,128)(2,1)S(1)} %get-tuple-element.109), channel_id=1, source_target_pairs={{0,8},{4,12},{8,0},{12,4},{1,9},{5,13},{9,1},{13,5},{2,10},{6,14},... | collective-permute-start | bytes 24584 | tf_op jit(solution)/shard_map/ppermute | solution.py:589
  56.8 0.0 collective-permute-done.12.refs_6_
  56.8 1.7 %collective-permute-start.16 = (bf16[8,512]{1,0:T(8,128)(2,1)S(1)}, bf16[8,512]{1,0:T(8,128)(2,1)S(1)}, u32[]{:S(2)}, u32[]{:S(2)}) collective-permute-start(bf16[8,512]{1,0:T(8,128)(2,1)S(1)} %get-tuple-element.110), channel_id=1, source_target_pairs={{0,12},{4,0},{8,4},{12,8},{1,13},{5,1},{9,5},{13,9},{2,14},{6,2},{... | collective-permute-start | bytes 24584 | tf_op jit(solution)/shard_map/ppermute | solution.py:589
  58.4 0.1 pad_add_fusion.2.refs_0_
  58.5 1.5 %out.2 = (f32[1024,512]{1,0:T(8,128)S(1)}, s32[1]{0:T(128)}) custom-call(s32[3]{0:T(128)S(1)} %pad_add_fusion.2.refs_0_, bf16[1024,128]{1,0:T(8,128)(2,1)S(1)} %get-tuple-element.100.refs_1_, bf16[1024,128]{1,0:T(8,128)(2,1)S(1)} %get-tuple-element.103.refs_2_, bf16[1024,128]{1,0:T(8,128)(2,1)S(1)} %get-tuple-element.101.refs_3_, ...), custom_call_target="tpu_custom_call" | custom-call | flops 1048576 | bytes 1024 | tf_op jit(solution)/shard_map/out/pallas_call | solution.py:411
  60.7 0.0 collective-permute-done.15.refs_1_
  60.7 0.0 collective-permute-done.16.refs_2_
  60.7 0.6 pool_own.1.refs_3_
  61.3 1.6 %collective-permute-start.17 = (bf16[8,512]{1,0:T(8,128)(2,1)S(1)}, bf16[8,512]{1,0:T(8,128)(2,1)S(1)}, u32[]{:S(2)}, u32[]{:S(2)}) collective-permute-start(bf16[8,512]{1,0:T(8,128)(2,1)S(1)} %pool_own.1.refs_3_), channel_id=1, source_target_pairs={{0,2},{2,0},{1,3},{3,1},{4,6},{6,4},{5,7},{7,5},{8,10},{10,8},{9,1... | collective-permute-start | bytes 24584 | tf_op jit(solution)/shard_map/ppermute | solution.py:475
  62.9 0.1 pad_add_fusion.refs_0_
  63.0 2.1 %collective-permute-done.17.refs_4_ = bf16[8,512]{1,0:T(8,128)(2,1)S(1)} collective-permute-done((bf16[8,512]{1,0:T(8,128)(2,1)S(1)}, bf16[8,512]{1,0:T(8,128)(2,1)S(1)}, u32[]{:S(2)}, u32[]{:S(2)}) %collective-permute-start.17) | collective-permute-done | bytes 8224 | tf_op jit(solution)/shard_map/ppermute | solution.py:475
  65.0 0.0 collective-permute-done.10.refs_1_
  65.0 0.0 collective-permute-done.11.refs_2_
  65.1 2.0 %out.3 = (bf16[1024,512]{1,0:T(8,128)(2,1)}, f32[8,512]{1,0:T(8,128)}, s32[1]{0:T(128)}) custom-call(s32[3]{0:T(128)S(1)} %pad_add_fusion.refs_0_, bf16[1024,128]{1,0:T(8,128)(2,1)S(1)} %collective-permute-done.10.refs_1_, bf16[1024,128]{1,0:T(8,128)(2,1)S(1)} %collective-permute-done.11.refs_2_, bf16[8,512]{1,0:T(8,128)(2,1)S(1)} %pool_own.1.refs_3_, ...), custom_call_target="tpu_custom_call" | custom-call | flops 1048576 | bytes 1024 | tf_op jit(solution)/shard_map/out/pallas_call | solution.py:411
  (16 shorter events, 0.3 us)
Async XLA Ops:
  0.7 13.2 %copy-start.2 = (f32[4,512]{1,0:T(4,128)S(1)}, f32[4,512]{1,0:T(4,128)}, u32[]{:S(2)}) copy-start(f32[4,512]{1,0:T(4,128)} %refs_5_.8) | copy-start | bytes 24580
  9.3 1.5 %collective-permute-start = (bf16[256,256]{1,0:T(8,128)(2,1)S(1)}, bf16[256,256]{1,0:T(8,128)(2,1)S(1)}, u32[]{:S(2)}, u32[]{:S(2)}) collective-permute-start(bf16[256,256]{1,0:T(8,128)(2,1)S(1)} %get-tuple-element.59), channel_id=1, source_target_pairs={{0,1},{1,0},{2,3},{3,2},{4,5},{5,4},{6,7},{7,6},{8,9},{9,8},{10,11... | collective-permute-start | bytes 393224 | tf_op jit(solution)/shard_map/ppermute | solution.py:470
  10.9 10.6 %collective-permute-start.2 = (bf16[256,256]{1,0:T(8,128)(2,1)S(1)}, bf16[256,256]{1,0:T(8,128)(2,1)S(1)}, u32[]{:S(2)}, u32[]{:S(2)}) collective-permute-start(bf16[256,256]{1,0:T(8,128)(2,1)S(1)} %add_convert_fusion.2), channel_id=1, source_target_pairs={{0,4},{4,0},{8,12},{12,8},{1,5},{5,1},{9,13},{13,9},{2,6},{6,2},{1... | collective-permute-start | bytes 393224 | tf_op jit(solution)/shard_map/ppermute | solution.py:470
  13.9 13.7 %copy-start = (bf16[1024,512]{1,0:T(8,128)(2,1)S(1)}, bf16[1024,512]{1,0:T(8,128)(2,1)}, u32[]{:S(2)}) copy-start(bf16[1024,512]{1,0:T(8,128)(2,1)} %wq_ref.3) | copy-start | bytes 3145732
  20.5 4.9 %collective-permute-start.1 = (bf16[512,256]{1,0:T(8,128)(2,1)S(1)}, bf16[512,256]{1,0:T(8,128)(2,1)S(1)}, u32[]{:S(2)}, u32[]{:S(2)}) collective-permute-start(bf16[512,256]{1,0:T(8,128)(2,1)S(1)} %get-tuple-element.67), channel_id=1, source_target_pairs={{0,1},{1,0},{2,3},{3,2},{4,5},{5,4},{6,7},{7,6},{8,9},{9,8},{10,11... | collective-permute-start | bytes 786440 | tf_op jit(solution)/shard_map/ppermute | solution.py:470
  20.6 7.0 %collective-permute-start.5 = (bf16[256,256]{1,0:T(8,128)(2,1)S(1)}, bf16[256,256]{1,0:T(8,128)(2,1)S(1)}, u32[]{:S(2)}, u32[]{:S(2)}) collective-permute-start(bf16[256,256]{1,0:T(8,128)(2,1)S(1)} %get-tuple-element.79), channel_id=1, source_target_pairs={{1,4},{5,8},{9,12},{4,1},{8,5},{12,9},{3,6},{7,10},{11,14},{6,3},{... | collective-permute-start | bytes 393224 | tf_op jit(solution)/shard_map/ppermute | solution.py:553
  21.5 12.1 %collective-permute-start.4 = (bf16[256,256]{1,0:T(8,128)(2,1)S(1)}, bf16[256,256]{1,0:T(8,128)(2,1)S(1)}, u32[]{:S(2)}, u32[]{:S(2)}) collective-permute-start(bf16[256,256]{1,0:T(8,128)(2,1)S(1)} %add_convert_fusion.1.a_ref), channel_id=1, source_target_pairs={{0,8},{4,12},{8,0},{12,4},{1,9},{5,13},{9,1},{13,5},{2,10},{6,14},... | collective-permute-start | bytes 393224 | tf_op jit(solution)/shard_map/ppermute | solution.py:470
  25.5 8.3 %collective-permute-start.3 = (bf16[256,256]{1,0:T(8,128)(2,1)S(1)}, bf16[256,256]{1,0:T(8,128)(2,1)S(1)}, u32[]{:S(2)}, u32[]{:S(2)}) collective-permute-start(bf16[256,256]{1,0:T(8,128)(2,1)S(1)} %add_convert_fusion.a_ref), channel_id=1, source_target_pairs={{0,4},{4,0},{8,12},{12,8},{1,5},{5,1},{9,13},{13,9},{2,6},{6,2},{1... | collective-permute-start | bytes 393224 | tf_op jit(solution)/shard_map/ppermute | solution.py:470
  27.6 8.2 %copy-start.3 = (s32[64,2]{0,1:T(2,128)S(1)}, s32[64,2]{0,1:T(2,128)}, u32[]{:S(2)}) copy-start(s32[64,2]{0,1:T(2,128)} %param.17) | copy-start | bytes 1540
  33.7 2.2 %collective-permute-start.7 = (bf16[256,256]{1,0:T(8,128)(2,1)S(1)}, bf16[256,256]{1,0:T(8,128)(2,1)S(1)}, u32[]{:S(2)}, u32[]{:S(2)}) collective-permute-start(bf16[256,256]{1,0:T(8,128)(2,1)S(1)} %add.62.refs_3_), channel_id=1, source_target_pairs={{0,1},{1,0},{2,3},{3,2},{4,5},{5,4},{6,7},{7,6},{8,9},{9,8},{10,11... | collective-permute-start | bytes 393224 | tf_op jit(solution)/shard_map/ppermute | solution.py:470
  33.8 11.4 %collective-permute-start.6 = (bf16[256,256]{1,0:T(8,128)(2,1)S(1)}, bf16[256,256]{1,0:T(8,128)(2,1)S(1)}, u32[]{:S(2)}, u32[]{:S(2)}) collective-permute-start(bf16[256,256]{1,0:T(8,128)(2,1)S(1)} %add.61.a_ref), channel_id=1, source_target_pairs={{0,8},{4,12},{8,0},{12,4},{1,9},{5,13},{9,1},{13,5},{2,10},{6,14},... | collective-permute-start | bytes 393224 | tf_op jit(solution)/shard_map/ppermute | solution.py:470
  38.9 9.3 %collective-permute-start.9 = (bf16[1024,128]{1,0:T(8,128)(2,1)S(1)}, bf16[1024,128]{1,0:T(8,128)(2,1)S(1)}, u32[]{:S(2)}, u32[]{:S(2)}) collective-permute-start(bf16[1024,128]{1,0:T(8,128)(2,1)S(1)} %get-tuple-element.100.refs_1_), channel_id=1, source_target_pairs={{0,2},{2,0},{1,3},{3,1},{4,6},{6,4},{5,7},{7,5},{8,10},{10,8},{9,1... | collective-permute-start | bytes 786440 | tf_op jit(solution)/shard_map/ppermute | solution.py:475
  40.5 16.3 %collective-permute-start.12 = (bf16[1024,128]{1,0:T(8,128)(2,1)S(1)}, bf16[1024,128]{1,0:T(8,128)(2,1)S(1)}, u32[]{:S(2)}, u32[]{:S(2)}) collective-permute-start(bf16[1024,128]{1,0:T(8,128)(2,1)S(1)} %get-tuple-element.103.refs_2_), channel_id=1, source_target_pairs={{0,2},{2,0},{1,3},{3,1},{4,6},{6,4},{5,7},{7,5},{8,10},{10,8},{9,1... | collective-permute-start | bytes 786440 | tf_op jit(solution)/shard_map/ppermute | solution.py:475
  45.2 13.3 %copy-start.1 = (bf16[1024,512]{1,0:T(8,128)(2,1)S(1)}, bf16[1024,512]{1,0:T(8,128)(2,1)}, u32[]{:S(2)}) copy-start(bf16[1024,512]{1,0:T(8,128)(2,1)} %refs_5_.9) | copy-start | bytes 3145732
  45.2 3.0 %collective-permute-start.8 = (bf16[256,256]{1,0:T(8,128)(2,1)S(1)}, bf16[256,256]{1,0:T(8,128)(2,1)S(1)}, u32[]{:S(2)}, u32[]{:S(2)}) collective-permute-start(bf16[256,256]{1,0:T(8,128)(2,1)S(1)} %add.63.refs_3_), channel_id=1, source_target_pairs={{0,1},{1,0},{2,3},{3,2},{4,5},{5,4},{6,7},{7,6},{8,9},{9,8},{10,11... | collective-permute-start | bytes 393224 | tf_op jit(solution)/shard_map/ppermute | solution.py:470
  51.2 13.8 %collective-permute-start.10 = (bf16[1024,128]{1,0:T(8,128)(2,1)S(1)}, bf16[1024,128]{1,0:T(8,128)(2,1)S(1)}, u32[]{:S(2)}, u32[]{:S(2)}) collective-permute-start(bf16[1024,128]{1,0:T(8,128)(2,1)S(1)} %get-tuple-element.101.refs_3_), channel_id=1, source_target_pairs={{0,2},{2,0},{1,3},{3,1},{4,6},{6,4},{5,7},{7,5},{8,10},{10,8},{9,1... | collective-permute-start | bytes 786440 | tf_op jit(solution)/shard_map/ppermute | solution.py:475
  52.8 12.3 %collective-permute-start.11 = (bf16[1024,128]{1,0:T(8,128)(2,1)S(1)}, bf16[1024,128]{1,0:T(8,128)(2,1)S(1)}, u32[]{:S(2)}, u32[]{:S(2)}) collective-permute-start(bf16[1024,128]{1,0:T(8,128)(2,1)S(1)} %get-tuple-element.102.refs_4_), channel_id=1, source_target_pairs={{0,2},{2,0},{1,3},{3,1},{4,6},{6,4},{5,7},{7,5},{8,10},{10,8},{9,1... | collective-permute-start | bytes 786440 | tf_op jit(solution)/shard_map/ppermute | solution.py:475
  53.3 1.2 %collective-permute-start.13 = (bf16[32,512]{1,0:T(8,128)(2,1)S(1)}, bf16[32,512]{1,0:T(8,128)(2,1)S(1)}, u32[]{:S(2)}, u32[]{:S(2)}) collective-permute-start(bf16[32,512]{1,0:T(8,128)(2,1)S(1)} %get-tuple-element.106), channel_id=1, source_target_pairs={{0,1},{1,0},{2,3},{3,2},{4,5},{5,4},{6,7},{7,6},{8,9},{9,8},{10,11... | collective-permute-start | bytes 98312 | tf_op jit(solution)/shard_map/ppermute | solution.py:470
  54.6 6.1 %collective-permute-start.14 = (bf16[8,512]{1,0:T(8,128)(2,1)S(1)}, bf16[8,512]{1,0:T(8,128)(2,1)S(1)}, u32[]{:S(2)}, u32[]{:S(2)}) collective-permute-start(bf16[8,512]{1,0:T(8,128)(2,1)S(1)} %get-tuple-element.108), channel_id=1, source_target_pairs={{0,4},{4,8},{8,12},{12,0},{1,5},{5,9},{9,13},{13,1},{2,6},{6,10},{... | collective-permute-start | bytes 24584 | tf_op jit(solution)/shard_map/ppermute | solution.py:589
  55.8 5.0 %collective-permute-start.15 = (bf16[8,512]{1,0:T(8,128)(2,1)S(1)}, bf16[8,512]{1,0:T(8,128)(2,1)S(1)}, u32[]{:S(2)}, u32[]{:S(2)}) collective-permute-start(bf16[8,512]{1,0:T(8,128)(2,1)S(1)} %get-tuple-element.109), channel_id=1, source_target_pairs={{0,8},{4,12},{8,0},{12,4},{1,9},{5,13},{9,1},{13,5},{2,10},{6,14},... | collective-permute-start | bytes 24584 | tf_op jit(solution)/shard_map/ppermute | solution.py:589
  56.8 4.0 %collective-permute-start.16 = (bf16[8,512]{1,0:T(8,128)(2,1)S(1)}, bf16[8,512]{1,0:T(8,128)(2,1)S(1)}, u32[]{:S(2)}, u32[]{:S(2)}) collective-permute-start(bf16[8,512]{1,0:T(8,128)(2,1)S(1)} %get-tuple-element.110), channel_id=1, source_target_pairs={{0,12},{4,0},{8,4},{12,8},{1,13},{5,1},{9,5},{13,9},{2,14},{6,2},{... | collective-permute-start | bytes 24584 | tf_op jit(solution)/shard_map/ppermute | solution.py:589
  61.3 3.7 %collective-permute-start.17 = (bf16[8,512]{1,0:T(8,128)(2,1)S(1)}, bf16[8,512]{1,0:T(8,128)(2,1)S(1)}, u32[]{:S(2)}, u32[]{:S(2)}) collective-permute-start(bf16[8,512]{1,0:T(8,128)(2,1)S(1)} %pool_own.1.refs_3_), channel_id=1, source_target_pairs={{0,2},{2,0},{1,3},{3,1},{4,6},{6,4},{5,7},{7,5},{8,10},{10,8},{9,1... | collective-permute-start | bytes 24584 | tf_op jit(solution)/shard_map/ppermute | solution.py:475

commit v6 on v5

--- a/solution.py
+++ b/solution.py
@@ -18,6 +18,7 @@
 VMEM_LIMIT = 40 << 20
 COST = pl.CostEstimate(flops=1 << 20, bytes_accessed=1 << 10, transcendentals=0)
 
+LONG = pl.CostEstimate(flops=1 << 33, bytes_accessed=1 << 10, transcendentals=0)
 TURN = jax.ShapeDtypeStruct((4,), jnp.int32)
 
 softcap = 5.0
@@ -81,71 +82,80 @@
 def front_kernel(first, last, group, pairs, tile, *refs):
     ids_ref, refs = refs[0], list(refs[1:])
     if first:
-        x_hbm, gain_ref = refs.pop(0), refs.pop(0)
+        x_hbm, gain_hbm, dual_hbm, wk_hbm, wv_hbm, wp_hbm = refs[:6]
+        refs = refs[6:]
     else:
-        normed_ref = refs.pop(0)
-    wk_hbm, wv_hbm, wp_hbm, dual_ref = refs[:4]
-    refs = refs[4:]
+        given_ref, dual_ref, kv_ref, wp_ref = refs[:4]
+        refs = refs[4:]
+        if not last:
+            wk_hbm, wv_hbm, wp_hbm = refs[:3]
+            refs = refs[3:]
     earlier = [refs.pop(0) for _ in range(group)] if last else []
-    out = refs.pop(0)
+    normed_ref, near_ref, keep_ref, send_ref = refs[:4]
+    edge_refs = refs[4 : 5 + len(earlier)]
+    turn_ref = refs[5 + len(earlier)]
+    refs = refs[6 + len(earlier) :]
+    pass_turn(ids_ref, turn_ref)
+    if not last:
+        next_kv_ref, next_wp_ref = refs[:2]
+        refs = refs[2:]
+    raw_ref, p_ref, sem = refs[:3]
     if first:
-        normed_ref = out
-    near_ref, keep_ref, send_ref, edge_ref, turn_ref = refs[:5]
-    refs = refs[5:]
-    pass_turn(ids_ref, turn_ref)
-    raw_ref, p_ref, wk_ref, wv_ref, wp_ref, sem = refs[:6]
-    if first:
-        x_ref, gain_hbm, dual_hbm = refs[6], gain_ref, dual_ref
-        gain_ref, dual_ref = refs[7:]
+        kv_ref, wp_ref, x_ref, gain_ref, dual_ref = refs[3:]
     rows = normed_ref.shape[0]
     width = pairs * LANES
     chunks = rows // tile
-    own = pl.ds(group * width, width)
-
-    def copy(source, target, slot):
-        made = pltpu.make_async_copy(source, target, sem.at[slot])
+    used = 0
+
+    def copy(source, target):
+        nonlocal used
+        made = pltpu.make_async_copy(source, target, sem.at[used])
+        used += 1
         made.start()
         return made
 
+    def weight_copies(g, kv, wp):
+        own = pl.ds(g * width, width)
+        heads = [
+            copy(wk_hbm.at[:, own], kv.at[:, pl.ds(0, width)]),
+            copy(wv_hbm.at[:, own], kv.at[:, pl.ds(width, width)]),
+        ]
+        return heads, [copy(wp_hbm.at[:, pl.ds(g * pairs * 2 * R, pairs * 2 * R)], wp)]
+
     def token_copy(i):
         at = pl.ds(i * tile, tile)
-        return copy(x_hbm.at[at, :], x_ref.at[at, :], i)
-
-    token_copies = [token_copy(0)] if first else []
+        return copy(x_hbm.at[at, :], x_ref.at[at, :])
+
+    kv_copies, proj_copies, next_copies = [], [], []
     if first:
-        gain_copy = copy(gain_hbm, gain_ref, chunks + 2 + pairs)
-        dual_copy = copy(dual_hbm, dual_ref, chunks + 3 + pairs)
-    key_copy = copy(wk_hbm.at[:, own], wk_ref, chunks)
-    value_copy = copy(wv_hbm.at[:, own], wv_ref, chunks + 1)
-    proj_copies = []
-    for p in range(pairs):
-        cols = pl.ds((group * pairs + p) * 2 * R, 2 * R)
-        proj_copies.append(copy(wp_hbm.at[:, cols], wp_ref.at[:, pl.ds(p * 2 * R, 2 * R)], chunks + 2 + p))
-        if first and p == 0:
-            token_copies += [token_copy(i) for i in range(1, chunks)]
+        token_copies = [token_copy(0)]
+        small_copies = [copy(gain_hbm, gain_ref), copy(dual_hbm, dual_ref)]
+        kv_copies, proj_copies = weight_copies(group, kv_ref, wp_ref)
+        token_copies += [token_copy(i) for i in range(1, chunks)]
+    if not last:
+        next_copies = sum(weight_copies(group + 1, next_kv_ref, next_wp_ref), [])
     for i in range(chunks):
         at = pl.ds(i * tile, tile)
         if first:
             token_copies[i].wait()
             if i == 0:
-                gain_copy.wait()
-                dual_copy.wait()
+                for made in small_copies:
+                    made.wait()
             normed_ref[at, :] = token_norm(x_ref[at, :], gain_ref[...])
         normed = normed_ref[at, :]
         if i == 0:
-            key_copy.wait()
-            value_copy.wait()
-        key = dot(normed, wk_ref[...])
-        value = dot(normed, wv_ref[...])
+            for made in kv_copies:
+                made.wait()
+        both = dot(normed, kv_ref[...])
+        key, value = both[:, :width], both[:, width:]
         for p in range(pairs):
             cols = slice(p * LANES, (p + 1) * LANES)
             raw = jnp.concatenate([key[:, cols], value[:, cols]], axis=1).astype(BF)
             raw_ref[2 * p * LANES : 2 * (p + 1) * LANES, at] = raw.T
-        for p in range(pairs):
-            cols = slice(2 * p * R, 2 * (p + 1) * R)
-            if i == 0:
-                proj_copies[p].wait()
-            p_ref[at, cols] = exp_capped(dot(normed, wp_ref[:, cols]), 1.0).astype(BF)
+        if i == 0:
+            for made in proj_copies:
+                made.wait()
+        p_ref[at, :] = exp_capped(dot(normed, wp_ref[...]), 1.0).astype(BF)
         near_ref[at, :width] = head_norm(key, dual_ref[0:1, group * width : (group + 1) * width])
         near_ref[at, width:] = head_norm(value, dual_ref[1:2, group * width : (group + 1) * width])
     total = []
@@ -154,6 +164,8 @@
         for part in range(4):
             head = part % 2
             total.append(full[part * DH : (part + 1) * DH, head * R : (head + 1) * R])
+    for made in next_copies:
+        made.wait()
     total = jnp.concatenate(total, axis=0).astype(BF)
     half = total.shape[0] // 2
     mine = ids_ref[0] == 0
@@ -165,19 +177,19 @@
         for i, ref in enumerate(earlier):
             before = jnp.where(mine, ref[edge:, :], ref[:edge, :])
             send_ref[half + i * edge : half + (i + 1) * edge, :] = before
-            edge_ref[i * edge : (i + 1) * edge, :] = jnp.where(mine, ref[:edge, :], ref[edge:, :])
+            edge_refs[i][...] = jnp.where(mine, ref[:edge, :], ref[edge:, :])
         send_ref[half + group * edge :, :] = jnp.where(mine, tail, head)
-        edge_ref[group * edge :, :] = jnp.where(mine, head, tail)
+        edge_refs[group][...] = jnp.where(mine, head, tail)
     else:
-        edge_ref[:edge, :] = head
-        edge_ref[edge:, :] = tail
+        edge_refs[0][:edge, :] = head
+        edge_refs[0][edge:, :] = tail
 
 
 def in_hbm(values):
     return pltpu.with_memory_space_constraint(values, pltpu.HBM)
 
 
-def front(first, last, group, pairs, ids, tokens, gain, wk, wv, wp, dual, earlier):
+def front(first, last, group, pairs, ids, tokens, gain, wk, wv, wp, dual, earlier, fetched):
     rows, depth = tokens.shape
     width = pairs * LANES
     half = pairs * R // 2
@@ -188,34 +200,47 @@
         jax.ShapeDtypeStruct((rows, 2 * width), BF),
         jax.ShapeDtypeStruct((half, R), BF),
         jax.ShapeDtypeStruct((half + edge, R), BF),
-        jax.ShapeDtypeStruct((edge if last else 2 * pairs * HALF, R), BF),
+        *[jax.ShapeDtypeStruct(((1 if last else 2) * pairs * HALF, R), BF)] * (group + 1 if last else 1),
         TURN,
     ]
+    if not last:
+        outs += [jax.ShapeDtypeStruct((depth, 2 * width), BF), jax.ShapeDtypeStruct((depth, 2 * pairs * R), BF)]
     hbm = pl.BlockSpec(memory_space=pltpu.HBM)
     earlier = earlier if last else []
-    ins = [smem()] + [hbm if first else vmem()] * (2 if first else 1) + [hbm] * 3 + [hbm if first else vmem()]
-    ins += [vmem()] * len(earlier)
-    args = [ids] + ([in_hbm(tokens), in_hbm(gain)] if first else [tokens])
-    args += [in_hbm(wk), in_hbm(wv), in_hbm(wp), in_hbm(dual) if first else dual] + earlier
+    weights = [in_hbm(wk), in_hbm(wv), in_hbm(wp)]
+    if first:
+        ins = [hbm] * 6
+        args = [in_hbm(tokens), in_hbm(gain), in_hbm(dual)] + weights
+    else:
+        ins = [vmem()] * 4 + ([] if last else [hbm] * 3)
+        args = [tokens, dual, *fetched] + ([] if last else weights)
+    ins = [smem()] + ins + [vmem()] * len(earlier)
+    args = [ids] + args + earlier
     scratch = [
         pltpu.VMEM((2 * width, rows), BF),
         pltpu.VMEM((rows, 2 * pairs * R), BF),
-        pltpu.VMEM((depth, width), BF),
-        pltpu.VMEM((depth, width), BF),
-        pltpu.VMEM((depth, 2 * pairs * R), BF),
-        pltpu.SemaphoreType.DMA((rows // tile + 4 + pairs,)),
+        pltpu.SemaphoreType.DMA((rows // tile + 8,)),
     ]
     if first:
-        scratch += [pltpu.VMEM((rows, depth), BF), pltpu.VMEM((1, depth), F32), pltpu.VMEM(dual.shape, F32)]
+        scratch += [
+            pltpu.VMEM((depth, 2 * width), BF),
+            pltpu.VMEM((depth, 2 * pairs * R), BF),
+            pltpu.VMEM((rows, depth), BF),
+            pltpu.VMEM((1, depth), F32),
+            pltpu.VMEM(dual.shape, F32),
+        ]
+    is_turn = [o is TURN for o in outs]
     return pl.pallas_call(
         functools.partial(front_kernel, first, last, group, pairs, tile),
         input_output_aliases={} if first else {1: 0},
         in_specs=ins,
-        out_specs=[vmem()] * (len(outs) - 1) + [smem()],
+        out_specs=[smem() if t else vmem() for t in is_turn],
         out_shape=outs,
         scratch_shapes=scratch,
         compiler_params=pltpu.CompilerParams(vmem_limit_bytes=VMEM_LIMIT),
-        cost_estimate=COST,
+        cost_estimate=pl.CostEstimate(
+            flops=2 * rows * depth * (2 * width + 2 * pairs * R), bytes_accessed=4 << 20, transcendentals=0
+        ),
         name="front",
     )(*args)
 
@@ -239,21 +264,30 @@
     )
 
 
-def near_kernel(pairs, group, ids_ref, tokens_ref, core_ref, chip_ref, wq_ref, near_ref,
-                normed_ref, q_ref, out_ref, turn_ref, pad_ref):
-    rows = normed_ref.shape[0]
+def near_kernel(pairs, group, groups, ids_ref, *refs):
     width = pairs * LANES
+    if group == 0:
+        normed_ref, wq_ref, core_ref, chip_ref, near_ref = refs[:5]
+        q_refs, (out_ref, turn_ref, pad_ref) = refs[-3 - groups : -3], refs[-3:]
+        q_ref, rows = q_refs[0], normed_ref.shape[0]
+        for start in range(0, rows, 256):
+            at = slice(start, start + 256)
+            q = dot(normed_ref[at, :], wq_ref[...])
+            for g in range(groups):
+                q_refs[g][at, :] = q[:, g * width : (g + 1) * width].astype(BF)
+    else:
+        given_ref, core_ref, chip_ref, near_ref, q_ref, out_ref, turn_ref, pad_ref = refs
+        rows = q_ref.shape[0]
     is_first = ids_ref[0] == 0
     row = lax.broadcasted_iota(jnp.int32, (2 * SEG, LANES), 0)
     ones = jnp.ones((2 * SEG, LANES), F32)
     has_prev = jnp.where(ids_ref[1] != 0, 1.0, 0.0)
     has_next = jnp.where(ids_ref[2] != 0, 1.0, 0.0)
     segments = rows // SEG
-    offset = core_ref.shape[0] - chip_ref.shape[0]
-    q_ref[...] = dot(normed_ref[...], wq_ref[:, group * width : (group + 1) * width]).astype(BF)
+    offset = core_ref.shape[0] - (groups - group) * chip_ref.shape[0]
     pad_ref[HALF : HALF + rows, :] = near_ref[...]
     for c in range(pairs):
-        at = (group * pairs + c) * HALF
+        at = c * HALF
         core = core_ref[offset + at : offset + at + HALF, :]
         chip = chip_ref[at : at + HALF, :]
         lanes = slice(2 * c * LANES, 2 * (c + 1) * LANES)
@@ -279,25 +313,24 @@
     pass_turn(ids_ref, turn_ref)
 
 
-def near(pairs, group, ids, normed, core, chip, wq, near_pairs):
-    rows = normed.shape[0]
+def near(pairs, group, groups, ids, source, wq, core, chips, near_pairs):
+    rows = near_pairs.shape[0]
     width = pairs * LANES
+    q = jax.ShapeDtypeStruct((rows, width), BF)
+    count = groups if group == 0 else 1
+    args = [source, wq] if group == 0 else [source]
+    others = chips[1:] if group == 0 else []
     return pl.pallas_call(
-        functools.partial(near_kernel, pairs, group),
-        in_specs=[smem()] + [vmem()] * 5,
-        out_specs=[vmem()] * 3 + [smem()],
-        out_shape=[
-            jax.ShapeDtypeStruct(normed.shape, BF),
-            jax.ShapeDtypeStruct((rows, width), BF),
-            jax.ShapeDtypeStruct((rows, 2 * width), F32),
-            TURN,
-        ],
-        input_output_aliases={1: 0},
+        functools.partial(near_kernel, pairs, group, groups),
+        in_specs=[smem()] + [vmem()] * (len(args) + 3) + [pl.BlockSpec(memory_space=pl.ANY)] * len(others),
+        out_specs=[vmem()] * (count + 1) + [smem()],
+        out_shape=[q] * count + [jax.ShapeDtypeStruct((rows, 2 * width), F32), TURN],
+        input_output_aliases={} if group == 0 else {1: 0},
         scratch_shapes=[pltpu.VMEM((rows + SEG, 2 * width), BF)],
         compiler_params=pltpu.CompilerParams(vmem_limit_bytes=VMEM_LIMIT),
         cost_estimate=COST,
         name="near",
-    )(ids, normed, core, chip, wq, near_pairs)
+    )(ids, *args, core, chips[group], near_pairs, *others)
 
 
 def far_kernel(pairs, group, block, spread, *refs):
@@ -380,24 +413,36 @@
     ids_ref, refs = refs[0], refs[1:]
     tokens, refs = [refs[j * pairs : (j + 1) * pairs] for j in range(count)], refs[count * pairs :]
     pooled, refs = refs[:spans], refs[spans:]
+    if spans:
+        *refs, stage_ref, sem = refs
     *refs, turn_ref = refs
     turn_ref[0] = ids_ref[0]
     outs = refs[-2:] if spans else refs[-1:]
     weight_ref, *acc = refs[: -len(outs)]
     rows, width = tokens[0][0].shape[0], pairs * LANES
+    tile = min(256, rows)
 
     def weight(j, size):
         return weight_ref[pl.ds(pl.multiple_of(ids_ref[j] * size, size), size), :]
 
-    for start in range(0, rows, 256):
-        at = slice(start, start + 256)
+    made = []
+    for start in range(0, rows, tile):
+        at = slice(start, start + tile)
         total = acc[0][at, :] if acc else None
         for j in range(count):
             term = dot(jnp.concatenate([ref[at, :] for ref in tokens[j]], axis=1), weight(j, width))
             total = term if total is None else total + term
-        outs[0][at, :] = total.astype(outs[0].dtype)
+        if not spans:
+            outs[0][at, :] = total.astype(outs[0].dtype)
+            continue
+        stage_ref[at, :] = total.astype(outs[0].dtype)
+        here = pl.ds(start, tile)
+        made.append(pltpu.make_async_copy(stage_ref.at[here, :], outs[0].at[here, :], sem.at[start // tile]))
+        made[-1].start()
     if spans:
         outs[1][...] = sum(dot(ref[...], weight(count + k, ref.shape[1])) for k, ref in enumerate(pooled))
+    for copy in made:
+        copy.wait()
 
 
 def out_part(parts, index, weight, acc, dtype, pooled=()):
@@ -411,8 +456,9 @@
     return pl.pallas_call(
         functools.partial(out_kernel, count, pairs, len(pooled)),
         in_specs=[smem()] + [vmem()] * (count * pairs + len(pooled) + 1 + len(extra)),
-        out_specs=[vmem()] * len(shapes) + [smem()],
+        out_specs=[pl.BlockSpec(memory_space=pltpu.HBM) if pooled else vmem()] + [vmem()] * (len(shapes) - 1) + [smem()],
         out_shape=shapes + [jax.ShapeDtypeStruct((1,), jnp.int32)],
+        scratch_shapes=[pltpu.VMEM((rows, columns), dtype), pltpu.SemaphoreType.DMA((pl.cdiv(rows, 256),))] if pooled else [],
         compiler_params=pltpu.CompilerParams(vmem_limit_bytes=VMEM_LIMIT),
         cost_estimate=COST,
         name="out",
@@ -475,22 +521,19 @@
     return lax.ppermute(values, "head", [(i, (i + step) % count) for i in range(count)])
 
 
-def add(a, b):
-    return (a.astype(F32) + b.astype(F32)).astype(BF)
-
-
 def add_kernel(a_ref, b_ref, out_ref):
-    out_ref[...] = (a_ref[...].astype(F32) + b_ref[...].astype(F32)).astype(BF)
-
-
-def add_call(a, b):
+    count = a_ref.shape[0]
+    out_ref[...] = (a_ref[...].astype(F32) + b_ref[:count, :].astype(F32)).astype(BF)
+
+
+def add_call(a, b, cost=COST):
     return pl.pallas_call(
         add_kernel,
         in_specs=[vmem()] * 2,
         out_specs=vmem(),
         out_shape=jax.ShapeDtypeStruct(a.shape, BF),
         compiler_params=pltpu.CompilerParams(vmem_limit_bytes=VMEM_LIMIT),
-        cost_estimate=COST,
+        cost_estimate=cost,
         name="add",
     )(a, b)
 
@@ -536,23 +579,25 @@
 
     fronts, mine, normed = [], [], book_tokens
     turn = ids
+    fetched = []
     for g in range(groups):
         last = g == groups - 1
-        normed, *outs, turn = front(g == 0, last, g, pairs, turn, normed, gain, key_weight, value_weight, proj_weight,
-                                    dual_gains, [f[3] for f in fronts])
+        normed, *outs = front(g == 0, last, g, pairs, turn, normed, gain, key_weight, value_weight, proj_weight,
+                              dual_gains, [f[3] for f in fronts], fetched)
+        edges = outs[3 : 4 + g if last else 4]
+        outs, turn, fetched = outs[:4], outs[3 + len(edges)], outs[4 + len(edges) :]
         fronts.append(outs)
-        send, edge = outs[2], outs[3]
+        send = outs[2]
         if last:
             for f in range(g):
                 for step in steps[:-1]:
                     got, turn = tie((swap(mine[f], "seq", step), turn))
-                    mine[f] = add(mine[f], got)
+                    mine[f] = add_call(mine[f], got, LONG)
                 mine[f], turn = tie((mine[f], turn))
         core = swap(send, "rep", 1)
         if last:
-            chip = lax.ppermute(edge, both, chips)
-        got, turn = tie((core[: outs[1].shape[0]], turn))
-        mine.append(add(outs[1], got))
+            chip = [lax.ppermute(edge, both, chips) for edge in edges]
+        mine.append(add_call(outs[1], core))
         mine[g], turn = tie((mine[g], turn))
 
     if groups == 1:
@@ -560,9 +605,12 @@
             mine[0] = add_call(mine[0], swap(mine[0], "seq", step))
 
     spread = lax.axis_size("seq")
-    outs, before, arrived, others, other_index = [], (), [], [], []
+    outs, before, arrived, others, other_index, queries = [], (), [], [], [], []
     for g in range(groups):
-        normed, q, near_sums, turn = near(pairs, g, turn, normed, core, chip, query_weight, fronts[g][0])
+        source = queries[g] if g else normed
+        *made, near_sums, turn = near(pairs, g, groups, turn, source, query_weight, core, chip, fronts[g][0])
+        queries = queries if g else made
+        q = made[0]
         got, turn = tie((swap(mine[g], "seq", steps[-1]), turn))
         total = add_call(mine[g], got)
         other = swap(total, "rep", 1)

time: 67.3 us -> 67.9 us (level)
  starting transfers between devices: 22.3 us -> 26.3 us
  Pallas kernels: 33.8 us -> 30.5 us
    ppermute x9, starting transfers between devices: 11.8 us -> 14.9 us  [swap(): return lax.ppermute(values, axis, [(i, i ^ step) for i in range(count)])]
    pallas_call x2, Pallas kernels: 8.27 us -> 5.69 us  [near(): pl.pallas_call(functools.partial(near_kernel, pairs, group, groups), in_s...]
    ppermute x9, waiting for transfers between devices: 4.07 us -> 2.21 us  [swap(): return lax.ppermute(values, axis, [(i, i ^ step) for i in range(count)])]
    ppermute x5, waiting for transfers between devices: 5.02 us -> 6.85 us  [across_heads(): lax.ppermute(values, 'head', [(i, (i + step) % count) for i in range(coun...]
    pallas_call x2, Pallas kernels: 15.2 us -> 14 us  [front(): pl.pallas_call(functools.partial(front_kernel, first, last, group, pairs,...]
    ppermute x1 -> x2, starting transfers between devices: 0.85 us -> 1.5 us  [per_device(): chip = [lax.ppermute(edge, both, chips) for edge in edges]]
  transfers between devices with their start and end apart: 18 -> 19, of which waited for: 5 -> 4; matrix products, arithmetic and copies ran while one was open for 0% -> 0% of each run, Pallas kernels for 34% -> 29%
where the time goes in v6:
time: 67.9 us; the launch traced here: 67.8 us
  Pallas kernels  30.5 us (45%)
  starting transfers between devices  26.3 us (39%)
  waiting for transfers between devices  9.07 us (13%)
  between operations  1.64 us (2%)
    ppermute x9, starting transfers between devices, swap(): return lax.ppermute(values, axis, [(i, i ^ step) for i in range(count)])  14.9 us
    pallas_call x2, Pallas kernels, front(): pl.pallas_call(functools.partial(front_kernel, first, last, group, pairs,...  14 us
    ppermute x5, waiting for transfers between devices, across_heads(): lax.ppermute(values, 'head', [(i, (i + step) % count) for i in range(coun...  6.85 us
    pallas_call x2, Pallas kernels, far(): pl.pallas_call(functools.partial(far_kernel, pairs, group, 256, spread),...  6.05 us
    ppermute x5, starting transfers between devices, across_heads(): lax.ppermute(values, 'head', [(i, (i + step) % count) for i in range(coun...  5.73 us
    pallas_call x2, Pallas kernels, near(): pl.pallas_call(functools.partial(near_kernel, pairs, group, groups), in_s...  5.69 us
    ppermute x3, starting transfers between devices, per_device(): lax.ppermute(piece, 'seq', [(i, (i + k + 1) % spread) for i in range(spre...  4.19 us
    pallas_call x2, Pallas kernels, out_part(): pl.pallas_call(functools.partial(out_kernel, count, pairs, len(pooled)),...  3.93 us
  transfers between devices with their start and end apart: 19, of which 4 were waited for; matrix products, arithmetic and copies ran while one was open for 0% of the time, Pallas kernels for 29%

profile of v6, /device:TPU:0, one launch (start us, length us, event | category | flops | bytes accessed | tf_op | source)
XLA Modules:
  0.0 67.8 jit_solution(9299083716511239755)
XLA Ops:
  0.6 0.1 pad_add_fusion.1.refs_0_
  0.7 8.6 %front.2 = (bf16[1024,1024]{1,0:T(8,128)(2,1)S(1)}, bf16[1024,512]{1,0:T(8,128)(2,1)S(1)}, bf16[256,256]{1,0:T(8,128)(2,1)S(1)}, bf16[256,256]{1,0:T(8,128)(2,1)...) custom-call(s32[4]{0:T(128)S(1)} %pad_add_fusion.1.refs_0_, ...), custom_call_target="tpu_custom_call" | custom-call | flops 3221225472 | bytes 4194304 | tf_op jit(solution)/shard_map/front/pallas_call | solution.py:233
  9.4 0.5 collective-permute-start
  9.9 1.0 %collective-permute-done.b_ref = bf16[256,256]{1,0:T(8,128)(2,1)S(1)} collective-permute-done((bf16[256,256]{1,0:T(8,128)(2,1)S(1)}, bf16[256,256]{1,0:T(8,128)(2,1)S(1)}, u32[]{:S(2)}, u32[]{:S(2)}) %collective-permute-start) | collective-permute-done | bytes 131104 | tf_op jit(solution)/shard_map/ppermute | solution.py:516
  10.9 3.0 %collective-permute-start.2 = (bf16[256,256]{1,0:T(8,128)(2,1)S(1)}, bf16[256,256]{1,0:T(8,128)(2,1)S(1)}, u32[]{:S(2)}, u32[]{:S(2)}) collective-permute-start(bf16[256,256]{1,0:T(8,128)(2,1)S(1)} %add.49.a_ref), channel_id=1, source_target_pairs={{0,4},{4,0},{8,12},{12,8},{1,5},{5,1},{9,13},{13,9},{2,6},{6,2},{1... | collective-permute-start | bytes 393224 | tf_op jit(solution)/shard_map/ppermute | solution.py:516
  13.9 5.4 %front.3 = (bf16[1024,1024]{1,0:T(8,128)(2,1)S(1)}, bf16[1024,512]{1,0:T(8,128)(2,1)S(1)}, bf16[256,256]{1,0:T(8,128)(2,1)S(1)}, bf16[512,256]{1,0:T(8,128)(2,1)...) custom-call(s32[4]{0:T(128)S(1)} %get-tuple-element.60.refs_0_, ...), custom_call_target="tpu_custom_call", output_to_operand_aliasing={{0}: (1, {})} | custom-call | flops 3221225472 | bytes 4194304 | tf_op jit(solution)/shard_map/front/pallas_call | solution.py:233
  19.3 0.1 collective-permute-start.1
  19.4 0.0 collective-permute-done.2.b_ref
  19.4 0.0 copy-start.1
  19.5 2.7 %collective-permute-start.4 = (bf16[256,256]{1,0:T(8,128)(2,1)S(1)}, bf16[256,256]{1,0:T(8,128)(2,1)S(1)}, u32[]{:S(2)}, u32[]{:S(2)}) collective-permute-start(bf16[256,256]{1,0:T(8,128)(2,1)S(1)} %add.51.a_ref), channel_id=1, source_target_pairs={{0,8},{4,12},{8,0},{12,4},{1,9},{5,13},{9,1},{13,5},{2,10},{6,14},... | collective-permute-start | bytes 393224 | tf_op jit(solution)/shard_map/ppermute | solution.py:516
  22.1 0.7 collective-permute-start.5
  22.8 0.8 %collective-permute-start.6 = (bf16[128,256]{1,0:T(8,128)(2,1)S(1)}, bf16[128,256]{1,0:T(8,128)(2,1)S(1)}, u32[]{:S(2)}, u32[]{:S(2)}) collective-permute-start(bf16[128,256]{1,0:T(8,128)(2,1)S(1)} %get-tuple-element.78), channel_id=1, source_target_pairs={{1,4},{5,8},{9,12},{4,1},{8,5},{12,9},{3,6},{7,10},{11,14},{6,3},{... | collective-permute-start | bytes 196616 | tf_op jit(solution)/shard_map/ppermute | solution.py:599
  23.6 0.0 collective-permute-done.1.b_ref.refs_2_.refs_1_
  23.7 4.7 %collective-permute-start.3 = (bf16[256,256]{1,0:T(8,128)(2,1)S(1)}, bf16[256,256]{1,0:T(8,128)(2,1)S(1)}, u32[]{:S(2)}, u32[]{:S(2)}) collective-permute-start(bf16[256,256]{1,0:T(8,128)(2,1)S(1)} %add.50.a_ref), channel_id=1, source_target_pairs={{0,4},{4,0},{8,12},{12,8},{1,5},{5,1},{9,13},{13,9},{2,6},{6,2},{1... | collective-permute-start | bytes 393224 | tf_op jit(solution)/shard_map/ppermute | solution.py:516
  28.4 0.0 collective-permute-done.5.refs_3_
  28.4 0.0 collective-permute-done.6.refs_5_.refs_2_
  28.4 0.0 copy-start.3
  28.5 3.5 %near.2 = (bf16[1024,256]{1,0:T(8,128)(2,1)S(1)}, bf16[1024,256]{1,0:T(8,128)(2,1)S(1)}, f32[1024,512]{1,0:T(8,128)S(1)}, s32[4]{0:T(128)S(1)}) custom-call(s32[4]{0:T(128)S(1)} %get-tuple-element.74.ids_ref, bf16[1024,1024]{1,0:T(8,128)(2,1)S(1)} %get-tuple-element.75.refs_0_, bf16[1024,512]{1,0:T(8,128)(2,1)S(1)} %copy-done.1, ...), custom_call_target="tpu_custom_call" | custom-call | flops 1048576 | bytes 1024 | tf_op jit(solution)/shard_map/near/pallas_call | solution.py:323
  32.0 1.8 %collective-permute-start.8 = (bf16[256,256]{1,0:T(8,128)(2,1)S(1)}, bf16[256,256]{1,0:T(8,128)(2,1)S(1)}, u32[]{:S(2)}, u32[]{:S(2)}) collective-permute-start(bf16[256,256]{1,0:T(8,128)(2,1)S(1)} %add.53.refs_3_), channel_id=1, source_target_pairs={{0,1},{1,0},{2,3},{3,2},{4,5},{5,4},{6,7},{7,6},{8,9},{9,8},{10,11... | collective-permute-start | bytes 393224 | tf_op jit(solution)/shard_map/ppermute | solution.py:516
  33.8 0.0 collective-permute-done.3.b_ref
  33.8 2.0 %collective-permute-start.7 = (bf16[256,256]{1,0:T(8,128)(2,1)S(1)}, bf16[256,256]{1,0:T(8,128)(2,1)S(1)}, u32[]{:S(2)}, u32[]{:S(2)}) collective-permute-start(bf16[256,256]{1,0:T(8,128)(2,1)S(1)} %add.52.a_ref), channel_id=1, source_target_pairs={{0,8},{4,12},{8,0},{12,4},{1,9},{5,13},{9,1},{13,5},{2,10},{6,14},... | collective-permute-start | bytes 393224 | tf_op jit(solution)/shard_map/ppermute | solution.py:516
  35.8 0.0 collective-permute-done.8.refs_4_
  35.8 3.1 %far.2 = (bf16[1024,128]{1,0:T(8,128)(2,1)S(1)}, bf16[1024,128]{1,0:T(8,128)(2,1)S(1)}, f32[32,256]{1,0:T(8,128)S(1)}, bf16[32,256]{1,0:T(8,128)(2,1)S(1)}, s32[4]{0:T(128)S(1)}) custom-call(s32[4]{0:T(128)S(1)} %get-tuple-element.84.refs_0_, bf16[1024,256]{1,0:T(8,128)(2,1)S(1)} %get-tuple-element.85.refs_1_, f32[1024,512]{1,0:T(8,128)S(1)} %get-tuple-element.86.refs_2_, ...), custom_call_target="tpu_custom_call" | custom-call | flops 1048576 | bytes 1024 | tf_op jit(solution)/shard_map/far/pallas_call | solution.py:396
  38.9 1.5 %collective-permute-start.10 = (bf16[1024,128]{1,0:T(8,128)(2,1)S(1)}, bf16[1024,128]{1,0:T(8,128)(2,1)S(1)}, u32[]{:S(2)}, u32[]{:S(2)}) collective-permute-start(bf16[1024,128]{1,0:T(8,128)(2,1)S(1)} %get-tuple-element.98.refs_1_), channel_id=1, source_target_pairs={{0,2},{2,0},{1,3},{3,1},{4,6},{6,4},{5,7},{7,5},{8,10},{10,8},{9,1... | collective-permute-start | bytes 786440 | tf_op jit(solution)/shard_map/ppermute | solution.py:521
  40.4 0.5 collective-permute-start.13
  41.0 2.2 %near.3 = (bf16[1024,256]{1,0:T(8,128)(2,1)S(1)}, f32[1024,512]{1,0:T(8,128)S(1)}, s32[4]{0:T(128)S(1)}) custom-call(s32[4]{0:T(128)S(1)} %get-tuple-element.88.ids_ref, bf16[1024,256]{1,0:T(8,128)(2,1)S(1)} %get-tuple-element.89.refs_0_, bf16[512,256]{1,0:T(8,128)(2,1)S(1)} %collective-permute-done.1.b_ref.refs_2_.refs_1_, ...), custom_call_target="tpu_custom_call", output_to_operand_aliasing={{0}: (1, {})} | custom-call | flops 1048576 | bytes 1024 | tf_op jit(solution)/shard_map/near/pallas_call | solution.py:323
  43.2 0.0 copy-start
  43.2 0.0 collective-permute-done.7.b_ref
  43.3 0.1 collective-permute-start.9
  43.4 4.7 %collective-permute-done.10.refs_9_.refs_5_ = bf16[1024,128]{1,0:T(8,128)(2,1)S(1)} collective-permute-done((bf16[1024,128]{1,0:T(8,128)(2,1)S(1)}, bf16[1024,128]{1,0:T(8,128)(2,1)S(1)}, u32[]{:S(2)}, u32[]{:S(2)}) %collective-permute-start.10) | collective-permute-done | bytes 262176 | tf_op jit(solution)/shard_map/ppermute | solution.py:521
  48.1 0.0 collective-permute-done.9.refs_4_
  48.1 3.0 %far.3 = (bf16[1024,128]{1,0:T(8,128)(2,1)S(1)}, bf16[1024,128]{1,0:T(8,128)(2,1)S(1)}, f32[32,512]{1,0:T(8,128)S(1)}, bf16[32,512]{1,0:T(8,128)(2,1)S(1)}, s32[4]{0:T(128)}) custom-call(s32[4]{0:T(128)S(1)} %get-tuple-element.92.refs_0_, bf16[1024,256]{1,0:T(8,128)(2,1)S(1)} %get-tuple-element.93.refs_1_, f32[1024,512]{1,0:T(8,128)S(1)} %get-tuple-element.94.refs_2_, ...), custom_call_target="tpu_custom_call" | custom-call | flops 1048576 | bytes 1024 | tf_op jit(solution)/shard_map/far/pallas_call | solution.py:396
  51.1 1.5 %collective-permute-start.11 = (bf16[1024,128]{1,0:T(8,128)(2,1)S(1)}, bf16[1024,128]{1,0:T(8,128)(2,1)S(1)}, u32[]{:S(2)}, u32[]{:S(2)}) collective-permute-start(bf16[1024,128]{1,0:T(8,128)(2,1)S(1)} %get-tuple-element.99.refs_3_), channel_id=1, source_target_pairs={{0,2},{2,0},{1,3},{3,1},{4,6},{6,4},{5,7},{7,5},{8,10},{10,8},{9,1... | collective-permute-start | bytes 786440 | tf_op jit(solution)/shard_map/ppermute | solution.py:521
  52.7 0.5 collective-permute-start.12
  53.2 1.2 %collective-permute-done.14.got_ref = bf16[32,512]{1,0:T(8,128)(2,1)S(1)} collective-permute-done((bf16[32,512]{1,0:T(8,128)(2,1)S(1)}, bf16[32,512]{1,0:T(8,128)(2,1)S(1)}, u32[]{:S(2)}, u32[]{:S(2)}) %collective-permute-start.14) | collective-permute-done | bytes 32800 | tf_op jit(solution)/shard_map/ppermute | solution.py:516
  54.4 1.3 %collective-permute-start.15 = (bf16[8,512]{1,0:T(8,128)(2,1)S(1)}, bf16[8,512]{1,0:T(8,128)(2,1)S(1)}, u32[]{:S(2)}, u32[]{:S(2)}) collective-permute-start(bf16[8,512]{1,0:T(8,128)(2,1)S(1)} %get-tuple-element.106), channel_id=1, source_target_pairs={{0,4},{4,8},{8,12},{12,0},{1,5},{5,9},{9,13},{13,1},{2,6},{6,10},{... | collective-permute-start | bytes 24584 | tf_op jit(solution)/shard_map/ppermute | solution.py:637
  55.7 1.2 %collective-permute-start.16 = (bf16[8,512]{1,0:T(8,128)(2,1)S(1)}, bf16[8,512]{1,0:T(8,128)(2,1)S(1)}, u32[]{:S(2)}, u32[]{:S(2)}) collective-permute-start(bf16[8,512]{1,0:T(8,128)(2,1)S(1)} %get-tuple-element.107), channel_id=1, source_target_pairs={{0,8},{4,12},{8,0},{12,4},{1,9},{5,13},{9,1},{13,5},{2,10},{6,14},... | collective-permute-start | bytes 24584 | tf_op jit(solution)/shard_map/ppermute | solution.py:637
  56.9 1.7 %collective-permute-start.17 = (bf16[8,512]{1,0:T(8,128)(2,1)S(1)}, bf16[8,512]{1,0:T(8,128)(2,1)S(1)}, u32[]{:S(2)}, u32[]{:S(2)}) collective-permute-start(bf16[8,512]{1,0:T(8,128)(2,1)S(1)} %get-tuple-element.108), channel_id=1, source_target_pairs={{0,12},{4,0},{8,4},{12,8},{1,13},{5,1},{9,5},{13,9},{2,14},{6,2},{... | collective-permute-start | bytes 24584 | tf_op jit(solution)/shard_map/ppermute | solution.py:637
  58.6 0.1 pad_add_fusion.2.refs_0_
  58.7 1.5 %out.2 = (f32[1024,512]{1,0:T(8,128)S(1)}, s32[1]{0:T(128)}) custom-call(s32[3]{0:T(128)S(1)} %pad_add_fusion.2.refs_0_, bf16[1024,128]{1,0:T(8,128)(2,1)S(1)} %get-tuple-element.98.refs_1_, bf16[1024,128]{1,0:T(8,128)(2,1)S(1)} %get-tuple-element.101.refs_2_, bf16[1024,128]{1,0:T(8,128)(2,1)S(1)} %get-tuple-element.99.refs_3_, ...), custom_call_target="tpu_custom_call" | custom-call | flops 1048576 | bytes 1024 | tf_op jit(solution)/shard_map/out/pallas_call | solution.py:456
  60.9 0.0 collective-permute-done.15.refs_0_
  60.9 0.0 collective-permute-done.16.refs_1_
  60.9 0.6 pool_own.1.refs_3_
  61.5 1.5 %collective-permute-start.18 = (bf16[8,512]{1,0:T(8,128)(2,1)S(1)}, bf16[8,512]{1,0:T(8,128)(2,1)S(1)}, u32[]{:S(2)}, u32[]{:S(2)}) collective-permute-start(bf16[8,512]{1,0:T(8,128)(2,1)S(1)} %pool_own.1.refs_3_), channel_id=1, source_target_pairs={{0,2},{2,0},{1,3},{3,1},{4,6},{6,4},{5,7},{7,5},{8,10},{10,8},{9,1... | collective-permute-start | bytes 24584 | tf_op jit(solution)/shard_map/ppermute | solution.py:521
  63.0 0.1 pad_add_fusion.refs_0_
  63.1 2.1 %collective-permute-done.18.refs_4_ = bf16[8,512]{1,0:T(8,128)(2,1)S(1)} collective-permute-done((bf16[8,512]{1,0:T(8,128)(2,1)S(1)}, bf16[8,512]{1,0:T(8,128)(2,1)S(1)}, u32[]{:S(2)}, u32[]{:S(2)}) %collective-permute-start.18) | collective-permute-done | bytes 8224 | tf_op jit(solution)/shard_map/ppermute | solution.py:521
  65.2 0.0 collective-permute-done.12.refs_2_
  65.2 2.4 %out.3 = (bf16[1024,512]{1,0:T(8,128)(2,1)}, f32[8,512]{1,0:T(8,128)}, s32[1]{0:T(128)}) custom-call(s32[3]{0:T(128)S(1)} %pad_add_fusion.refs_0_, bf16[1024,128]{1,0:T(8,128)(2,1)S(1)} %collective-permute-done.11.refs_1_, bf16[1024,128]{1,0:T(8,128)(2,1)S(1)} %collective-permute-done.12.refs_2_, bf16[8,512]{1,0:T(8,128)(2,1)S(1)} %pool_own.1.refs_3_, ...), custom_call_target="tpu_custom_call" | custom-call | flops 1048576 | bytes 1024 | tf_op jit(solution)/shard_map/out/pallas_call | solution.py:456
  (17 shorter events, 0.2 us)
Async XLA Ops:
  0.7 13.2 %copy-start.2 = (f32[4,512]{1,0:T(4,128)S(1)}, f32[4,512]{1,0:T(4,128)}, u32[]{:S(2)}) copy-start(f32[4,512]{1,0:T(4,128)} %refs_5_.6) | copy-start | bytes 24580
  9.4 1.5 %collective-permute-start = (bf16[256,256]{1,0:T(8,128)(2,1)S(1)}, bf16[256,256]{1,0:T(8,128)(2,1)S(1)}, u32[]{:S(2)}, u32[]{:S(2)}) collective-permute-start(bf16[256,256]{1,0:T(8,128)(2,1)S(1)} %get-tuple-element.58), channel_id=1, source_target_pairs={{0,1},{1,0},{2,3},{3,2},{4,5},{5,4},{6,7},{7,6},{8,9},{9,8},{10,11... | collective-permute-start | bytes 393224 | tf_op jit(solution)/shard_map/ppermute | solution.py:516
  10.9 8.5 %collective-permute-start.2 = (bf16[256,256]{1,0:T(8,128)(2,1)S(1)}, bf16[256,256]{1,0:T(8,128)(2,1)S(1)}, u32[]{:S(2)}, u32[]{:S(2)}) collective-permute-start(bf16[256,256]{1,0:T(8,128)(2,1)S(1)} %add.49.a_ref), channel_id=1, source_target_pairs={{0,4},{4,0},{8,12},{12,8},{1,5},{5,1},{9,13},{13,9},{2,6},{6,2},{1... | collective-permute-start | bytes 393224 | tf_op jit(solution)/shard_map/ppermute | solution.py:516
  19.3 4.3 %collective-permute-start.1 = (bf16[512,256]{1,0:T(8,128)(2,1)S(1)}, bf16[512,256]{1,0:T(8,128)(2,1)S(1)}, u32[]{:S(2)}, u32[]{:S(2)}) collective-permute-start(bf16[512,256]{1,0:T(8,128)(2,1)S(1)} %get-tuple-element.66), channel_id=1, source_target_pairs={{0,1},{1,0},{2,3},{3,2},{4,5},{5,4},{6,7},{7,6},{8,9},{9,8},{10,11... | collective-permute-start | bytes 786440 | tf_op jit(solution)/shard_map/ppermute | solution.py:516
  19.4 9.0 %copy-start.1 = (bf16[1024,512]{1,0:T(8,128)(2,1)S(1)}, bf16[1024,512]{1,0:T(8,128)(2,1)}, u32[]{:S(2)}) copy-start(bf16[1024,512]{1,0:T(8,128)(2,1)} %refs_1_.3) | copy-start | bytes 3145732
  19.5 12.5 %collective-permute-start.4 = (bf16[256,256]{1,0:T(8,128)(2,1)S(1)}, bf16[256,256]{1,0:T(8,128)(2,1)S(1)}, u32[]{:S(2)}, u32[]{:S(2)}) collective-permute-start(bf16[256,256]{1,0:T(8,128)(2,1)S(1)} %add.51.a_ref), channel_id=1, source_target_pairs={{0,8},{4,12},{8,0},{12,4},{1,9},{5,13},{9,1},{13,5},{2,10},{6,14},... | collective-permute-start | bytes 393224 | tf_op jit(solution)/shard_map/ppermute | solution.py:516
  22.1 6.3 %collective-permute-start.5 = (bf16[128,256]{1,0:T(8,128)(2,1)S(1)}, bf16[128,256]{1,0:T(8,128)(2,1)S(1)}, u32[]{:S(2)}, u32[]{:S(2)}) collective-permute-start(bf16[128,256]{1,0:T(8,128)(2,1)S(1)} %get-tuple-element.76), channel_id=1, source_target_pairs={{1,4},{5,8},{9,12},{4,1},{8,5},{12,9},{3,6},{7,10},{11,14},{6,3},{... | collective-permute-start | bytes 196616 | tf_op jit(solution)/shard_map/ppermute | solution.py:599
  22.8 5.7 %collective-permute-start.6 = (bf16[128,256]{1,0:T(8,128)(2,1)S(1)}, bf16[128,256]{1,0:T(8,128)(2,1)S(1)}, u32[]{:S(2)}, u32[]{:S(2)}) collective-permute-start(bf16[128,256]{1,0:T(8,128)(2,1)S(1)} %get-tuple-element.78), channel_id=1, source_target_pairs={{1,4},{5,8},{9,12},{4,1},{8,5},{12,9},{3,6},{7,10},{11,14},{6,3},{... | collective-permute-start | bytes 196616 | tf_op jit(solution)/shard_map/ppermute | solution.py:599
  23.7 10.1 %collective-permute-start.3 = (bf16[256,256]{1,0:T(8,128)(2,1)S(1)}, bf16[256,256]{1,0:T(8,128)(2,1)S(1)}, u32[]{:S(2)}, u32[]{:S(2)}) collective-permute-start(bf16[256,256]{1,0:T(8,128)(2,1)S(1)} %add.50.a_ref), channel_id=1, source_target_pairs={{0,4},{4,0},{8,12},{12,8},{1,5},{5,1},{9,13},{13,9},{2,6},{6,2},{1... | collective-permute-start | bytes 393224 | tf_op jit(solution)/shard_map/ppermute | solution.py:516
  28.4 7.4 %copy-start.3 = (s32[64,2]{0,1:T(2,128)S(1)}, s32[64,2]{0,1:T(2,128)}, u32[]{:S(2)}) copy-start(s32[64,2]{0,1:T(2,128)} %param.17) | copy-start | bytes 1540
  32.0 3.8 %collective-permute-start.8 = (bf16[256,256]{1,0:T(8,128)(2,1)S(1)}, bf16[256,256]{1,0:T(8,128)(2,1)S(1)}, u32[]{:S(2)}, u32[]{:S(2)}) collective-permute-start(bf16[256,256]{1,0:T(8,128)(2,1)S(1)} %add.53.refs_3_), channel_id=1, source_target_pairs={{0,1},{1,0},{2,3},{3,2},{4,5},{5,4},{6,7},{7,6},{8,9},{9,8},{10,11... | collective-permute-start | bytes 393224 | tf_op jit(solution)/shard_map/ppermute | solution.py:516
  33.8 9.4 %collective-permute-start.7 = (bf16[256,256]{1,0:T(8,128)(2,1)S(1)}, bf16[256,256]{1,0:T(8,128)(2,1)S(1)}, u32[]{:S(2)}, u32[]{:S(2)}) collective-permute-start(bf16[256,256]{1,0:T(8,128)(2,1)S(1)} %add.52.a_ref), channel_id=1, source_target_pairs={{0,8},{4,12},{8,0},{12,4},{1,9},{5,13},{9,1},{13,5},{2,10},{6,14},... | collective-permute-start | bytes 393224 | tf_op jit(solution)/shard_map/ppermute | solution.py:516
  38.9 9.2 %collective-permute-start.10 = (bf16[1024,128]{1,0:T(8,128)(2,1)S(1)}, bf16[1024,128]{1,0:T(8,128)(2,1)S(1)}, u32[]{:S(2)}, u32[]{:S(2)}) collective-permute-start(bf16[1024,128]{1,0:T(8,128)(2,1)S(1)} %get-tuple-element.98.refs_1_), channel_id=1, source_target_pairs={{0,2},{2,0},{1,3},{3,1},{4,6},{6,4},{5,7},{7,5},{8,10},{10,8},{9,1... | collective-permute-start | bytes 786440 | tf_op jit(solution)/shard_map/ppermute | solution.py:521
  40.4 16.5 %collective-permute-start.13 = (bf16[1024,128]{1,0:T(8,128)(2,1)S(1)}, bf16[1024,128]{1,0:T(8,128)(2,1)S(1)}, u32[]{:S(2)}, u32[]{:S(2)}) collective-permute-start(bf16[1024,128]{1,0:T(8,128)(2,1)S(1)} %get-tuple-element.101.refs_2_), channel_id=1, source_target_pairs={{0,2},{2,0},{1,3},{3,1},{4,6},{6,4},{5,7},{7,5},{8,10},{10,8},{9,1... | collective-permute-start | bytes 786440 | tf_op jit(solution)/shard_map/ppermute | solution.py:521
  43.2 15.5 %copy-start = (bf16[1024,512]{1,0:T(8,128)(2,1)S(1)}, bf16[1024,512]{1,0:T(8,128)(2,1)}, u32[]{:S(2)}) copy-start(bf16[1024,512]{1,0:T(8,128)(2,1)} %refs_5_.7) | copy-start | bytes 3145732
  43.3 4.8 %collective-permute-start.9 = (bf16[256,256]{1,0:T(8,128)(2,1)S(1)}, bf16[256,256]{1,0:T(8,128)(2,1)S(1)}, u32[]{:S(2)}, u32[]{:S(2)}) collective-permute-start(bf16[256,256]{1,0:T(8,128)(2,1)S(1)} %add.54.refs_3_), channel_id=1, source_target_pairs={{0,1},{1,0},{2,3},{3,2},{4,5},{5,4},{6,7},{7,6},{8,9},{9,8},{10,11... | collective-permute-start | bytes 393224 | tf_op jit(solution)/shard_map/ppermute | solution.py:516
  51.1 14.1 %collective-permute-start.11 = (bf16[1024,128]{1,0:T(8,128)(2,1)S(1)}, bf16[1024,128]{1,0:T(8,128)(2,1)S(1)}, u32[]{:S(2)}, u32[]{:S(2)}) collective-permute-start(bf16[1024,128]{1,0:T(8,128)(2,1)S(1)} %get-tuple-element.99.refs_3_), channel_id=1, source_target_pairs={{0,2},{2,0},{1,3},{3,1},{4,6},{6,4},{5,7},{7,5},{8,10},{10,8},{9,1... | collective-permute-start | bytes 786440 | tf_op jit(solution)/shard_map/ppermute | solution.py:521
  52.7 12.5 %collective-permute-start.12 = (bf16[1024,128]{1,0:T(8,128)(2,1)S(1)}, bf16[1024,128]{1,0:T(8,128)(2,1)S(1)}, u32[]{:S(2)}, u32[]{:S(2)}) collective-permute-start(bf16[1024,128]{1,0:T(8,128)(2,1)S(1)} %get-tuple-element.100.refs_4_), channel_id=1, source_target_pairs={{0,2},{2,0},{1,3},{3,1},{4,6},{6,4},{5,7},{7,5},{8,10},{10,8},{9,1... | collective-permute-start | bytes 786440 | tf_op jit(solution)/shard_map/ppermute | solution.py:521
  53.2 1.2 %collective-permute-start.14 = (bf16[32,512]{1,0:T(8,128)(2,1)S(1)}, bf16[32,512]{1,0:T(8,128)(2,1)S(1)}, u32[]{:S(2)}, u32[]{:S(2)}) collective-permute-start(bf16[32,512]{1,0:T(8,128)(2,1)S(1)} %get-tuple-element.104), channel_id=1, source_target_pairs={{0,1},{1,0},{2,3},{3,2},{4,5},{5,4},{6,7},{7,6},{8,9},{9,8},{10,11... | collective-permute-start | bytes 98312 | tf_op jit(solution)/shard_map/ppermute | solution.py:516
  54.4 6.4 %collective-permute-start.15 = (bf16[8,512]{1,0:T(8,128)(2,1)S(1)}, bf16[8,512]{1,0:T(8,128)(2,1)S(1)}, u32[]{:S(2)}, u32[]{:S(2)}) collective-permute-start(bf16[8,512]{1,0:T(8,128)(2,1)S(1)} %get-tuple-element.106), channel_id=1, source_target_pairs={{0,4},{4,8},{8,12},{12,0},{1,5},{5,9},{9,13},{13,1},{2,6},{6,10},{... | collective-permute-start | bytes 24584 | tf_op jit(solution)/shard_map/ppermute | solution.py:637
  55.7 5.1 %collective-permute-start.16 = (bf16[8,512]{1,0:T(8,128)(2,1)S(1)}, bf16[8,512]{1,0:T(8,128)(2,1)S(1)}, u32[]{:S(2)}, u32[]{:S(2)}) collective-permute-start(bf16[8,512]{1,0:T(8,128)(2,1)S(1)} %get-tuple-element.107), channel_id=1, source_target_pairs={{0,8},{4,12},{8,0},{12,4},{1,9},{5,13},{9,1},{13,5},{2,10},{6,14},... | collective-permute-start | bytes 24584 | tf_op jit(solution)/shard_map/ppermute | solution.py:637
  56.9 3.9 %collective-permute-start.17 = (bf16[8,512]{1,0:T(8,128)(2,1)S(1)}, bf16[8,512]{1,0:T(8,128)(2,1)S(1)}, u32[]{:S(2)}, u32[]{:S(2)}) collective-permute-start(bf16[8,512]{1,0:T(8,128)(2,1)S(1)} %get-tuple-element.108), channel_id=1, source_target_pairs={{0,12},{4,0},{8,4},{12,8},{1,13},{5,1},{9,5},{13,9},{2,14},{6,2},{... | collective-permute-start | bytes 24584 | tf_op jit(solution)/shard_map/ppermute | solution.py:637
  61.5 3.7 %collective-permute-start.18 = (bf16[8,512]{1,0:T(8,128)(2,1)S(1)}, bf16[8,512]{1,0:T(8,128)(2,1)S(1)}, u32[]{:S(2)}, u32[]{:S(2)}) collective-permute-start(bf16[8,512]{1,0:T(8,128)(2,1)S(1)} %pool_own.1.refs_3_), channel_id=1, source_target_pairs={{0,2},{2,0},{1,3},{3,1},{4,6},{6,4},{5,7},{7,5},{8,10},{10,8},{9,1... | collective-permute-start | bytes 24584 | tf_op jit(solution)/shard_map/ppermute | solution.py:521

commit v7 on v6

--- a/solution.py
+++ b/solution.py
@@ -91,10 +91,8 @@
             wk_hbm, wv_hbm, wp_hbm = refs[:3]
             refs = refs[3:]
     earlier = [refs.pop(0) for _ in range(group)] if last else []
-    normed_ref, near_ref, keep_ref, send_ref = refs[:4]
-    edge_refs = refs[4 : 5 + len(earlier)]
-    turn_ref = refs[5 + len(earlier)]
-    refs = refs[6 + len(earlier) :]
+    normed_ref, near_ref, keep_ref, send_ref, edge_ref, turn_ref = refs[:6]
+    refs = refs[6:]
     pass_turn(ids_ref, turn_ref)
     if not last:
         next_kv_ref, next_wp_ref = refs[:2]
@@ -177,12 +175,12 @@
         for i, ref in enumerate(earlier):
             before = jnp.where(mine, ref[edge:, :], ref[:edge, :])
             send_ref[half + i * edge : half + (i + 1) * edge, :] = before
-            edge_refs[i][...] = jnp.where(mine, ref[:edge, :], ref[edge:, :])
+            edge_ref[i * edge : (i + 1) * edge, :] = jnp.where(mine, ref[:edge, :], ref[edge:, :])
         send_ref[half + group * edge :, :] = jnp.where(mine, tail, head)
-        edge_refs[group][...] = jnp.where(mine, head, tail)
+        edge_ref[group * edge :, :] = jnp.where(mine, head, tail)
     else:
-        edge_refs[0][:edge, :] = head
-        edge_refs[0][edge:, :] = tail
+        edge_ref[:edge, :] = head
+        edge_ref[edge:, :] = tail
 
 
 def in_hbm(values):
@@ -200,7 +198,7 @@
         jax.ShapeDtypeStruct((rows, 2 * width), BF),
         jax.ShapeDtypeStruct((half, R), BF),
         jax.ShapeDtypeStruct((half + edge, R), BF),
-        *[jax.ShapeDtypeStruct(((1 if last else 2) * pairs * HALF, R), BF)] * (group + 1 if last else 1),
+        jax.ShapeDtypeStruct((edge if last else 2 * pairs * HALF, R), BF),
         TURN,
     ]
     if not last:
@@ -268,7 +266,7 @@
     width = pairs * LANES
     if group == 0:
         normed_ref, wq_ref, core_ref, chip_ref, near_ref = refs[:5]
-        q_refs, (out_ref, turn_ref, pad_ref) = refs[-3 - groups : -3], refs[-3:]
+        q_refs, (out_ref, turn_ref, pad_ref) = refs[5:-3], refs[-3:]
         q_ref, rows = q_refs[0], normed_ref.shape[0]
         for start in range(0, rows, 256):
             at = slice(start, start + 256)
@@ -284,10 +282,10 @@
     has_prev = jnp.where(ids_ref[1] != 0, 1.0, 0.0)
     has_next = jnp.where(ids_ref[2] != 0, 1.0, 0.0)
     segments = rows // SEG
-    offset = core_ref.shape[0] - (groups - group) * chip_ref.shape[0]
+    offset = core_ref.shape[0] - chip_ref.shape[0]
     pad_ref[HALF : HALF + rows, :] = near_ref[...]
     for c in range(pairs):
-        at = c * HALF
+        at = (group * pairs + c) * HALF
         core = core_ref[offset + at : offset + at + HALF, :]
         chip = chip_ref[at : at + HALF, :]
         lanes = slice(2 * c * LANES, 2 * (c + 1) * LANES)
@@ -313,16 +311,15 @@
     pass_turn(ids_ref, turn_ref)
 
 
-def near(pairs, group, groups, ids, source, wq, core, chips, near_pairs):
+def near(pairs, group, groups, ids, source, wq, core, chip, near_pairs):
     rows = near_pairs.shape[0]
     width = pairs * LANES
     q = jax.ShapeDtypeStruct((rows, width), BF)
     count = groups if group == 0 else 1
     args = [source, wq] if group == 0 else [source]
-    others = chips[1:] if group == 0 else []
     return pl.pallas_call(
         functools.partial(near_kernel, pairs, group, groups),
-        in_specs=[smem()] + [vmem()] * (len(args) + 3) + [pl.BlockSpec(memory_space=pl.ANY)] * len(others),
+        in_specs=[smem()] + [vmem()] * (len(args) + 3),
         out_specs=[vmem()] * (count + 1) + [smem()],
         out_shape=[q] * count + [jax.ShapeDtypeStruct((rows, 2 * width), F32), TURN],
         input_output_aliases={} if group == 0 else {1: 0},
@@ -330,14 +327,15 @@
         compiler_params=pltpu.CompilerParams(vmem_limit_bytes=VMEM_LIMIT),
         cost_estimate=COST,
         name="near",
-    )(ids, *args, core, chips[group], near_pairs, *others)
-
-
-def far_kernel(pairs, group, block, spread, *refs):
+    )(ids, *args, core, chip, near_pairs)
+
+
+def far_kernel(pairs, group, which, block, spread, *refs):
     (ids_ref, q_ref, near_ref, mine_ref, other_ref, gains_ref, bounds_ref), refs = refs[:7], refs[7:]
     keep_ref, send_ref, turn_ref = refs[-3:]
-    out_refs = refs[-3 - pairs : -3]
-    before = refs[:2] if group else ()
+    out_refs = refs[-3 - len(which) : -3]
+    done = (group * pairs + which[0]) * LANES
+    before = refs[:2] if done else ()
     pass_turn(ids_ref, turn_ref)
     rows = q_ref.shape[0]
     width = pairs * LANES
@@ -346,7 +344,7 @@
     bottom = jnp.where(is_first, other_ref[...], mine_ref[...])
     total = jnp.concatenate([top, bottom], axis=0)
     ones = jnp.ones((LANES, R), BF)
-    for p in range(pairs):
+    for out_ref, p in zip(out_refs, which):
         cols = slice(p * LANES, (p + 1) * LANES)
 
         base = group * width + p * LANES
@@ -371,7 +369,7 @@
             top, bottom = unstack(dot(weights, values, ((1,), (1,))))
             top = top + near_ref[start : start + block, 2 * p * LANES : (2 * p + 1) * LANES]
             bottom = bottom + near_ref[start : start + block, (2 * p + 1) * LANES : (2 * p + 2) * LANES]
-            out_refs[p][start : start + block, :] = (top / bottom).astype(BF)
+            out_ref[start : start + block, :] = (top / bottom).astype(BF)
     spans = bounds_ref.shape[1]
     position = ids_ref[3] + lax.broadcasted_iota(jnp.int32, (rows, spans), 0)
     member = (position >= bounds_ref[0:1, :]) & (position < bounds_ref[1:2, :])
@@ -380,25 +378,25 @@
     count = spans // (2 * spread)
     even = jnp.concatenate([sums[2 * i * count : (2 * i + 1) * count] for i in range(spread)], axis=0)
     odd = jnp.concatenate([sums[(2 * i + 1) * count : (2 * i + 2) * count] for i in range(spread)], axis=0)
-    lanes = slice(group * width, (group + 1) * width)
+    lanes = slice(done, done + len(which) * LANES)
     if before:
-        keep_ref[:, : group * width] = before[0][...]
-        send_ref[:, : group * width] = before[1][...]
+        keep_ref[:, :done] = before[0][...]
+        send_ref[:, :done] = before[1][...]
     keep_ref[:, lanes] = jnp.where(is_first, even, odd)
     send_ref[:, lanes] = jnp.where(is_first, odd, even).astype(BF)
 
 
-def far(pairs, group, spread, ids, q, near_sums, mine, other, gains, bounds, before, arrived):
+def far(pairs, group, which, spread, ids, q, near_sums, mine, other, gains, bounds, before, arrived):
     rows = q.shape[0]
     width = pairs * LANES
     spans = bounds.shape[1]
-    shape = (spans // 2, (group + 1) * width)
+    shape = (spans // 2, (group * pairs + which[-1] + 1) * LANES)
     return pl.pallas_call(
-        functools.partial(far_kernel, pairs, group, 256, spread),
+        functools.partial(far_kernel, pairs, group, which, 256, spread),
         in_specs=[smem()] + [vmem()] * (6 + len(before)) + [pl.BlockSpec(memory_space=pl.ANY)] * len(arrived),
-        out_specs=[vmem()] * (2 + pairs) + [smem()],
+        out_specs=[vmem()] * (2 + len(which)) + [smem()],
         out_shape=[
-            *[jax.ShapeDtypeStruct((rows, LANES), BF)] * pairs,
+            *[jax.ShapeDtypeStruct((rows, LANES), BF)] * len(which),
             jax.ShapeDtypeStruct(shape, F32),
             jax.ShapeDtypeStruct(shape, BF),
             TURN,
@@ -413,8 +411,6 @@
     ids_ref, refs = refs[0], refs[1:]
     tokens, refs = [refs[j * pairs : (j + 1) * pairs] for j in range(count)], refs[count * pairs :]
     pooled, refs = refs[:spans], refs[spans:]
-    if spans:
-        *refs, stage_ref, sem = refs
     *refs, turn_ref = refs
     turn_ref[0] = ids_ref[0]
     outs = refs[-2:] if spans else refs[-1:]
@@ -425,24 +421,15 @@
     def weight(j, size):
         return weight_ref[pl.ds(pl.multiple_of(ids_ref[j] * size, size), size), :]
 
-    made = []
     for start in range(0, rows, tile):
         at = slice(start, start + tile)
         total = acc[0][at, :] if acc else None
         for j in range(count):
             term = dot(jnp.concatenate([ref[at, :] for ref in tokens[j]], axis=1), weight(j, width))
             total = term if total is None else total + term
-        if not spans:
-            outs[0][at, :] = total.astype(outs[0].dtype)
-            continue
-        stage_ref[at, :] = total.astype(outs[0].dtype)
-        here = pl.ds(start, tile)
-        made.append(pltpu.make_async_copy(stage_ref.at[here, :], outs[0].at[here, :], sem.at[start // tile]))
-        made[-1].start()
+        outs[0][at, :] = total.astype(outs[0].dtype)
     if spans:
         outs[1][...] = sum(dot(ref[...], weight(count + k, ref.shape[1])) for k, ref in enumerate(pooled))
-    for copy in made:
-        copy.wait()
 
 
 def out_part(parts, index, weight, acc, dtype, pooled=()):
@@ -456,9 +443,8 @@
     return pl.pallas_call(
         functools.partial(out_kernel, count, pairs, len(pooled)),
         in_specs=[smem()] + [vmem()] * (count * pairs + len(pooled) + 1 + len(extra)),
-        out_specs=[pl.BlockSpec(memory_space=pltpu.HBM) if pooled else vmem()] + [vmem()] * (len(shapes) - 1) + [smem()],
+        out_specs=[vmem()] * len(shapes) + [smem()],
         out_shape=shapes + [jax.ShapeDtypeStruct((1,), jnp.int32)],
-        scratch_shapes=[pltpu.VMEM((rows, columns), dtype), pltpu.SemaphoreType.DMA((pl.cdiv(rows, 256),))] if pooled else [],
         compiler_params=pltpu.CompilerParams(vmem_limit_bytes=VMEM_LIMIT),
         cost_estimate=COST,
         name="out",
@@ -584,10 +570,9 @@
         last = g == groups - 1
         normed, *outs = front(g == 0, last, g, pairs, turn, normed, gain, key_weight, value_weight, proj_weight,
                               dual_gains, [f[3] for f in fronts], fetched)
-        edges = outs[3 : 4 + g if last else 4]
-        outs, turn, fetched = outs[:4], outs[3 + len(edges)], outs[4 + len(edges) :]
+        outs, turn, fetched = outs[:4], outs[4], outs[5:]
         fronts.append(outs)
-        send = outs[2]
+        send, edge = outs[2], outs[3]
         if last:
             for f in range(g):
                 for step in steps[:-1]:
@@ -596,7 +581,7 @@
                 mine[f], turn = tie((mine[f], turn))
         core = swap(send, "rep", 1)
         if last:
-            chip = [lax.ppermute(edge, both, chips) for edge in edges]
+            chip = lax.ppermute(edge, both, chips)
         mine.append(add_call(outs[1], core))
         mine[g], turn = tie((mine[g], turn))
 
@@ -619,8 +604,12 @@
                 got, turn = tie((swap(mine[-1], "seq", step), turn))
                 mine[-1] = add_call(mine[-1], got)
             mine[-1], turn = tie((mine[-1], turn))
-        *out, keep, send, turn = far(pairs, g, spread, turn, q, near_sums, total, other, dual_gains, bounds, before, arrived)
-        before = [keep, send]
+        out = []
+        for which in [[p] for p in range(pairs)] if g < groups - 1 else [list(range(pairs))]:
+            *made, keep, send, turn = far(pairs, g, which, spread, turn, q, near_sums, total, other, dual_gains, bounds,
+                                          before, arrived)
+            before = [keep, send]
+            out += made
         outs.append(out)
         moved = [[across_heads(piece, k) for piece in out] for k in range(1, head_devices)]
         arrived = [moved[0][0]] if g < groups - 1 and moved else []

time: 67.9 us -> 65.5 us (0.965)
  starting transfers between devices: 26.3 us -> 22.4 us
  Pallas kernels: 30.5 us -> 31.7 us
    ppermute x9, starting transfers between devices: 14.9 us -> 11.9 us  [swap(): return lax.ppermute(values, axis, [(i, i ^ step) for i in range(count)])]
    ppermute x9, waiting for transfers between devices: 2.21 us -> 4.74 us  [swap(): return lax.ppermute(values, axis, [(i, i ^ step) for i in range(count)])]
    ppermute x5, waiting for transfers between devices: 6.85 us -> 4.64 us  [across_heads(): lax.ppermute(values, 'head', [(i, (i + step) % count) for i in range(coun...]
    pallas_call x2 -> x3, Pallas kernels: 6.05 us -> 7.45 us  [far(): pl.pallas_call(functools.partial(far_kernel, pairs, group, which, 256, sp...]
    ppermute x2 -> x1, starting transfers between devices: 1.5 us -> 0.85 us  [per_device(): chip = lax.ppermute(edge, both, chips)]
  transfers between devices with their start and end apart: 19 -> 18, of which waited for: 4 -> 5; matrix products, arithmetic and copies ran while one was open for 0% -> 0% of each run, Pallas kernels for 29% -> 32%
where the time goes in v7:
time: 65.5 us; the launch traced here: 65.3 us
  Pallas kernels  31.7 us (48%)
  starting transfers between devices  22.4 us (34%)
  waiting for transfers between devices  9.39 us (14%)
  between operations  1.62 us (2%)
    pallas_call x2, Pallas kernels, front(): pl.pallas_call(functools.partial(front_kernel, first, last, group, pairs,...  14.2 us
    ppermute x9, starting transfers between devices, swap(): return lax.ppermute(values, axis, [(i, i ^ step) for i in range(count)])  11.9 us
    pallas_call x3, Pallas kernels, far(): pl.pallas_call(functools.partial(far_kernel, pairs, group, which, 256, sp...  7.45 us
    ppermute x5, starting transfers between devices, across_heads(): lax.ppermute(values, 'head', [(i, (i + step) % count) for i in range(coun...  5.79 us
    pallas_call x2, Pallas kernels, near(): pl.pallas_call(functools.partial(near_kernel, pairs, group, groups), in_s...  5.7 us
    ppermute x9, waiting for transfers between devices, swap(): return lax.ppermute(values, axis, [(i, i ^ step) for i in range(count)])  4.74 us
    ppermute x5, waiting for transfers between devices, across_heads(): lax.ppermute(values, 'head', [(i, (i + step) % count) for i in range(coun...  4.64 us
    ppermute x3, starting transfers between devices, per_device(): lax.ppermute(piece, 'seq', [(i, (i + k + 1) % spread) for i in range(spre...  3.88 us
  transfers between devices with their start and end apart: 18, of which 5 were waited for; matrix products, arithmetic and copies ran while one was open for 0% of the time, Pallas kernels for 32%

profile of v7, /device:TPU:0, one launch (start us, length us, event | category | flops | bytes accessed | tf_op | source)
XLA Modules:
  0.0 65.3 jit_solution(2705833107087104874)
XLA Ops:
  0.6 0.1 pad_add_fusion.1.refs_0_
  0.7 8.6 %front.2 = (bf16[1024,1024]{1,0:T(8,128)(2,1)S(1)}, bf16[1024,512]{1,0:T(8,128)(2,1)S(1)}, bf16[256,256]{1,0:T(8,128)(2,1)S(1)}, bf16[256,256]{1,0:T(8,128)(2,1)...) custom-call(s32[4]{0:T(128)S(1)} %pad_add_fusion.1.refs_0_, ...), custom_call_target="tpu_custom_call" | custom-call | flops 3221225472 | bytes 4194304 | tf_op jit(solution)/shard_map/front/pallas_call | solution.py:231
  9.4 0.5 collective-permute-start
  9.9 1.0 %collective-permute-done.b_ref = bf16[256,256]{1,0:T(8,128)(2,1)S(1)} collective-permute-done((bf16[256,256]{1,0:T(8,128)(2,1)S(1)}, bf16[256,256]{1,0:T(8,128)(2,1)S(1)}, u32[]{:S(2)}, u32[]{:S(2)}) %collective-permute-start) | collective-permute-done | bytes 131104 | tf_op jit(solution)/shard_map/ppermute | solution.py:502
  10.9 3.0 %collective-permute-start.2 = (bf16[256,256]{1,0:T(8,128)(2,1)S(1)}, bf16[256,256]{1,0:T(8,128)(2,1)S(1)}, u32[]{:S(2)}, u32[]{:S(2)}) collective-permute-start(bf16[256,256]{1,0:T(8,128)(2,1)S(1)} %add.49.a_ref), channel_id=1, source_target_pairs={{0,4},{4,0},{8,12},{12,8},{1,5},{5,1},{9,13},{13,9},{2,6},{6,2},{1... | collective-permute-start | bytes 393224 | tf_op jit(solution)/shard_map/ppermute | solution.py:502
  13.9 5.6 %front.3 = (bf16[1024,1024]{1,0:T(8,128)(2,1)S(1)}, bf16[1024,512]{1,0:T(8,128)(2,1)S(1)}, bf16[256,256]{1,0:T(8,128)(2,1)S(1)}, bf16[512,256]{1,0:T(8,128)(2,1)...) custom-call(s32[4]{0:T(128)S(1)} %get-tuple-element.62.refs_0_, ...), custom_call_target="tpu_custom_call", output_to_operand_aliasing={{0}: (1, {})} | custom-call | flops 3221225472 | bytes 4194304 | tf_op jit(solution)/shard_map/front/pallas_call | solution.py:231
  19.5 0.1 collective-permute-start.1
  19.6 0.8 %collective-permute-start.5 = (bf16[256,256]{1,0:T(8,128)(2,1)S(1)}, bf16[256,256]{1,0:T(8,128)(2,1)S(1)}, u32[]{:S(2)}, u32[]{:S(2)}) collective-permute-start(bf16[256,256]{1,0:T(8,128)(2,1)S(1)} %get-tuple-element.78), channel_id=1, source_target_pairs={{1,4},{5,8},{9,12},{4,1},{8,5},{12,9},{3,6},{7,10},{11,14},{6,3},{... | collective-permute-start | bytes 393224 | tf_op jit(solution)/shard_map/ppermute | solution.py:584
  20.4 0.0 collective-permute-done.2.b_ref
  20.4 0.0 copy-start.1
  20.5 3.9 %collective-permute-start.4 = (bf16[256,256]{1,0:T(8,128)(2,1)S(1)}, bf16[256,256]{1,0:T(8,128)(2,1)S(1)}, u32[]{:S(2)}, u32[]{:S(2)}) collective-permute-start(bf16[256,256]{1,0:T(8,128)(2,1)S(1)} %add.51.a_ref), channel_id=1, source_target_pairs={{0,8},{4,12},{8,0},{12,4},{1,9},{5,13},{9,1},{13,5},{2,10},{6,14},... | collective-permute-start | bytes 393224 | tf_op jit(solution)/shard_map/ppermute | solution.py:502
  24.4 0.0 collective-permute-done.1.b_ref.refs_2_.refs_1_
  24.4 2.2 %collective-permute-start.3 = (bf16[256,256]{1,0:T(8,128)(2,1)S(1)}, bf16[256,256]{1,0:T(8,128)(2,1)S(1)}, u32[]{:S(2)}, u32[]{:S(2)}) collective-permute-start(bf16[256,256]{1,0:T(8,128)(2,1)S(1)} %add.50.a_ref), channel_id=1, source_target_pairs={{0,4},{4,0},{8,12},{12,8},{1,5},{5,1},{9,13},{13,9},{2,6},{6,2},{1... | collective-permute-start | bytes 393224 | tf_op jit(solution)/shard_map/ppermute | solution.py:502
  26.6 0.0 collective-permute-done.5.refs_3_.refs_2_
  26.6 3.5 %near.2 = (bf16[1024,256]{1,0:T(8,128)(2,1)S(1)}, bf16[1024,256]{1,0:T(8,128)(2,1)S(1)}, f32[1024,512]{1,0:T(8,128)S(1)}, s32[4]{0:T(128)S(1)}) custom-call(s32[4]{0:T(128)S(1)} %get-tuple-element.76.ids_ref, bf16[1024,1024]{1,0:T(8,128)(2,1)S(1)} %get-tuple-element.77.refs_0_, bf16[1024,512]{1,0:T(8,128)(2,1)S(1)} %copy-done.1, ...), custom_call_target="tpu_custom_call" | custom-call | flops 1048576 | bytes 1024 | tf_op jit(solution)/shard_map/near/pallas_call | solution.py:320
  30.1 2.5 %collective-permute-done.4.b_ref = bf16[256,256]{1,0:T(8,128)(2,1)S(1)} collective-permute-done((bf16[256,256]{1,0:T(8,128)(2,1)S(1)}, bf16[256,256]{1,0:T(8,128)(2,1)S(1)}, u32[]{:S(2)}, u32[]{:S(2)}) %collective-permute-start.4) | collective-permute-done | bytes 131104 | tf_op jit(solution)/shard_map/ppermute | solution.py:502
  32.7 0.1 collective-permute-start.7
  32.8 2.0 %collective-permute-start.6 = (bf16[256,256]{1,0:T(8,128)(2,1)S(1)}, bf16[256,256]{1,0:T(8,128)(2,1)S(1)}, u32[]{:S(2)}, u32[]{:S(2)}) collective-permute-start(bf16[256,256]{1,0:T(8,128)(2,1)S(1)} %add.52.a_ref), channel_id=1, source_target_pairs={{0,8},{4,12},{8,0},{12,4},{1,9},{5,13},{9,1},{13,5},{2,10},{6,14},... | collective-permute-start | bytes 393224 | tf_op jit(solution)/shard_map/ppermute | solution.py:502
  34.8 0.0 collective-permute-done.7.refs_4_
  34.8 2.2 %far.3 = (bf16[1024,128]{1,0:T(8,128)(2,1)S(1)}, f32[32,128]{1,0:T(8,128)S(1)}, bf16[32,128]{1,0:T(8,128)(2,1)S(1)}, s32[4]{0:T(128)S(1)}) custom-call(s32[4]{0:T(128)S(1)} %get-tuple-element.85.refs_0_, bf16[1024,256]{1,0:T(8,128)(2,1)S(1)} %get-tuple-element.86.refs_1_, f32[1024,512]{1,0:T(8,128)S(1)} %get-tuple-element.87.refs_2_, ...), custom_call_target="tpu_custom_call" | custom-call | flops 1048576 | bytes 1024 | tf_op jit(solution)/shard_map/far/pallas_call | solution.py:394
  37.1 1.6 %collective-permute-start.9 = (bf16[1024,128]{1,0:T(8,128)(2,1)S(1)}, bf16[1024,128]{1,0:T(8,128)(2,1)S(1)}, u32[]{:S(2)}, u32[]{:S(2)}) collective-permute-start(bf16[1024,128]{1,0:T(8,128)(2,1)S(1)} %get-tuple-element.102.refs_1_), channel_id=1, source_target_pairs={{0,2},{2,0},{1,3},{3,1},{4,6},{6,4},{5,7},{7,5},{8,10},{10,8},{9,1... | collective-permute-start | bytes 786440 | tf_op jit(solution)/shard_map/ppermute | solution.py:507
  38.6 2.2 %far.4 = (bf16[1024,128]{1,0:T(8,128)(2,1)S(1)}, f32[32,256]{1,0:T(8,128)S(1)}, bf16[32,256]{1,0:T(8,128)(2,1)S(1)}, s32[4]{0:T(128)S(1)}) custom-call(s32[4]{0:T(128)S(1)} %get-tuple-element.89.refs_0_, bf16[1024,256]{1,0:T(8,128)(2,1)S(1)} %get-tuple-element.86.refs_1_, f32[1024,512]{1,0:T(8,128)S(1)} %get-tuple-element.87.refs_2_, ...), custom_call_target="tpu_custom_call" | custom-call | flops 1048576 | bytes 1024 | tf_op jit(solution)/shard_map/far/pallas_call | solution.py:394
  40.9 0.6 collective-permute-start.12
  41.5 2.2 %near.3 = (bf16[1024,256]{1,0:T(8,128)(2,1)S(1)}, f32[1024,512]{1,0:T(8,128)S(1)}, s32[4]{0:T(128)S(1)}) custom-call(s32[4]{0:T(128)S(1)} %get-tuple-element.92.ids_ref, bf16[1024,256]{1,0:T(8,128)(2,1)S(1)} %get-tuple-element.93.refs_0_, bf16[512,256]{1,0:T(8,128)(2,1)S(1)} %collective-permute-done.1.b_ref.refs_2_.refs_1_, ...), custom_call_target="tpu_custom_call", output_to_operand_aliasing={{0}: (1, {})} | custom-call | flops 1048576 | bytes 1024 | tf_op jit(solution)/shard_map/near/pallas_call | solution.py:320
  43.7 0.0 copy-start
  43.7 0.0 collective-permute-done.6.b_ref
  43.8 0.1 collective-permute-start.8
  43.9 2.5 %collective-permute-done.9.refs_9_.refs_5_ = bf16[1024,128]{1,0:T(8,128)(2,1)S(1)} collective-permute-done((bf16[1024,128]{1,0:T(8,128)(2,1)S(1)}, bf16[1024,128]{1,0:T(8,128)(2,1)S(1)}, u32[]{:S(2)}, u32[]{:S(2)}) %collective-permute-start.9) | collective-permute-done | bytes 262176 | tf_op jit(solution)/shard_map/ppermute | solution.py:507
  46.4 0.0 collective-permute-done.8.refs_4_
  46.4 3.0 %far.5 = (bf16[1024,128]{1,0:T(8,128)(2,1)S(1)}, bf16[1024,128]{1,0:T(8,128)(2,1)S(1)}, f32[32,512]{1,0:T(8,128)S(1)}, bf16[32,512]{1,0:T(8,128)(2,1)S(1)}, s32[4]{0:T(128)}) custom-call(s32[4]{0:T(128)S(1)} %get-tuple-element.96.refs_0_, bf16[1024,256]{1,0:T(8,128)(2,1)S(1)} %get-tuple-element.97.refs_1_, f32[1024,512]{1,0:T(8,128)S(1)} %get-tuple-element.98.refs_2_, ...), custom_call_target="tpu_custom_call" | custom-call | flops 1048576 | bytes 1024 | tf_op jit(solution)/shard_map/far/pallas_call | solution.py:394
  49.4 1.5 %collective-permute-start.10 = (bf16[1024,128]{1,0:T(8,128)(2,1)S(1)}, bf16[1024,128]{1,0:T(8,128)(2,1)S(1)}, u32[]{:S(2)}, u32[]{:S(2)}) collective-permute-start(bf16[1024,128]{1,0:T(8,128)(2,1)S(1)} %get-tuple-element.103.refs_3_), channel_id=1, source_target_pairs={{0,2},{2,0},{1,3},{3,1},{4,6},{6,4},{5,7},{7,5},{8,10},{10,8},{9,1... | collective-permute-start | bytes 786440 | tf_op jit(solution)/shard_map/ppermute | solution.py:507
  50.9 0.5 collective-permute-start.11
  51.5 1.2 %collective-permute-done.13.got_ref = bf16[32,512]{1,0:T(8,128)(2,1)S(1)} collective-permute-done((bf16[32,512]{1,0:T(8,128)(2,1)S(1)}, bf16[32,512]{1,0:T(8,128)(2,1)S(1)}, u32[]{:S(2)}, u32[]{:S(2)}) %collective-permute-start.13) | collective-permute-done | bytes 32800 | tf_op jit(solution)/shard_map/ppermute | solution.py:502
  52.7 1.2 %collective-permute-start.14 = (bf16[8,512]{1,0:T(8,128)(2,1)S(1)}, bf16[8,512]{1,0:T(8,128)(2,1)S(1)}, u32[]{:S(2)}, u32[]{:S(2)}) collective-permute-start(bf16[8,512]{1,0:T(8,128)(2,1)S(1)} %get-tuple-element.110), channel_id=1, source_target_pairs={{0,4},{4,8},{8,12},{12,0},{1,5},{5,9},{9,13},{13,1},{2,6},{6,10},{... | collective-permute-start | bytes 24584 | tf_op jit(solution)/shard_map/ppermute | solution.py:626
  53.9 1.0 %collective-permute-start.15 = (bf16[8,512]{1,0:T(8,128)(2,1)S(1)}, bf16[8,512]{1,0:T(8,128)(2,1)S(1)}, u32[]{:S(2)}, u32[]{:S(2)}) collective-permute-start(bf16[8,512]{1,0:T(8,128)(2,1)S(1)} %get-tuple-element.111), channel_id=1, source_target_pairs={{0,8},{4,12},{8,0},{12,4},{1,9},{5,13},{9,1},{13,5},{2,10},{6,14},... | collective-permute-start | bytes 24584 | tf_op jit(solution)/shard_map/ppermute | solution.py:626
  54.9 0.0 collective-permute-done.12.refs_6_
  54.9 1.7 %collective-permute-start.16 = (bf16[8,512]{1,0:T(8,128)(2,1)S(1)}, bf16[8,512]{1,0:T(8,128)(2,1)S(1)}, u32[]{:S(2)}, u32[]{:S(2)}) collective-permute-start(bf16[8,512]{1,0:T(8,128)(2,1)S(1)} %get-tuple-element.112), channel_id=1, source_target_pairs={{0,12},{4,0},{8,4},{12,8},{1,13},{5,1},{9,5},{13,9},{2,14},{6,2},{... | collective-permute-start | bytes 24584 | tf_op jit(solution)/shard_map/ppermute | solution.py:626
  56.6 0.1 pad_add_fusion.2.refs_0_
  56.7 1.5 %out.2 = (f32[1024,512]{1,0:T(8,128)S(1)}, s32[1]{0:T(128)}) custom-call(s32[3]{0:T(128)S(1)} %pad_add_fusion.2.refs_0_, bf16[1024,128]{1,0:T(8,128)(2,1)S(1)} %get-tuple-element.102.refs_1_, bf16[1024,128]{1,0:T(8,128)(2,1)S(1)} %get-tuple-element.105.refs_2_, bf16[1024,128]{1,0:T(8,128)(2,1)S(1)} %get-tuple-element.103.refs_3_, ...), custom_call_target="tpu_custom_call" | custom-call | flops 1048576 | bytes 1024 | tf_op jit(solution)/shard_map/out/pallas_call | solution.py:443
  58.8 0.0 collective-permute-done.14.refs_0_
  58.8 0.0 collective-permute-done.15.refs_1_
  58.9 0.6 pool_own.1.refs_3_
  59.4 1.5 %collective-permute-start.17 = (bf16[8,512]{1,0:T(8,128)(2,1)S(1)}, bf16[8,512]{1,0:T(8,128)(2,1)S(1)}, u32[]{:S(2)}, u32[]{:S(2)}) collective-permute-start(bf16[8,512]{1,0:T(8,128)(2,1)S(1)} %pool_own.1.refs_3_), channel_id=1, source_target_pairs={{0,2},{2,0},{1,3},{3,1},{4,6},{6,4},{5,7},{7,5},{8,10},{10,8},{9,1... | collective-permute-start | bytes 24584 | tf_op jit(solution)/shard_map/ppermute | solution.py:507
  61.0 0.1 pad_add_fusion.refs_0_
  61.1 2.1 %collective-permute-done.17.refs_4_ = bf16[8,512]{1,0:T(8,128)(2,1)S(1)} collective-permute-done((bf16[8,512]{1,0:T(8,128)(2,1)S(1)}, bf16[8,512]{1,0:T(8,128)(2,1)S(1)}, u32[]{:S(2)}, u32[]{:S(2)}) %collective-permute-start.17) | collective-permute-done | bytes 8224 | tf_op jit(solution)/shard_map/ppermute | solution.py:507
  63.2 0.0 collective-permute-done.10.refs_1_
  63.2 0.0 collective-permute-done.11.refs_2_
  63.2 2.0 %out.3 = (bf16[1024,512]{1,0:T(8,128)(2,1)}, f32[8,512]{1,0:T(8,128)}, s32[1]{0:T(128)}) custom-call(s32[3]{0:T(128)S(1)} %pad_add_fusion.refs_0_, bf16[1024,128]{1,0:T(8,128)(2,1)S(1)} %collective-permute-done.10.refs_1_, bf16[1024,128]{1,0:T(8,128)(2,1)S(1)} %collective-permute-done.11.refs_2_, bf16[8,512]{1,0:T(8,128)(2,1)S(1)} %pool_own.1.refs_3_, ...), custom_call_target="tpu_custom_call" | custom-call | flops 1048576 | bytes 1024 | tf_op jit(solution)/shard_map/out/pallas_call | solution.py:443
  (16 shorter events, 0.2 us)
Async XLA Ops:
  0.7 13.2 %copy-start.2 = (f32[4,512]{1,0:T(4,128)S(1)}, f32[4,512]{1,0:T(4,128)}, u32[]{:S(2)}) copy-start(f32[4,512]{1,0:T(4,128)} %refs_5_.8) | copy-start | bytes 24580
  9.4 1.5 %collective-permute-start = (bf16[256,256]{1,0:T(8,128)(2,1)S(1)}, bf16[256,256]{1,0:T(8,128)(2,1)S(1)}, u32[]{:S(2)}, u32[]{:S(2)}) collective-permute-start(bf16[256,256]{1,0:T(8,128)(2,1)S(1)} %get-tuple-element.60), channel_id=1, source_target_pairs={{0,1},{1,0},{2,3},{3,2},{4,5},{5,4},{6,7},{7,6},{8,9},{9,8},{10,11... | collective-permute-start | bytes 393224 | tf_op jit(solution)/shard_map/ppermute | solution.py:502
  10.9 9.5 %collective-permute-start.2 = (bf16[256,256]{1,0:T(8,128)(2,1)S(1)}, bf16[256,256]{1,0:T(8,128)(2,1)S(1)}, u32[]{:S(2)}, u32[]{:S(2)}) collective-permute-start(bf16[256,256]{1,0:T(8,128)(2,1)S(1)} %add.49.a_ref), channel_id=1, source_target_pairs={{0,4},{4,0},{8,12},{12,8},{1,5},{5,1},{9,13},{13,9},{2,6},{6,2},{1... | collective-permute-start | bytes 393224 | tf_op jit(solution)/shard_map/ppermute | solution.py:502
  19.5 4.9 %collective-permute-start.1 = (bf16[512,256]{1,0:T(8,128)(2,1)S(1)}, bf16[512,256]{1,0:T(8,128)(2,1)S(1)}, u32[]{:S(2)}, u32[]{:S(2)}) collective-permute-start(bf16[512,256]{1,0:T(8,128)(2,1)S(1)} %get-tuple-element.68), channel_id=1, source_target_pairs={{0,1},{1,0},{2,3},{3,2},{4,5},{5,4},{6,7},{7,6},{8,9},{9,8},{10,11... | collective-permute-start | bytes 786440 | tf_op jit(solution)/shard_map/ppermute | solution.py:502
  19.6 7.0 %collective-permute-start.5 = (bf16[256,256]{1,0:T(8,128)(2,1)S(1)}, bf16[256,256]{1,0:T(8,128)(2,1)S(1)}, u32[]{:S(2)}, u32[]{:S(2)}) collective-permute-start(bf16[256,256]{1,0:T(8,128)(2,1)S(1)} %get-tuple-element.78), channel_id=1, source_target_pairs={{1,4},{5,8},{9,12},{4,1},{8,5},{12,9},{3,6},{7,10},{11,14},{6,3},{... | collective-permute-start | bytes 393224 | tf_op jit(solution)/shard_map/ppermute | solution.py:584
  20.4 6.2 %copy-start.1 = (bf16[1024,512]{1,0:T(8,128)(2,1)S(1)}, bf16[1024,512]{1,0:T(8,128)(2,1)}, u32[]{:S(2)}) copy-start(bf16[1024,512]{1,0:T(8,128)(2,1)} %refs_1_.3) | copy-start | bytes 3145732
  20.5 12.1 %collective-permute-start.4 = (bf16[256,256]{1,0:T(8,128)(2,1)S(1)}, bf16[256,256]{1,0:T(8,128)(2,1)S(1)}, u32[]{:S(2)}, u32[]{:S(2)}) collective-permute-start(bf16[256,256]{1,0:T(8,128)(2,1)S(1)} %add.51.a_ref), channel_id=1, source_target_pairs={{0,8},{4,12},{8,0},{12,4},{1,9},{5,13},{9,1},{13,5},{2,10},{6,14},... | collective-permute-start | bytes 393224 | tf_op jit(solution)/shard_map/ppermute | solution.py:502
  24.4 8.3 %collective-permute-start.3 = (bf16[256,256]{1,0:T(8,128)(2,1)S(1)}, bf16[256,256]{1,0:T(8,128)(2,1)S(1)}, u32[]{:S(2)}, u32[]{:S(2)}) collective-permute-start(bf16[256,256]{1,0:T(8,128)(2,1)S(1)} %add.50.a_ref), channel_id=1, source_target_pairs={{0,4},{4,0},{8,12},{12,8},{1,5},{5,1},{9,13},{13,9},{2,6},{6,2},{1... | collective-permute-start | bytes 393224 | tf_op jit(solution)/shard_map/ppermute | solution.py:502
  26.6 8.2 %copy-start.3 = (s32[64,2]{0,1:T(2,128)S(1)}, s32[64,2]{0,1:T(2,128)}, u32[]{:S(2)}) copy-start(s32[64,2]{0,1:T(2,128)} %param.17) | copy-start | bytes 1540
  32.7 2.2 %collective-permute-start.7 = (bf16[256,256]{1,0:T(8,128)(2,1)S(1)}, bf16[256,256]{1,0:T(8,128)(2,1)S(1)}, u32[]{:S(2)}, u32[]{:S(2)}) collective-permute-start(bf16[256,256]{1,0:T(8,128)(2,1)S(1)} %add.53.refs_3_), channel_id=1, source_target_pairs={{0,1},{1,0},{2,3},{3,2},{4,5},{5,4},{6,7},{7,6},{8,9},{9,8},{10,11... | collective-permute-start | bytes 393224 | tf_op jit(solution)/shard_map/ppermute | solution.py:502
  32.8 10.9 %collective-permute-start.6 = (bf16[256,256]{1,0:T(8,128)(2,1)S(1)}, bf16[256,256]{1,0:T(8,128)(2,1)S(1)}, u32[]{:S(2)}, u32[]{:S(2)}) collective-permute-start(bf16[256,256]{1,0:T(8,128)(2,1)S(1)} %add.52.a_ref), channel_id=1, source_target_pairs={{0,8},{4,12},{8,0},{12,4},{1,9},{5,13},{9,1},{13,5},{2,10},{6,14},... | collective-permute-start | bytes 393224 | tf_op jit(solution)/shard_map/ppermute | solution.py:502
  37.1 9.3 %collective-permute-start.9 = (bf16[1024,128]{1,0:T(8,128)(2,1)S(1)}, bf16[1024,128]{1,0:T(8,128)(2,1)S(1)}, u32[]{:S(2)}, u32[]{:S(2)}) collective-permute-start(bf16[1024,128]{1,0:T(8,128)(2,1)S(1)} %get-tuple-element.102.refs_1_), channel_id=1, source_target_pairs={{0,2},{2,0},{1,3},{3,1},{4,6},{6,4},{5,7},{7,5},{8,10},{10,8},{9,1... | collective-permute-start | bytes 786440 | tf_op jit(solution)/shard_map/ppermute | solution.py:507
  40.9 14.1 %collective-permute-start.12 = (bf16[1024,128]{1,0:T(8,128)(2,1)S(1)}, bf16[1024,128]{1,0:T(8,128)(2,1)S(1)}, u32[]{:S(2)}, u32[]{:S(2)}) collective-permute-start(bf16[1024,128]{1,0:T(8,128)(2,1)S(1)} %get-tuple-element.105.refs_2_), channel_id=1, source_target_pairs={{0,2},{2,0},{1,3},{3,1},{4,6},{6,4},{5,7},{7,5},{8,10},{10,8},{9,1... | collective-permute-start | bytes 786440 | tf_op jit(solution)/shard_map/ppermute | solution.py:507
  43.7 13.0 %copy-start = (bf16[1024,512]{1,0:T(8,128)(2,1)S(1)}, bf16[1024,512]{1,0:T(8,128)(2,1)}, u32[]{:S(2)}) copy-start(bf16[1024,512]{1,0:T(8,128)(2,1)} %refs_5_.9) | copy-start | bytes 3145732
  43.8 2.6 %collective-permute-start.8 = (bf16[256,256]{1,0:T(8,128)(2,1)S(1)}, bf16[256,256]{1,0:T(8,128)(2,1)S(1)}, u32[]{:S(2)}, u32[]{:S(2)}) collective-permute-start(bf16[256,256]{1,0:T(8,128)(2,1)S(1)} %add.54.refs_3_), channel_id=1, source_target_pairs={{0,1},{1,0},{2,3},{3,2},{4,5},{5,4},{6,7},{7,6},{8,9},{9,8},{10,11... | collective-permute-start | bytes 393224 | tf_op jit(solution)/shard_map/ppermute | solution.py:502
  49.4 13.8 %collective-permute-start.10 = (bf16[1024,128]{1,0:T(8,128)(2,1)S(1)}, bf16[1024,128]{1,0:T(8,128)(2,1)S(1)}, u32[]{:S(2)}, u32[]{:S(2)}) collective-permute-start(bf16[1024,128]{1,0:T(8,128)(2,1)S(1)} %get-tuple-element.103.refs_3_), channel_id=1, source_target_pairs={{0,2},{2,0},{1,3},{3,1},{4,6},{6,4},{5,7},{7,5},{8,10},{10,8},{9,1... | collective-permute-start | bytes 786440 | tf_op jit(solution)/shard_map/ppermute | solution.py:507
  50.9 12.2 %collective-permute-start.11 = (bf16[1024,128]{1,0:T(8,128)(2,1)S(1)}, bf16[1024,128]{1,0:T(8,128)(2,1)S(1)}, u32[]{:S(2)}, u32[]{:S(2)}) collective-permute-start(bf16[1024,128]{1,0:T(8,128)(2,1)S(1)} %get-tuple-element.104.refs_4_), channel_id=1, source_target_pairs={{0,2},{2,0},{1,3},{3,1},{4,6},{6,4},{5,7},{7,5},{8,10},{10,8},{9,1... | collective-permute-start | bytes 786440 | tf_op jit(solution)/shard_map/ppermute | solution.py:507
  51.5 1.2 %collective-permute-start.13 = (bf16[32,512]{1,0:T(8,128)(2,1)S(1)}, bf16[32,512]{1,0:T(8,128)(2,1)S(1)}, u32[]{:S(2)}, u32[]{:S(2)}) collective-permute-start(bf16[32,512]{1,0:T(8,128)(2,1)S(1)} %get-tuple-element.108), channel_id=1, source_target_pairs={{0,1},{1,0},{2,3},{3,2},{4,5},{5,4},{6,7},{7,6},{8,9},{9,8},{10,11... | collective-permute-start | bytes 98312 | tf_op jit(solution)/shard_map/ppermute | solution.py:502
  52.7 6.1 %collective-permute-start.14 = (bf16[8,512]{1,0:T(8,128)(2,1)S(1)}, bf16[8,512]{1,0:T(8,128)(2,1)S(1)}, u32[]{:S(2)}, u32[]{:S(2)}) collective-permute-start(bf16[8,512]{1,0:T(8,128)(2,1)S(1)} %get-tuple-element.110), channel_id=1, source_target_pairs={{0,4},{4,8},{8,12},{12,0},{1,5},{5,9},{9,13},{13,1},{2,6},{6,10},{... | collective-permute-start | bytes 24584 | tf_op jit(solution)/shard_map/ppermute | solution.py:626
  53.9 5.0 %collective-permute-start.15 = (bf16[8,512]{1,0:T(8,128)(2,1)S(1)}, bf16[8,512]{1,0:T(8,128)(2,1)S(1)}, u32[]{:S(2)}, u32[]{:S(2)}) collective-permute-start(bf16[8,512]{1,0:T(8,128)(2,1)S(1)} %get-tuple-element.111), channel_id=1, source_target_pairs={{0,8},{4,12},{8,0},{12,4},{1,9},{5,13},{9,1},{13,5},{2,10},{6,14},... | collective-permute-start | bytes 24584 | tf_op jit(solution)/shard_map/ppermute | solution.py:626
  54.9 3.9 %collective-permute-start.16 = (bf16[8,512]{1,0:T(8,128)(2,1)S(1)}, bf16[8,512]{1,0:T(8,128)(2,1)S(1)}, u32[]{:S(2)}, u32[]{:S(2)}) collective-permute-start(bf16[8,512]{1,0:T(8,128)(2,1)S(1)} %get-tuple-element.112), channel_id=1, source_target_pairs={{0,12},{4,0},{8,4},{12,8},{1,13},{5,1},{9,5},{13,9},{2,14},{6,2},{... | collective-permute-start | bytes 24584 | tf_op jit(solution)/shard_map/ppermute | solution.py:626
  59.4 3.7 %collective-permute-start.17 = (bf16[8,512]{1,0:T(8,128)(2,1)S(1)}, bf16[8,512]{1,0:T(8,128)(2,1)S(1)}, u32[]{:S(2)}, u32[]{:S(2)}) collective-permute-start(bf16[8,512]{1,0:T(8,128)(2,1)S(1)} %pool_own.1.refs_3_), channel_id=1, source_target_pairs={{0,2},{2,0},{1,3},{3,1},{4,6},{6,4},{5,7},{7,5},{8,10},{10,8},{9,1... | collective-permute-start | bytes 24584 | tf_op jit(solution)/shard_map/ppermute | solution.py:507

commit v8 on v7

--- a/solution.py
+++ b/solution.py
@@ -130,8 +130,6 @@
         small_copies = [copy(gain_hbm, gain_ref), copy(dual_hbm, dual_ref)]
         kv_copies, proj_copies = weight_copies(group, kv_ref, wp_ref)
         token_copies += [token_copy(i) for i in range(1, chunks)]
-    if not last:
-        next_copies = sum(weight_copies(group + 1, next_kv_ref, next_wp_ref), [])
     for i in range(chunks):
         at = pl.ds(i * tile, tile)
         if first:
@@ -153,6 +151,8 @@
         if i == 0:
             for made in proj_copies:
                 made.wait()
+        if i == 0 and not last:
+            next_copies = sum(weight_copies(group + 1, next_kv_ref, next_wp_ref), [])
         p_ref[at, :] = exp_capped(dot(normed, wp_ref[...]), 1.0).astype(BF)
         near_ref[at, :width] = head_norm(key, dual_ref[0:1, group * width : (group + 1) * width])
         near_ref[at, width:] = head_norm(value, dual_ref[1:2, group * width : (group + 1) * width])
@@ -330,81 +330,89 @@
     )(ids, *args, core, chip, near_pairs)
 
 
-def far_kernel(pairs, group, which, block, spread, *refs):
-    (ids_ref, q_ref, near_ref, mine_ref, other_ref, gains_ref, bounds_ref), refs = refs[:7], refs[7:]
-    keep_ref, send_ref, turn_ref = refs[-3:]
-    out_refs = refs[-3 - len(which) : -3]
-    done = (group * pairs + which[0]) * LANES
-    before = refs[:2] if done else ()
+def far_kernel(pairs, group, part, block, spread, waits, final, *refs):
+    ids_ref, q_ref, near_ref, gains_ref = refs[:4]
+    refs = refs[4:]
+    is_first = ids_ref[0] == 0
+    if part == "all":
+        mine, other = refs[0][...], refs[1][...]
+        total = jnp.concatenate([jnp.where(is_first, mine, other), jnp.where(is_first, other, mine)], axis=0)
+        p, refs = 0, refs[2:]
+    else:
+        total = refs[0][...]
+        p, refs = ids_ref[0] if part == "own" else 1 - ids_ref[0], refs[1:]
+    refs = refs[waits:]
+    if final:
+        bounds_ref, *earlier = refs[:-4]
+        out_ref, keep_ref, send_ref, turn_ref = refs[-4:]
+    else:
+        out_ref, turn_ref = refs
     pass_turn(ids_ref, turn_ref)
     rows = q_ref.shape[0]
-    width = pairs * LANES
-    is_first = ids_ref[0] == 0
-    top = jnp.where(is_first, mine_ref[...], other_ref[...])
-    bottom = jnp.where(is_first, other_ref[...], mine_ref[...])
-    total = jnp.concatenate([top, bottom], axis=0)
-    ones = jnp.ones((LANES, R), BF)
-    for out_ref, p in zip(out_refs, which):
-        cols = slice(p * LANES, (p + 1) * LANES)
-
-        base = group * width + p * LANES
-        gains = jnp.concatenate([gains_ref[:, base : base + LANES]] * 2, axis=0).T
-
-        def land(kind):
-            parts = []
-            for h in range(2):
-                at = p * R + kind * LANES + h * DH
-                values = total[at : at + DH].astype(F32)
-                centred = values - jnp.mean(values, axis=0, keepdims=True)
-                spread = jnp.mean(centred * centred, axis=0, keepdims=True)
-                gain = gains[h * DH : (h + 1) * DH, 2 + kind : 3 + kind]
-                parts.append((centred * lax.rsqrt(spread + epsilon) * gain).astype(BF))
-            return jnp.concatenate(parts, axis=0)
-
-        keys = land(0)
-        values = jnp.concatenate([land(1), ones], axis=0)
-        for start in range(0, rows, block):
-            q = stacked(q_ref[start : start + block, cols])
-            weights = exp_capped(dot(q, keys), SCORE_SCALE).astype(BF)
-            top, bottom = unstack(dot(weights, values, ((1,), (1,))))
-            top = top + near_ref[start : start + block, 2 * p * LANES : (2 * p + 1) * LANES]
-            bottom = bottom + near_ref[start : start + block, (2 * p + 1) * LANES : (2 * p + 2) * LANES]
-            out_ref[start : start + block, :] = (top / bottom).astype(BF)
+
+    def lanes(offset, scale=1):
+        start = (offset + p) * scale * LANES
+        return pl.ds(start if part == "all" else pl.multiple_of(start, LANES), scale * LANES)
+
+    gains = jnp.concatenate([gains_ref[:, lanes(group * pairs)]] * 2, axis=0).T
+
+    def land(kind):
+        parts = []
+        for h in range(2):
+            at = kind * LANES + h * DH
+            values = total[at : at + DH].astype(F32)
+            centred = values - jnp.mean(values, axis=0, keepdims=True)
+            spread = jnp.mean(centred * centred, axis=0, keepdims=True)
+            gain = gains[h * DH : (h + 1) * DH, 2 + kind : 3 + kind]
+            parts.append((centred * lax.rsqrt(spread + epsilon) * gain).astype(BF))
+        return jnp.concatenate(parts, axis=0)
+
+    keys = land(0)
+    values = jnp.concatenate([land(1), jnp.ones((LANES, R), BF)], axis=0)
+    for start in range(0, rows, block):
+        at = slice(start, start + block)
+        weights = exp_capped(dot(stacked(q_ref[at, lanes(0)]), keys), SCORE_SCALE).astype(BF)
+        top, bottom = unstack(dot(weights, values, ((1,), (1,))))
+        near_sums = near_ref[at, lanes(0, 2)]
+        out_ref[at, :] = ((top + near_sums[:, :LANES]) / (bottom + near_sums[:, LANES:])).astype(BF)
+    if not final:
+        return
     spans = bounds_ref.shape[1]
     position = ids_ref[3] + lax.broadcasted_iota(jnp.int32, (rows, spans), 0)
     member = (position >= bounds_ref[0:1, :]) & (position < bounds_ref[1:2, :])
-    outs = jnp.concatenate([ref[...] for ref in out_refs], axis=1)
-    sums = dot(jnp.where(member, 1.0, 0.0).astype(BF), outs, ((0,), (0,)))
+    pieces = jnp.concatenate([ref[...] for ref in earlier + [out_ref]], axis=1)
+    sums = dot(jnp.where(member, 1.0, 0.0).astype(BF), pieces, ((0,), (0,)))
+    if part != "all":
+        ordered = []
+        for at in range(0, sums.shape[1], 2 * LANES):
+            low, high = sums[:, at : at + LANES], sums[:, at + LANES : at + 2 * LANES]
+            ordered += [jnp.where(is_first, low, high), jnp.where(is_first, high, low)]
+        sums = jnp.concatenate(ordered, axis=1)
     count = spans // (2 * spread)
     even = jnp.concatenate([sums[2 * i * count : (2 * i + 1) * count] for i in range(spread)], axis=0)
     odd = jnp.concatenate([sums[(2 * i + 1) * count : (2 * i + 2) * count] for i in range(spread)], axis=0)
-    lanes = slice(done, done + len(which) * LANES)
-    if before:
-        keep_ref[:, :done] = before[0][...]
-        send_ref[:, :done] = before[1][...]
-    keep_ref[:, lanes] = jnp.where(is_first, even, odd)
-    send_ref[:, lanes] = jnp.where(is_first, odd, even).astype(BF)
-
-
-def far(pairs, group, which, spread, ids, q, near_sums, mine, other, gains, bounds, before, arrived):
+    keep_ref[...] = jnp.where(is_first, even, odd)
+    send_ref[...] = jnp.where(is_first, odd, even).astype(BF)
+
+
+def far(pairs, group, part, spread, ids, q, near_sums, gains, halves, arrived, final):
     rows = q.shape[0]
-    width = pairs * LANES
-    spans = bounds.shape[1]
-    shape = (spans // 2, (group * pairs + which[-1] + 1) * LANES)
+    shapes = [jax.ShapeDtypeStruct((rows, LANES), BF)]
+    if final:
+        shape = (final[0].shape[1] // 2, len(final) * LANES)
+        shapes += [jax.ShapeDtypeStruct(shape, F32), jax.ShapeDtypeStruct(shape, BF)]
     return pl.pallas_call(
-        functools.partial(far_kernel, pairs, group, which, 256, spread),
-        in_specs=[smem()] + [vmem()] * (6 + len(before)) + [pl.BlockSpec(memory_space=pl.ANY)] * len(arrived),
-        out_specs=[vmem()] * (2 + len(which)) + [smem()],
-        out_shape=[
-            *[jax.ShapeDtypeStruct((rows, LANES), BF)] * len(which),
-            jax.ShapeDtypeStruct(shape, F32),
-            jax.ShapeDtypeStruct(shape, BF),
-            TURN,
-        ],
+        functools.partial(far_kernel, pairs, group, part, 256, spread, len(arrived), bool(final)),
+        in_specs=[smem()]
+        + [vmem()] * (3 + len(halves))
+        + [pl.BlockSpec(memory_space=pl.ANY)] * len(arrived)
+        + [vmem()] * len(final),
+        out_specs=[vmem()] * len(shapes) + [smem()],
+        out_shape=shapes + [TURN],
         compiler_params=pltpu.CompilerParams(vmem_limit_bytes=VMEM_LIMIT),
         cost_estimate=COST,
         name="far",
-    )(ids, q, near_sums, mine, other, gains, bounds, *before, *arrived)
+    )(ids, q, near_sums, gains, *halves, *arrived, *final)
 
 
 def out_kernel(count, pairs, spans, *refs):
@@ -421,11 +429,20 @@
     def weight(j, size):
         return weight_ref[pl.ds(pl.multiple_of(ids_ref[j] * size, size), size), :]
 
+    def head_weight(j):
+        if pairs == 1:
+            return weight(j, width)
+        first = ids_ref[count + spans]
+        blocks = [weight_ref[pl.ds(pl.multiple_of(ids_ref[j] * width + p * LANES, LANES), LANES), :] for p in (first, 1 - first)]
+        return jnp.concatenate(blocks, axis=0)
+
+    weights = [head_weight(j) for j in range(count)]
+
     for start in range(0, rows, tile):
         at = slice(start, start + tile)
         total = acc[0][at, :] if acc else None
         for j in range(count):
-            term = dot(jnp.concatenate([ref[at, :] for ref in tokens[j]], axis=1), weight(j, width))
+            term = dot(jnp.concatenate([ref[at, :] for ref in tokens[j]], axis=1), weights[j])
             total = term if total is None else total + term
         outs[0][at, :] = total.astype(outs[0].dtype)
     if spans:
@@ -549,7 +566,7 @@
     head_index = lax.axis_index("head")
     first_row = seq_index * rows
     all_pairs = query_weight.shape[1] // LANES
-    groups = 2 if all_pairs % 2 == 0 else 1
+    groups = 2 if all_pairs == 4 else all_pairs
     pairs = all_pairs // groups
     ids = jnp.stack(
         [lax.axis_index("rep"), (seq_index > 0).astype(jnp.int32), (seq_index < seq_devices - 1).astype(jnp.int32), first_row]
@@ -590,7 +607,7 @@
             mine[0] = add_call(mine[0], swap(mine[0], "seq", step))
 
     spread = lax.axis_size("seq")
-    outs, before, arrived, others, other_index, queries = [], (), [], [], [], []
+    outs, arrived, others, other_index, queries = [], [], [], [], []
     for g in range(groups):
         source = queries[g] if g else normed
         *made, near_sums, turn = near(pairs, g, groups, turn, source, query_weight, core, chip, fronts[g][0])
@@ -605,11 +622,14 @@
                 mine[-1] = add_call(mine[-1], got)
             mine[-1], turn = tie((mine[-1], turn))
         out = []
-        for which in [[p] for p in range(pairs)] if g < groups - 1 else [list(range(pairs))]:
-            *made, keep, send, turn = far(pairs, g, which, spread, turn, q, near_sums, total, other, dual_gains, bounds,
-                                          before, arrived)
-            before = [keep, send]
-            out += made
+        calls = [("own", [total]), ("other", [other])] if pairs == 2 else [("all", [total, other])]
+        for part, halves in calls:
+            final = []
+            if g == groups - 1 and part != "own":
+                final = [bounds] + [piece for o in outs for piece in o] + out
+            made, *sums, turn = far(pairs, g, part, spread, turn, q, near_sums, dual_gains, halves, arrived, final)
+            arrived = []
+            out.append(made)
         outs.append(out)
         moved = [[across_heads(piece, k) for piece in out] for k in range(1, head_devices)]
         arrived = [moved[0][0]] if g < groups - 1 and moved else []
@@ -619,21 +639,21 @@
     own_index = [head_index * groups + g for g in range(groups)]
     early = len(others) - (head_devices - 1)
 
-    keep, send = before
+    keep, send = sums
     place = lax.axis_index("seq").astype(jnp.int32)[None]
     own, *pieces = pool_pieces(place, keep, swap(send, "rep", 1), spread)
     pieces = [
         lax.ppermute(piece, "seq", [(i, (i + k + 1) % spread) for i in range(spread)]) for k, piece in enumerate(pieces)
     ]
     parts = outs + others[:early]
-    index = jnp.stack(own_index + other_index[:early]).astype(jnp.int32)
+    index = jnp.stack(own_index + other_index[:early] + [lax.axis_index("rep")]).astype(jnp.int32)
     acc, turn = out_part(parts, index, out_weight, None, F32)
     place = (seq_index * own.shape[0]).astype(jnp.int32)[None]
     place = place + (turn - index[:1])
     own = pool_own(place, bounds, own, pieces)
     pooled = [own] + [across_heads(own, k) for k in range(1, head_devices)]
     pooled_index = [lax.rem(head_index - k + head_devices, head_devices) for k in range(head_devices)]
-    index = jnp.stack(other_index[early:] + pooled_index).astype(jnp.int32)
+    index = jnp.stack(other_index[early:] + pooled_index + [lax.axis_index("rep")]).astype(jnp.int32)
     return tuple(out_part(others[early:], index, out_weight, acc, BF, pooled)[:2])
 
 

time: 65.5 us -> 65.9 us (level)
    pallas_call x3 -> x4, Pallas kernels: 7.45 us -> 7.06 us  [far(): pl.pallas_call(functools.partial(far_kernel, pairs, group, part, 256, spr...]
where the time goes in v8:
time: 65.9 us; the launch traced here: 65.7 us
  Pallas kernels  31.3 us (47%)
  starting transfers between devices  22.4 us (34%)
  waiting for transfers between devices  10 us (15%)
  between operations  1.72 us (3%)
    pallas_call x2, Pallas kernels, front(): pl.pallas_call(functools.partial(front_kernel, first, last, group, pairs,...  14 us
    ppermute x9, starting transfers between devices, swap(): return lax.ppermute(values, axis, [(i, i ^ step) for i in range(count)])  11.9 us
    pallas_call x4, Pallas kernels, far(): pl.pallas_call(functools.partial(far_kernel, pairs, group, part, 256, spr...  7.06 us
    ppermute x5, starting transfers between devices, across_heads(): lax.ppermute(values, 'head', [(i, (i + step) % count) for i in range(coun...  5.8 us
    pallas_call x2, Pallas kernels, near(): pl.pallas_call(functools.partial(near_kernel, pairs, group, groups), in_s...  5.68 us
    ppermute x5, waiting for transfers between devices, across_heads(): lax.ppermute(values, 'head', [(i, (i + step) % count) for i in range(coun...  5.24 us
    ppermute x9, waiting for transfers between devices, swap(): return lax.ppermute(values, axis, [(i, i ^ step) for i in range(count)])  4.75 us
    ppermute x3, starting transfers between devices, per_device(): lax.ppermute(piece, 'seq', [(i, (i + k + 1) % spread) for i in range(spre...  3.88 us
  transfers between devices with their start and end apart: 18, of which 5 were waited for; matrix products, arithmetic and copies ran while one was open for 0% of the time, Pallas kernels for 32%

profile of v8, /device:TPU:0, one launch (start us, length us, event | category | flops | bytes accessed | tf_op | source)
XLA Modules:
  0.0 65.7 jit_solution(16966061770404885980)
XLA Ops:
  0.6 0.1 pad_add_fusion.refs_0_
  0.7 8.6 %front.2 = (bf16[1024,1024]{1,0:T(8,128)(2,1)S(1)}, bf16[1024,512]{1,0:T(8,128)(2,1)S(1)}, bf16[256,256]{1,0:T(8,128)(2,1)S(1)}, bf16[256,256]{1,0:T(8,128)(2,1)...) custom-call(s32[4]{0:T(128)S(1)} %pad_add_fusion.refs_0_, ...), custom_call_target="tpu_custom_call" | custom-call | flops 3221225472 | bytes 4194304 | tf_op jit(solution)/shard_map/front/pallas_call | solution.py:231
  9.4 0.5 collective-permute-start
  9.9 1.0 %collective-permute-done.b_ref = bf16[256,256]{1,0:T(8,128)(2,1)S(1)} collective-permute-done((bf16[256,256]{1,0:T(8,128)(2,1)S(1)}, bf16[256,256]{1,0:T(8,128)(2,1)S(1)}, u32[]{:S(2)}, u32[]{:S(2)}) %collective-permute-start) | collective-permute-done | bytes 131104 | tf_op jit(solution)/shard_map/ppermute | solution.py:519
  10.9 3.0 %collective-permute-start.2 = (bf16[256,256]{1,0:T(8,128)(2,1)S(1)}, bf16[256,256]{1,0:T(8,128)(2,1)S(1)}, u32[]{:S(2)}, u32[]{:S(2)}) collective-permute-start(bf16[256,256]{1,0:T(8,128)(2,1)S(1)} %add.53.a_ref), channel_id=1, source_target_pairs={{0,4},{4,0},{8,12},{12,8},{1,5},{5,1},{9,13},{13,9},{2,6},{6,2},{1... | collective-permute-start | bytes 393224 | tf_op jit(solution)/shard_map/ppermute | solution.py:519
  13.9 5.4 %front.3 = (bf16[1024,1024]{1,0:T(8,128)(2,1)S(1)}, bf16[1024,512]{1,0:T(8,128)(2,1)S(1)}, bf16[256,256]{1,0:T(8,128)(2,1)S(1)}, bf16[512,256]{1,0:T(8,128)(2,1)...) custom-call(s32[4]{0:T(128)S(1)} %get-tuple-element.59.refs_0_, ...), custom_call_target="tpu_custom_call", output_to_operand_aliasing={{0}: (1, {})} | custom-call | flops 3221225472 | bytes 4194304 | tf_op jit(solution)/shard_map/front/pallas_call | solution.py:231
  19.3 0.1 collective-permute-start.1
  19.4 0.8 %collective-permute-start.5 = (bf16[256,256]{1,0:T(8,128)(2,1)S(1)}, bf16[256,256]{1,0:T(8,128)(2,1)S(1)}, u32[]{:S(2)}, u32[]{:S(2)}) collective-permute-start(bf16[256,256]{1,0:T(8,128)(2,1)S(1)} %get-tuple-element.75), channel_id=1, source_target_pairs={{1,4},{5,8},{9,12},{4,1},{8,5},{12,9},{3,6},{7,10},{11,14},{6,3},{... | collective-permute-start | bytes 393224 | tf_op jit(solution)/shard_map/ppermute | solution.py:601
  20.2 0.0 collective-permute-done.2.b_ref
  20.3 0.0 copy-start.1
  20.3 3.9 %collective-permute-start.4 = (bf16[256,256]{1,0:T(8,128)(2,1)S(1)}, bf16[256,256]{1,0:T(8,128)(2,1)S(1)}, u32[]{:S(2)}, u32[]{:S(2)}) collective-permute-start(bf16[256,256]{1,0:T(8,128)(2,1)S(1)} %add.55.a_ref), channel_id=1, source_target_pairs={{0,8},{4,12},{8,0},{12,4},{1,9},{5,13},{9,1},{13,5},{2,10},{6,14},... | collective-permute-start | bytes 393224 | tf_op jit(solution)/shard_map/ppermute | solution.py:519
  24.2 0.0 collective-permute-done.1.b_ref.refs_2_.refs_1_
  24.3 2.2 %collective-permute-start.3 = (bf16[256,256]{1,0:T(8,128)(2,1)S(1)}, bf16[256,256]{1,0:T(8,128)(2,1)S(1)}, u32[]{:S(2)}, u32[]{:S(2)}) collective-permute-start(bf16[256,256]{1,0:T(8,128)(2,1)S(1)} %add.54.a_ref), channel_id=1, source_target_pairs={{0,4},{4,0},{8,12},{12,8},{1,5},{5,1},{9,13},{13,9},{2,6},{6,2},{1... | collective-permute-start | bytes 393224 | tf_op jit(solution)/shard_map/ppermute | solution.py:519
  26.4 0.0 collective-permute-done.5.refs_3_.refs_2_
  26.4 3.5 %near.2 = (bf16[1024,256]{1,0:T(8,128)(2,1)S(1)}, bf16[1024,256]{1,0:T(8,128)(2,1)S(1)}, f32[1024,512]{1,0:T(8,128)S(1)}, s32[4]{0:T(128)S(1)}) custom-call(s32[4]{0:T(128)S(1)} %get-tuple-element.73.ids_ref, bf16[1024,1024]{1,0:T(8,128)(2,1)S(1)} %get-tuple-element.74.refs_0_, bf16[1024,512]{1,0:T(8,128)(2,1)S(1)} %copy-done.1, ...), custom_call_target="tpu_custom_call" | custom-call | flops 1048576 | bytes 1024 | tf_op jit(solution)/shard_map/near/pallas_call | solution.py:320
  29.9 2.5 %collective-permute-done.4.b_ref = bf16[256,256]{1,0:T(8,128)(2,1)S(1)} collective-permute-done((bf16[256,256]{1,0:T(8,128)(2,1)S(1)}, bf16[256,256]{1,0:T(8,128)(2,1)S(1)}, u32[]{:S(2)}, u32[]{:S(2)}) %collective-permute-start.4) | collective-permute-done | bytes 131104 | tf_op jit(solution)/shard_map/ppermute | solution.py:519
  32.5 0.1 collective-permute-start.7
  32.6 0.0 collective-permute-done.3.b_ref
  32.6 2.0 %collective-permute-start.6 = (bf16[256,256]{1,0:T(8,128)(2,1)S(1)}, bf16[256,256]{1,0:T(8,128)(2,1)S(1)}, u32[]{:S(2)}, u32[]{:S(2)}) collective-permute-start(bf16[256,256]{1,0:T(8,128)(2,1)S(1)} %add.56.a_ref), channel_id=1, source_target_pairs={{0,8},{4,12},{8,0},{12,4},{1,9},{5,13},{9,1},{13,5},{2,10},{6,14},... | collective-permute-start | bytes 393224 | tf_op jit(solution)/shard_map/ppermute | solution.py:519
  34.7 1.6 %far.4 = (bf16[1024,128]{1,0:T(8,128)(2,1)S(1)}, s32[4]{0:T(128)S(1)}) custom-call(s32[4]{0:T(128)S(1)} %get-tuple-element.82.refs_0_, bf16[1024,256]{1,0:T(8,128)(2,1)S(1)} %get-tuple-element.83.refs_1_, f32[1024,512]{1,0:T(8,128)S(1)} %get-tuple-element.84.refs_2_, f32[4,512]{1,0:T(4,128)S(1)} %copy-done.2, bf16[256,256]{1,0:T(8,128)(2,1)S(1)} %add.57.refs_4_), custom_call_target="tpu_custom_call" | custom-call | flops 1048576 | bytes 1024 | tf_op jit(solution)/shard_map/far/pallas_call | solution.py:404
  36.3 1.6 %collective-permute-start.8 = (bf16[1024,128]{1,0:T(8,128)(2,1)S(1)}, bf16[1024,128]{1,0:T(8,128)(2,1)S(1)}, u32[]{:S(2)}, u32[]{:S(2)}) collective-permute-start(bf16[1024,128]{1,0:T(8,128)(2,1)S(1)} %get-tuple-element.95.refs_6_.refs_1_), channel_id=1, source_target_pairs={{0,2},{2,0},{1,3},{3,1},{4,6},{6,4},{5,7},{7,5},{8,10},{10,8},{9,1... | collective-permute-start | bytes 786440 | tf_op jit(solution)/shard_map/ppermute | solution.py:524
  37.8 0.0 collective-permute-done.7.refs_4_
  37.8 1.6 %far.5 = (bf16[1024,128]{1,0:T(8,128)(2,1)S(1)}, s32[4]{0:T(128)S(1)}) custom-call(s32[4]{0:T(128)S(1)} %get-tuple-element.86.refs_0_, bf16[1024,256]{1,0:T(8,128)(2,1)S(1)} %get-tuple-element.83.refs_1_, f32[1024,512]{1,0:T(8,128)S(1)} %get-tuple-element.84.refs_2_, f32[4,512]{1,0:T(4,128)S(1)} %copy-done.2, bf16[256,256]{1,0:T(8,128)(2,1)S(1)} %collective-permute-done.7.refs_4_), custom_call_target="tpu_custom_call" | custom-call | flops 1048576 | bytes 1024 | tf_op jit(solution)/shard_map/far/pallas_call | solution.py:404
  39.5 0.6 collective-permute-start.12
  40.1 2.2 %near.3 = (bf16[1024,256]{1,0:T(8,128)(2,1)S(1)}, f32[1024,512]{1,0:T(8,128)S(1)}, s32[4]{0:T(128)S(1)}) custom-call(s32[4]{0:T(128)S(1)} %get-tuple-element.87.ids_ref, bf16[1024,256]{1,0:T(8,128)(2,1)S(1)} %get-tuple-element.88.refs_0_, bf16[512,256]{1,0:T(8,128)(2,1)S(1)} %collective-permute-done.1.b_ref.refs_2_.refs_1_, ...), custom_call_target="tpu_custom_call", output_to_operand_aliasing={{0}: (1, {})} | custom-call | flops 1048576 | bytes 1024 | tf_op jit(solution)/shard_map/near/pallas_call | solution.py:320
  42.3 0.0 copy-start.3
  42.3 0.0 collective-permute-done.6.b_ref
  42.4 0.1 collective-permute-start.10
  42.4 3.1 %collective-permute-done.8.refs_5_ = bf16[1024,128]{1,0:T(8,128)(2,1)S(1)} collective-permute-done((bf16[1024,128]{1,0:T(8,128)(2,1)S(1)}, bf16[1024,128]{1,0:T(8,128)(2,1)S(1)}, u32[]{:S(2)}, u32[]{:S(2)}) %collective-permute-start.8) | collective-permute-done | bytes 262176 | tf_op jit(solution)/shard_map/ppermute | solution.py:524
  45.6 1.6 %far.6 = (bf16[1024,128]{1,0:T(8,128)(2,1)S(1)}, s32[4]{0:T(128)S(1)}) custom-call(s32[4]{0:T(128)S(1)} %get-tuple-element.91.refs_0_, bf16[1024,256]{1,0:T(8,128)(2,1)S(1)} %get-tuple-element.92.refs_1_, f32[1024,512]{1,0:T(8,128)S(1)} %get-tuple-element.93.refs_2_, f32[4,512]{1,0:T(4,128)S(1)} %copy-done.2, bf16[256,256]{1,0:T(8,128)(2,1)S(1)} %add.58.refs_4_, ...), custom_call_target="tpu_custom_call" | custom-call | flops 1048576 | bytes 1024 | tf_op jit(solution)/shard_map/far/pallas_call | solution.py:404
  47.2 0.0 copy-start
  47.3 2.2 %far.7 = (bf16[1024,128]{1,0:T(8,128)(2,1)S(1)}, f32[32,512]{1,0:T(8,128)S(1)}, bf16[32,512]{1,0:T(8,128)(2,1)S(1)}, s32[4]{0:T(128)}) custom-call(s32[4]{0:T(128)S(1)} %get-tuple-element.97.refs_0_, bf16[1024,256]{1,0:T(8,128)(2,1)S(1)} %get-tuple-element.92.refs_1_, f32[1024,512]{1,0:T(8,128)S(1)} %get-tuple-element.93.refs_2_, f32[4,512]{1,0:T(4,128)S(1)} %copy-done.2, ...), custom_call_target="tpu_custom_call" | custom-call | flops 1048576 | bytes 1024 | tf_op jit(solution)/shard_map/far/pallas_call | solution.py:404
  49.5 1.6 %collective-permute-start.11 = (bf16[1024,128]{1,0:T(8,128)(2,1)S(1)}, bf16[1024,128]{1,0:T(8,128)(2,1)S(1)}, u32[]{:S(2)}, u32[]{:S(2)}) collective-permute-start(bf16[1024,128]{1,0:T(8,128)(2,1)S(1)} %get-tuple-element.99.refs_4_), channel_id=1, source_target_pairs={{0,2},{2,0},{1,3},{3,1},{4,6},{6,4},{5,7},{7,5},{8,10},{10,8},{9,1... | collective-permute-start | bytes 786440 | tf_op jit(solution)/shard_map/ppermute | solution.py:524
  51.0 0.5 collective-permute-start.9
  51.6 1.2 %collective-permute-done.13.got_ref = bf16[32,512]{1,0:T(8,128)(2,1)S(1)} collective-permute-done((bf16[32,512]{1,0:T(8,128)(2,1)S(1)}, bf16[32,512]{1,0:T(8,128)(2,1)S(1)}, u32[]{:S(2)}, u32[]{:S(2)}) %collective-permute-start.13) | collective-permute-done | bytes 32800 | tf_op jit(solution)/shard_map/ppermute | solution.py:519
  52.8 1.2 %collective-permute-start.14 = (bf16[8,512]{1,0:T(8,128)(2,1)S(1)}, bf16[8,512]{1,0:T(8,128)(2,1)S(1)}, u32[]{:S(2)}, u32[]{:S(2)}) collective-permute-start(bf16[8,512]{1,0:T(8,128)(2,1)S(1)} %get-tuple-element.104), channel_id=1, source_target_pairs={{0,4},{4,8},{8,12},{12,0},{1,5},{5,9},{9,13},{13,1},{2,6},{6,10},{... | collective-permute-start | bytes 24584 | tf_op jit(solution)/shard_map/ppermute | solution.py:646
  54.0 0.2 collective-permute-start.15
  54.1 0.0 collective-permute-done.12.refs_6_
  54.1 2.5 %collective-permute-start.16 = (bf16[8,512]{1,0:T(8,128)(2,1)S(1)}, bf16[8,512]{1,0:T(8,128)(2,1)S(1)}, u32[]{:S(2)}, u32[]{:S(2)}) collective-permute-start(bf16[8,512]{1,0:T(8,128)(2,1)S(1)} %get-tuple-element.106), channel_id=1, source_target_pairs={{0,12},{4,0},{8,4},{12,8},{1,13},{5,1},{9,5},{13,9},{2,14},{6,2},{... | collective-permute-start | bytes 24584 | tf_op jit(solution)/shard_map/ppermute | solution.py:646
  56.7 0.1 add_add_fusion.1.refs_0_
  56.7 1.8 %out.2 = (f32[1024,512]{1,0:T(8,128)S(1)}, s32[1]{0:T(128)}) custom-call(s32[4]{0:T(128)S(1)} %add_add_fusion.1.refs_0_, bf16[1024,128]{1,0:T(8,128)(2,1)S(1)} %get-tuple-element.95.refs_6_.refs_1_, bf16[1024,128]{1,0:T(8,128)(2,1)S(1)} %get-tuple-element.98.refs_7_.refs_2_, bf16[1024,128]{1,0:T(8,128)(2,1)S(1)} %get-tuple-element.96.refs_8_.refs_3_, ...), custom_call_target="tpu_custom_call" | custom-call | flops 1048576 | bytes 1024 | tf_op jit(solution)/shard_map/out/pallas_call | solution.py:460
  59.2 0.0 collective-permute-done.14.refs_0_
  59.2 0.0 collective-permute-done.15.refs_1_
  59.3 0.6 pool_own.1.refs_3_
  59.8 1.6 %collective-permute-start.17 = (bf16[8,512]{1,0:T(8,128)(2,1)S(1)}, bf16[8,512]{1,0:T(8,128)(2,1)S(1)}, u32[]{:S(2)}, u32[]{:S(2)}) collective-permute-start(bf16[8,512]{1,0:T(8,128)(2,1)S(1)} %pool_own.1.refs_3_), channel_id=1, source_target_pairs={{0,2},{2,0},{1,3},{3,1},{4,6},{6,4},{5,7},{7,5},{8,10},{10,8},{9,1... | collective-permute-start | bytes 24584 | tf_op jit(solution)/shard_map/ppermute | solution.py:524
  61.4 0.1 add_add_fusion.refs_0_
  61.5 2.1 %collective-permute-done.17.refs_4_ = bf16[8,512]{1,0:T(8,128)(2,1)S(1)} collective-permute-done((bf16[8,512]{1,0:T(8,128)(2,1)S(1)}, bf16[8,512]{1,0:T(8,128)(2,1)S(1)}, u32[]{:S(2)}, u32[]{:S(2)}) %collective-permute-start.17) | collective-permute-done | bytes 8224 | tf_op jit(solution)/shard_map/ppermute | solution.py:524
  63.6 2.0 %out.3 = (bf16[1024,512]{1,0:T(8,128)(2,1)}, f32[8,512]{1,0:T(8,128)}, s32[1]{0:T(128)}) custom-call(s32[4]{0:T(128)S(1)} %add_add_fusion.refs_0_, bf16[1024,128]{1,0:T(8,128)(2,1)S(1)} %collective-permute-done.9.refs_1_, bf16[1024,128]{1,0:T(8,128)(2,1)S(1)} %collective-permute-done.11.refs_2_, bf16[8,512]{1,0:T(8,128)(2,1)S(1)} %pool_own.1.refs_3_, ...), custom_call_target="tpu_custom_call" | custom-call | flops 1048576 | bytes 1024 | tf_op jit(solution)/shard_map/out/pallas_call | solution.py:460
  (17 shorter events, 0.2 us)
Async XLA Ops:
  0.7 13.2 %copy-start.2 = (f32[4,512]{1,0:T(4,128)S(1)}, f32[4,512]{1,0:T(4,128)}, u32[]{:S(2)}) copy-start(f32[4,512]{1,0:T(4,128)} %refs_3_.9) | copy-start | bytes 24580
  9.4 1.5 %collective-permute-start = (bf16[256,256]{1,0:T(8,128)(2,1)S(1)}, bf16[256,256]{1,0:T(8,128)(2,1)S(1)}, u32[]{:S(2)}, u32[]{:S(2)}) collective-permute-start(bf16[256,256]{1,0:T(8,128)(2,1)S(1)} %get-tuple-element.57), channel_id=1, source_target_pairs={{0,1},{1,0},{2,3},{3,2},{4,5},{5,4},{6,7},{7,6},{8,9},{9,8},{10,11... | collective-permute-start | bytes 393224 | tf_op jit(solution)/shard_map/ppermute | solution.py:519
  10.9 9.3 %collective-permute-start.2 = (bf16[256,256]{1,0:T(8,128)(2,1)S(1)}, bf16[256,256]{1,0:T(8,128)(2,1)S(1)}, u32[]{:S(2)}, u32[]{:S(2)}) collective-permute-start(bf16[256,256]{1,0:T(8,128)(2,1)S(1)} %add.53.a_ref), channel_id=1, source_target_pairs={{0,4},{4,0},{8,12},{12,8},{1,5},{5,1},{9,13},{13,9},{2,6},{6,2},{1... | collective-permute-start | bytes 393224 | tf_op jit(solution)/shard_map/ppermute | solution.py:519
  19.3 4.9 %collective-permute-start.1 = (bf16[512,256]{1,0:T(8,128)(2,1)S(1)}, bf16[512,256]{1,0:T(8,128)(2,1)S(1)}, u32[]{:S(2)}, u32[]{:S(2)}) collective-permute-start(bf16[512,256]{1,0:T(8,128)(2,1)S(1)} %get-tuple-element.65), channel_id=1, source_target_pairs={{0,1},{1,0},{2,3},{3,2},{4,5},{5,4},{6,7},{7,6},{8,9},{9,8},{10,11... | collective-permute-start | bytes 786440 | tf_op jit(solution)/shard_map/ppermute | solution.py:519
  19.4 7.0 %collective-permute-start.5 = (bf16[256,256]{1,0:T(8,128)(2,1)S(1)}, bf16[256,256]{1,0:T(8,128)(2,1)S(1)}, u32[]{:S(2)}, u32[]{:S(2)}) collective-permute-start(bf16[256,256]{1,0:T(8,128)(2,1)S(1)} %get-tuple-element.75), channel_id=1, source_target_pairs={{1,4},{5,8},{9,12},{4,1},{8,5},{12,9},{3,6},{7,10},{11,14},{6,3},{... | collective-permute-start | bytes 393224 | tf_op jit(solution)/shard_map/ppermute | solution.py:601
  20.3 6.2 %copy-start.1 = (bf16[1024,512]{1,0:T(8,128)(2,1)S(1)}, bf16[1024,512]{1,0:T(8,128)(2,1)}, u32[]{:S(2)}) copy-start(bf16[1024,512]{1,0:T(8,128)(2,1)} %refs_1_.3) | copy-start | bytes 3145732
  20.3 12.1 %collective-permute-start.4 = (bf16[256,256]{1,0:T(8,128)(2,1)S(1)}, bf16[256,256]{1,0:T(8,128)(2,1)S(1)}, u32[]{:S(2)}, u32[]{:S(2)}) collective-permute-start(bf16[256,256]{1,0:T(8,128)(2,1)S(1)} %add.55.a_ref), channel_id=1, source_target_pairs={{0,8},{4,12},{8,0},{12,4},{1,9},{5,13},{9,1},{13,5},{2,10},{6,14},... | collective-permute-start | bytes 393224 | tf_op jit(solution)/shard_map/ppermute | solution.py:519
  24.3 8.3 %collective-permute-start.3 = (bf16[256,256]{1,0:T(8,128)(2,1)S(1)}, bf16[256,256]{1,0:T(8,128)(2,1)S(1)}, u32[]{:S(2)}, u32[]{:S(2)}) collective-permute-start(bf16[256,256]{1,0:T(8,128)(2,1)S(1)} %add.54.a_ref), channel_id=1, source_target_pairs={{0,4},{4,0},{8,12},{12,8},{1,5},{5,1},{9,13},{13,9},{2,6},{6,2},{1... | collective-permute-start | bytes 393224 | tf_op jit(solution)/shard_map/ppermute | solution.py:519
  32.5 5.4 %collective-permute-start.7 = (bf16[256,256]{1,0:T(8,128)(2,1)S(1)}, bf16[256,256]{1,0:T(8,128)(2,1)S(1)}, u32[]{:S(2)}, u32[]{:S(2)}) collective-permute-start(bf16[256,256]{1,0:T(8,128)(2,1)S(1)} %add.57.refs_4_), channel_id=1, source_target_pairs={{0,1},{1,0},{2,3},{3,2},{4,5},{5,4},{6,7},{7,6},{8,9},{9,8},{10,11... | collective-permute-start | bytes 393224 | tf_op jit(solution)/shard_map/ppermute | solution.py:519
  32.6 9.7 %collective-permute-start.6 = (bf16[256,256]{1,0:T(8,128)(2,1)S(1)}, bf16[256,256]{1,0:T(8,128)(2,1)S(1)}, u32[]{:S(2)}, u32[]{:S(2)}) collective-permute-start(bf16[256,256]{1,0:T(8,128)(2,1)S(1)} %add.56.a_ref), channel_id=1, source_target_pairs={{0,8},{4,12},{8,0},{12,4},{1,9},{5,13},{9,1},{13,5},{2,10},{6,14},... | collective-permute-start | bytes 393224 | tf_op jit(solution)/shard_map/ppermute | solution.py:519
  36.3 9.3 %collective-permute-start.8 = (bf16[1024,128]{1,0:T(8,128)(2,1)S(1)}, bf16[1024,128]{1,0:T(8,128)(2,1)S(1)}, u32[]{:S(2)}, u32[]{:S(2)}) collective-permute-start(bf16[1024,128]{1,0:T(8,128)(2,1)S(1)} %get-tuple-element.95.refs_6_.refs_1_), channel_id=1, source_target_pairs={{0,2},{2,0},{1,3},{3,1},{4,6},{6,4},{5,7},{7,5},{8,10},{10,8},{9,1... | collective-permute-start | bytes 786440 | tf_op jit(solution)/shard_map/ppermute | solution.py:524
  39.5 14.7 %collective-permute-start.12 = (bf16[1024,128]{1,0:T(8,128)(2,1)S(1)}, bf16[1024,128]{1,0:T(8,128)(2,1)S(1)}, u32[]{:S(2)}, u32[]{:S(2)}) collective-permute-start(bf16[1024,128]{1,0:T(8,128)(2,1)S(1)} %get-tuple-element.98.refs_7_.refs_2_), channel_id=1, source_target_pairs={{0,2},{2,0},{1,3},{3,1},{4,6},{6,4},{5,7},{7,5},{8,10},{10,8},{9,1... | collective-permute-start | bytes 786440 | tf_op jit(solution)/shard_map/ppermute | solution.py:524
  42.3 4.9 %copy-start.3 = (s32[64,2]{0,1:T(2,128)S(1)}, s32[64,2]{0,1:T(2,128)}, u32[]{:S(2)}) copy-start(s32[64,2]{0,1:T(2,128)} %param.17) | copy-start | bytes 1540
  42.4 4.9 %collective-permute-start.10 = (bf16[256,256]{1,0:T(8,128)(2,1)S(1)}, bf16[256,256]{1,0:T(8,128)(2,1)S(1)}, u32[]{:S(2)}, u32[]{:S(2)}) collective-permute-start(bf16[256,256]{1,0:T(8,128)(2,1)S(1)} %add.58.refs_4_), channel_id=1, source_target_pairs={{0,1},{1,0},{2,3},{3,2},{4,5},{5,4},{6,7},{7,6},{8,9},{9,8},{10,11... | collective-permute-start | bytes 393224 | tf_op jit(solution)/shard_map/ppermute | solution.py:519
  47.2 9.5 %copy-start = (bf16[1024,512]{1,0:T(8,128)(2,1)S(1)}, bf16[1024,512]{1,0:T(8,128)(2,1)}, u32[]{:S(2)}) copy-start(bf16[1024,512]{1,0:T(8,128)(2,1)} %refs_5_.3) | copy-start | bytes 3145732
  49.5 14.1 %collective-permute-start.11 = (bf16[1024,128]{1,0:T(8,128)(2,1)S(1)}, bf16[1024,128]{1,0:T(8,128)(2,1)S(1)}, u32[]{:S(2)}, u32[]{:S(2)}) collective-permute-start(bf16[1024,128]{1,0:T(8,128)(2,1)S(1)} %get-tuple-element.99.refs_4_), channel_id=1, source_target_pairs={{0,2},{2,0},{1,3},{3,1},{4,6},{6,4},{5,7},{7,5},{8,10},{10,8},{9,1... | collective-permute-start | bytes 786440 | tf_op jit(solution)/shard_map/ppermute | solution.py:524
  51.0 12.6 %collective-permute-start.9 = (bf16[1024,128]{1,0:T(8,128)(2,1)S(1)}, bf16[1024,128]{1,0:T(8,128)(2,1)S(1)}, u32[]{:S(2)}, u32[]{:S(2)}) collective-permute-start(bf16[1024,128]{1,0:T(8,128)(2,1)S(1)} %get-tuple-element.96.refs_8_.refs_3_), channel_id=1, source_target_pairs={{0,2},{2,0},{1,3},{3,1},{4,6},{6,4},{5,7},{7,5},{8,10},{10,8},{9,1... | collective-permute-start | bytes 786440 | tf_op jit(solution)/shard_map/ppermute | solution.py:524
  51.6 1.2 %collective-permute-start.13 = (bf16[32,512]{1,0:T(8,128)(2,1)S(1)}, bf16[32,512]{1,0:T(8,128)(2,1)S(1)}, u32[]{:S(2)}, u32[]{:S(2)}) collective-permute-start(bf16[32,512]{1,0:T(8,128)(2,1)S(1)} %get-tuple-element.102), channel_id=1, source_target_pairs={{0,1},{1,0},{2,3},{3,2},{4,5},{5,4},{6,7},{7,6},{8,9},{9,8},{10,11... | collective-permute-start | bytes 98312 | tf_op jit(solution)/shard_map/ppermute | solution.py:519
  52.8 6.4 %collective-permute-start.14 = (bf16[8,512]{1,0:T(8,128)(2,1)S(1)}, bf16[8,512]{1,0:T(8,128)(2,1)S(1)}, u32[]{:S(2)}, u32[]{:S(2)}) collective-permute-start(bf16[8,512]{1,0:T(8,128)(2,1)S(1)} %get-tuple-element.104), channel_id=1, source_target_pairs={{0,4},{4,8},{8,12},{12,0},{1,5},{5,9},{9,13},{13,1},{2,6},{6,10},{... | collective-permute-start | bytes 24584 | tf_op jit(solution)/shard_map/ppermute | solution.py:646
  54.0 5.3 %collective-permute-start.15 = (bf16[8,512]{1,0:T(8,128)(2,1)S(1)}, bf16[8,512]{1,0:T(8,128)(2,1)S(1)}, u32[]{:S(2)}, u32[]{:S(2)}) collective-permute-start(bf16[8,512]{1,0:T(8,128)(2,1)S(1)} %get-tuple-element.105), channel_id=1, source_target_pairs={{0,8},{4,12},{8,0},{12,4},{1,9},{5,13},{9,1},{13,5},{2,10},{6,14},... | collective-permute-start | bytes 24584 | tf_op jit(solution)/shard_map/ppermute | solution.py:646
  54.1 5.1 %collective-permute-start.16 = (bf16[8,512]{1,0:T(8,128)(2,1)S(1)}, bf16[8,512]{1,0:T(8,128)(2,1)S(1)}, u32[]{:S(2)}, u32[]{:S(2)}) collective-permute-start(bf16[8,512]{1,0:T(8,128)(2,1)S(1)} %get-tuple-element.106), channel_id=1, source_target_pairs={{0,12},{4,0},{8,4},{12,8},{1,13},{5,1},{9,5},{13,9},{2,14},{6,2},{... | collective-permute-start | bytes 24584 | tf_op jit(solution)/shard_map/ppermute | solution.py:646
  59.8 3.7 %collective-permute-start.17 = (bf16[8,512]{1,0:T(8,128)(2,1)S(1)}, bf16[8,512]{1,0:T(8,128)(2,1)S(1)}, u32[]{:S(2)}, u32[]{:S(2)}) collective-permute-start(bf16[8,512]{1,0:T(8,128)(2,1)S(1)} %pool_own.1.refs_3_), channel_id=1, source_target_pairs={{0,2},{2,0},{1,3},{3,1},{4,6},{6,4},{5,7},{7,5},{8,10},{10,8},{9,1... | collective-permute-start | bytes 24584 | tf_op jit(solution)/shard_map/ppermute | solution.py:524

commit v9 on v8

--- a/solution.py
+++ b/solution.py
@@ -615,18 +615,21 @@
         q = made[0]
         got, turn = tie((swap(mine[g], "seq", steps[-1]), turn))
         total = add_call(mine[g], got)
-        other = swap(total, "rep", 1)
-        if g == groups - 2:
-            for step in steps[:-1]:
-                got, turn = tie((swap(mine[-1], "seq", step), turn))
-                mine[-1] = add_call(mine[-1], got)
-            mine[-1], turn = tie((mine[-1], turn))
         out = []
-        calls = [("own", [total]), ("other", [other])] if pairs == 2 else [("all", [total, other])]
-        for part, halves in calls:
-            final = []
-            if g == groups - 1 and part != "own":
-                final = [bounds] + [piece for o in outs for piece in o] + out
+        for part in ("own", "other") if pairs == 2 else ("all",):
+            halves, final = [total], []
+            if part != "own":
+                if part == "other" and g < groups - 1:
+                    total, turn = tie((total, turn))
+                other = swap(total, "rep", 1)
+                halves = [other] if part == "other" else [total, other]
+                if g == groups - 2:
+                    for step in steps[:-1]:
+                        got, turn = tie((swap(mine[-1], "seq", step), turn))
+                        mine[-1] = add_call(mine[-1], got)
+                    mine[-1], turn = tie((mine[-1], turn))
+                if g == groups - 1:
+                    final = [bounds] + [piece for o in outs for piece in o] + out
             made, *sums, turn = far(pairs, g, part, spread, turn, q, near_sums, dual_gains, halves, arrived, final)
             arrived = []
             out.append(made)

time: 65.9 us -> 65.4 us (level)
  starting transfers between devices: 22.4 us -> 20.2 us
  waiting for transfers between devices: 10 us -> 11.8 us
    ppermute x9, waiting for transfers between devices: 4.75 us -> 8.73 us  [swap(): return lax.ppermute(values, axis, [(i, i ^ step) for i in range(count)])]
    ppermute x5, waiting for transfers between devices: 5.24 us -> 3.04 us  [across_heads(): lax.ppermute(values, 'head', [(i, (i + step) % count) for i in range(coun...]
    ppermute x9, starting transfers between devices: 11.9 us -> 10.5 us  [swap(): return lax.ppermute(values, axis, [(i, i ^ step) for i in range(count)])]
    ppermute x5, starting transfers between devices: 5.8 us -> 4.95 us  [across_heads(): lax.ppermute(values, 'head', [(i, (i + step) % count) for i in range(coun...]
where the time goes in v9:
time: 65.4 us; the launch traced here: 65.2 us
  Pallas kernels  31.4 us (48%)
  starting transfers between devices  20.2 us (31%)
  waiting for transfers between devices  11.8 us (18%)
  between operations  1.68 us (3%)
    pallas_call x2, Pallas kernels, front(): pl.pallas_call(functools.partial(front_kernel, first, last, group, pairs,...  14 us
    ppermute x9, starting transfers between devices, swap(): return lax.ppermute(values, axis, [(i, i ^ step) for i in range(count)])  10.5 us
    ppermute x9, waiting for transfers between devices, swap(): return lax.ppermute(values, axis, [(i, i ^ step) for i in range(count)])  8.73 us
    pallas_call x4, Pallas kernels, far(): pl.pallas_call(functools.partial(far_kernel, pairs, group, part, 256, spr...  7.07 us
    pallas_call x2, Pallas kernels, near(): pl.pallas_call(functools.partial(near_kernel, pairs, group, groups), in_s...  5.68 us
    ppermute x5, starting transfers between devices, across_heads(): lax.ppermute(values, 'head', [(i, (i + step) % count) for i in range(coun...  4.95 us
    ppermute x3, starting transfers between devices, per_device(): lax.ppermute(piece, 'seq', [(i, (i + k + 1) % spread) for i in range(spre...  3.87 us
    pallas_call x2, Pallas kernels, out_part(): pl.pallas_call(functools.partial(out_kernel, count, pairs, len(pooled)),...  3.77 us
  transfers between devices with their start and end apart: 18, of which 5 were waited for; matrix products, arithmetic and copies ran while one was open for 0% of the time, Pallas kernels for 32%

profile of v9, /device:TPU:0, one launch (start us, length us, event | category | flops | bytes accessed | tf_op | source)
XLA Modules:
  0.0 65.2 jit_solution(7927511667089744336)
XLA Ops:
  0.6 0.1 pad_add_fusion.refs_0_
  0.7 8.6 %front.2 = (bf16[1024,1024]{1,0:T(8,128)(2,1)S(1)}, bf16[1024,512]{1,0:T(8,128)(2,1)S(1)}, bf16[256,256]{1,0:T(8,128)(2,1)S(1)}, bf16[256,256]{1,0:T(8,128)(2,1)...) custom-call(s32[4]{0:T(128)S(1)} %pad_add_fusion.refs_0_, ...), custom_call_target="tpu_custom_call" | custom-call | flops 3221225472 | bytes 4194304 | tf_op jit(solution)/shard_map/front/pallas_call | solution.py:231
  9.4 0.5 collective-permute-start
  9.9 1.0 %collective-permute-done.b_ref = bf16[256,256]{1,0:T(8,128)(2,1)S(1)} collective-permute-done((bf16[256,256]{1,0:T(8,128)(2,1)S(1)}, bf16[256,256]{1,0:T(8,128)(2,1)S(1)}, u32[]{:S(2)}, u32[]{:S(2)}) %collective-permute-start) | collective-permute-done | bytes 131104 | tf_op jit(solution)/shard_map/ppermute | solution.py:519
  10.9 3.0 %collective-permute-start.2 = (bf16[256,256]{1,0:T(8,128)(2,1)S(1)}, bf16[256,256]{1,0:T(8,128)(2,1)S(1)}, u32[]{:S(2)}, u32[]{:S(2)}) collective-permute-start(bf16[256,256]{1,0:T(8,128)(2,1)S(1)} %add.53.a_ref), channel_id=1, source_target_pairs={{0,4},{4,0},{8,12},{12,8},{1,5},{5,1},{9,13},{13,9},{2,6},{6,2},{1... | collective-permute-start | bytes 393224 | tf_op jit(solution)/shard_map/ppermute | solution.py:519
  13.9 5.4 %front.3 = (bf16[1024,1024]{1,0:T(8,128)(2,1)S(1)}, bf16[1024,512]{1,0:T(8,128)(2,1)S(1)}, bf16[256,256]{1,0:T(8,128)(2,1)S(1)}, bf16[512,256]{1,0:T(8,128)(2,1)...) custom-call(s32[4]{0:T(128)S(1)} %get-tuple-element.61.refs_0_, ...), custom_call_target="tpu_custom_call", output_to_operand_aliasing={{0}: (1, {})} | custom-call | flops 3221225472 | bytes 4194304 | tf_op jit(solution)/shard_map/front/pallas_call | solution.py:231
  19.3 0.1 collective-permute-start.1
  19.4 0.8 %collective-permute-start.5 = (bf16[256,256]{1,0:T(8,128)(2,1)S(1)}, bf16[256,256]{1,0:T(8,128)(2,1)S(1)}, u32[]{:S(2)}, u32[]{:S(2)}) collective-permute-start(bf16[256,256]{1,0:T(8,128)(2,1)S(1)} %get-tuple-element.77), channel_id=1, source_target_pairs={{1,4},{5,8},{9,12},{4,1},{8,5},{12,9},{3,6},{7,10},{11,14},{6,3},{... | collective-permute-start | bytes 393224 | tf_op jit(solution)/shard_map/ppermute | solution.py:601
  20.3 0.0 copy-start.1
  20.3 3.9 %collective-permute-start.4 = (bf16[256,256]{1,0:T(8,128)(2,1)S(1)}, bf16[256,256]{1,0:T(8,128)(2,1)S(1)}, u32[]{:S(2)}, u32[]{:S(2)}) collective-permute-start(bf16[256,256]{1,0:T(8,128)(2,1)S(1)} %add.55.a_ref), channel_id=1, source_target_pairs={{0,8},{4,12},{8,0},{12,4},{1,9},{5,13},{9,1},{13,5},{2,10},{6,14},... | collective-permute-start | bytes 393224 | tf_op jit(solution)/shard_map/ppermute | solution.py:519
  24.3 2.2 %collective-permute-start.3 = (bf16[256,256]{1,0:T(8,128)(2,1)S(1)}, bf16[256,256]{1,0:T(8,128)(2,1)S(1)}, u32[]{:S(2)}, u32[]{:S(2)}) collective-permute-start(bf16[256,256]{1,0:T(8,128)(2,1)S(1)} %add.54.a_ref), channel_id=1, source_target_pairs={{0,4},{4,0},{8,12},{12,8},{1,5},{5,1},{9,13},{13,9},{2,6},{6,2},{1... | collective-permute-start | bytes 393224 | tf_op jit(solution)/shard_map/ppermute | solution.py:519
  26.4 3.5 %near.2 = (bf16[1024,256]{1,0:T(8,128)(2,1)S(1)}, bf16[1024,256]{1,0:T(8,128)(2,1)S(1)}, f32[1024,512]{1,0:T(8,128)S(1)}, s32[4]{0:T(128)S(1)}) custom-call(s32[4]{0:T(128)S(1)} %get-tuple-element.75.ids_ref, bf16[1024,1024]{1,0:T(8,128)(2,1)S(1)} %get-tuple-element.76.refs_0_, bf16[1024,512]{1,0:T(8,128)(2,1)S(1)} %copy-done.1, ...), custom_call_target="tpu_custom_call" | custom-call | flops 1048576 | bytes 1024 | tf_op jit(solution)/shard_map/near/pallas_call | solution.py:320
  29.9 2.5 %collective-permute-done.4.b_ref = bf16[256,256]{1,0:T(8,128)(2,1)S(1)} collective-permute-done((bf16[256,256]{1,0:T(8,128)(2,1)S(1)}, bf16[256,256]{1,0:T(8,128)(2,1)S(1)}, u32[]{:S(2)}, u32[]{:S(2)}) %collective-permute-start.4) | collective-permute-done | bytes 131104 | tf_op jit(solution)/shard_map/ppermute | solution.py:519
  32.5 1.6 %far.4 = (bf16[1024,128]{1,0:T(8,128)(2,1)S(1)}, s32[4]{0:T(128)S(1)}) custom-call(s32[4]{0:T(128)S(1)} %get-tuple-element.81.refs_0_, bf16[1024,256]{1,0:T(8,128)(2,1)S(1)} %get-tuple-element.82.refs_1_, f32[1024,512]{1,0:T(8,128)S(1)} %get-tuple-element.83.refs_2_, f32[4,512]{1,0:T(4,128)S(1)} %copy-done.2, bf16[256,256]{1,0:T(8,128)(2,1)S(1)} %add.56.refs_4_), custom_call_target="tpu_custom_call" | custom-call | flops 1048576 | bytes 1024 | tf_op jit(solution)/shard_map/far/pallas_call | solution.py:404
  34.1 0.1 collective-permute-start.7
  34.2 1.6 %collective-permute-start.8 = (bf16[1024,128]{1,0:T(8,128)(2,1)S(1)}, bf16[1024,128]{1,0:T(8,128)(2,1)S(1)}, u32[]{:S(2)}, u32[]{:S(2)}) collective-permute-start(bf16[1024,128]{1,0:T(8,128)(2,1)S(1)} %get-tuple-element.99.refs_6_.refs_1_), channel_id=1, source_target_pairs={{0,2},{2,0},{1,3},{3,1},{4,6},{6,4},{5,7},{7,5},{8,10},{10,8},{9,1... | collective-permute-start | bytes 786440 | tf_op jit(solution)/shard_map/ppermute | solution.py:524
  35.7 0.0 collective-permute-done.3.b_ref
  35.8 0.6 collective-permute-start.6
  36.4 0.0 collective-permute-done.7.refs_4_
  36.4 1.6 %far.5 = (bf16[1024,128]{1,0:T(8,128)(2,1)S(1)}, s32[4]{0:T(128)S(1)}) custom-call(s32[4]{0:T(128)S(1)} %get-tuple-element.89.refs_0_, bf16[1024,256]{1,0:T(8,128)(2,1)S(1)} %get-tuple-element.82.refs_1_, f32[1024,512]{1,0:T(8,128)S(1)} %get-tuple-element.83.refs_2_, f32[4,512]{1,0:T(4,128)S(1)} %copy-done.2, bf16[256,256]{1,0:T(8,128)(2,1)S(1)} %collective-permute-done.7.refs_4_), custom_call_target="tpu_custom_call" | custom-call | flops 1048576 | bytes 1024 | tf_op jit(solution)/shard_map/far/pallas_call | solution.py:404
  38.1 0.6 collective-permute-start.12
  38.7 2.2 %near.3 = (bf16[1024,256]{1,0:T(8,128)(2,1)S(1)}, f32[1024,512]{1,0:T(8,128)S(1)}, s32[4]{0:T(128)S(1)}) custom-call(s32[4]{0:T(128)S(1)} %get-tuple-element.91.ids_ref, bf16[1024,256]{1,0:T(8,128)(2,1)S(1)} %get-tuple-element.92.refs_0_, bf16[512,256]{1,0:T(8,128)(2,1)S(1)} %collective-permute-done.1.b_ref.refs_2_.refs_1_, ...), custom_call_target="tpu_custom_call", output_to_operand_aliasing={{0}: (1, {})} | custom-call | flops 1048576 | bytes 1024 | tf_op jit(solution)/shard_map/near/pallas_call | solution.py:320
  40.9 0.0 copy-start.3
  41.0 4.0 %collective-permute-done.6.b_ref = bf16[256,256]{1,0:T(8,128)(2,1)S(1)} collective-permute-done((bf16[256,256]{1,0:T(8,128)(2,1)S(1)}, bf16[256,256]{1,0:T(8,128)(2,1)S(1)}, u32[]{:S(2)}, u32[]{:S(2)}) %collective-permute-start.6) | collective-permute-done | bytes 131104 | tf_op jit(solution)/shard_map/ppermute | solution.py:519
  45.0 0.1 collective-permute-start.10
  45.1 1.6 %far.6 = (bf16[1024,128]{1,0:T(8,128)(2,1)S(1)}, s32[4]{0:T(128)S(1)}) custom-call(s32[4]{0:T(128)S(1)} %get-tuple-element.95.refs_0_, bf16[1024,256]{1,0:T(8,128)(2,1)S(1)} %get-tuple-element.96.refs_1_, f32[1024,512]{1,0:T(8,128)S(1)} %get-tuple-element.97.refs_2_, f32[4,512]{1,0:T(4,128)S(1)} %copy-done.2, bf16[256,256]{1,0:T(8,128)(2,1)S(1)} %add.58.refs_4_, ...), custom_call_target="tpu_custom_call" | custom-call | flops 1048576 | bytes 1024 | tf_op jit(solution)/shard_map/far/pallas_call | solution.py:404
  46.7 0.0 copy-start
  46.7 0.6 collective-permute-start.9
  47.3 0.0 collective-permute-done.10.refs_4_
  47.3 2.2 %far.7 = (bf16[1024,128]{1,0:T(8,128)(2,1)S(1)}, f32[32,512]{1,0:T(8,128)S(1)}, bf16[32,512]{1,0:T(8,128)(2,1)S(1)}, s32[4]{0:T(128)}) custom-call(s32[4]{0:T(128)S(1)} %get-tuple-element.101.refs_0_, bf16[1024,256]{1,0:T(8,128)(2,1)S(1)} %get-tuple-element.96.refs_1_, f32[1024,512]{1,0:T(8,128)S(1)} %get-tuple-element.97.refs_2_, f32[4,512]{1,0:T(4,128)S(1)} %copy-done.2, ...), custom_call_target="tpu_custom_call" | custom-call | flops 1048576 | bytes 1024 | tf_op jit(solution)/shard_map/far/pallas_call | solution.py:404
  49.5 1.5 %collective-permute-start.11 = (bf16[1024,128]{1,0:T(8,128)(2,1)S(1)}, bf16[1024,128]{1,0:T(8,128)(2,1)S(1)}, u32[]{:S(2)}, u32[]{:S(2)}) collective-permute-start(bf16[1024,128]{1,0:T(8,128)(2,1)S(1)} %get-tuple-element.103.refs_4_), channel_id=1, source_target_pairs={{0,2},{2,0},{1,3},{3,1},{4,6},{6,4},{5,7},{7,5},{8,10},{10,8},{9,1... | collective-permute-start | bytes 786440 | tf_op jit(solution)/shard_map/ppermute | solution.py:524
  51.1 0.0 collective-permute-start.13
  51.1 1.2 %collective-permute-done.13.got_ref = bf16[32,512]{1,0:T(8,128)(2,1)S(1)} collective-permute-done((bf16[32,512]{1,0:T(8,128)(2,1)S(1)}, bf16[32,512]{1,0:T(8,128)(2,1)S(1)}, u32[]{:S(2)}, u32[]{:S(2)}) %collective-permute-start.13) | collective-permute-done | bytes 32800 | tf_op jit(solution)/shard_map/ppermute | solution.py:519
  52.3 0.1 collective-permute-start.14
  52.4 1.9 %collective-permute-start.15 = (bf16[8,512]{1,0:T(8,128)(2,1)S(1)}, bf16[8,512]{1,0:T(8,128)(2,1)S(1)}, u32[]{:S(2)}, u32[]{:S(2)}) collective-permute-start(bf16[8,512]{1,0:T(8,128)(2,1)S(1)} %get-tuple-element.109), channel_id=1, source_target_pairs={{0,8},{4,12},{8,0},{12,4},{1,9},{5,13},{9,1},{13,5},{2,10},{6,14},... | collective-permute-start | bytes 24584 | tf_op jit(solution)/shard_map/ppermute | solution.py:649
  54.3 0.0 collective-permute-done.12.refs_6_
  54.3 1.9 %collective-permute-start.16 = (bf16[8,512]{1,0:T(8,128)(2,1)S(1)}, bf16[8,512]{1,0:T(8,128)(2,1)S(1)}, u32[]{:S(2)}, u32[]{:S(2)}) collective-permute-start(bf16[8,512]{1,0:T(8,128)(2,1)S(1)} %get-tuple-element.110), channel_id=1, source_target_pairs={{0,12},{4,0},{8,4},{12,8},{1,13},{5,1},{9,5},{13,9},{2,14},{6,2},{... | collective-permute-start | bytes 24584 | tf_op jit(solution)/shard_map/ppermute | solution.py:649
  56.2 0.1 add_add_fusion.1.refs_0_
  56.3 1.8 %out.2 = (f32[1024,512]{1,0:T(8,128)S(1)}, s32[1]{0:T(128)}) custom-call(s32[4]{0:T(128)S(1)} %add_add_fusion.1.refs_0_, bf16[1024,128]{1,0:T(8,128)(2,1)S(1)} %get-tuple-element.99.refs_6_.refs_1_, bf16[1024,128]{1,0:T(8,128)(2,1)S(1)} %get-tuple-element.102.refs_7_.refs_2_, bf16[1024,128]{1,0:T(8,128)(2,1)S(1)} %get-tuple-element.100.refs_8_.refs_3_, ...), custom_call_target="tpu_custom_call" | custom-call | flops 1048576 | bytes 1024 | tf_op jit(solution)/shard_map/out/pallas_call | solution.py:460
  58.8 0.0 collective-permute-done.15.refs_1_
  58.8 0.0 collective-permute-done.16.refs_2_
  58.8 0.6 pool_own.1.refs_3_
  59.4 0.6 collective-permute-start.17
  60.0 0.1 add_add_fusion.refs_0_
  60.1 3.0 %collective-permute-done.17.refs_4_ = bf16[8,512]{1,0:T(8,128)(2,1)S(1)} collective-permute-done((bf16[8,512]{1,0:T(8,128)(2,1)S(1)}, bf16[8,512]{1,0:T(8,128)(2,1)S(1)}, u32[]{:S(2)}, u32[]{:S(2)}) %collective-permute-start.17) | collective-permute-done | bytes 8224 | tf_op jit(solution)/shard_map/ppermute | solution.py:524
  63.1 0.0 collective-permute-done.9.refs_1_
  63.1 0.0 collective-permute-done.11.refs_2_
  63.1 2.0 %out.3 = (bf16[1024,512]{1,0:T(8,128)(2,1)}, f32[8,512]{1,0:T(8,128)}, s32[1]{0:T(128)}) custom-call(s32[4]{0:T(128)S(1)} %add_add_fusion.refs_0_, bf16[1024,128]{1,0:T(8,128)(2,1)S(1)} %collective-permute-done.9.refs_1_, bf16[1024,128]{1,0:T(8,128)(2,1)S(1)} %collective-permute-done.11.refs_2_, bf16[8,512]{1,0:T(8,128)(2,1)S(1)} %pool_own.1.refs_3_, ...), custom_call_target="tpu_custom_call" | custom-call | flops 1048576 | bytes 1024 | tf_op jit(solution)/shard_map/out/pallas_call | solution.py:460
  (17 shorter events, 0.2 us)
Async XLA Ops:
  0.7 13.2 %copy-start.2 = (f32[4,512]{1,0:T(4,128)S(1)}, f32[4,512]{1,0:T(4,128)}, u32[]{:S(2)}) copy-start(f32[4,512]{1,0:T(4,128)} %refs_3_.9) | copy-start | bytes 24580
  9.4 1.5 %collective-permute-start = (bf16[256,256]{1,0:T(8,128)(2,1)S(1)}, bf16[256,256]{1,0:T(8,128)(2,1)S(1)}, u32[]{:S(2)}, u32[]{:S(2)}) collective-permute-start(bf16[256,256]{1,0:T(8,128)(2,1)S(1)} %get-tuple-element.59), channel_id=1, source_target_pairs={{0,1},{1,0},{2,3},{3,2},{4,5},{5,4},{6,7},{7,6},{8,9},{9,8},{10,11... | collective-permute-start | bytes 393224 | tf_op jit(solution)/shard_map/ppermute | solution.py:519
  10.9 9.3 %collective-permute-start.2 = (bf16[256,256]{1,0:T(8,128)(2,1)S(1)}, bf16[256,256]{1,0:T(8,128)(2,1)S(1)}, u32[]{:S(2)}, u32[]{:S(2)}) collective-permute-start(bf16[256,256]{1,0:T(8,128)(2,1)S(1)} %add.53.a_ref), channel_id=1, source_target_pairs={{0,4},{4,0},{8,12},{12,8},{1,5},{5,1},{9,13},{13,9},{2,6},{6,2},{1... | collective-permute-start | bytes 393224 | tf_op jit(solution)/shard_map/ppermute | solution.py:519
  19.3 4.9 %collective-permute-start.1 = (bf16[512,256]{1,0:T(8,128)(2,1)S(1)}, bf16[512,256]{1,0:T(8,128)(2,1)S(1)}, u32[]{:S(2)}, u32[]{:S(2)}) collective-permute-start(bf16[512,256]{1,0:T(8,128)(2,1)S(1)} %get-tuple-element.67), channel_id=1, source_target_pairs={{0,1},{1,0},{2,3},{3,2},{4,5},{5,4},{6,7},{7,6},{8,9},{9,8},{10,11... | collective-permute-start | bytes 786440 | tf_op jit(solution)/shard_map/ppermute | solution.py:519
  19.4 7.0 %collective-permute-start.5 = (bf16[256,256]{1,0:T(8,128)(2,1)S(1)}, bf16[256,256]{1,0:T(8,128)(2,1)S(1)}, u32[]{:S(2)}, u32[]{:S(2)}) collective-permute-start(bf16[256,256]{1,0:T(8,128)(2,1)S(1)} %get-tuple-element.77), channel_id=1, source_target_pairs={{1,4},{5,8},{9,12},{4,1},{8,5},{12,9},{3,6},{7,10},{11,14},{6,3},{... | collective-permute-start | bytes 393224 | tf_op jit(solution)/shard_map/ppermute | solution.py:601
  20.3 6.2 %copy-start.1 = (bf16[1024,512]{1,0:T(8,128)(2,1)S(1)}, bf16[1024,512]{1,0:T(8,128)(2,1)}, u32[]{:S(2)}) copy-start(bf16[1024,512]{1,0:T(8,128)(2,1)} %refs_1_.3) | copy-start | bytes 3145732
  20.3 12.1 %collective-permute-start.4 = (bf16[256,256]{1,0:T(8,128)(2,1)S(1)}, bf16[256,256]{1,0:T(8,128)(2,1)S(1)}, u32[]{:S(2)}, u32[]{:S(2)}) collective-permute-start(bf16[256,256]{1,0:T(8,128)(2,1)S(1)} %add.55.a_ref), channel_id=1, source_target_pairs={{0,8},{4,12},{8,0},{12,4},{1,9},{5,13},{9,1},{13,5},{2,10},{6,14},... | collective-permute-start | bytes 393224 | tf_op jit(solution)/shard_map/ppermute | solution.py:519
  24.3 11.5 %collective-permute-start.3 = (bf16[256,256]{1,0:T(8,128)(2,1)S(1)}, bf16[256,256]{1,0:T(8,128)(2,1)S(1)}, u32[]{:S(2)}, u32[]{:S(2)}) collective-permute-start(bf16[256,256]{1,0:T(8,128)(2,1)S(1)} %add.54.a_ref), channel_id=1, source_target_pairs={{0,4},{4,0},{8,12},{12,8},{1,5},{5,1},{9,13},{13,9},{2,6},{6,2},{1... | collective-permute-start | bytes 393224 | tf_op jit(solution)/shard_map/ppermute | solution.py:519
  34.1 2.3 %collective-permute-start.7 = (bf16[256,256]{1,0:T(8,128)(2,1)S(1)}, bf16[256,256]{1,0:T(8,128)(2,1)S(1)}, u32[]{:S(2)}, u32[]{:S(2)}) collective-permute-start(bf16[256,256]{1,0:T(8,128)(2,1)S(1)} %add.56.refs_4_), channel_id=1, source_target_pairs={{0,1},{1,0},{2,3},{3,2},{4,5},{5,4},{6,7},{7,6},{8,9},{9,8},{10,11... | collective-permute-start | bytes 393224 | tf_op jit(solution)/shard_map/ppermute | solution.py:519
  34.2 10.9 %collective-permute-start.8 = (bf16[1024,128]{1,0:T(8,128)(2,1)S(1)}, bf16[1024,128]{1,0:T(8,128)(2,1)S(1)}, u32[]{:S(2)}, u32[]{:S(2)}) collective-permute-start(bf16[1024,128]{1,0:T(8,128)(2,1)S(1)} %get-tuple-element.99.refs_6_.refs_1_), channel_id=1, source_target_pairs={{0,2},{2,0},{1,3},{3,1},{4,6},{6,4},{5,7},{7,5},{8,10},{10,8},{9,1... | collective-permute-start | bytes 786440 | tf_op jit(solution)/shard_map/ppermute | solution.py:524
  35.8 9.1 %collective-permute-start.6 = (bf16[256,256]{1,0:T(8,128)(2,1)S(1)}, bf16[256,256]{1,0:T(8,128)(2,1)S(1)}, u32[]{:S(2)}, u32[]{:S(2)}) collective-permute-start(bf16[256,256]{1,0:T(8,128)(2,1)S(1)} %add.57.a_ref), channel_id=1, source_target_pairs={{0,8},{4,12},{8,0},{12,4},{1,9},{5,13},{9,1},{13,5},{2,10},{6,14},... | collective-permute-start | bytes 393224 | tf_op jit(solution)/shard_map/ppermute | solution.py:519
  38.1 16.2 %collective-permute-start.12 = (bf16[1024,128]{1,0:T(8,128)(2,1)S(1)}, bf16[1024,128]{1,0:T(8,128)(2,1)S(1)}, u32[]{:S(2)}, u32[]{:S(2)}) collective-permute-start(bf16[1024,128]{1,0:T(8,128)(2,1)S(1)} %get-tuple-element.102.refs_7_.refs_2_), channel_id=1, source_target_pairs={{0,2},{2,0},{1,3},{3,1},{4,6},{6,4},{5,7},{7,5},{8,10},{10,8},{9,1... | collective-permute-start | bytes 786440 | tf_op jit(solution)/shard_map/ppermute | solution.py:524
  40.9 6.4 %copy-start.3 = (s32[64,2]{0,1:T(2,128)S(1)}, s32[64,2]{0,1:T(2,128)}, u32[]{:S(2)}) copy-start(s32[64,2]{0,1:T(2,128)} %param.17) | copy-start | bytes 1540
  45.0 2.4 %collective-permute-start.10 = (bf16[256,256]{1,0:T(8,128)(2,1)S(1)}, bf16[256,256]{1,0:T(8,128)(2,1)S(1)}, u32[]{:S(2)}, u32[]{:S(2)}) collective-permute-start(bf16[256,256]{1,0:T(8,128)(2,1)S(1)} %add.58.refs_4_), channel_id=1, source_target_pairs={{0,1},{1,0},{2,3},{3,2},{4,5},{5,4},{6,7},{7,6},{8,9},{9,8},{10,11... | collective-permute-start | bytes 393224 | tf_op jit(solution)/shard_map/ppermute | solution.py:519
  46.7 9.6 %copy-start = (bf16[1024,512]{1,0:T(8,128)(2,1)S(1)}, bf16[1024,512]{1,0:T(8,128)(2,1)}, u32[]{:S(2)}) copy-start(bf16[1024,512]{1,0:T(8,128)(2,1)} %refs_5_.3) | copy-start | bytes 3145732
  46.7 16.4 %collective-permute-start.9 = (bf16[1024,128]{1,0:T(8,128)(2,1)S(1)}, bf16[1024,128]{1,0:T(8,128)(2,1)S(1)}, u32[]{:S(2)}, u32[]{:S(2)}) collective-permute-start(bf16[1024,128]{1,0:T(8,128)(2,1)S(1)} %get-tuple-element.100.refs_8_.refs_3_), channel_id=1, source_target_pairs={{0,2},{2,0},{1,3},{3,1},{4,6},{6,4},{5,7},{7,5},{8,10},{10,8},{9,1... | collective-permute-start | bytes 786440 | tf_op jit(solution)/shard_map/ppermute | solution.py:524
  49.5 13.6 %collective-permute-start.11 = (bf16[1024,128]{1,0:T(8,128)(2,1)S(1)}, bf16[1024,128]{1,0:T(8,128)(2,1)S(1)}, u32[]{:S(2)}, u32[]{:S(2)}) collective-permute-start(bf16[1024,128]{1,0:T(8,128)(2,1)S(1)} %get-tuple-element.103.refs_4_), channel_id=1, source_target_pairs={{0,2},{2,0},{1,3},{3,1},{4,6},{6,4},{5,7},{7,5},{8,10},{10,8},{9,1... | collective-permute-start | bytes 786440 | tf_op jit(solution)/shard_map/ppermute | solution.py:524
  51.1 1.2 %collective-permute-start.13 = (bf16[32,512]{1,0:T(8,128)(2,1)S(1)}, bf16[32,512]{1,0:T(8,128)(2,1)S(1)}, u32[]{:S(2)}, u32[]{:S(2)}) collective-permute-start(bf16[32,512]{1,0:T(8,128)(2,1)S(1)} %get-tuple-element.106), channel_id=1, source_target_pairs={{0,1},{1,0},{2,3},{3,2},{4,5},{5,4},{6,7},{7,6},{8,9},{9,8},{10,11... | collective-permute-start | bytes 98312 | tf_op jit(solution)/shard_map/ppermute | solution.py:519
  52.3 6.4 %collective-permute-start.14 = (bf16[8,512]{1,0:T(8,128)(2,1)S(1)}, bf16[8,512]{1,0:T(8,128)(2,1)S(1)}, u32[]{:S(2)}, u32[]{:S(2)}) collective-permute-start(bf16[8,512]{1,0:T(8,128)(2,1)S(1)} %get-tuple-element.108), channel_id=1, source_target_pairs={{0,4},{4,8},{8,12},{12,0},{1,5},{5,9},{9,13},{13,1},{2,6},{6,10},{... | collective-permute-start | bytes 24584 | tf_op jit(solution)/shard_map/ppermute | solution.py:649
  52.4 6.4 %collective-permute-start.15 = (bf16[8,512]{1,0:T(8,128)(2,1)S(1)}, bf16[8,512]{1,0:T(8,128)(2,1)S(1)}, u32[]{:S(2)}, u32[]{:S(2)}) collective-permute-start(bf16[8,512]{1,0:T(8,128)(2,1)S(1)} %get-tuple-element.109), channel_id=1, source_target_pairs={{0,8},{4,12},{8,0},{12,4},{1,9},{5,13},{9,1},{13,5},{2,10},{6,14},... | collective-permute-start | bytes 24584 | tf_op jit(solution)/shard_map/ppermute | solution.py:649
  54.3 4.5 %collective-permute-start.16 = (bf16[8,512]{1,0:T(8,128)(2,1)S(1)}, bf16[8,512]{1,0:T(8,128)(2,1)S(1)}, u32[]{:S(2)}, u32[]{:S(2)}) collective-permute-start(bf16[8,512]{1,0:T(8,128)(2,1)S(1)} %get-tuple-element.110), channel_id=1, source_target_pairs={{0,12},{4,0},{8,4},{12,8},{1,13},{5,1},{9,5},{13,9},{2,14},{6,2},{... | collective-permute-start | bytes 24584 | tf_op jit(solution)/shard_map/ppermute | solution.py:649
  59.4 3.7 %collective-permute-start.17 = (bf16[8,512]{1,0:T(8,128)(2,1)S(1)}, bf16[8,512]{1,0:T(8,128)(2,1)S(1)}, u32[]{:S(2)}, u32[]{:S(2)}) collective-permute-start(bf16[8,512]{1,0:T(8,128)(2,1)S(1)} %pool_own.1.refs_3_), channel_id=1, source_target_pairs={{0,2},{2,0},{1,3},{3,1},{4,6},{6,4},{5,7},{7,5},{8,10},{10,8},{9,1... | collective-permute-start | bytes 24584 | tf_op jit(solution)/shard_map/ppermute | solution.py:524

commit v10 on v9

--- a/solution.py
+++ b/solution.py
@@ -619,7 +619,7 @@
         for part in ("own", "other") if pairs == 2 else ("all",):
             halves, final = [total], []
             if part != "own":
-                if part == "other" and g < groups - 1:
+                if part == "other":
                     total, turn = tie((total, turn))
                 other = swap(total, "rep", 1)
                 halves = [other] if part == "other" else [total, other]

time: 65.4 us -> 65.6 us (level)
    ppermute x9, waiting for transfers between devices: 8.73 us -> 10 us  [swap(): return lax.ppermute(values, axis, [(i, i ^ step) for i in range(count)])]
    ppermute x5, waiting for transfers between devices: 3.04 us -> 2.32 us  [across_heads(): lax.ppermute(values, 'head', [(i, (i + step) % count) for i in range(coun...]
  transfers between devices with their start and end apart: 18 -> 18, of which waited for: 5 -> 7; matrix products, arithmetic and copies ran while one was open for 0% -> 0% of each run, Pallas kernels for 32% -> 32%
where the time goes in v10:
time: 65.6 us; the launch traced here: 65.5 us
  Pallas kernels  31.3 us (48%)
  starting transfers between devices  19.8 us (30%)
  waiting for transfers between devices  12.4 us (19%)
  between operations  1.68 us (3%)
    pallas_call x2, Pallas kernels, front(): pl.pallas_call(functools.partial(front_kernel, first, last, group, pairs,...  14 us
    ppermute x9, starting transfers between devices, swap(): return lax.ppermute(values, axis, [(i, i ^ step) for i in range(count)])  10.2 us
    ppermute x9, waiting for transfers between devices, swap(): return lax.ppermute(values, axis, [(i, i ^ step) for i in range(count)])  10 us
    pallas_call x4, Pallas kernels, far(): pl.pallas_call(functools.partial(far_kernel, pairs, group, part, 256, spr...  7.07 us
    pallas_call x2, Pallas kernels, near(): pl.pallas_call(functools.partial(near_kernel, pairs, group, groups), in_s...  5.68 us
    ppermute x5, starting transfers between devices, across_heads(): lax.ppermute(values, 'head', [(i, (i + step) % count) for i in range(coun...  4.87 us
    ppermute x3, starting transfers between devices, per_device(): lax.ppermute(piece, 'seq', [(i, (i + k + 1) % spread) for i in range(spre...  3.87 us
    pallas_call x2, Pallas kernels, out_part(): pl.pallas_call(functools.partial(out_kernel, count, pairs, len(pooled)),...  3.77 us
  transfers between devices with their start and end apart: 18, of which 7 were waited for; matrix products, arithmetic and copies ran while one was open for 0% of the time, Pallas kernels for 32%

profile of v10, /device:TPU:0, one launch (start us, length us, event | category | flops | bytes accessed | tf_op | source)
XLA Modules:
  0.0 65.5 jit_solution(14070523399728237751)
XLA Ops:
  0.6 0.1 pad_add_fusion.refs_0_
  0.7 8.6 %front.2 = (bf16[1024,1024]{1,0:T(8,128)(2,1)S(1)}, bf16[1024,512]{1,0:T(8,128)(2,1)S(1)}, bf16[256,256]{1,0:T(8,128)(2,1)S(1)}, bf16[256,256]{1,0:T(8,128)(2,1)...) custom-call(s32[4]{0:T(128)S(1)} %pad_add_fusion.refs_0_, ...), custom_call_target="tpu_custom_call" | custom-call | flops 3221225472 | bytes 4194304 | tf_op jit(solution)/shard_map/front/pallas_call | solution.py:231
  9.4 0.5 collective-permute-start
  9.9 1.0 %collective-permute-done.b_ref = bf16[256,256]{1,0:T(8,128)(2,1)S(1)} collective-permute-done((bf16[256,256]{1,0:T(8,128)(2,1)S(1)}, bf16[256,256]{1,0:T(8,128)(2,1)S(1)}, u32[]{:S(2)}, u32[]{:S(2)}) %collective-permute-start) | collective-permute-done | bytes 131104 | tf_op jit(solution)/shard_map/ppermute | solution.py:519
  10.9 3.0 %collective-permute-start.2 = (bf16[256,256]{1,0:T(8,128)(2,1)S(1)}, bf16[256,256]{1,0:T(8,128)(2,1)S(1)}, u32[]{:S(2)}, u32[]{:S(2)}) collective-permute-start(bf16[256,256]{1,0:T(8,128)(2,1)S(1)} %add.53.a_ref), channel_id=1, source_target_pairs={{0,4},{4,0},{8,12},{12,8},{1,5},{5,1},{9,13},{13,9},{2,6},{6,2},{1... | collective-permute-start | bytes 393224 | tf_op jit(solution)/shard_map/ppermute | solution.py:519
  13.9 5.4 %front.3 = (bf16[1024,1024]{1,0:T(8,128)(2,1)S(1)}, bf16[1024,512]{1,0:T(8,128)(2,1)S(1)}, bf16[256,256]{1,0:T(8,128)(2,1)S(1)}, bf16[512,256]{1,0:T(8,128)(2,1)...) custom-call(s32[4]{0:T(128)S(1)} %get-tuple-element.63.refs_0_, ...), custom_call_target="tpu_custom_call", output_to_operand_aliasing={{0}: (1, {})} | custom-call | flops 3221225472 | bytes 4194304 | tf_op jit(solution)/shard_map/front/pallas_call | solution.py:231
  19.3 0.1 collective-permute-start.1
  19.4 0.8 %collective-permute-start.5 = (bf16[256,256]{1,0:T(8,128)(2,1)S(1)}, bf16[256,256]{1,0:T(8,128)(2,1)S(1)}, u32[]{:S(2)}, u32[]{:S(2)}) collective-permute-start(bf16[256,256]{1,0:T(8,128)(2,1)S(1)} %get-tuple-element.79), channel_id=1, source_target_pairs={{1,4},{5,8},{9,12},{4,1},{8,5},{12,9},{3,6},{7,10},{11,14},{6,3},{... | collective-permute-start | bytes 393224 | tf_op jit(solution)/shard_map/ppermute | solution.py:601
  20.2 0.0 collective-permute-done.2.b_ref
  20.3 0.0 copy-start.1
  20.3 3.9 %collective-permute-start.4 = (bf16[256,256]{1,0:T(8,128)(2,1)S(1)}, bf16[256,256]{1,0:T(8,128)(2,1)S(1)}, u32[]{:S(2)}, u32[]{:S(2)}) collective-permute-start(bf16[256,256]{1,0:T(8,128)(2,1)S(1)} %add.55.a_ref), channel_id=1, source_target_pairs={{0,8},{4,12},{8,0},{12,4},{1,9},{5,13},{9,1},{13,5},{2,10},{6,14},... | collective-permute-start | bytes 393224 | tf_op jit(solution)/shard_map/ppermute | solution.py:519
  24.2 0.0 collective-permute-done.1.b_ref.refs_2_.refs_1_
  24.3 2.2 %collective-permute-start.3 = (bf16[256,256]{1,0:T(8,128)(2,1)S(1)}, bf16[256,256]{1,0:T(8,128)(2,1)S(1)}, u32[]{:S(2)}, u32[]{:S(2)}) collective-permute-start(bf16[256,256]{1,0:T(8,128)(2,1)S(1)} %add.54.a_ref), channel_id=1, source_target_pairs={{0,4},{4,0},{8,12},{12,8},{1,5},{5,1},{9,13},{13,9},{2,6},{6,2},{1... | collective-permute-start | bytes 393224 | tf_op jit(solution)/shard_map/ppermute | solution.py:519
  26.4 0.0 collective-permute-done.5.refs_3_.refs_2_
  26.4 3.5 %near.2 = (bf16[1024,256]{1,0:T(8,128)(2,1)S(1)}, bf16[1024,256]{1,0:T(8,128)(2,1)S(1)}, f32[1024,512]{1,0:T(8,128)S(1)}, s32[4]{0:T(128)S(1)}) custom-call(s32[4]{0:T(128)S(1)} %get-tuple-element.77.ids_ref, bf16[1024,1024]{1,0:T(8,128)(2,1)S(1)} %get-tuple-element.78.refs_0_, bf16[1024,512]{1,0:T(8,128)(2,1)S(1)} %copy-done.1, ...), custom_call_target="tpu_custom_call" | custom-call | flops 1048576 | bytes 1024 | tf_op jit(solution)/shard_map/near/pallas_call | solution.py:320
  29.9 2.5 %collective-permute-done.4.b_ref = bf16[256,256]{1,0:T(8,128)(2,1)S(1)} collective-permute-done((bf16[256,256]{1,0:T(8,128)(2,1)S(1)}, bf16[256,256]{1,0:T(8,128)(2,1)S(1)}, u32[]{:S(2)}, u32[]{:S(2)}) %collective-permute-start.4) | collective-permute-done | bytes 131104 | tf_op jit(solution)/shard_map/ppermute | solution.py:519
  32.5 1.6 %far.4 = (bf16[1024,128]{1,0:T(8,128)(2,1)S(1)}, s32[4]{0:T(128)S(1)}) custom-call(s32[4]{0:T(128)S(1)} %get-tuple-element.83.refs_0_, bf16[1024,256]{1,0:T(8,128)(2,1)S(1)} %get-tuple-element.84.refs_1_, f32[1024,512]{1,0:T(8,128)S(1)} %get-tuple-element.85.refs_2_, f32[4,512]{1,0:T(4,128)S(1)} %copy-done.2, bf16[256,256]{1,0:T(8,128)(2,1)S(1)} %add.56.refs_4_), custom_call_target="tpu_custom_call" | custom-call | flops 1048576 | bytes 1024 | tf_op jit(solution)/shard_map/far/pallas_call | solution.py:404
  34.1 1.6 %collective-permute-start.8 = (bf16[1024,128]{1,0:T(8,128)(2,1)S(1)}, bf16[1024,128]{1,0:T(8,128)(2,1)S(1)}, u32[]{:S(2)}, u32[]{:S(2)}) collective-permute-start(bf16[1024,128]{1,0:T(8,128)(2,1)S(1)} %get-tuple-element.101.refs_6_.refs_1_), channel_id=1, source_target_pairs={{0,2},{2,0},{1,3},{3,1},{4,6},{6,4},{5,7},{7,5},{8,10},{10,8},{9,1... | collective-permute-start | bytes 786440 | tf_op jit(solution)/shard_map/ppermute | solution.py:524
  35.7 0.0 collective-permute-start.7
  35.7 0.0 collective-permute-done.3.b_ref
  35.7 0.4 collective-permute-start.6
  36.2 0.9 %collective-permute-done.7.refs_4_ = bf16[256,256]{1,0:T(8,128)(2,1)S(1)} collective-permute-done((bf16[256,256]{1,0:T(8,128)(2,1)S(1)}, bf16[256,256]{1,0:T(8,128)(2,1)S(1)}, u32[]{:S(2)}, u32[]{:S(2)}) %collective-permute-start.7) | collective-permute-done | bytes 131104 | tf_op jit(solution)/shard_map/ppermute | solution.py:519
  37.0 1.6 %far.5 = (bf16[1024,128]{1,0:T(8,128)(2,1)S(1)}, s32[4]{0:T(128)S(1)}) custom-call(s32[4]{0:T(128)S(1)} %get-tuple-element.91.refs_0_, bf16[1024,256]{1,0:T(8,128)(2,1)S(1)} %get-tuple-element.84.refs_1_, f32[1024,512]{1,0:T(8,128)S(1)} %get-tuple-element.85.refs_2_, f32[4,512]{1,0:T(4,128)S(1)} %copy-done.2, bf16[256,256]{1,0:T(8,128)(2,1)S(1)} %collective-permute-done.7.refs_4_), custom_call_target="tpu_custom_call" | custom-call | flops 1048576 | bytes 1024 | tf_op jit(solution)/shard_map/far/pallas_call | solution.py:404
  38.6 0.6 collective-permute-start.12
  39.3 2.2 %near.3 = (bf16[1024,256]{1,0:T(8,128)(2,1)S(1)}, f32[1024,512]{1,0:T(8,128)S(1)}, s32[4]{0:T(128)S(1)}) custom-call(s32[4]{0:T(128)S(1)} %get-tuple-element.93.ids_ref, bf16[1024,256]{1,0:T(8,128)(2,1)S(1)} %get-tuple-element.94.refs_0_, bf16[512,256]{1,0:T(8,128)(2,1)S(1)} %collective-permute-done.1.b_ref.refs_2_.refs_1_, ...), custom_call_target="tpu_custom_call", output_to_operand_aliasing={{0}: (1, {})} | custom-call | flops 1048576 | bytes 1024 | tf_op jit(solution)/shard_map/near/pallas_call | solution.py:320
  41.5 0.0 copy-start.3
  41.5 3.7 %collective-permute-done.6.b_ref = bf16[256,256]{1,0:T(8,128)(2,1)S(1)} collective-permute-done((bf16[256,256]{1,0:T(8,128)(2,1)S(1)}, bf16[256,256]{1,0:T(8,128)(2,1)S(1)}, u32[]{:S(2)}, u32[]{:S(2)}) %collective-permute-start.6) | collective-permute-done | bytes 131104 | tf_op jit(solution)/shard_map/ppermute | solution.py:519
  45.2 0.0 collective-permute-done.8.refs_5_
  45.2 1.6 %far.6 = (bf16[1024,128]{1,0:T(8,128)(2,1)S(1)}, s32[4]{0:T(128)S(1)}) custom-call(s32[4]{0:T(128)S(1)} %get-tuple-element.97.refs_0_, bf16[1024,256]{1,0:T(8,128)(2,1)S(1)} %get-tuple-element.98.refs_1_, f32[1024,512]{1,0:T(8,128)S(1)} %get-tuple-element.99.refs_2_, f32[4,512]{1,0:T(4,128)S(1)} %copy-done.2, bf16[256,256]{1,0:T(8,128)(2,1)S(1)} %add.58.refs_4_, ...), custom_call_target="tpu_custom_call" | custom-call | flops 1048576 | bytes 1024 | tf_op jit(solution)/shard_map/far/pallas_call | solution.py:404
  46.9 0.0 copy-start
  46.9 0.1 collective-permute-start.10
  47.0 0.6 collective-permute-start.9
  47.6 0.7 %collective-permute-done.10.refs_4_ = bf16[256,256]{1,0:T(8,128)(2,1)S(1)} collective-permute-done((bf16[256,256]{1,0:T(8,128)(2,1)S(1)}, bf16[256,256]{1,0:T(8,128)(2,1)S(1)}, u32[]{:S(2)}, u32[]{:S(2)}) %collective-permute-start.10) | collective-permute-done | bytes 131104 | tf_op jit(solution)/shard_map/ppermute | solution.py:519
  48.3 2.2 %far.7 = (bf16[1024,128]{1,0:T(8,128)(2,1)S(1)}, f32[32,512]{1,0:T(8,128)S(1)}, bf16[32,512]{1,0:T(8,128)(2,1)S(1)}, s32[4]{0:T(128)}) custom-call(s32[4]{0:T(128)S(1)} %get-tuple-element.104.refs_0_, bf16[1024,256]{1,0:T(8,128)(2,1)S(1)} %get-tuple-element.98.refs_1_, f32[1024,512]{1,0:T(8,128)S(1)} %get-tuple-element.99.refs_2_, f32[4,512]{1,0:T(4,128)S(1)} %copy-done.2, ...), custom_call_target="tpu_custom_call" | custom-call | flops 1048576 | bytes 1024 | tf_op jit(solution)/shard_map/far/pallas_call | solution.py:404
  50.5 0.8 %collective-permute-start.11 = (bf16[1024,128]{1,0:T(8,128)(2,1)S(1)}, bf16[1024,128]{1,0:T(8,128)(2,1)S(1)}, u32[]{:S(2)}, u32[]{:S(2)}) collective-permute-start(bf16[1024,128]{1,0:T(8,128)(2,1)S(1)} %get-tuple-element.107.refs_4_), channel_id=1, source_target_pairs={{0,2},{2,0},{1,3},{3,1},{4,6},{6,4},{5,7},{7,5},{8,10},{10,8},{9,1... | collective-permute-start | bytes 786440 | tf_op jit(solution)/shard_map/ppermute | solution.py:524
  51.3 0.0 collective-permute-start.13
  51.3 1.2 %collective-permute-done.13.got_ref = bf16[32,512]{1,0:T(8,128)(2,1)S(1)} collective-permute-done((bf16[32,512]{1,0:T(8,128)(2,1)S(1)}, bf16[32,512]{1,0:T(8,128)(2,1)S(1)}, u32[]{:S(2)}, u32[]{:S(2)}) %collective-permute-start.13) | collective-permute-done | bytes 32800 | tf_op jit(solution)/shard_map/ppermute | solution.py:519
  52.6 0.1 collective-permute-start.14
  52.6 1.9 %collective-permute-start.15 = (bf16[8,512]{1,0:T(8,128)(2,1)S(1)}, bf16[8,512]{1,0:T(8,128)(2,1)S(1)}, u32[]{:S(2)}, u32[]{:S(2)}) collective-permute-start(bf16[8,512]{1,0:T(8,128)(2,1)S(1)} %get-tuple-element.113), channel_id=1, source_target_pairs={{0,8},{4,12},{8,0},{12,4},{1,9},{5,13},{9,1},{13,5},{2,10},{6,14},... | collective-permute-start | bytes 24584 | tf_op jit(solution)/shard_map/ppermute | solution.py:649
  54.6 1.9 %collective-permute-start.16 = (bf16[8,512]{1,0:T(8,128)(2,1)S(1)}, bf16[8,512]{1,0:T(8,128)(2,1)S(1)}, u32[]{:S(2)}, u32[]{:S(2)}) collective-permute-start(bf16[8,512]{1,0:T(8,128)(2,1)S(1)} %get-tuple-element.114), channel_id=1, source_target_pairs={{0,12},{4,0},{8,4},{12,8},{1,13},{5,1},{9,5},{13,9},{2,14},{6,2},{... | collective-permute-start | bytes 24584 | tf_op jit(solution)/shard_map/ppermute | solution.py:649
  56.4 0.1 add_add_fusion.1.refs_0_
  56.5 1.8 %out.2 = (f32[1024,512]{1,0:T(8,128)S(1)}, s32[1]{0:T(128)}) custom-call(s32[4]{0:T(128)S(1)} %add_add_fusion.1.refs_0_, bf16[1024,128]{1,0:T(8,128)(2,1)S(1)} %get-tuple-element.101.refs_6_.refs_1_, bf16[1024,128]{1,0:T(8,128)(2,1)S(1)} %get-tuple-element.106.refs_7_.refs_2_, bf16[1024,128]{1,0:T(8,128)(2,1)S(1)} %get-tuple-element.102.refs_8_.refs_3_, ...), custom_call_target="tpu_custom_call" | custom-call | flops 1048576 | bytes 1024 | tf_op jit(solution)/shard_map/out/pallas_call | solution.py:460
  59.0 0.0 collective-permute-done.15.refs_1_
  59.0 0.6 pool_own.1.refs_3_
  59.6 1.3 %collective-permute-start.17 = (bf16[8,512]{1,0:T(8,128)(2,1)S(1)}, bf16[8,512]{1,0:T(8,128)(2,1)S(1)}, u32[]{:S(2)}, u32[]{:S(2)}) collective-permute-start(bf16[8,512]{1,0:T(8,128)(2,1)S(1)} %pool_own.1.refs_3_), channel_id=1, source_target_pairs={{0,2},{2,0},{1,3},{3,1},{4,6},{6,4},{5,7},{7,5},{8,10},{10,8},{9,1... | collective-permute-start | bytes 24584 | tf_op jit(solution)/shard_map/ppermute | solution.py:524
  61.0 0.1 add_add_fusion.refs_0_
  61.0 2.3 %collective-permute-done.17.refs_4_ = bf16[8,512]{1,0:T(8,128)(2,1)S(1)} collective-permute-done((bf16[8,512]{1,0:T(8,128)(2,1)S(1)}, bf16[8,512]{1,0:T(8,128)(2,1)S(1)}, u32[]{:S(2)}, u32[]{:S(2)}) %collective-permute-start.17) | collective-permute-done | bytes 8224 | tf_op jit(solution)/shard_map/ppermute | solution.py:524
  63.4 2.0 %out.3 = (bf16[1024,512]{1,0:T(8,128)(2,1)}, f32[8,512]{1,0:T(8,128)}, s32[1]{0:T(128)}) custom-call(s32[4]{0:T(128)S(1)} %add_add_fusion.refs_0_, bf16[1024,128]{1,0:T(8,128)(2,1)S(1)} %collective-permute-done.9.refs_1_, bf16[1024,128]{1,0:T(8,128)(2,1)S(1)} %collective-permute-done.11.refs_2_, bf16[8,512]{1,0:T(8,128)(2,1)S(1)} %pool_own.1.refs_3_, ...), custom_call_target="tpu_custom_call" | custom-call | flops 1048576 | bytes 1024 | tf_op jit(solution)/shard_map/out/pallas_call | solution.py:460
  (17 shorter events, 0.2 us)
Async XLA Ops:
  0.7 13.2 %copy-start.2 = (f32[4,512]{1,0:T(4,128)S(1)}, f32[4,512]{1,0:T(4,128)}, u32[]{:S(2)}) copy-start(f32[4,512]{1,0:T(4,128)} %refs_3_.9) | copy-start | bytes 24580
  9.4 1.5 %collective-permute-start = (bf16[256,256]{1,0:T(8,128)(2,1)S(1)}, bf16[256,256]{1,0:T(8,128)(2,1)S(1)}, u32[]{:S(2)}, u32[]{:S(2)}) collective-permute-start(bf16[256,256]{1,0:T(8,128)(2,1)S(1)} %get-tuple-element.61), channel_id=1, source_target_pairs={{0,1},{1,0},{2,3},{3,2},{4,5},{5,4},{6,7},{7,6},{8,9},{9,8},{10,11... | collective-permute-start | bytes 393224 | tf_op jit(solution)/shard_map/ppermute | solution.py:519
  10.9 9.3 %collective-permute-start.2 = (bf16[256,256]{1,0:T(8,128)(2,1)S(1)}, bf16[256,256]{1,0:T(8,128)(2,1)S(1)}, u32[]{:S(2)}, u32[]{:S(2)}) collective-permute-start(bf16[256,256]{1,0:T(8,128)(2,1)S(1)} %add.53.a_ref), channel_id=1, source_target_pairs={{0,4},{4,0},{8,12},{12,8},{1,5},{5,1},{9,13},{13,9},{2,6},{6,2},{1... | collective-permute-start | bytes 393224 | tf_op jit(solution)/shard_map/ppermute | solution.py:519
  19.3 4.9 %collective-permute-start.1 = (bf16[512,256]{1,0:T(8,128)(2,1)S(1)}, bf16[512,256]{1,0:T(8,128)(2,1)S(1)}, u32[]{:S(2)}, u32[]{:S(2)}) collective-permute-start(bf16[512,256]{1,0:T(8,128)(2,1)S(1)} %get-tuple-element.69), channel_id=1, source_target_pairs={{0,1},{1,0},{2,3},{3,2},{4,5},{5,4},{6,7},{7,6},{8,9},{9,8},{10,11... | collective-permute-start | bytes 786440 | tf_op jit(solution)/shard_map/ppermute | solution.py:519
  19.4 7.0 %collective-permute-start.5 = (bf16[256,256]{1,0:T(8,128)(2,1)S(1)}, bf16[256,256]{1,0:T(8,128)(2,1)S(1)}, u32[]{:S(2)}, u32[]{:S(2)}) collective-permute-start(bf16[256,256]{1,0:T(8,128)(2,1)S(1)} %get-tuple-element.79), channel_id=1, source_target_pairs={{1,4},{5,8},{9,12},{4,1},{8,5},{12,9},{3,6},{7,10},{11,14},{6,3},{... | collective-permute-start | bytes 393224 | tf_op jit(solution)/shard_map/ppermute | solution.py:601
  20.3 6.2 %copy-start.1 = (bf16[1024,512]{1,0:T(8,128)(2,1)S(1)}, bf16[1024,512]{1,0:T(8,128)(2,1)}, u32[]{:S(2)}) copy-start(bf16[1024,512]{1,0:T(8,128)(2,1)} %refs_1_.3) | copy-start | bytes 3145732
  20.3 12.1 %collective-permute-start.4 = (bf16[256,256]{1,0:T(8,128)(2,1)S(1)}, bf16[256,256]{1,0:T(8,128)(2,1)S(1)}, u32[]{:S(2)}, u32[]{:S(2)}) collective-permute-start(bf16[256,256]{1,0:T(8,128)(2,1)S(1)} %add.55.a_ref), channel_id=1, source_target_pairs={{0,8},{4,12},{8,0},{12,4},{1,9},{5,13},{9,1},{13,5},{2,10},{6,14},... | collective-permute-start | bytes 393224 | tf_op jit(solution)/shard_map/ppermute | solution.py:519
  24.3 11.4 %collective-permute-start.3 = (bf16[256,256]{1,0:T(8,128)(2,1)S(1)}, bf16[256,256]{1,0:T(8,128)(2,1)S(1)}, u32[]{:S(2)}, u32[]{:S(2)}) collective-permute-start(bf16[256,256]{1,0:T(8,128)(2,1)S(1)} %add.54.a_ref), channel_id=1, source_target_pairs={{0,4},{4,0},{8,12},{12,8},{1,5},{5,1},{9,13},{13,9},{2,6},{6,2},{1... | collective-permute-start | bytes 393224 | tf_op jit(solution)/shard_map/ppermute | solution.py:519
  34.1 11.1 %collective-permute-start.8 = (bf16[1024,128]{1,0:T(8,128)(2,1)S(1)}, bf16[1024,128]{1,0:T(8,128)(2,1)S(1)}, u32[]{:S(2)}, u32[]{:S(2)}) collective-permute-start(bf16[1024,128]{1,0:T(8,128)(2,1)S(1)} %get-tuple-element.101.refs_6_.refs_1_), channel_id=1, source_target_pairs={{0,2},{2,0},{1,3},{3,1},{4,6},{6,4},{5,7},{7,5},{8,10},{10,8},{9,1... | collective-permute-start | bytes 786440 | tf_op jit(solution)/shard_map/ppermute | solution.py:524
  35.7 1.3 %collective-permute-start.7 = (bf16[256,256]{1,0:T(8,128)(2,1)S(1)}, bf16[256,256]{1,0:T(8,128)(2,1)S(1)}, u32[]{:S(2)}, u32[]{:S(2)}) collective-permute-start(bf16[256,256]{1,0:T(8,128)(2,1)S(1)} %add.56.refs_4_), channel_id=1, source_target_pairs={{0,1},{1,0},{2,3},{3,2},{4,5},{5,4},{6,7},{7,6},{8,9},{9,8},{10,11... | collective-permute-start | bytes 393224 | tf_op jit(solution)/shard_map/ppermute | solution.py:519
  35.7 9.5 %collective-permute-start.6 = (bf16[256,256]{1,0:T(8,128)(2,1)S(1)}, bf16[256,256]{1,0:T(8,128)(2,1)S(1)}, u32[]{:S(2)}, u32[]{:S(2)}) collective-permute-start(bf16[256,256]{1,0:T(8,128)(2,1)S(1)} %add.57.a_ref), channel_id=1, source_target_pairs={{0,8},{4,12},{8,0},{12,4},{1,9},{5,13},{9,1},{13,5},{2,10},{6,14},... | collective-permute-start | bytes 393224 | tf_op jit(solution)/shard_map/ppermute | solution.py:519
  38.6 15.9 %collective-permute-start.12 = (bf16[1024,128]{1,0:T(8,128)(2,1)S(1)}, bf16[1024,128]{1,0:T(8,128)(2,1)S(1)}, u32[]{:S(2)}, u32[]{:S(2)}) collective-permute-start(bf16[1024,128]{1,0:T(8,128)(2,1)S(1)} %get-tuple-element.106.refs_7_.refs_2_), channel_id=1, source_target_pairs={{0,2},{2,0},{1,3},{3,1},{4,6},{6,4},{5,7},{7,5},{8,10},{10,8},{9,1... | collective-permute-start | bytes 786440 | tf_op jit(solution)/shard_map/ppermute | solution.py:524
  41.5 6.8 %copy-start.3 = (s32[64,2]{0,1:T(2,128)S(1)}, s32[64,2]{0,1:T(2,128)}, u32[]{:S(2)}) copy-start(s32[64,2]{0,1:T(2,128)} %param.17) | copy-start | bytes 1540
  46.9 9.6 %copy-start = (bf16[1024,512]{1,0:T(8,128)(2,1)S(1)}, bf16[1024,512]{1,0:T(8,128)(2,1)}, u32[]{:S(2)}) copy-start(bf16[1024,512]{1,0:T(8,128)(2,1)} %refs_5_.3) | copy-start | bytes 3145732
  46.9 1.4 %collective-permute-start.10 = (bf16[256,256]{1,0:T(8,128)(2,1)S(1)}, bf16[256,256]{1,0:T(8,128)(2,1)S(1)}, u32[]{:S(2)}, u32[]{:S(2)}) collective-permute-start(bf16[256,256]{1,0:T(8,128)(2,1)S(1)} %add.58.refs_4_), channel_id=1, source_target_pairs={{0,1},{1,0},{2,3},{3,2},{4,5},{5,4},{6,7},{7,6},{8,9},{9,8},{10,11... | collective-permute-start | bytes 393224 | tf_op jit(solution)/shard_map/ppermute | solution.py:519
  47.0 16.3 %collective-permute-start.9 = (bf16[1024,128]{1,0:T(8,128)(2,1)S(1)}, bf16[1024,128]{1,0:T(8,128)(2,1)S(1)}, u32[]{:S(2)}, u32[]{:S(2)}) collective-permute-start(bf16[1024,128]{1,0:T(8,128)(2,1)S(1)} %get-tuple-element.102.refs_8_.refs_3_), channel_id=1, source_target_pairs={{0,2},{2,0},{1,3},{3,1},{4,6},{6,4},{5,7},{7,5},{8,10},{10,8},{9,1... | collective-permute-start | bytes 786440 | tf_op jit(solution)/shard_map/ppermute | solution.py:524
  50.5 12.8 %collective-permute-start.11 = (bf16[1024,128]{1,0:T(8,128)(2,1)S(1)}, bf16[1024,128]{1,0:T(8,128)(2,1)S(1)}, u32[]{:S(2)}, u32[]{:S(2)}) collective-permute-start(bf16[1024,128]{1,0:T(8,128)(2,1)S(1)} %get-tuple-element.107.refs_4_), channel_id=1, source_target_pairs={{0,2},{2,0},{1,3},{3,1},{4,6},{6,4},{5,7},{7,5},{8,10},{10,8},{9,1... | collective-permute-start | bytes 786440 | tf_op jit(solution)/shard_map/ppermute | solution.py:524
  51.3 1.2 %collective-permute-start.13 = (bf16[32,512]{1,0:T(8,128)(2,1)S(1)}, bf16[32,512]{1,0:T(8,128)(2,1)S(1)}, u32[]{:S(2)}, u32[]{:S(2)}) collective-permute-start(bf16[32,512]{1,0:T(8,128)(2,1)S(1)} %get-tuple-element.110), channel_id=1, source_target_pairs={{0,1},{1,0},{2,3},{3,2},{4,5},{5,4},{6,7},{7,6},{8,9},{9,8},{10,11... | collective-permute-start | bytes 98312 | tf_op jit(solution)/shard_map/ppermute | solution.py:519
  52.6 6.4 %collective-permute-start.14 = (bf16[8,512]{1,0:T(8,128)(2,1)S(1)}, bf16[8,512]{1,0:T(8,128)(2,1)S(1)}, u32[]{:S(2)}, u32[]{:S(2)}) collective-permute-start(bf16[8,512]{1,0:T(8,128)(2,1)S(1)} %get-tuple-element.112), channel_id=1, source_target_pairs={{0,4},{4,8},{8,12},{12,0},{1,5},{5,9},{9,13},{13,1},{2,6},{6,10},{... | collective-permute-start | bytes 24584 | tf_op jit(solution)/shard_map/ppermute | solution.py:649
  52.6 6.4 %collective-permute-start.15 = (bf16[8,512]{1,0:T(8,128)(2,1)S(1)}, bf16[8,512]{1,0:T(8,128)(2,1)S(1)}, u32[]{:S(2)}, u32[]{:S(2)}) collective-permute-start(bf16[8,512]{1,0:T(8,128)(2,1)S(1)} %get-tuple-element.113), channel_id=1, source_target_pairs={{0,8},{4,12},{8,0},{12,4},{1,9},{5,13},{9,1},{13,5},{2,10},{6,14},... | collective-permute-start | bytes 24584 | tf_op jit(solution)/shard_map/ppermute | solution.py:649
  54.6 4.5 %collective-permute-start.16 = (bf16[8,512]{1,0:T(8,128)(2,1)S(1)}, bf16[8,512]{1,0:T(8,128)(2,1)S(1)}, u32[]{:S(2)}, u32[]{:S(2)}) collective-permute-start(bf16[8,512]{1,0:T(8,128)(2,1)S(1)} %get-tuple-element.114), channel_id=1, source_target_pairs={{0,12},{4,0},{8,4},{12,8},{1,13},{5,1},{9,5},{13,9},{2,14},{6,2},{... | collective-permute-start | bytes 24584 | tf_op jit(solution)/shard_map/ppermute | solution.py:649
  59.6 3.7 %collective-permute-start.17 = (bf16[8,512]{1,0:T(8,128)(2,1)S(1)}, bf16[8,512]{1,0:T(8,128)(2,1)S(1)}, u32[]{:S(2)}, u32[]{:S(2)}) collective-permute-start(bf16[8,512]{1,0:T(8,128)(2,1)S(1)} %pool_own.1.refs_3_), channel_id=1, source_target_pairs={{0,2},{2,0},{1,3},{3,1},{4,6},{6,4},{5,7},{7,5},{8,10},{10,8},{9,1... | collective-permute-start | bytes 24584 | tf_op jit(solution)/shard_map/ppermute | solution.py:524

commit v11 on v8

--- a/solution.py
+++ b/solution.py
@@ -330,18 +330,14 @@
     )(ids, *args, core, chip, near_pairs)
 
 
-def far_kernel(pairs, group, part, block, spread, waits, final, *refs):
+def far_kernel(pairs, group, p, block, spread, waits, final, *refs):
     ids_ref, q_ref, near_ref, gains_ref = refs[:4]
     refs = refs[4:]
     is_first = ids_ref[0] == 0
-    if part == "all":
-        mine, other = refs[0][...], refs[1][...]
-        total = jnp.concatenate([jnp.where(is_first, mine, other), jnp.where(is_first, other, mine)], axis=0)
-        p, refs = 0, refs[2:]
-    else:
-        total = refs[0][...]
-        p, refs = ids_ref[0] if part == "own" else 1 - ids_ref[0], refs[1:]
-    refs = refs[waits:]
+    mine, other = refs[0][...], refs[1][...]
+    total = jnp.concatenate([jnp.where(is_first, mine, other), jnp.where(is_first, other, mine)], axis=0)
+    total = total[p * R : (p + 1) * R]
+    refs = refs[2 + waits :]
     if final:
         bounds_ref, *earlier = refs[:-4]
         out_ref, keep_ref, send_ref, turn_ref = refs[-4:]
@@ -351,8 +347,7 @@
     rows = q_ref.shape[0]
 
     def lanes(offset, scale=1):
-        start = (offset + p) * scale * LANES
-        return pl.ds(start if part == "all" else pl.multiple_of(start, LANES), scale * LANES)
+        return pl.ds((offset + p) * scale * LANES, scale * LANES)
 
     gains = jnp.concatenate([gains_ref[:, lanes(group * pairs)]] * 2, axis=0).T
 
@@ -382,12 +377,6 @@
     member = (position >= bounds_ref[0:1, :]) & (position < bounds_ref[1:2, :])
     pieces = jnp.concatenate([ref[...] for ref in earlier + [out_ref]], axis=1)
     sums = dot(jnp.where(member, 1.0, 0.0).astype(BF), pieces, ((0,), (0,)))
-    if part != "all":
-        ordered = []
-        for at in range(0, sums.shape[1], 2 * LANES):
-            low, high = sums[:, at : at + LANES], sums[:, at + LANES : at + 2 * LANES]
-            ordered += [jnp.where(is_first, low, high), jnp.where(is_first, high, low)]
-        sums = jnp.concatenate(ordered, axis=1)
     count = spans // (2 * spread)
     even = jnp.concatenate([sums[2 * i * count : (2 * i + 1) * count] for i in range(spread)], axis=0)
     odd = jnp.concatenate([sums[(2 * i + 1) * count : (2 * i + 2) * count] for i in range(spread)], axis=0)
@@ -395,14 +384,14 @@
     send_ref[...] = jnp.where(is_first, odd, even).astype(BF)
 
 
-def far(pairs, group, part, spread, ids, q, near_sums, gains, halves, arrived, final):
+def far(pairs, group, p, spread, ids, q, near_sums, gains, halves, arrived, final):
     rows = q.shape[0]
     shapes = [jax.ShapeDtypeStruct((rows, LANES), BF)]
     if final:
         shape = (final[0].shape[1] // 2, len(final) * LANES)
         shapes += [jax.ShapeDtypeStruct(shape, F32), jax.ShapeDtypeStruct(shape, BF)]
     return pl.pallas_call(
-        functools.partial(far_kernel, pairs, group, part, 256, spread, len(arrived), bool(final)),
+        functools.partial(far_kernel, pairs, group, p, 256, spread, len(arrived), bool(final)),
         in_specs=[smem()]
         + [vmem()] * (3 + len(halves))
         + [pl.BlockSpec(memory_space=pl.ANY)] * len(arrived)
@@ -429,20 +418,11 @@
     def weight(j, size):
         return weight_ref[pl.ds(pl.multiple_of(ids_ref[j] * size, size), size), :]
 
-    def head_weight(j):
-        if pairs == 1:
-            return weight(j, width)
-        first = ids_ref[count + spans]
-        blocks = [weight_ref[pl.ds(pl.multiple_of(ids_ref[j] * width + p * LANES, LANES), LANES), :] for p in (first, 1 - first)]
-        return jnp.concatenate(blocks, axis=0)
-
-    weights = [head_weight(j) for j in range(count)]
-
     for start in range(0, rows, tile):
         at = slice(start, start + tile)
         total = acc[0][at, :] if acc else None
         for j in range(count):
-            term = dot(jnp.concatenate([ref[at, :] for ref in tokens[j]], axis=1), weights[j])
+            term = dot(jnp.concatenate([ref[at, :] for ref in tokens[j]], axis=1), weight(j, width))
             total = term if total is None else total + term
         outs[0][at, :] = total.astype(outs[0].dtype)
     if spans:
@@ -622,12 +602,11 @@
                 mine[-1] = add_call(mine[-1], got)
             mine[-1], turn = tie((mine[-1], turn))
         out = []
-        calls = [("own", [total]), ("other", [other])] if pairs == 2 else [("all", [total, other])]
-        for part, halves in calls:
+        for p in range(pairs):
             final = []
-            if g == groups - 1 and part != "own":
+            if g == groups - 1 and p == pairs - 1:
                 final = [bounds] + [piece for o in outs for piece in o] + out
-            made, *sums, turn = far(pairs, g, part, spread, turn, q, near_sums, dual_gains, halves, arrived, final)
+            made, *sums, turn = far(pairs, g, p, spread, turn, q, near_sums, dual_gains, [total, other], arrived, final)
             arrived = []
             out.append(made)
         outs.append(out)
@@ -646,14 +625,14 @@
         lax.ppermute(piece, "seq", [(i, (i + k + 1) % spread) for i in range(spread)]) for k, piece in enumerate(pieces)
     ]
     parts = outs + others[:early]
-    index = jnp.stack(own_index + other_index[:early] + [lax.axis_index("rep")]).astype(jnp.int32)
+    index = jnp.stack(own_index + other_index[:early]).astype(jnp.int32)
     acc, turn = out_part(parts, index, out_weight, None, F32)
     place = (seq_index * own.shape[0]).astype(jnp.int32)[None]
     place = place + (turn - index[:1])
     own = pool_own(place, bounds, own, pieces)
     pooled = [own] + [across_heads(own, k) for k in range(1, head_devices)]
     pooled_index = [lax.rem(head_index - k + head_devices, head_devices) for k in range(head_devices)]
-    index = jnp.stack(other_index[early:] + pooled_index + [lax.axis_index("rep")]).astype(jnp.int32)
+    index = jnp.stack(other_index[early:] + pooled_index).astype(jnp.int32)
     return tuple(out_part(others[early:], index, out_weight, acc, BF, pooled)[:2])
 
 

time: 65.9 us -> 65.1 us (0.988)
  transfers between devices with their start and end apart: 18 -> 18, of which waited for: 5 -> 5; matrix products, arithmetic and copies ran while one was open for 0% -> 0% of each run, Pallas kernels for 32% -> 31%
where the time goes in v11:
time: 65.1 us; the launch traced here: 65 us
  Pallas kernels  30.7 us (47%)
  starting transfers between devices  22.4 us (34%)
  waiting for transfers between devices  10 us (15%)
  between operations  1.59 us (2%)
    pallas_call x2, Pallas kernels, front(): pl.pallas_call(functools.partial(front_kernel, first, last, group, pairs,...  14 us
    ppermute x9, starting transfers between devices, swap(): return lax.ppermute(values, axis, [(i, i ^ step) for i in range(count)])  11.9 us
    pallas_call x4, Pallas kernels, far(): pl.pallas_call(functools.partial(far_kernel, pairs, group, p, 256, spread...  6.72 us
    ppermute x5, starting transfers between devices, across_heads(): lax.ppermute(values, 'head', [(i, (i + step) % count) for i in range(coun...  5.8 us
    pallas_call x2, Pallas kernels, near(): pl.pallas_call(functools.partial(near_kernel, pairs, group, groups), in_s...  5.68 us
    ppermute x5, waiting for transfers between devices, across_heads(): lax.ppermute(values, 'head', [(i, (i + step) % count) for i in range(coun...  5.25 us
    ppermute x9, waiting for transfers between devices, swap(): return lax.ppermute(values, axis, [(i, i ^ step) for i in range(count)])  4.75 us
    ppermute x3, starting transfers between devices, per_device(): lax.ppermute(piece, 'seq', [(i, (i + k + 1) % spread) for i in range(spre...  3.88 us
  transfers between devices with their start and end apart: 18, of which 5 were waited for; matrix products, arithmetic and copies ran while one was open for 0% of the time, Pallas kernels for 31%

profile of v11, /device:TPU:0, one launch (start us, length us, event | category | flops | bytes accessed | tf_op | source)
XLA Modules:
  0.0 65.0 jit_solution(2282283027048528990)
XLA Ops:
  0.6 0.1 pad_add_fusion.1.refs_0_
  0.7 8.6 %front.2 = (bf16[1024,1024]{1,0:T(8,128)(2,1)S(1)}, bf16[1024,512]{1,0:T(8,128)(2,1)S(1)}, bf16[256,256]{1,0:T(8,128)(2,1)S(1)}, bf16[256,256]{1,0:T(8,128)(2,1)...) custom-call(s32[4]{0:T(128)S(1)} %pad_add_fusion.1.refs_0_, ...), custom_call_target="tpu_custom_call" | custom-call | flops 3221225472 | bytes 4194304 | tf_op jit(solution)/shard_map/front/pallas_call | solution.py:231
  9.4 0.5 collective-permute-start
  9.9 1.0 %collective-permute-done.b_ref = bf16[256,256]{1,0:T(8,128)(2,1)S(1)} collective-permute-done((bf16[256,256]{1,0:T(8,128)(2,1)S(1)}, bf16[256,256]{1,0:T(8,128)(2,1)S(1)}, u32[]{:S(2)}, u32[]{:S(2)}) %collective-permute-start) | collective-permute-done | bytes 131104 | tf_op jit(solution)/shard_map/ppermute | solution.py:499
  10.9 3.0 %collective-permute-start.2 = (bf16[256,256]{1,0:T(8,128)(2,1)S(1)}, bf16[256,256]{1,0:T(8,128)(2,1)S(1)}, u32[]{:S(2)}, u32[]{:S(2)}) collective-permute-start(bf16[256,256]{1,0:T(8,128)(2,1)S(1)} %add.49.a_ref), channel_id=1, source_target_pairs={{0,4},{4,0},{8,12},{12,8},{1,5},{5,1},{9,13},{13,9},{2,6},{6,2},{1... | collective-permute-start | bytes 393224 | tf_op jit(solution)/shard_map/ppermute | solution.py:499
  13.9 5.4 %front.3 = (bf16[1024,1024]{1,0:T(8,128)(2,1)S(1)}, bf16[1024,512]{1,0:T(8,128)(2,1)S(1)}, bf16[256,256]{1,0:T(8,128)(2,1)S(1)}, bf16[512,256]{1,0:T(8,128)(2,1)...) custom-call(s32[4]{0:T(128)S(1)} %get-tuple-element.59.refs_0_, ...), custom_call_target="tpu_custom_call", output_to_operand_aliasing={{0}: (1, {})} | custom-call | flops 3221225472 | bytes 4194304 | tf_op jit(solution)/shard_map/front/pallas_call | solution.py:231
  19.3 0.1 collective-permute-start.1
  19.4 0.8 %collective-permute-start.5 = (bf16[256,256]{1,0:T(8,128)(2,1)S(1)}, bf16[256,256]{1,0:T(8,128)(2,1)S(1)}, u32[]{:S(2)}, u32[]{:S(2)}) collective-permute-start(bf16[256,256]{1,0:T(8,128)(2,1)S(1)} %get-tuple-element.75), channel_id=1, source_target_pairs={{1,4},{5,8},{9,12},{4,1},{8,5},{12,9},{3,6},{7,10},{11,14},{6,3},{... | collective-permute-start | bytes 393224 | tf_op jit(solution)/shard_map/ppermute | solution.py:581
  20.2 0.0 collective-permute-done.2.b_ref
  20.3 0.0 copy-start.1
  20.3 3.9 %collective-permute-start.4 = (bf16[256,256]{1,0:T(8,128)(2,1)S(1)}, bf16[256,256]{1,0:T(8,128)(2,1)S(1)}, u32[]{:S(2)}, u32[]{:S(2)}) collective-permute-start(bf16[256,256]{1,0:T(8,128)(2,1)S(1)} %add.51.a_ref), channel_id=1, source_target_pairs={{0,8},{4,12},{8,0},{12,4},{1,9},{5,13},{9,1},{13,5},{2,10},{6,14},... | collective-permute-start | bytes 393224 | tf_op jit(solution)/shard_map/ppermute | solution.py:499
  24.3 2.2 %collective-permute-start.3 = (bf16[256,256]{1,0:T(8,128)(2,1)S(1)}, bf16[256,256]{1,0:T(8,128)(2,1)S(1)}, u32[]{:S(2)}, u32[]{:S(2)}) collective-permute-start(bf16[256,256]{1,0:T(8,128)(2,1)S(1)} %add.50.a_ref), channel_id=1, source_target_pairs={{0,4},{4,0},{8,12},{12,8},{1,5},{5,1},{9,13},{13,9},{2,6},{6,2},{1... | collective-permute-start | bytes 393224 | tf_op jit(solution)/shard_map/ppermute | solution.py:499
  26.4 3.5 %near.2 = (bf16[1024,256]{1,0:T(8,128)(2,1)S(1)}, bf16[1024,256]{1,0:T(8,128)(2,1)S(1)}, f32[1024,512]{1,0:T(8,128)S(1)}, s32[4]{0:T(128)S(1)}) custom-call(s32[4]{0:T(128)S(1)} %get-tuple-element.73.ids_ref, bf16[1024,1024]{1,0:T(8,128)(2,1)S(1)} %get-tuple-element.74.refs_0_, bf16[1024,512]{1,0:T(8,128)(2,1)S(1)} %copy-done.1, ...), custom_call_target="tpu_custom_call" | custom-call | flops 1048576 | bytes 1024 | tf_op jit(solution)/shard_map/near/pallas_call | solution.py:320
  29.9 2.5 %collective-permute-done.4.b_ref = bf16[256,256]{1,0:T(8,128)(2,1)S(1)} collective-permute-done((bf16[256,256]{1,0:T(8,128)(2,1)S(1)}, bf16[256,256]{1,0:T(8,128)(2,1)S(1)}, u32[]{:S(2)}, u32[]{:S(2)}) %collective-permute-start.4) | collective-permute-done | bytes 131104 | tf_op jit(solution)/shard_map/ppermute | solution.py:499
  32.5 0.1 collective-permute-start.7
  32.6 0.0 collective-permute-done.3.b_ref
  32.6 2.0 %collective-permute-start.6 = (bf16[256,256]{1,0:T(8,128)(2,1)S(1)}, bf16[256,256]{1,0:T(8,128)(2,1)S(1)}, u32[]{:S(2)}, u32[]{:S(2)}) collective-permute-start(bf16[256,256]{1,0:T(8,128)(2,1)S(1)} %add.52.a_ref), channel_id=1, source_target_pairs={{0,8},{4,12},{8,0},{12,4},{1,9},{5,13},{9,1},{13,5},{2,10},{6,14},... | collective-permute-start | bytes 393224 | tf_op jit(solution)/shard_map/ppermute | solution.py:499
  34.6 0.0 collective-permute-done.7.refs_5_
  34.7 1.6 %far.4 = (bf16[1024,128]{1,0:T(8,128)(2,1)S(1)}, s32[4]{0:T(128)S(1)}) custom-call(s32[4]{0:T(128)S(1)} %get-tuple-element.82.refs_0_, bf16[1024,256]{1,0:T(8,128)(2,1)S(1)} %get-tuple-element.83.refs_1_, f32[1024,512]{1,0:T(8,128)S(1)} %get-tuple-element.84.refs_2_, f32[4,512]{1,0:T(4,128)S(1)} %copy-done.2, bf16[256,256]{1,0:T(8,128)(2,1)S(1)} %add.53.refs_4_, ...), custom_call_target="tpu_custom_call" | custom-call | flops 1048576 | bytes 1024 | tf_op jit(solution)/shard_map/far/pallas_call | solution.py:393
  36.3 1.6 %collective-permute-start.9 = (bf16[1024,128]{1,0:T(8,128)(2,1)S(1)}, bf16[1024,128]{1,0:T(8,128)(2,1)S(1)}, u32[]{:S(2)}, u32[]{:S(2)}) collective-permute-start(bf16[1024,128]{1,0:T(8,128)(2,1)S(1)} %get-tuple-element.95.refs_7_.refs_1_), channel_id=1, source_target_pairs={{0,2},{2,0},{1,3},{3,1},{4,6},{6,4},{5,7},{7,5},{8,10},{10,8},{9,1... | collective-permute-start | bytes 786440 | tf_op jit(solution)/shard_map/ppermute | solution.py:504
  37.8 1.6 %far.5 = (bf16[1024,128]{1,0:T(8,128)(2,1)S(1)}, s32[4]{0:T(128)S(1)}) custom-call(s32[4]{0:T(128)S(1)} %get-tuple-element.86.refs_0_, bf16[1024,256]{1,0:T(8,128)(2,1)S(1)} %get-tuple-element.83.refs_1_, f32[1024,512]{1,0:T(8,128)S(1)} %get-tuple-element.84.refs_2_, f32[4,512]{1,0:T(4,128)S(1)} %copy-done.2, bf16[256,256]{1,0:T(8,128)(2,1)S(1)} %add.53.refs_4_, ...), custom_call_target="tpu_custom_call" | custom-call | flops 1048576 | bytes 1024 | tf_op jit(solution)/shard_map/far/pallas_call | solution.py:393
  39.5 0.6 collective-permute-start.12
  40.1 2.2 %near.3 = (bf16[1024,256]{1,0:T(8,128)(2,1)S(1)}, f32[1024,512]{1,0:T(8,128)S(1)}, s32[4]{0:T(128)S(1)}) custom-call(s32[4]{0:T(128)S(1)} %get-tuple-element.87.ids_ref, bf16[1024,256]{1,0:T(8,128)(2,1)S(1)} %get-tuple-element.88.refs_0_, bf16[512,256]{1,0:T(8,128)(2,1)S(1)} %collective-permute-done.1.b_ref.refs_2_.refs_1_, ...), custom_call_target="tpu_custom_call", output_to_operand_aliasing={{0}: (1, {})} | custom-call | flops 1048576 | bytes 1024 | tf_op jit(solution)/shard_map/near/pallas_call | solution.py:320
  42.3 0.0 copy-start.3
  42.4 0.1 collective-permute-start.8
  42.4 3.2 %collective-permute-done.9.refs_6_.refs_5_ = bf16[1024,128]{1,0:T(8,128)(2,1)S(1)} collective-permute-done((bf16[1024,128]{1,0:T(8,128)(2,1)S(1)}, bf16[1024,128]{1,0:T(8,128)(2,1)S(1)}, u32[]{:S(2)}, u32[]{:S(2)}) %collective-permute-start.9) | collective-permute-done | bytes 262176 | tf_op jit(solution)/shard_map/ppermute | solution.py:504
  45.6 0.0 collective-permute-done.8.refs_5_
  45.6 1.6 %far.6 = (bf16[1024,128]{1,0:T(8,128)(2,1)S(1)}, s32[4]{0:T(128)S(1)}) custom-call(s32[4]{0:T(128)S(1)} %get-tuple-element.91.refs_0_, bf16[1024,256]{1,0:T(8,128)(2,1)S(1)} %get-tuple-element.92.refs_1_, f32[1024,512]{1,0:T(8,128)S(1)} %get-tuple-element.93.refs_2_, f32[4,512]{1,0:T(4,128)S(1)} %copy-done.2, bf16[256,256]{1,0:T(8,128)(2,1)S(1)} %add.54.refs_4_, ...), custom_call_target="tpu_custom_call" | custom-call | flops 1048576 | bytes 1024 | tf_op jit(solution)/shard_map/far/pallas_call | solution.py:393
  47.2 0.0 copy-start
  47.2 1.9 %far.7 = (bf16[1024,128]{1,0:T(8,128)(2,1)S(1)}, f32[32,512]{1,0:T(8,128)S(1)}, bf16[32,512]{1,0:T(8,128)(2,1)S(1)}, s32[4]{0:T(128)}) custom-call(s32[4]{0:T(128)S(1)} %get-tuple-element.97.refs_0_, bf16[1024,256]{1,0:T(8,128)(2,1)S(1)} %get-tuple-element.92.refs_1_, f32[1024,512]{1,0:T(8,128)S(1)} %get-tuple-element.93.refs_2_, f32[4,512]{1,0:T(4,128)S(1)} %copy-done.2, ...), custom_call_target="tpu_custom_call" | custom-call | flops 1048576 | bytes 1024 | tf_op jit(solution)/shard_map/far/pallas_call | solution.py:393
  49.1 1.6 %collective-permute-start.11 = (bf16[1024,128]{1,0:T(8,128)(2,1)S(1)}, bf16[1024,128]{1,0:T(8,128)(2,1)S(1)}, u32[]{:S(2)}, u32[]{:S(2)}) collective-permute-start(bf16[1024,128]{1,0:T(8,128)(2,1)S(1)} %get-tuple-element.99.refs_4_), channel_id=1, source_target_pairs={{0,2},{2,0},{1,3},{3,1},{4,6},{6,4},{5,7},{7,5},{8,10},{10,8},{9,1... | collective-permute-start | bytes 786440 | tf_op jit(solution)/shard_map/ppermute | solution.py:504
  50.7 0.5 collective-permute-start.10
  51.2 1.2 %collective-permute-done.13.got_ref = bf16[32,512]{1,0:T(8,128)(2,1)S(1)} collective-permute-done((bf16[32,512]{1,0:T(8,128)(2,1)S(1)}, bf16[32,512]{1,0:T(8,128)(2,1)S(1)}, u32[]{:S(2)}, u32[]{:S(2)}) %collective-permute-start.13) | collective-permute-done | bytes 32800 | tf_op jit(solution)/shard_map/ppermute | solution.py:499
  52.4 1.2 %collective-permute-start.14 = (bf16[8,512]{1,0:T(8,128)(2,1)S(1)}, bf16[8,512]{1,0:T(8,128)(2,1)S(1)}, u32[]{:S(2)}, u32[]{:S(2)}) collective-permute-start(bf16[8,512]{1,0:T(8,128)(2,1)S(1)} %get-tuple-element.104), channel_id=1, source_target_pairs={{0,4},{4,8},{8,12},{12,0},{1,5},{5,9},{9,13},{13,1},{2,6},{6,10},{... | collective-permute-start | bytes 24584 | tf_op jit(solution)/shard_map/ppermute | solution.py:625
  53.6 1.0 %collective-permute-start.15 = (bf16[8,512]{1,0:T(8,128)(2,1)S(1)}, bf16[8,512]{1,0:T(8,128)(2,1)S(1)}, u32[]{:S(2)}, u32[]{:S(2)}) collective-permute-start(bf16[8,512]{1,0:T(8,128)(2,1)S(1)} %get-tuple-element.105), channel_id=1, source_target_pairs={{0,8},{4,12},{8,0},{12,4},{1,9},{5,13},{9,1},{13,5},{2,10},{6,14},... | collective-permute-start | bytes 24584 | tf_op jit(solution)/shard_map/ppermute | solution.py:625
  54.6 0.0 collective-permute-done.12.refs_6_
  54.6 1.7 %collective-permute-start.16 = (bf16[8,512]{1,0:T(8,128)(2,1)S(1)}, bf16[8,512]{1,0:T(8,128)(2,1)S(1)}, u32[]{:S(2)}, u32[]{:S(2)}) collective-permute-start(bf16[8,512]{1,0:T(8,128)(2,1)S(1)} %get-tuple-element.106), channel_id=1, source_target_pairs={{0,12},{4,0},{8,4},{12,8},{1,13},{5,1},{9,5},{13,9},{2,14},{6,2},{... | collective-permute-start | bytes 24584 | tf_op jit(solution)/shard_map/ppermute | solution.py:625
  56.3 0.1 pad_add_fusion.2.refs_0_
  56.4 1.5 %out.2 = (f32[1024,512]{1,0:T(8,128)S(1)}, s32[1]{0:T(128)}) custom-call(s32[3]{0:T(128)S(1)} %pad_add_fusion.2.refs_0_, bf16[1024,128]{1,0:T(8,128)(2,1)S(1)} %get-tuple-element.95.refs_7_.refs_1_, bf16[1024,128]{1,0:T(8,128)(2,1)S(1)} %get-tuple-element.98.refs_8_.refs_2_, bf16[1024,128]{1,0:T(8,128)(2,1)S(1)} %get-tuple-element.96.refs_9_.refs_3_, ...), custom_call_target="tpu_custom_call" | custom-call | flops 1048576 | bytes 1024 | tf_op jit(solution)/shard_map/out/pallas_call | solution.py:440
  58.5 0.0 collective-permute-done.15.refs_1_
  58.5 0.0 collective-permute-done.16.refs_2_
  58.5 0.6 pool_own.1.refs_3_
  59.1 1.6 %collective-permute-start.17 = (bf16[8,512]{1,0:T(8,128)(2,1)S(1)}, bf16[8,512]{1,0:T(8,128)(2,1)S(1)}, u32[]{:S(2)}, u32[]{:S(2)}) collective-permute-start(bf16[8,512]{1,0:T(8,128)(2,1)S(1)} %pool_own.1.refs_3_), channel_id=1, source_target_pairs={{0,2},{2,0},{1,3},{3,1},{4,6},{6,4},{5,7},{7,5},{8,10},{10,8},{9,1... | collective-permute-start | bytes 24584 | tf_op jit(solution)/shard_map/ppermute | solution.py:504
  60.7 0.1 pad_add_fusion.refs_0_
  60.7 2.1 %collective-permute-done.17.refs_4_ = bf16[8,512]{1,0:T(8,128)(2,1)S(1)} collective-permute-done((bf16[8,512]{1,0:T(8,128)(2,1)S(1)}, bf16[8,512]{1,0:T(8,128)(2,1)S(1)}, u32[]{:S(2)}, u32[]{:S(2)}) %collective-permute-start.17) | collective-permute-done | bytes 8224 | tf_op jit(solution)/shard_map/ppermute | solution.py:504
  62.8 0.0 collective-permute-done.11.refs_2_
  62.8 0.0 collective-permute-done.10.refs_1_
  62.8 2.0 %out.3 = (bf16[1024,512]{1,0:T(8,128)(2,1)}, f32[8,512]{1,0:T(8,128)}, s32[1]{0:T(128)}) custom-call(s32[3]{0:T(128)S(1)} %pad_add_fusion.refs_0_, bf16[1024,128]{1,0:T(8,128)(2,1)S(1)} %collective-permute-done.10.refs_1_, bf16[1024,128]{1,0:T(8,128)(2,1)S(1)} %collective-permute-done.11.refs_2_, bf16[8,512]{1,0:T(8,128)(2,1)S(1)} %pool_own.1.refs_3_, ...), custom_call_target="tpu_custom_call" | custom-call | flops 1048576 | bytes 1024 | tf_op jit(solution)/shard_map/out/pallas_call | solution.py:440
  (17 shorter events, 0.2 us)
Async XLA Ops:
  0.7 13.2 %copy-start.2 = (f32[4,512]{1,0:T(4,128)S(1)}, f32[4,512]{1,0:T(4,128)}, u32[]{:S(2)}) copy-start(f32[4,512]{1,0:T(4,128)} %refs_3_.9) | copy-start | bytes 24580
  9.4 1.5 %collective-permute-start = (bf16[256,256]{1,0:T(8,128)(2,1)S(1)}, bf16[256,256]{1,0:T(8,128)(2,1)S(1)}, u32[]{:S(2)}, u32[]{:S(2)}) collective-permute-start(bf16[256,256]{1,0:T(8,128)(2,1)S(1)} %get-tuple-element.57), channel_id=1, source_target_pairs={{0,1},{1,0},{2,3},{3,2},{4,5},{5,4},{6,7},{7,6},{8,9},{9,8},{10,11... | collective-permute-start | bytes 393224 | tf_op jit(solution)/shard_map/ppermute | solution.py:499
  10.9 9.3 %collective-permute-start.2 = (bf16[256,256]{1,0:T(8,128)(2,1)S(1)}, bf16[256,256]{1,0:T(8,128)(2,1)S(1)}, u32[]{:S(2)}, u32[]{:S(2)}) collective-permute-start(bf16[256,256]{1,0:T(8,128)(2,1)S(1)} %add.49.a_ref), channel_id=1, source_target_pairs={{0,4},{4,0},{8,12},{12,8},{1,5},{5,1},{9,13},{13,9},{2,6},{6,2},{1... | collective-permute-start | bytes 393224 | tf_op jit(solution)/shard_map/ppermute | solution.py:499
  19.3 4.9 %collective-permute-start.1 = (bf16[512,256]{1,0:T(8,128)(2,1)S(1)}, bf16[512,256]{1,0:T(8,128)(2,1)S(1)}, u32[]{:S(2)}, u32[]{:S(2)}) collective-permute-start(bf16[512,256]{1,0:T(8,128)(2,1)S(1)} %get-tuple-element.65), channel_id=1, source_target_pairs={{0,1},{1,0},{2,3},{3,2},{4,5},{5,4},{6,7},{7,6},{8,9},{9,8},{10,11... | collective-permute-start | bytes 786440 | tf_op jit(solution)/shard_map/ppermute | solution.py:499
  19.4 7.0 %collective-permute-start.5 = (bf16[256,256]{1,0:T(8,128)(2,1)S(1)}, bf16[256,256]{1,0:T(8,128)(2,1)S(1)}, u32[]{:S(2)}, u32[]{:S(2)}) collective-permute-start(bf16[256,256]{1,0:T(8,128)(2,1)S(1)} %get-tuple-element.75), channel_id=1, source_target_pairs={{1,4},{5,8},{9,12},{4,1},{8,5},{12,9},{3,6},{7,10},{11,14},{6,3},{... | collective-permute-start | bytes 393224 | tf_op jit(solution)/shard_map/ppermute | solution.py:581
  20.3 6.2 %copy-start.1 = (bf16[1024,512]{1,0:T(8,128)(2,1)S(1)}, bf16[1024,512]{1,0:T(8,128)(2,1)}, u32[]{:S(2)}) copy-start(bf16[1024,512]{1,0:T(8,128)(2,1)} %refs_1_.3) | copy-start | bytes 3145732
  20.3 12.1 %collective-permute-start.4 = (bf16[256,256]{1,0:T(8,128)(2,1)S(1)}, bf16[256,256]{1,0:T(8,128)(2,1)S(1)}, u32[]{:S(2)}, u32[]{:S(2)}) collective-permute-start(bf16[256,256]{1,0:T(8,128)(2,1)S(1)} %add.51.a_ref), channel_id=1, source_target_pairs={{0,8},{4,12},{8,0},{12,4},{1,9},{5,13},{9,1},{13,5},{2,10},{6,14},... | collective-permute-start | bytes 393224 | tf_op jit(solution)/shard_map/ppermute | solution.py:499
  24.3 8.3 %collective-permute-start.3 = (bf16[256,256]{1,0:T(8,128)(2,1)S(1)}, bf16[256,256]{1,0:T(8,128)(2,1)S(1)}, u32[]{:S(2)}, u32[]{:S(2)}) collective-permute-start(bf16[256,256]{1,0:T(8,128)(2,1)S(1)} %add.50.a_ref), channel_id=1, source_target_pairs={{0,4},{4,0},{8,12},{12,8},{1,5},{5,1},{9,13},{13,9},{2,6},{6,2},{1... | collective-permute-start | bytes 393224 | tf_op jit(solution)/shard_map/ppermute | solution.py:499
  32.5 2.2 %collective-permute-start.7 = (bf16[256,256]{1,0:T(8,128)(2,1)S(1)}, bf16[256,256]{1,0:T(8,128)(2,1)S(1)}, u32[]{:S(2)}, u32[]{:S(2)}) collective-permute-start(bf16[256,256]{1,0:T(8,128)(2,1)S(1)} %add.53.refs_4_), channel_id=1, source_target_pairs={{0,1},{1,0},{2,3},{3,2},{4,5},{5,4},{6,7},{7,6},{8,9},{9,8},{10,11... | collective-permute-start | bytes 393224 | tf_op jit(solution)/shard_map/ppermute | solution.py:499
  32.6 9.7 %collective-permute-start.6 = (bf16[256,256]{1,0:T(8,128)(2,1)S(1)}, bf16[256,256]{1,0:T(8,128)(2,1)S(1)}, u32[]{:S(2)}, u32[]{:S(2)}) collective-permute-start(bf16[256,256]{1,0:T(8,128)(2,1)S(1)} %add.52.a_ref), channel_id=1, source_target_pairs={{0,8},{4,12},{8,0},{12,4},{1,9},{5,13},{9,1},{13,5},{2,10},{6,14},... | collective-permute-start | bytes 393224 | tf_op jit(solution)/shard_map/ppermute | solution.py:499
  36.3 9.3 %collective-permute-start.9 = (bf16[1024,128]{1,0:T(8,128)(2,1)S(1)}, bf16[1024,128]{1,0:T(8,128)(2,1)S(1)}, u32[]{:S(2)}, u32[]{:S(2)}) collective-permute-start(bf16[1024,128]{1,0:T(8,128)(2,1)S(1)} %get-tuple-element.95.refs_7_.refs_1_), channel_id=1, source_target_pairs={{0,2},{2,0},{1,3},{3,1},{4,6},{6,4},{5,7},{7,5},{8,10},{10,8},{9,1... | collective-permute-start | bytes 786440 | tf_op jit(solution)/shard_map/ppermute | solution.py:504
  39.5 15.2 %collective-permute-start.12 = (bf16[1024,128]{1,0:T(8,128)(2,1)S(1)}, bf16[1024,128]{1,0:T(8,128)(2,1)S(1)}, u32[]{:S(2)}, u32[]{:S(2)}) collective-permute-start(bf16[1024,128]{1,0:T(8,128)(2,1)S(1)} %get-tuple-element.98.refs_8_.refs_2_), channel_id=1, source_target_pairs={{0,2},{2,0},{1,3},{3,1},{4,6},{6,4},{5,7},{7,5},{8,10},{10,8},{9,1... | collective-permute-start | bytes 786440 | tf_op jit(solution)/shard_map/ppermute | solution.py:504
  42.3 4.9 %copy-start.3 = (s32[64,2]{0,1:T(2,128)S(1)}, s32[64,2]{0,1:T(2,128)}, u32[]{:S(2)}) copy-start(s32[64,2]{0,1:T(2,128)} %param.17) | copy-start | bytes 1540
  42.4 3.2 %collective-permute-start.8 = (bf16[256,256]{1,0:T(8,128)(2,1)S(1)}, bf16[256,256]{1,0:T(8,128)(2,1)S(1)}, u32[]{:S(2)}, u32[]{:S(2)}) collective-permute-start(bf16[256,256]{1,0:T(8,128)(2,1)S(1)} %add.54.refs_4_), channel_id=1, source_target_pairs={{0,1},{1,0},{2,3},{3,2},{4,5},{5,4},{6,7},{7,6},{8,9},{9,8},{10,11... | collective-permute-start | bytes 393224 | tf_op jit(solution)/shard_map/ppermute | solution.py:499
  47.2 9.2 %copy-start = (bf16[1024,512]{1,0:T(8,128)(2,1)S(1)}, bf16[1024,512]{1,0:T(8,128)(2,1)}, u32[]{:S(2)}) copy-start(bf16[1024,512]{1,0:T(8,128)(2,1)} %refs_5_.3) | copy-start | bytes 3145732
  49.1 13.7 %collective-permute-start.11 = (bf16[1024,128]{1,0:T(8,128)(2,1)S(1)}, bf16[1024,128]{1,0:T(8,128)(2,1)S(1)}, u32[]{:S(2)}, u32[]{:S(2)}) collective-permute-start(bf16[1024,128]{1,0:T(8,128)(2,1)S(1)} %get-tuple-element.99.refs_4_), channel_id=1, source_target_pairs={{0,2},{2,0},{1,3},{3,1},{4,6},{6,4},{5,7},{7,5},{8,10},{10,8},{9,1... | collective-permute-start | bytes 786440 | tf_op jit(solution)/shard_map/ppermute | solution.py:504
  50.7 12.2 %collective-permute-start.10 = (bf16[1024,128]{1,0:T(8,128)(2,1)S(1)}, bf16[1024,128]{1,0:T(8,128)(2,1)S(1)}, u32[]{:S(2)}, u32[]{:S(2)}) collective-permute-start(bf16[1024,128]{1,0:T(8,128)(2,1)S(1)} %get-tuple-element.96.refs_9_.refs_3_), channel_id=1, source_target_pairs={{0,2},{2,0},{1,3},{3,1},{4,6},{6,4},{5,7},{7,5},{8,10},{10,8},{9,1... | collective-permute-start | bytes 786440 | tf_op jit(solution)/shard_map/ppermute | solution.py:504
  51.2 1.2 %collective-permute-start.13 = (bf16[32,512]{1,0:T(8,128)(2,1)S(1)}, bf16[32,512]{1,0:T(8,128)(2,1)S(1)}, u32[]{:S(2)}, u32[]{:S(2)}) collective-permute-start(bf16[32,512]{1,0:T(8,128)(2,1)S(1)} %get-tuple-element.102), channel_id=1, source_target_pairs={{0,1},{1,0},{2,3},{3,2},{4,5},{5,4},{6,7},{7,6},{8,9},{9,8},{10,11... | collective-permute-start | bytes 98312 | tf_op jit(solution)/shard_map/ppermute | solution.py:499
  52.4 6.1 %collective-permute-start.14 = (bf16[8,512]{1,0:T(8,128)(2,1)S(1)}, bf16[8,512]{1,0:T(8,128)(2,1)S(1)}, u32[]{:S(2)}, u32[]{:S(2)}) collective-permute-start(bf16[8,512]{1,0:T(8,128)(2,1)S(1)} %get-tuple-element.104), channel_id=1, source_target_pairs={{0,4},{4,8},{8,12},{12,0},{1,5},{5,9},{9,13},{13,1},{2,6},{6,10},{... | collective-permute-start | bytes 24584 | tf_op jit(solution)/shard_map/ppermute | solution.py:625
  53.6 4.9 %collective-permute-start.15 = (bf16[8,512]{1,0:T(8,128)(2,1)S(1)}, bf16[8,512]{1,0:T(8,128)(2,1)S(1)}, u32[]{:S(2)}, u32[]{:S(2)}) collective-permute-start(bf16[8,512]{1,0:T(8,128)(2,1)S(1)} %get-tuple-element.105), channel_id=1, source_target_pairs={{0,8},{4,12},{8,0},{12,4},{1,9},{5,13},{9,1},{13,5},{2,10},{6,14},... | collective-permute-start | bytes 24584 | tf_op jit(solution)/shard_map/ppermute | solution.py:625
  54.6 3.9 %collective-permute-start.16 = (bf16[8,512]{1,0:T(8,128)(2,1)S(1)}, bf16[8,512]{1,0:T(8,128)(2,1)S(1)}, u32[]{:S(2)}, u32[]{:S(2)}) collective-permute-start(bf16[8,512]{1,0:T(8,128)(2,1)S(1)} %get-tuple-element.106), channel_id=1, source_target_pairs={{0,12},{4,0},{8,4},{12,8},{1,13},{5,1},{9,5},{13,9},{2,14},{6,2},{... | collective-permute-start | bytes 24584 | tf_op jit(solution)/shard_map/ppermute | solution.py:625
  59.1 3.7 %collective-permute-start.17 = (bf16[8,512]{1,0:T(8,128)(2,1)S(1)}, bf16[8,512]{1,0:T(8,128)(2,1)S(1)}, u32[]{:S(2)}, u32[]{:S(2)}) collective-permute-start(bf16[8,512]{1,0:T(8,128)(2,1)S(1)} %pool_own.1.refs_3_), channel_id=1, source_target_pairs={{0,2},{2,0},{1,3},{3,1},{4,6},{6,4},{5,7},{7,5},{8,10},{10,8},{9,1... | collective-permute-start | bytes 24584 | tf_op jit(solution)/shard_map/ppermute | solution.py:504

commit v12 on v11

--- a/solution.py
+++ b/solution.py
@@ -151,9 +151,9 @@
         if i == 0:
             for made in proj_copies:
                 made.wait()
+        p_ref[at, :] = exp_capped(dot(normed, wp_ref[...]), 1.0).astype(BF)
         if i == 0 and not last:
             next_copies = sum(weight_copies(group + 1, next_kv_ref, next_wp_ref), [])
-        p_ref[at, :] = exp_capped(dot(normed, wp_ref[...]), 1.0).astype(BF)
         near_ref[at, :width] = head_norm(key, dual_ref[0:1, group * width : (group + 1) * width])
         near_ref[at, width:] = head_norm(value, dual_ref[1:2, group * width : (group + 1) * width])
     total = []

time: 65.1 us -> 65.1 us (level)
  no operation moved by 1% of the time
where the time goes in v12:
time: 65.1 us; the launch traced here: 65 us
  Pallas kernels  30.7 us (47%)
  starting transfers between devices  22.4 us (34%)
  waiting for transfers between devices  10 us (15%)
  between operations  1.59 us (2%)
    pallas_call x2, Pallas kernels, front(): pl.pallas_call(functools.partial(front_kernel, first, last, group, pairs,...  14 us
    ppermute x9, starting transfers between devices, swap(): return lax.ppermute(values, axis, [(i, i ^ step) for i in range(count)])  11.9 us
    pallas_call x4, Pallas kernels, far(): pl.pallas_call(functools.partial(far_kernel, pairs, group, p, 256, spread...  6.72 us
    ppermute x5, starting transfers between devices, across_heads(): lax.ppermute(values, 'head', [(i, (i + step) % count) for i in range(coun...  5.8 us
    pallas_call x2, Pallas kernels, near(): pl.pallas_call(functools.partial(near_kernel, pairs, group, groups), in_s...  5.68 us
    ppermute x5, waiting for transfers between devices, across_heads(): lax.ppermute(values, 'head', [(i, (i + step) % count) for i in range(coun...  5.25 us
    ppermute x9, waiting for transfers between devices, swap(): return lax.ppermute(values, axis, [(i, i ^ step) for i in range(count)])  4.75 us
    ppermute x3, starting transfers between devices, per_device(): lax.ppermute(piece, 'seq', [(i, (i + k + 1) % spread) for i in range(spre...  3.88 us
  transfers between devices with their start and end apart: 18, of which 5 were waited for; matrix products, arithmetic and copies ran while one was open for 0% of the time, Pallas kernels for 31%

profile of v12, /device:TPU:0, one launch (start us, length us, event | category | flops | bytes accessed | tf_op | source)
XLA Modules:
  0.0 65.0 jit_solution(2282283027048528990)
XLA Ops:
  0.6 0.1 pad_add_fusion.1.refs_0_
  0.7 8.6 %front.2 = (bf16[1024,1024]{1,0:T(8,128)(2,1)S(1)}, bf16[1024,512]{1,0:T(8,128)(2,1)S(1)}, bf16[256,256]{1,0:T(8,128)(2,1)S(1)}, bf16[256,256]{1,0:T(8,128)(2,1)...) custom-call(s32[4]{0:T(128)S(1)} %pad_add_fusion.1.refs_0_, ...), custom_call_target="tpu_custom_call" | custom-call | flops 3221225472 | bytes 4194304 | tf_op jit(solution)/shard_map/front/pallas_call | solution.py:231
  9.4 0.5 collective-permute-start
  9.9 1.0 %collective-permute-done.b_ref = bf16[256,256]{1,0:T(8,128)(2,1)S(1)} collective-permute-done((bf16[256,256]{1,0:T(8,128)(2,1)S(1)}, bf16[256,256]{1,0:T(8,128)(2,1)S(1)}, u32[]{:S(2)}, u32[]{:S(2)}) %collective-permute-start) | collective-permute-done | bytes 131104 | tf_op jit(solution)/shard_map/ppermute | solution.py:499
  10.9 3.0 %collective-permute-start.2 = (bf16[256,256]{1,0:T(8,128)(2,1)S(1)}, bf16[256,256]{1,0:T(8,128)(2,1)S(1)}, u32[]{:S(2)}, u32[]{:S(2)}) collective-permute-start(bf16[256,256]{1,0:T(8,128)(2,1)S(1)} %add.49.a_ref), channel_id=1, source_target_pairs={{0,4},{4,0},{8,12},{12,8},{1,5},{5,1},{9,13},{13,9},{2,6},{6,2},{1... | collective-permute-start | bytes 393224 | tf_op jit(solution)/shard_map/ppermute | solution.py:499
  13.9 5.4 %front.3 = (bf16[1024,1024]{1,0:T(8,128)(2,1)S(1)}, bf16[1024,512]{1,0:T(8,128)(2,1)S(1)}, bf16[256,256]{1,0:T(8,128)(2,1)S(1)}, bf16[512,256]{1,0:T(8,128)(2,1)...) custom-call(s32[4]{0:T(128)S(1)} %get-tuple-element.59.refs_0_, ...), custom_call_target="tpu_custom_call", output_to_operand_aliasing={{0}: (1, {})} | custom-call | flops 3221225472 | bytes 4194304 | tf_op jit(solution)/shard_map/front/pallas_call | solution.py:231
  19.3 0.1 collective-permute-start.1
  19.4 0.8 %collective-permute-start.5 = (bf16[256,256]{1,0:T(8,128)(2,1)S(1)}, bf16[256,256]{1,0:T(8,128)(2,1)S(1)}, u32[]{:S(2)}, u32[]{:S(2)}) collective-permute-start(bf16[256,256]{1,0:T(8,128)(2,1)S(1)} %get-tuple-element.75), channel_id=1, source_target_pairs={{1,4},{5,8},{9,12},{4,1},{8,5},{12,9},{3,6},{7,10},{11,14},{6,3},{... | collective-permute-start | bytes 393224 | tf_op jit(solution)/shard_map/ppermute | solution.py:581
  20.2 0.0 collective-permute-done.2.b_ref
  20.3 0.0 copy-start.1
  20.3 3.9 %collective-permute-start.4 = (bf16[256,256]{1,0:T(8,128)(2,1)S(1)}, bf16[256,256]{1,0:T(8,128)(2,1)S(1)}, u32[]{:S(2)}, u32[]{:S(2)}) collective-permute-start(bf16[256,256]{1,0:T(8,128)(2,1)S(1)} %add.51.a_ref), channel_id=1, source_target_pairs={{0,8},{4,12},{8,0},{12,4},{1,9},{5,13},{9,1},{13,5},{2,10},{6,14},... | collective-permute-start | bytes 393224 | tf_op jit(solution)/shard_map/ppermute | solution.py:499
  24.3 2.2 %collective-permute-start.3 = (bf16[256,256]{1,0:T(8,128)(2,1)S(1)}, bf16[256,256]{1,0:T(8,128)(2,1)S(1)}, u32[]{:S(2)}, u32[]{:S(2)}) collective-permute-start(bf16[256,256]{1,0:T(8,128)(2,1)S(1)} %add.50.a_ref), channel_id=1, source_target_pairs={{0,4},{4,0},{8,12},{12,8},{1,5},{5,1},{9,13},{13,9},{2,6},{6,2},{1... | collective-permute-start | bytes 393224 | tf_op jit(solution)/shard_map/ppermute | solution.py:499
  26.4 3.5 %near.2 = (bf16[1024,256]{1,0:T(8,128)(2,1)S(1)}, bf16[1024,256]{1,0:T(8,128)(2,1)S(1)}, f32[1024,512]{1,0:T(8,128)S(1)}, s32[4]{0:T(128)S(1)}) custom-call(s32[4]{0:T(128)S(1)} %get-tuple-element.73.ids_ref, bf16[1024,1024]{1,0:T(8,128)(2,1)S(1)} %get-tuple-element.74.refs_0_, bf16[1024,512]{1,0:T(8,128)(2,1)S(1)} %copy-done.1, ...), custom_call_target="tpu_custom_call" | custom-call | flops 1048576 | bytes 1024 | tf_op jit(solution)/shard_map/near/pallas_call | solution.py:320
  29.9 2.5 %collective-permute-done.4.b_ref = bf16[256,256]{1,0:T(8,128)(2,1)S(1)} collective-permute-done((bf16[256,256]{1,0:T(8,128)(2,1)S(1)}, bf16[256,256]{1,0:T(8,128)(2,1)S(1)}, u32[]{:S(2)}, u32[]{:S(2)}) %collective-permute-start.4) | collective-permute-done | bytes 131104 | tf_op jit(solution)/shard_map/ppermute | solution.py:499
  32.5 0.1 collective-permute-start.7
  32.6 0.0 collective-permute-done.3.b_ref
  32.6 2.0 %collective-permute-start.6 = (bf16[256,256]{1,0:T(8,128)(2,1)S(1)}, bf16[256,256]{1,0:T(8,128)(2,1)S(1)}, u32[]{:S(2)}, u32[]{:S(2)}) collective-permute-start(bf16[256,256]{1,0:T(8,128)(2,1)S(1)} %add.52.a_ref), channel_id=1, source_target_pairs={{0,8},{4,12},{8,0},{12,4},{1,9},{5,13},{9,1},{13,5},{2,10},{6,14},... | collective-permute-start | bytes 393224 | tf_op jit(solution)/shard_map/ppermute | solution.py:499
  34.6 0.0 collective-permute-done.7.refs_5_
  34.7 1.6 %far.4 = (bf16[1024,128]{1,0:T(8,128)(2,1)S(1)}, s32[4]{0:T(128)S(1)}) custom-call(s32[4]{0:T(128)S(1)} %get-tuple-element.82.refs_0_, bf16[1024,256]{1,0:T(8,128)(2,1)S(1)} %get-tuple-element.83.refs_1_, f32[1024,512]{1,0:T(8,128)S(1)} %get-tuple-element.84.refs_2_, f32[4,512]{1,0:T(4,128)S(1)} %copy-done.2, bf16[256,256]{1,0:T(8,128)(2,1)S(1)} %add.53.refs_4_, ...), custom_call_target="tpu_custom_call" | custom-call | flops 1048576 | bytes 1024 | tf_op jit(solution)/shard_map/far/pallas_call | solution.py:393
  36.3 1.6 %collective-permute-start.9 = (bf16[1024,128]{1,0:T(8,128)(2,1)S(1)}, bf16[1024,128]{1,0:T(8,128)(2,1)S(1)}, u32[]{:S(2)}, u32[]{:S(2)}) collective-permute-start(bf16[1024,128]{1,0:T(8,128)(2,1)S(1)} %get-tuple-element.95.refs_7_.refs_1_), channel_id=1, source_target_pairs={{0,2},{2,0},{1,3},{3,1},{4,6},{6,4},{5,7},{7,5},{8,10},{10,8},{9,1... | collective-permute-start | bytes 786440 | tf_op jit(solution)/shard_map/ppermute | solution.py:504
  37.8 1.6 %far.5 = (bf16[1024,128]{1,0:T(8,128)(2,1)S(1)}, s32[4]{0:T(128)S(1)}) custom-call(s32[4]{0:T(128)S(1)} %get-tuple-element.86.refs_0_, bf16[1024,256]{1,0:T(8,128)(2,1)S(1)} %get-tuple-element.83.refs_1_, f32[1024,512]{1,0:T(8,128)S(1)} %get-tuple-element.84.refs_2_, f32[4,512]{1,0:T(4,128)S(1)} %copy-done.2, bf16[256,256]{1,0:T(8,128)(2,1)S(1)} %add.53.refs_4_, ...), custom_call_target="tpu_custom_call" | custom-call | flops 1048576 | bytes 1024 | tf_op jit(solution)/shard_map/far/pallas_call | solution.py:393
  39.5 0.6 collective-permute-start.12
  40.1 2.2 %near.3 = (bf16[1024,256]{1,0:T(8,128)(2,1)S(1)}, f32[1024,512]{1,0:T(8,128)S(1)}, s32[4]{0:T(128)S(1)}) custom-call(s32[4]{0:T(128)S(1)} %get-tuple-element.87.ids_ref, bf16[1024,256]{1,0:T(8,128)(2,1)S(1)} %get-tuple-element.88.refs_0_, bf16[512,256]{1,0:T(8,128)(2,1)S(1)} %collective-permute-done.1.b_ref.refs_2_.refs_1_, ...), custom_call_target="tpu_custom_call", output_to_operand_aliasing={{0}: (1, {})} | custom-call | flops 1048576 | bytes 1024 | tf_op jit(solution)/shard_map/near/pallas_call | solution.py:320
  42.3 0.0 copy-start.3
  42.4 0.1 collective-permute-start.8
  42.4 3.2 %collective-permute-done.9.refs_6_.refs_5_ = bf16[1024,128]{1,0:T(8,128)(2,1)S(1)} collective-permute-done((bf16[1024,128]{1,0:T(8,128)(2,1)S(1)}, bf16[1024,128]{1,0:T(8,128)(2,1)S(1)}, u32[]{:S(2)}, u32[]{:S(2)}) %collective-permute-start.9) | collective-permute-done | bytes 262176 | tf_op jit(solution)/shard_map/ppermute | solution.py:504
  45.6 0.0 collective-permute-done.8.refs_5_
  45.6 1.6 %far.6 = (bf16[1024,128]{1,0:T(8,128)(2,1)S(1)}, s32[4]{0:T(128)S(1)}) custom-call(s32[4]{0:T(128)S(1)} %get-tuple-element.91.refs_0_, bf16[1024,256]{1,0:T(8,128)(2,1)S(1)} %get-tuple-element.92.refs_1_, f32[1024,512]{1,0:T(8,128)S(1)} %get-tuple-element.93.refs_2_, f32[4,512]{1,0:T(4,128)S(1)} %copy-done.2, bf16[256,256]{1,0:T(8,128)(2,1)S(1)} %add.54.refs_4_, ...), custom_call_target="tpu_custom_call" | custom-call | flops 1048576 | bytes 1024 | tf_op jit(solution)/shard_map/far/pallas_call | solution.py:393
  47.2 0.0 copy-start
  47.2 1.9 %far.7 = (bf16[1024,128]{1,0:T(8,128)(2,1)S(1)}, f32[32,512]{1,0:T(8,128)S(1)}, bf16[32,512]{1,0:T(8,128)(2,1)S(1)}, s32[4]{0:T(128)}) custom-call(s32[4]{0:T(128)S(1)} %get-tuple-element.97.refs_0_, bf16[1024,256]{1,0:T(8,128)(2,1)S(1)} %get-tuple-element.92.refs_1_, f32[1024,512]{1,0:T(8,128)S(1)} %get-tuple-element.93.refs_2_, f32[4,512]{1,0:T(4,128)S(1)} %copy-done.2, ...), custom_call_target="tpu_custom_call" | custom-call | flops 1048576 | bytes 1024 | tf_op jit(solution)/shard_map/far/pallas_call | solution.py:393
  49.1 1.6 %collective-permute-start.11 = (bf16[1024,128]{1,0:T(8,128)(2,1)S(1)}, bf16[1024,128]{1,0:T(8,128)(2,1)S(1)}, u32[]{:S(2)}, u32[]{:S(2)}) collective-permute-start(bf16[1024,128]{1,0:T(8,128)(2,1)S(1)} %get-tuple-element.99.refs_4_), channel_id=1, source_target_pairs={{0,2},{2,0},{1,3},{3,1},{4,6},{6,4},{5,7},{7,5},{8,10},{10,8},{9,1... | collective-permute-start | bytes 786440 | tf_op jit(solution)/shard_map/ppermute | solution.py:504
  50.7 0.5 collective-permute-start.10
  51.2 1.2 %collective-permute-done.13.got_ref = bf16[32,512]{1,0:T(8,128)(2,1)S(1)} collective-permute-done((bf16[32,512]{1,0:T(8,128)(2,1)S(1)}, bf16[32,512]{1,0:T(8,128)(2,1)S(1)}, u32[]{:S(2)}, u32[]{:S(2)}) %collective-permute-start.13) | collective-permute-done | bytes 32800 | tf_op jit(solution)/shard_map/ppermute | solution.py:499
  52.4 1.2 %collective-permute-start.14 = (bf16[8,512]{1,0:T(8,128)(2,1)S(1)}, bf16[8,512]{1,0:T(8,128)(2,1)S(1)}, u32[]{:S(2)}, u32[]{:S(2)}) collective-permute-start(bf16[8,512]{1,0:T(8,128)(2,1)S(1)} %get-tuple-element.104), channel_id=1, source_target_pairs={{0,4},{4,8},{8,12},{12,0},{1,5},{5,9},{9,13},{13,1},{2,6},{6,10},{... | collective-permute-start | bytes 24584 | tf_op jit(solution)/shard_map/ppermute | solution.py:625
  53.6 1.0 %collective-permute-start.15 = (bf16[8,512]{1,0:T(8,128)(2,1)S(1)}, bf16[8,512]{1,0:T(8,128)(2,1)S(1)}, u32[]{:S(2)}, u32[]{:S(2)}) collective-permute-start(bf16[8,512]{1,0:T(8,128)(2,1)S(1)} %get-tuple-element.105), channel_id=1, source_target_pairs={{0,8},{4,12},{8,0},{12,4},{1,9},{5,13},{9,1},{13,5},{2,10},{6,14},... | collective-permute-start | bytes 24584 | tf_op jit(solution)/shard_map/ppermute | solution.py:625
  54.6 0.0 collective-permute-done.12.refs_6_
  54.6 1.7 %collective-permute-start.16 = (bf16[8,512]{1,0:T(8,128)(2,1)S(1)}, bf16[8,512]{1,0:T(8,128)(2,1)S(1)}, u32[]{:S(2)}, u32[]{:S(2)}) collective-permute-start(bf16[8,512]{1,0:T(8,128)(2,1)S(1)} %get-tuple-element.106), channel_id=1, source_target_pairs={{0,12},{4,0},{8,4},{12,8},{1,13},{5,1},{9,5},{13,9},{2,14},{6,2},{... | collective-permute-start | bytes 24584 | tf_op jit(solution)/shard_map/ppermute | solution.py:625
  56.3 0.1 pad_add_fusion.2.refs_0_
  56.4 1.5 %out.2 = (f32[1024,512]{1,0:T(8,128)S(1)}, s32[1]{0:T(128)}) custom-call(s32[3]{0:T(128)S(1)} %pad_add_fusion.2.refs_0_, bf16[1024,128]{1,0:T(8,128)(2,1)S(1)} %get-tuple-element.95.refs_7_.refs_1_, bf16[1024,128]{1,0:T(8,128)(2,1)S(1)} %get-tuple-element.98.refs_8_.refs_2_, bf16[1024,128]{1,0:T(8,128)(2,1)S(1)} %get-tuple-element.96.refs_9_.refs_3_, ...), custom_call_target="tpu_custom_call" | custom-call | flops 1048576 | bytes 1024 | tf_op jit(solution)/shard_map/out/pallas_call | solution.py:440
  58.5 0.0 collective-permute-done.15.refs_1_
  58.5 0.0 collective-permute-done.16.refs_2_
  58.5 0.6 pool_own.1.refs_3_
  59.1 1.6 %collective-permute-start.17 = (bf16[8,512]{1,0:T(8,128)(2,1)S(1)}, bf16[8,512]{1,0:T(8,128)(2,1)S(1)}, u32[]{:S(2)}, u32[]{:S(2)}) collective-permute-start(bf16[8,512]{1,0:T(8,128)(2,1)S(1)} %pool_own.1.refs_3_), channel_id=1, source_target_pairs={{0,2},{2,0},{1,3},{3,1},{4,6},{6,4},{5,7},{7,5},{8,10},{10,8},{9,1... | collective-permute-start | bytes 24584 | tf_op jit(solution)/shard_map/ppermute | solution.py:504
  60.7 0.1 pad_add_fusion.refs_0_
  60.7 2.1 %collective-permute-done.17.refs_4_ = bf16[8,512]{1,0:T(8,128)(2,1)S(1)} collective-permute-done((bf16[8,512]{1,0:T(8,128)(2,1)S(1)}, bf16[8,512]{1,0:T(8,128)(2,1)S(1)}, u32[]{:S(2)}, u32[]{:S(2)}) %collective-permute-start.17) | collective-permute-done | bytes 8224 | tf_op jit(solution)/shard_map/ppermute | solution.py:504
  62.8 0.0 collective-permute-done.11.refs_2_
  62.8 0.0 collective-permute-done.10.refs_1_
  62.8 2.0 %out.3 = (bf16[1024,512]{1,0:T(8,128)(2,1)}, f32[8,512]{1,0:T(8,128)}, s32[1]{0:T(128)}) custom-call(s32[3]{0:T(128)S(1)} %pad_add_fusion.refs_0_, bf16[1024,128]{1,0:T(8,128)(2,1)S(1)} %collective-permute-done.10.refs_1_, bf16[1024,128]{1,0:T(8,128)(2,1)S(1)} %collective-permute-done.11.refs_2_, bf16[8,512]{1,0:T(8,128)(2,1)S(1)} %pool_own.1.refs_3_, ...), custom_call_target="tpu_custom_call" | custom-call | flops 1048576 | bytes 1024 | tf_op jit(solution)/shard_map/out/pallas_call | solution.py:440
  (17 shorter events, 0.2 us)
Async XLA Ops:
  0.7 13.2 %copy-start.2 = (f32[4,512]{1,0:T(4,128)S(1)}, f32[4,512]{1,0:T(4,128)}, u32[]{:S(2)}) copy-start(f32[4,512]{1,0:T(4,128)} %refs_3_.9) | copy-start | bytes 24580
  9.4 1.5 %collective-permute-start = (bf16[256,256]{1,0:T(8,128)(2,1)S(1)}, bf16[256,256]{1,0:T(8,128)(2,1)S(1)}, u32[]{:S(2)}, u32[]{:S(2)}) collective-permute-start(bf16[256,256]{1,0:T(8,128)(2,1)S(1)} %get-tuple-element.57), channel_id=1, source_target_pairs={{0,1},{1,0},{2,3},{3,2},{4,5},{5,4},{6,7},{7,6},{8,9},{9,8},{10,11... | collective-permute-start | bytes 393224 | tf_op jit(solution)/shard_map/ppermute | solution.py:499
  10.9 9.3 %collective-permute-start.2 = (bf16[256,256]{1,0:T(8,128)(2,1)S(1)}, bf16[256,256]{1,0:T(8,128)(2,1)S(1)}, u32[]{:S(2)}, u32[]{:S(2)}) collective-permute-start(bf16[256,256]{1,0:T(8,128)(2,1)S(1)} %add.49.a_ref), channel_id=1, source_target_pairs={{0,4},{4,0},{8,12},{12,8},{1,5},{5,1},{9,13},{13,9},{2,6},{6,2},{1... | collective-permute-start | bytes 393224 | tf_op jit(solution)/shard_map/ppermute | solution.py:499
  19.3 4.9 %collective-permute-start.1 = (bf16[512,256]{1,0:T(8,128)(2,1)S(1)}, bf16[512,256]{1,0:T(8,128)(2,1)S(1)}, u32[]{:S(2)}, u32[]{:S(2)}) collective-permute-start(bf16[512,256]{1,0:T(8,128)(2,1)S(1)} %get-tuple-element.65), channel_id=1, source_target_pairs={{0,1},{1,0},{2,3},{3,2},{4,5},{5,4},{6,7},{7,6},{8,9},{9,8},{10,11... | collective-permute-start | bytes 786440 | tf_op jit(solution)/shard_map/ppermute | solution.py:499
  19.4 7.0 %collective-permute-start.5 = (bf16[256,256]{1,0:T(8,128)(2,1)S(1)}, bf16[256,256]{1,0:T(8,128)(2,1)S(1)}, u32[]{:S(2)}, u32[]{:S(2)}) collective-permute-start(bf16[256,256]{1,0:T(8,128)(2,1)S(1)} %get-tuple-element.75), channel_id=1, source_target_pairs={{1,4},{5,8},{9,12},{4,1},{8,5},{12,9},{3,6},{7,10},{11,14},{6,3},{... | collective-permute-start | bytes 393224 | tf_op jit(solution)/shard_map/ppermute | solution.py:581
  20.3 6.2 %copy-start.1 = (bf16[1024,512]{1,0:T(8,128)(2,1)S(1)}, bf16[1024,512]{1,0:T(8,128)(2,1)}, u32[]{:S(2)}) copy-start(bf16[1024,512]{1,0:T(8,128)(2,1)} %refs_1_.3) | copy-start | bytes 3145732
  20.3 12.1 %collective-permute-start.4 = (bf16[256,256]{1,0:T(8,128)(2,1)S(1)}, bf16[256,256]{1,0:T(8,128)(2,1)S(1)}, u32[]{:S(2)}, u32[]{:S(2)}) collective-permute-start(bf16[256,256]{1,0:T(8,128)(2,1)S(1)} %add.51.a_ref), channel_id=1, source_target_pairs={{0,8},{4,12},{8,0},{12,4},{1,9},{5,13},{9,1},{13,5},{2,10},{6,14},... | collective-permute-start | bytes 393224 | tf_op jit(solution)/shard_map/ppermute | solution.py:499
  24.3 8.3 %collective-permute-start.3 = (bf16[256,256]{1,0:T(8,128)(2,1)S(1)}, bf16[256,256]{1,0:T(8,128)(2,1)S(1)}, u32[]{:S(2)}, u32[]{:S(2)}) collective-permute-start(bf16[256,256]{1,0:T(8,128)(2,1)S(1)} %add.50.a_ref), channel_id=1, source_target_pairs={{0,4},{4,0},{8,12},{12,8},{1,5},{5,1},{9,13},{13,9},{2,6},{6,2},{1... | collective-permute-start | bytes 393224 | tf_op jit(solution)/shard_map/ppermute | solution.py:499
  32.5 2.2 %collective-permute-start.7 = (bf16[256,256]{1,0:T(8,128)(2,1)S(1)}, bf16[256,256]{1,0:T(8,128)(2,1)S(1)}, u32[]{:S(2)}, u32[]{:S(2)}) collective-permute-start(bf16[256,256]{1,0:T(8,128)(2,1)S(1)} %add.53.refs_4_), channel_id=1, source_target_pairs={{0,1},{1,0},{2,3},{3,2},{4,5},{5,4},{6,7},{7,6},{8,9},{9,8},{10,11... | collective-permute-start | bytes 393224 | tf_op jit(solution)/shard_map/ppermute | solution.py:499
  32.6 9.7 %collective-permute-start.6 = (bf16[256,256]{1,0:T(8,128)(2,1)S(1)}, bf16[256,256]{1,0:T(8,128)(2,1)S(1)}, u32[]{:S(2)}, u32[]{:S(2)}) collective-permute-start(bf16[256,256]{1,0:T(8,128)(2,1)S(1)} %add.52.a_ref), channel_id=1, source_target_pairs={{0,8},{4,12},{8,0},{12,4},{1,9},{5,13},{9,1},{13,5},{2,10},{6,14},... | collective-permute-start | bytes 393224 | tf_op jit(solution)/shard_map/ppermute | solution.py:499
  36.3 9.3 %collective-permute-start.9 = (bf16[1024,128]{1,0:T(8,128)(2,1)S(1)}, bf16[1024,128]{1,0:T(8,128)(2,1)S(1)}, u32[]{:S(2)}, u32[]{:S(2)}) collective-permute-start(bf16[1024,128]{1,0:T(8,128)(2,1)S(1)} %get-tuple-element.95.refs_7_.refs_1_), channel_id=1, source_target_pairs={{0,2},{2,0},{1,3},{3,1},{4,6},{6,4},{5,7},{7,5},{8,10},{10,8},{9,1... | collective-permute-start | bytes 786440 | tf_op jit(solution)/shard_map/ppermute | solution.py:504
  39.5 15.2 %collective-permute-start.12 = (bf16[1024,128]{1,0:T(8,128)(2,1)S(1)}, bf16[1024,128]{1,0:T(8,128)(2,1)S(1)}, u32[]{:S(2)}, u32[]{:S(2)}) collective-permute-start(bf16[1024,128]{1,0:T(8,128)(2,1)S(1)} %get-tuple-element.98.refs_8_.refs_2_), channel_id=1, source_target_pairs={{0,2},{2,0},{1,3},{3,1},{4,6},{6,4},{5,7},{7,5},{8,10},{10,8},{9,1... | collective-permute-start | bytes 786440 | tf_op jit(solution)/shard_map/ppermute | solution.py:504
  42.3 4.9 %copy-start.3 = (s32[64,2]{0,1:T(2,128)S(1)}, s32[64,2]{0,1:T(2,128)}, u32[]{:S(2)}) copy-start(s32[64,2]{0,1:T(2,128)} %param.17) | copy-start | bytes 1540
  42.4 3.2 %collective-permute-start.8 = (bf16[256,256]{1,0:T(8,128)(2,1)S(1)}, bf16[256,256]{1,0:T(8,128)(2,1)S(1)}, u32[]{:S(2)}, u32[]{:S(2)}) collective-permute-start(bf16[256,256]{1,0:T(8,128)(2,1)S(1)} %add.54.refs_4_), channel_id=1, source_target_pairs={{0,1},{1,0},{2,3},{3,2},{4,5},{5,4},{6,7},{7,6},{8,9},{9,8},{10,11... | collective-permute-start | bytes 393224 | tf_op jit(solution)/shard_map/ppermute | solution.py:499
  47.2 9.2 %copy-start = (bf16[1024,512]{1,0:T(8,128)(2,1)S(1)}, bf16[1024,512]{1,0:T(8,128)(2,1)}, u32[]{:S(2)}) copy-start(bf16[1024,512]{1,0:T(8,128)(2,1)} %refs_5_.3) | copy-start | bytes 3145732
  49.1 13.7 %collective-permute-start.11 = (bf16[1024,128]{1,0:T(8,128)(2,1)S(1)}, bf16[1024,128]{1,0:T(8,128)(2,1)S(1)}, u32[]{:S(2)}, u32[]{:S(2)}) collective-permute-start(bf16[1024,128]{1,0:T(8,128)(2,1)S(1)} %get-tuple-element.99.refs_4_), channel_id=1, source_target_pairs={{0,2},{2,0},{1,3},{3,1},{4,6},{6,4},{5,7},{7,5},{8,10},{10,8},{9,1... | collective-permute-start | bytes 786440 | tf_op jit(solution)/shard_map/ppermute | solution.py:504
  50.7 12.2 %collective-permute-start.10 = (bf16[1024,128]{1,0:T(8,128)(2,1)S(1)}, bf16[1024,128]{1,0:T(8,128)(2,1)S(1)}, u32[]{:S(2)}, u32[]{:S(2)}) collective-permute-start(bf16[1024,128]{1,0:T(8,128)(2,1)S(1)} %get-tuple-element.96.refs_9_.refs_3_), channel_id=1, source_target_pairs={{0,2},{2,0},{1,3},{3,1},{4,6},{6,4},{5,7},{7,5},{8,10},{10,8},{9,1... | collective-permute-start | bytes 786440 | tf_op jit(solution)/shard_map/ppermute | solution.py:504
  51.2 1.2 %collective-permute-start.13 = (bf16[32,512]{1,0:T(8,128)(2,1)S(1)}, bf16[32,512]{1,0:T(8,128)(2,1)S(1)}, u32[]{:S(2)}, u32[]{:S(2)}) collective-permute-start(bf16[32,512]{1,0:T(8,128)(2,1)S(1)} %get-tuple-element.102), channel_id=1, source_target_pairs={{0,1},{1,0},{2,3},{3,2},{4,5},{5,4},{6,7},{7,6},{8,9},{9,8},{10,11... | collective-permute-start | bytes 98312 | tf_op jit(solution)/shard_map/ppermute | solution.py:499
  52.4 6.1 %collective-permute-start.14 = (bf16[8,512]{1,0:T(8,128)(2,1)S(1)}, bf16[8,512]{1,0:T(8,128)(2,1)S(1)}, u32[]{:S(2)}, u32[]{:S(2)}) collective-permute-start(bf16[8,512]{1,0:T(8,128)(2,1)S(1)} %get-tuple-element.104), channel_id=1, source_target_pairs={{0,4},{4,8},{8,12},{12,0},{1,5},{5,9},{9,13},{13,1},{2,6},{6,10},{... | collective-permute-start | bytes 24584 | tf_op jit(solution)/shard_map/ppermute | solution.py:625
  53.6 4.9 %collective-permute-start.15 = (bf16[8,512]{1,0:T(8,128)(2,1)S(1)}, bf16[8,512]{1,0:T(8,128)(2,1)S(1)}, u32[]{:S(2)}, u32[]{:S(2)}) collective-permute-start(bf16[8,512]{1,0:T(8,128)(2,1)S(1)} %get-tuple-element.105), channel_id=1, source_target_pairs={{0,8},{4,12},{8,0},{12,4},{1,9},{5,13},{9,1},{13,5},{2,10},{6,14},... | collective-permute-start | bytes 24584 | tf_op jit(solution)/shard_map/ppermute | solution.py:625
  54.6 3.9 %collective-permute-start.16 = (bf16[8,512]{1,0:T(8,128)(2,1)S(1)}, bf16[8,512]{1,0:T(8,128)(2,1)S(1)}, u32[]{:S(2)}, u32[]{:S(2)}) collective-permute-start(bf16[8,512]{1,0:T(8,128)(2,1)S(1)} %get-tuple-element.106), channel_id=1, source_target_pairs={{0,12},{4,0},{8,4},{12,8},{1,13},{5,1},{9,5},{13,9},{2,14},{6,2},{... | collective-permute-start | bytes 24584 | tf_op jit(solution)/shard_map/ppermute | solution.py:625
  59.1 3.7 %collective-permute-start.17 = (bf16[8,512]{1,0:T(8,128)(2,1)S(1)}, bf16[8,512]{1,0:T(8,128)(2,1)S(1)}, u32[]{:S(2)}, u32[]{:S(2)}) collective-permute-start(bf16[8,512]{1,0:T(8,128)(2,1)S(1)} %pool_own.1.refs_3_), channel_id=1, source_target_pairs={{0,2},{2,0},{1,3},{3,1},{4,6},{6,4},{5,7},{7,5},{8,10},{10,8},{9,1... | collective-permute-start | bytes 24584 | tf_op jit(solution)/shard_map/ppermute | solution.py:504
